TPU v7x, 256 devices: a whole 4x4x8 slice. The times are simulated.
256 devices in a mesh: grp: 8 (over x, y_hi), tile: 32 (over y_lo, z, core).
Axes of the slice: x: 4, y: 4 (y_hi: 2, y_lo: 2; y = y_hi * 2 + y_lo), z: 8, core: 2. Of those that a mesh axis runs over, the one named last changes fastest.
Arguments:
- adjoint_in: float32 [262144, 128], P(('grp', 'tile')), may hold values from -6 to 6
- departure: int32 [2, 262144], P(None, ('grp', 'tile')), may hold values from 0 to 262143, as said below
- fraction: float32 [2, 262144], P(None, ('grp', 'tile')), may hold values from 0 to 1
- level_map: float32 [2, 128, 128], replicated, may hold values from -0.5 to 0.5
- coarse_map: float32 [128, 8, 8], replicated, may hold values from -2 to 2
Outputs:
- adjoint_out: float32 [262144, 128], P(('grp', 'tile'))
Inputs may be any that keep to these rules, and one draw needn't show every extreme that they name: For each step, the departure cell of a column lies in the same block row, on the device whose tile index differs from the column's own by at most 2, counted periodically along tile. Of the columns of one device, at most 512 have departure cells on any one device, and on every device exactly 512 of them share one device.
All inputs are finite; a program needn't handle non-finite values.
Results may differ from a plain program's by a relative error of at most 0.00013.
Values sent between devices are 32-bit elements; how exact they have to be, the bound alone decides.
No kernel may reach another device: no remote copies, remote signals or barrier semaphores. Data moves between devices by JAX's collectives and lax.ppermute only.
A program may use at most 64 MiB of HBM per device.

v0:
```python
import functools

import jax
import jax.numpy as jnp
from jax import lax
from jax.experimental import pallas as pl
from jax.experimental.pallas import tpu as pltpu
from jax.sharding import PartitionSpec as P

REACH = 2
SHIFTS = (-2, 2, -1, 1)
COLS = 1024
LEV = 128
CAP = 512
ROWS = CAP + 16
BF = jnp.bfloat16
F32 = jnp.float32


def shifted(x, axis, by):
    length = lax.axis_size(axis)
    return lax.ppermute(x, axis, [(i, (i + by) % length) for i in range(length)])


def halves(x):
    high = x.astype(BF)
    low = (x - high.astype(F32)).astype(BF)
    return high, low


def dot(a, b):
    return lax.dot_general(a, b, (((1,), (0,)), ((), ())), preferred_element_type=F32)


def dot_nt(a, b):
    return lax.dot_general(a, b, (((1,), (1,)), ((), ())), preferred_element_type=F32)


def cubic_weights(a):
    return (
        -a * (1.0 - a) * (2.0 - a) * (1.0 / 6.0),
        (1.0 + a) * (1.0 - a) * (2.0 - a) * 0.5,
        (1.0 + a) * a * (2.0 - a) * 0.5,
        -(1.0 + a) * a * (1.0 - a) * (1.0 / 6.0),
    )


def locate(departure, tile_self, tile_count):
    place = departure % COLS
    target = (departure // COLS) % tile_count
    offset = (target - tile_self + REACH + tile_count) % tile_count - REACH
    return place, offset


def slots_of(offset):
    row = lax.broadcasted_iota(jnp.int32, (8, LEV), 0)
    lane_a = lax.broadcasted_iota(jnp.int32, (LEV, LEV), 0)
    lane_b = lax.broadcasted_iota(jnp.int32, (LEV, LEV), 1)
    before = jnp.where(lane_a < lane_b, 1.0, 0.0).astype(BF)
    number = jnp.full((1, COLS), 4, jnp.int32)
    for which, shift in enumerate(SHIFTS):
        number = jnp.where(offset == shift, which, number)
    members = []
    for c in range(COLS // LEV):
        part = number[:, c * LEV : (c + 1) * LEV]
        members.append(jnp.where(row == part, 1.0, 0.0))
    member = jnp.concatenate(members, axis=0)
    inside = dot(member.astype(BF), before)
    totals = jnp.sum(member, axis=1, keepdims=True)
    start = jnp.zeros((8, 1), F32)
    keys = []
    for c in range(COLS // LEV):
        block = slice(8 * c, 8 * c + 8)
        rank = inside[block] + start
        start = start + totals[block]
        key = jnp.sum(member[block] * (rank + row.astype(F32) * CAP), axis=0, keepdims=True)
        keys.append(key)
    return jnp.concatenate(keys, axis=1).astype(jnp.int32)


def spill_rows(place, offset, weights):
    row = lax.broadcasted_iota(jnp.int32, (8, COLS), 0)
    last = place == COLS - 1
    first_a = jnp.where(last, weights[2], jnp.where(place == COLS - 2, weights[3], 0.0))
    first_b = jnp.where(last, weights[3], 0.0)
    end = jnp.where(place == 0, weights[0], 0.0)
    rows = jnp.where(row == 0, first_a, jnp.where(row == 1, first_b, jnp.where(row == 7, end, 0.0)))
    spread = [jnp.where(offset == o, rows, 0.0) for o in range(-REACH, REACH + 1)]
    high, low = halves(jnp.concatenate(spread, axis=0))
    return jnp.concatenate([high, low], axis=0)


def meta_rows(place, fraction):
    a = fraction.astype(BF)
    rest = fraction - a.astype(F32)
    b = rest.astype(BF)
    c = rest - b.astype(F32)
    p_high = (place // 32).astype(F32)
    p_low = (place % 32).astype(F32)
    row = lax.broadcasted_iota(jnp.int32, (8, COLS), 0)
    out = jnp.where(row == 0, a.astype(F32), 0.0)
    out = jnp.where(row == 1, b.astype(F32), out)
    out = jnp.where(row == 2, c, out)
    out = jnp.where(row == 3, p_high, out)
    out = jnp.where(row == 4, p_low, out)
    return out.astype(BF)


def choose(keys, which):
    slot = lax.broadcasted_iota(jnp.int32, (CAP, COLS), 0) + which * CAP
    return jnp.where(slot == keys, 1.0, 0.0).astype(BF)


def spill_block(spilled, target):
    row = lax.broadcasted_iota(jnp.int32, (8, LEV), 0)
    out = jnp.zeros((8, LEV), F32)
    for o in (target - 1, target + 1):
        if -REACH <= o <= REACH:
            block = spilled[8 * (o + REACH) : 8 * (o + REACH) + 8]
            keep = row < 2 if o == target - 1 else row == 7
            out = out + jnp.where(keep, block, 0.0)
    return out


def spill_sums(spills, both):
    wide = dot(spills, both)
    count = 8 * (2 * REACH + 1)
    return (wide[:count, :LEV] + wide[:count, LEV:]) + (wide[count:, :LEV] + wide[count:, LEV:])


def index_values(self_ref, departure, fraction, tile_count):
    place, offset = locate(departure, self_ref[0], tile_count)
    keys = slots_of(offset)
    weights = cubic_weights(fraction)
    return place, offset, keys, weights


def write_meta(meta_out, base, meta, one_hot):
    got = dot_nt(meta, one_hot)
    fraction = got[0:1] + got[1:2] + got[2:3]
    place = got[3:4] * 32.0 + got[4:5]
    for c in range(CAP // LEV):
        meta_out[base + c : base + c + 1, :] = fraction[:, c * LEV : (c + 1) * LEV]
        meta_out[base + 4 + c : base + 5 + c, :] = place[:, c * LEV : (c + 1) * LEV]


def pack_payload(out, one_hot, both, spilled, shift):
    wide = dot(one_hot, both)
    out[0:CAP, :] = wide[:, :LEV] + wide[:, LEV:]
    out[CAP : CAP + 8, :] = spill_block(spilled, shift)


def first_pack_kernel(tile_count, self_ref, field, departure, fraction, *outs):
    place, offset, keys, weights = index_values(self_ref, departure[1:2, :], fraction[1:2, :], tile_count)
    meta = meta_rows(place, fraction[1:2, :])
    high, low = halves(field[...])
    both = jnp.concatenate([high, low], axis=1)
    spilled = spill_sums(spill_rows(place, offset, weights), both)
    outs[4][...] = spill_block(spilled, -3)
    outs[5][...] = spill_block(spilled, 3)
    outs[6][...] = spill_block(spilled, 0)
    for which, shift in enumerate(SHIFTS):
        one_hot = choose(keys, which)
        pack_payload(outs[which], one_hot, both, spilled, shift)
        write_meta(outs[which], CAP + 8, meta, one_hot)


def index_kernel(tile_count, self_ref, departure, fraction, keys_out, spill_out, meta_out):
    place, offset, keys, weights = index_values(self_ref, departure[0:1, :], fraction[0:1, :], tile_count)
    meta = meta_rows(place, fraction[0:1, :])
    keys_out[...] = keys
    spill_out[...] = spill_rows(place, offset, weights)
    for which in range(len(SHIFTS)):
        write_meta(meta_out, 8 * which, meta, choose(keys, which))


def second_pack_kernel(field, keys, spills, meta, *outs):
    high, low = halves(field[...])
    both = jnp.concatenate([high, low], axis=1)
    spilled = spill_sums(spills[...], both)
    outs[4][...] = spill_block(spilled, -3)
    outs[5][...] = spill_block(spilled, 3)
    outs[6][...] = spill_block(spilled, 0)
    for which, shift in enumerate(SHIFTS):
        pack_payload(outs[which], choose(keys[...], which), both, spilled, shift)
        outs[which][CAP + 8 : CAP + 16, :] = meta[8 * which : 8 * which + 8, :]


BLOCK = 128


def spread_block(first_cell, places, weights):
    cells = lax.broadcasted_iota(jnp.int32, (BLOCK, places.shape[1]), 0)
    distance = cells - (places - 1 - first_cell)
    spread = jnp.where(distance == 0, weights[0], 0.0)
    for k in (1, 2, 3):
        spread = jnp.where(distance == k, weights[k], spread)
    return halves(spread)


def own_kernel(step, tile_count, self_ref, field, departure, fraction, spilled, out, both_ref):
    departure = departure[step : step + 1, :]
    fraction = fraction[step : step + 1, :]
    place, offset = locate(departure, self_ref[0], tile_count)
    weights = [jnp.where(offset == 0, w, 0.0) for w in cubic_weights(fraction)]
    high, low = halves(field[...])
    both_ref[:, :LEV] = high
    both_ref[:, LEV:] = low

    @pl.loop(0, COLS // BLOCK)
    def _(b):
        high, low = spread_block(b * BLOCK, place, weights)
        wide = dot(high, both_ref[...]) + dot(low, both_ref[...])
        out[pl.ds(b * BLOCK, BLOCK), :] = wide[:, :LEV] + wide[:, LEV:]

    add_spill(out, spilled[...])


def add_spill(out, block):
    row = lax.broadcasted_iota(jnp.int32, (8, LEV), 0)
    out[0:8, :] = out[0:8, :] + jnp.where(row < 2, block, 0.0)
    out[COLS - 8 : COLS, :] = out[COLS - 8 : COLS, :] + jnp.where(row == 7, block, 0.0)


def deposit_kernel(step, own, p0, p1, p2, p3, tiny_a, tiny_b, level_map, out, both_ref, sum_ref):
    payloads = (p0, p1, p2, p3)
    spill = tiny_a[...] + tiny_b[...]
    for which, payload in enumerate(payloads):
        high, low = halves(payload[0:CAP, :])
        both_ref[which, :, :LEV] = high
        both_ref[which, :, LEV:] = low
        spill = spill + payload[CAP : CAP + 8, :]
    tables = []
    for payload in payloads:
        rows = [payload[CAP + 8 + c : CAP + 9 + c, :] for c in range(8)]
        fraction = jnp.concatenate(rows[:4], axis=1)
        place = jnp.concatenate(rows[4:], axis=1).astype(jnp.int32)
        tables.append((place, cubic_weights(fraction)))

    @pl.loop(0, COLS // BLOCK)
    def _(b):
        wide = jnp.zeros((BLOCK, 2 * LEV), F32)
        for which in range(4):
            place, weights = tables[which]
            high, low = spread_block(b * BLOCK, place, weights)
            wide = wide + dot(high, both_ref[which]) + dot(low, both_ref[which])
        sum_ref[pl.ds(b * BLOCK, BLOCK), :] = own[pl.ds(b * BLOCK, BLOCK), :] + wide[:, :LEV] + wide[:, LEV:]

    add_spill(sum_ref, spill)
    map_high, map_low = halves(level_map[step])
    high, low = halves(sum_ref[...])
    out[...] = dot_nt(high, map_high) + (dot_nt(high, map_low) + dot_nt(low, map_high))


def couple_kernel(table, x, out):
    count = x.shape[0]

    @pl.loop(0, x.shape[1] // 8)
    def _(r):
        rows = [x[e, pl.ds(r * 8, 8), :] for e in range(count)]
        for b in range(count):
            total = rows[0] * table[count * b : count * b + 1, :]
            for e in range(1, count):
                total = total + rows[e] * table[count * b + e : count * b + e + 1, :]
            out[b, pl.ds(r * 8, 8), :] = total


VM = pl.BlockSpec(memory_space=pltpu.MemorySpace.VMEM)
SM = pl.BlockSpec(memory_space=pltpu.MemorySpace.SMEM)
PARAMS = pltpu.CompilerParams(vmem_limit_bytes=40 * 1024 * 1024)
PACKED = [jax.ShapeDtypeStruct((ROWS, LEV), F32)] * 4 + [jax.ShapeDtypeStruct((8, LEV), F32)] * 3


def call(kernel, out_shape, in_specs, scratch=()):
    multiple = isinstance(out_shape, (list, tuple))
    return pl.pallas_call(
        kernel,
        out_shape=out_shape,
        in_specs=in_specs,
        out_specs=[VM] * len(out_shape) if multiple else VM,
        scratch_shapes=list(scratch),
        compiler_params=PARAMS,
    )


def send(packed):
    tiny = [shifted(packed[4], "tile", -3), shifted(packed[5], "tile", 3)]
    return [shifted(packed[w], "tile", s) for w, s in enumerate(SHIFTS)] + tiny


def own_part(step, tile_count, tile_self, field, departure, fraction, spilled):
    return call(
        functools.partial(own_kernel, step, tile_count),
        jax.ShapeDtypeStruct((COLS, LEV), F32),
        [SM, VM, VM, VM, VM],
        [pltpu.VMEM((COLS, 2 * LEV), BF)],
    )(tile_self, field, departure, fraction, spilled)


def deposited(step, own, arrived, level_map):
    return call(
        functools.partial(deposit_kernel, step),
        jax.ShapeDtypeStruct((COLS, LEV), F32),
        [VM] * 8,
        [pltpu.VMEM((4, CAP, 2 * LEV), BF), pltpu.VMEM((COLS, LEV), F32)],
    )(own, *arrived, level_map)


def body(adjoint_in, departure, fraction, level_map, coarse_map):
    tile_count = lax.axis_size("tile")
    groups = lax.axis_size("grp")
    tile_self = lax.axis_index("tile").astype(jnp.int32).reshape(1)
    packed = call(functools.partial(first_pack_kernel, tile_count), PACKED, [SM, VM, VM, VM])(
        tile_self, adjoint_in, departure, fraction
    )
    arrived = send(packed)
    own = own_part(1, tile_count, tile_self, adjoint_in, departure, fraction, packed[6])
    keys, spills, meta = call(
        functools.partial(index_kernel, tile_count),
        [
            jax.ShapeDtypeStruct((1, COLS), jnp.int32),
            jax.ShapeDtypeStruct((16 * (2 * REACH + 1), COLS), BF),
            jax.ShapeDtypeStruct((32, LEV), F32),
        ],
        [SM, VM, VM],
    )(tile_self, departure, fraction)
    table = coarse_map.transpose(1, 2, 0).reshape(groups * groups, LEV)
    second = deposited(1, own, arrived, level_map)

    parts = lax.all_to_all(second.reshape(groups, COLS // groups, LEV), "grp", 0, 0)
    mixed = call(couple_kernel, jax.ShapeDtypeStruct(parts.shape, F32), [VM, VM])(table, parts)
    coupled = lax.all_to_all(mixed, "grp", 0, 0).reshape(COLS, LEV)

    packed = call(second_pack_kernel, PACKED, [VM] * 4)(coupled, keys, spills, meta)
    arrived = send(packed)
    own = own_part(0, tile_count, tile_self, coupled, departure, fraction, packed[6])
    return deposited(0, own, arrived, level_map)


def solution(mesh):
    return jax.shard_map(
        body,
        mesh=mesh,
        in_specs=(
            P(("grp", "tile"), None),
            P(None, ("grp", "tile")),
            P(None, ("grp", "tile")),
            P(),
            P(),
        ),
        out_specs=P(("grp", "tile"), None),
        check_vma=False,
    )
```

profile of v0, /device:TPU:1, one launch (start us, length us, event | category | flops | bytes accessed | tf_op | source)
XLA Modules:
  0.0 87.8 jit_solution(12935248480031037121)
XLA Ops:
  0.0 0.0 copy-start
  0.0 1.0 %copy-done = f32[1024,128]{1,0:T(8,128)S(1)} copy-done((f32[1024,128]{1,0:T(8,128)S(1)}, f32[1024,128]{1,0:T(8,128)}, u32[]{:S(2)}) %copy-start) | copy-done | bytes 524312
  1.0 0.0 copy-start.2
  1.0 0.7 copy-done.2
  1.7 0.0 copy-start.4
  1.7 0.7 copy-done.4
  2.4 2.5 %shard_map.55 = (f32[528,128]{1,0:T(8,128)S(1)}, f32[528,128]{1,0:T(8,128)S(1)}, f32[528,128]{1,0:T(8,128)S(1)}, f32[528,128]{1,0:T(8,128)S(1)}, f32[8,128]{1,0:...) custom-call(s32[1]{0:T(128)} %bitcast.self_ref, f32[1024,128]{1,0:T(8,128)S(1)} %copy-done, ...), custom_call_target="tpu_custom_call" | custom-call | tf_op jit(solution)/shard_map/pallas_call | solution.py:313
  4.9 7.5 %collective-permute-start = (f32[528,128]{1,0:T(8,128)S(1)}, f32[528,128]{1,0:T(8,128)S(1)}, u32[]{:S(2)}, u32[]{:S(2)}) collective-permute-start(f32[528,128]{1,0:T(8,128)S(1)} %get-tuple-element.23), channel_id=1, source_target_pairs={{0,30},{1,31},{2,0},{3,1},{4,2},{5,3},{6,4},{7,5},{8,6},{9,7},{10,... | collective-permute-start | bytes 811016 | tf_op jit(solution)/shard_map/ppermute | solution.py:22
  12.4 0.0 collective-permute-start.1
  12.4 1.0 %collective-permute-start.2 = (f32[528,128]{1,0:T(8,128)S(1)}, f32[528,128]{1,0:T(8,128)S(1)}, u32[]{:S(2)}, u32[]{:S(2)}) collective-permute-start(f32[528,128]{1,0:T(8,128)S(1)} %get-tuple-element.25), channel_id=1, source_target_pairs={{0,31},{1,0},{2,1},{3,2},{4,3},{5,4},{6,5},{7,6},{8,7},{9,8},{10,9... | collective-permute-start | bytes 811016 | tf_op jit(solution)/shard_map/ppermute | solution.py:22
  13.4 0.8 collective-permute-start.3
  14.2 3.5 %collective-permute-start.4 = (f32[8,128]{1,0:T(8,128)S(1)}, f32[8,128]{1,0:T(8,128)S(1)}, u32[]{:S(2)}, u32[]{:S(2)}) collective-permute-start(f32[8,128]{1,0:T(8,128)S(1)} %get-tuple-element.27), channel_id=1, source_target_pairs={{0,29},{1,30},{2,31},{3,0},{4,1},{5,2},{6,3},{7,4},{8,5},{9,6},{10... | collective-permute-start | bytes 12296 | tf_op jit(solution)/shard_map/ppermute | solution.py:22
  17.6 1.2 %collective-permute-done.4.tiny_a = f32[8,128]{1,0:T(8,128)S(1)} collective-permute-done((f32[8,128]{1,0:T(8,128)S(1)}, f32[8,128]{1,0:T(8,128)S(1)}, u32[]{:S(2)}, u32[]{:S(2)}) %collective-permute-start.4) | collective-permute-done | bytes 4128 | tf_op jit(solution)/shard_map/ppermute | solution.py:22
  18.8 0.0 collective-permute-start.5
  18.9 0.0 copy-start.1
  18.9 3.0 %shard_map.56.own = f32[1024,128]{1,0:T(8,128)S(1)} custom-call(s32[1]{0:T(128)} %bitcast.self_ref, f32[1024,128]{1,0:T(8,128)S(1)} %copy-done, s32[2,1024]{1,0:T(2,128)S(1)} %copy-done.2, f32[2,1024]{1,0:T(2,128)S(1)} %copy-done.4, f32[8,128]{1,0:T(8,128)S(1)} %get-tuple-element.22.spilled), custom_call_target="tpu_custom_call" | custom-call | tf_op jit(solution)/shard_map/pallas_call | solution.py:292
  21.9 2.7 %collective-permute-done.5.tiny_b = f32[8,128]{1,0:T(8,128)S(1)} collective-permute-done((f32[8,128]{1,0:T(8,128)S(1)}, f32[8,128]{1,0:T(8,128)S(1)}, u32[]{:S(2)}, u32[]{:S(2)}) %collective-permute-start.5) | collective-permute-done | bytes 4128 | tf_op jit(solution)/shard_map/ppermute | solution.py:22
  24.6 0.0 collective-permute-done.p0
  24.6 0.0 collective-permute-done.1.p1
  24.6 0.0 collective-permute-done.2.p2
  24.6 0.0 collective-permute-done.3.p3
  24.6 0.0 copy-done.1
  24.6 6.0 %shard_map.57 = f32[1024,128]{1,0:T(8,128)S(1)} custom-call(f32[1024,128]{1,0:T(8,128)S(1)} %shard_map.56.own, f32[528,128]{1,0:T(8,128)S(1)} %collective-permute-done.p0, f32[528,128]{1,0:T(8,128)S(1)} %collective-permute-done.1.p1, f32[528,128]{1,0:T(8,128)S(1)} %collective-permute-done.2.p2, f32[528,128]{1,0:T(8,128)S(1)} %collective-permute-done.3.p3, ...), custom_call_target="tpu_custom_call" | custom-call | tf_op jit(solution)/shard_map/pallas_call | solution.py:301
  30.7 0.0 copy-start.6
  30.7 15.0 %all_to_all.10.x = f32[8,128,128]{2,1,0:T(8,128)S(1)} all-to-all(f32[8,128,128]{2,1,0:T(8,128)S(1)} %bitcast.8), channel_id=1, replica_groups=mesh['grp'=8,'tile'=32] {'grp'}, dimensions={0} | all-to-all | bytes 1048576 | tf_op jit(solution)/shard_map/all_to_all | solution.py:330
  45.7 0.0 copy-done.6
  45.7 1.2 %shard_map.58 = f32[8,128,128]{2,1,0:T(8,128)} custom-call(f32[64,128]{1,0:T(8,128)S(1)} %bitcast.9, f32[8,128,128]{2,1,0:T(8,128)S(1)} %all_to_all.10.x), custom_call_target="tpu_custom_call" | custom-call | tf_op jit(solution)/shard_map/pallas_call | solution.py:331
  46.8 0.0 copy-start.3
  46.8 0.0 copy-start.5
  46.8 3.6 %all-to-all-start.1 = ((f32[8,128,128]{2,1,0:T(8,128)}), f32[8,128,128]{2,1,0:T(8,128)S(1)}, u32[]{:S(2)}, u32[]{:S(2)}) async-start(f32[8,128,128]{2,1,0:T(8,128)} %shard_map.58), calls=%async_computation.1 | async-start | bytes 1048576 | tf_op jit(solution)/shard_map/all_to_all | solution.py:332
  50.5 0.0 copy-done.3
  50.5 0.0 copy-done.5
  50.5 1.4 %shard_map.59 = (s32[1,1024]{1,0:T(1,128)S(1)}, bf16[80,1024]{1,0:T(8,128)(2,1)S(1)}, f32[32,128]{1,0:T(8,128)S(1)}) custom-call(s32[1]{0:T(128)} %bitcast.self_ref, s32[2,1024]{1,0:T(2,128)S(1)} %copy-done.3, f32[2,1024]{1,0:T(2,128)S(1)} %copy-done.5), custom_call_target="tpu_custom_call" | custom-call | tf_op jit(solution)/shard_map/pallas_call | solution.py:318
  51.9 7.0 %all-to-all-done.1 = f32[8,128,128]{2,1,0:T(8,128)S(1)} async-done(((f32[8,128,128]{2,1,0:T(8,128)}), f32[8,128,128]{2,1,0:T(8,128)S(1)}, u32[]{:S(2)}, u32[]{:S(2)}) %all-to-all-start.1) | async-done | bytes 524320 | tf_op jit(solution)/shard_map/all_to_all | solution.py:332
  58.9 1.3 %shard_map.60 = (f32[528,128]{1,0:T(8,128)S(1)}, f32[528,128]{1,0:T(8,128)S(1)}, f32[528,128]{1,0:T(8,128)S(1)}, f32[528,128]{1,0:T(8,128)S(1)}, f32[8,128]{1,0:...) custom-call(f32[1024,128]{1,0:T(8,128)S(1)} %bitcast.6, s32[1,1024]{1,0:T(1,128)S(1)} %get-tuple-element.29.keys, ...), custom_call_target="tpu_custom_call" | custom-call | tf_op jit(solution)/shard_map/pallas_call | solution.py:334
  60.3 7.0 %collective-permute-start.6 = (f32[528,128]{1,0:T(8,128)S(1)}, f32[528,128]{1,0:T(8,128)S(1)}, u32[]{:S(2)}, u32[]{:S(2)}) collective-permute-start(f32[528,128]{1,0:T(8,128)S(1)} %get-tuple-element.33), channel_id=1, source_target_pairs={{0,30},{1,31},{2,0},{3,1},{4,2},{5,3},{6,4},{7,5},{8,6},{9,7},{10,... | collective-permute-start | bytes 811016 | tf_op jit(solution)/shard_map/ppermute | solution.py:22
  67.3 0.0 collective-permute-start.7
  67.3 1.3 %collective-permute-start.8 = (f32[528,128]{1,0:T(8,128)S(1)}, f32[528,128]{1,0:T(8,128)S(1)}, u32[]{:S(2)}, u32[]{:S(2)}) collective-permute-start(f32[528,128]{1,0:T(8,128)S(1)} %get-tuple-element.35), channel_id=1, source_target_pairs={{0,31},{1,0},{2,1},{3,2},{4,3},{5,4},{6,5},{7,6},{8,7},{9,8},{10,9... | collective-permute-start | bytes 811016 | tf_op jit(solution)/shard_map/ppermute | solution.py:22
  68.5 0.5 collective-permute-start.9
  69.0 3.1 %collective-permute-start.10 = (f32[8,128]{1,0:T(8,128)S(1)}, f32[8,128]{1,0:T(8,128)S(1)}, u32[]{:S(2)}, u32[]{:S(2)}) collective-permute-start(f32[8,128]{1,0:T(8,128)S(1)} %get-tuple-element.37), channel_id=1, source_target_pairs={{0,29},{1,30},{2,31},{3,0},{4,1},{5,2},{6,3},{7,4},{8,5},{9,6},{10... | collective-permute-start | bytes 12296 | tf_op jit(solution)/shard_map/ppermute | solution.py:22
  72.2 3.6 %collective-permute-done.10.tiny_a = f32[8,128]{1,0:T(8,128)S(1)} collective-permute-done((f32[8,128]{1,0:T(8,128)S(1)}, f32[8,128]{1,0:T(8,128)S(1)}, u32[]{:S(2)}, u32[]{:S(2)}) %collective-permute-start.10) | collective-permute-done | bytes 4128 | tf_op jit(solution)/shard_map/ppermute | solution.py:22
  75.8 0.0 collective-permute-start.11
  75.8 3.0 %shard_map.61.own = f32[1024,128]{1,0:T(8,128)S(1)} custom-call(s32[1]{0:T(128)} %bitcast.self_ref, f32[1024,128]{1,0:T(8,128)S(1)} %bitcast.7, s32[2,1024]{1,0:T(2,128)S(1)} %copy-done.3, f32[2,1024]{1,0:T(2,128)S(1)} %copy-done.5, f32[8,128]{1,0:T(8,128)S(1)} %get-tuple-element.32.spilled), custom_call_target="tpu_custom_call" | custom-call | tf_op jit(solution)/shard_map/pallas_call | solution.py:292
  78.8 2.1 %collective-permute-done.11.tiny_b = f32[8,128]{1,0:T(8,128)S(1)} collective-permute-done((f32[8,128]{1,0:T(8,128)S(1)}, f32[8,128]{1,0:T(8,128)S(1)}, u32[]{:S(2)}, u32[]{:S(2)}) %collective-permute-start.11) | collective-permute-done | bytes 4128 | tf_op jit(solution)/shard_map/ppermute | solution.py:22
  80.9 0.0 collective-permute-done.6.p0
  80.9 0.0 collective-permute-done.7.p1
  80.9 0.0 collective-permute-done.8.p2
  80.9 0.0 collective-permute-done.9.p3
  80.9 6.8 %shard_map.62 = f32[1024,128]{1,0:T(8,128)} custom-call(f32[1024,128]{1,0:T(8,128)S(1)} %shard_map.61.own, f32[528,128]{1,0:T(8,128)S(1)} %collective-permute-done.6.p0, f32[528,128]{1,0:T(8,128)S(1)} %collective-permute-done.7.p1, f32[528,128]{1,0:T(8,128)S(1)} %collective-permute-done.8.p2, f32[528,128]{1,0:T(8,128)S(1)} %collective-permute-done.9.p3, ...), custom_call_target="tpu_custom_call" | custom-call | tf_op jit(solution)/shard_map/pallas_call | solution.py:301
Async XLA Ops:
  0.0 1.0 %copy-start = (f32[1024,128]{1,0:T(8,128)S(1)}, f32[1024,128]{1,0:T(8,128)}, u32[]{:S(2)}) copy-start(f32[1024,128]{1,0:T(8,128)} %field.3) | copy-start | bytes 1572868
  1.0 0.7 copy-start.2
  1.7 0.7 copy-start.4
  4.9 19.7 %collective-permute-start = (f32[528,128]{1,0:T(8,128)S(1)}, f32[528,128]{1,0:T(8,128)S(1)}, u32[]{:S(2)}, u32[]{:S(2)}) collective-permute-start(f32[528,128]{1,0:T(8,128)S(1)} %get-tuple-element.23), channel_id=1, source_target_pairs={{0,30},{1,31},{2,0},{3,1},{4,2},{5,3},{6,4},{7,5},{8,6},{9,7},{10,... | collective-permute-start | bytes 811016 | tf_op jit(solution)/shard_map/ppermute | solution.py:22
  12.4 12.2 %collective-permute-start.1 = (f32[528,128]{1,0:T(8,128)S(1)}, f32[528,128]{1,0:T(8,128)S(1)}, u32[]{:S(2)}, u32[]{:S(2)}) collective-permute-start(f32[528,128]{1,0:T(8,128)S(1)} %get-tuple-element.24), channel_id=1, source_target_pairs={{0,2},{1,3},{2,4},{3,5},{4,6},{5,7},{6,8},{7,9},{8,10},{9,11},{10,... | collective-permute-start | bytes 811016 | tf_op jit(solution)/shard_map/ppermute | solution.py:22
  12.4 12.2 %collective-permute-start.2 = (f32[528,128]{1,0:T(8,128)S(1)}, f32[528,128]{1,0:T(8,128)S(1)}, u32[]{:S(2)}, u32[]{:S(2)}) collective-permute-start(f32[528,128]{1,0:T(8,128)S(1)} %get-tuple-element.25), channel_id=1, source_target_pairs={{0,31},{1,0},{2,1},{3,2},{4,3},{5,4},{6,5},{7,6},{8,7},{9,8},{10,9... | collective-permute-start | bytes 811016 | tf_op jit(solution)/shard_map/ppermute | solution.py:22
  13.4 11.2 %collective-permute-start.3 = (f32[528,128]{1,0:T(8,128)S(1)}, f32[528,128]{1,0:T(8,128)S(1)}, u32[]{:S(2)}, u32[]{:S(2)}) collective-permute-start(f32[528,128]{1,0:T(8,128)S(1)} %get-tuple-element.26), channel_id=1, source_target_pairs={{0,1},{1,2},{2,3},{3,4},{4,5},{5,6},{6,7},{7,8},{8,9},{9,10},{10,1... | collective-permute-start | bytes 811016 | tf_op jit(solution)/shard_map/ppermute | solution.py:22
  14.2 4.7 %collective-permute-start.4 = (f32[8,128]{1,0:T(8,128)S(1)}, f32[8,128]{1,0:T(8,128)S(1)}, u32[]{:S(2)}, u32[]{:S(2)}) collective-permute-start(f32[8,128]{1,0:T(8,128)S(1)} %get-tuple-element.27), channel_id=1, source_target_pairs={{0,29},{1,30},{2,31},{3,0},{4,1},{5,2},{6,3},{7,4},{8,5},{9,6},{10... | collective-permute-start | bytes 12296 | tf_op jit(solution)/shard_map/ppermute | solution.py:22
  18.8 5.7 %collective-permute-start.5 = (f32[8,128]{1,0:T(8,128)S(1)}, f32[8,128]{1,0:T(8,128)S(1)}, u32[]{:S(2)}, u32[]{:S(2)}) collective-permute-start(f32[8,128]{1,0:T(8,128)S(1)} %get-tuple-element.28), channel_id=1, source_target_pairs={{0,3},{1,4},{2,5},{3,6},{4,7},{5,8},{6,9},{7,10},{8,11},{9,12},{10... | collective-permute-start | bytes 12296 | tf_op jit(solution)/shard_map/ppermute | solution.py:22
  18.9 5.8 %copy-start.1 = (f32[2,128,128]{2,1,0:T(8,128)S(1)}, f32[2,128,128]{2,1,0:T(8,128)}, u32[]{:S(2)}) copy-start(f32[2,128,128]{2,1,0:T(8,128)} %level_map.3) | copy-start | bytes 393220
  30.7 15.0 %copy-start.6 = (f32[128,8,8]{0,2,1:T(8,128)S(1)}, f32[128,8,8]{0,2,1:T(8,128)}, u32[]{:S(2)}) copy-start(f32[128,8,8]{0,2,1:T(8,128)} %param.9) | copy-start | bytes 98308
  46.8 3.6 %copy-start.3 = (s32[2,1024]{1,0:T(2,128)S(1)}, s32[2,1024]{1,0:T(2,128)}, u32[]{:S(2)}) copy-start(s32[2,1024]{1,0:T(2,128)} %departure.7) | copy-start | bytes 24580
  46.8 3.6 %copy-start.5 = (f32[2,1024]{1,0:T(2,128)S(1)}, f32[2,1024]{1,0:T(2,128)}, u32[]{:S(2)}) copy-start(f32[2,1024]{1,0:T(2,128)} %fraction.7) | copy-start | bytes 24580
  46.8 12.1 %all-to-all-start.1 = ((f32[8,128,128]{2,1,0:T(8,128)}), f32[8,128,128]{2,1,0:T(8,128)S(1)}, u32[]{:S(2)}, u32[]{:S(2)}) async-start(f32[8,128,128]{2,1,0:T(8,128)} %shard_map.58), calls=%async_computation.1 | async-start | bytes 1048576 | tf_op jit(solution)/shard_map/all_to_all | solution.py:332
  60.3 20.7 %collective-permute-start.6 = (f32[528,128]{1,0:T(8,128)S(1)}, f32[528,128]{1,0:T(8,128)S(1)}, u32[]{:S(2)}, u32[]{:S(2)}) collective-permute-start(f32[528,128]{1,0:T(8,128)S(1)} %get-tuple-element.33), channel_id=1, source_target_pairs={{0,30},{1,31},{2,0},{3,1},{4,2},{5,3},{6,4},{7,5},{8,6},{9,7},{10,... | collective-permute-start | bytes 811016 | tf_op jit(solution)/shard_map/ppermute | solution.py:22
  67.3 13.7 %collective-permute-start.7 = (f32[528,128]{1,0:T(8,128)S(1)}, f32[528,128]{1,0:T(8,128)S(1)}, u32[]{:S(2)}, u32[]{:S(2)}) collective-permute-start(f32[528,128]{1,0:T(8,128)S(1)} %get-tuple-element.34), channel_id=1, source_target_pairs={{0,2},{1,3},{2,4},{3,5},{4,6},{5,7},{6,8},{7,9},{8,10},{9,11},{10,... | collective-permute-start | bytes 811016 | tf_op jit(solution)/shard_map/ppermute | solution.py:22
  67.3 13.7 %collective-permute-start.8 = (f32[528,128]{1,0:T(8,128)S(1)}, f32[528,128]{1,0:T(8,128)S(1)}, u32[]{:S(2)}, u32[]{:S(2)}) collective-permute-start(f32[528,128]{1,0:T(8,128)S(1)} %get-tuple-element.35), channel_id=1, source_target_pairs={{0,31},{1,0},{2,1},{3,2},{4,3},{5,4},{6,5},{7,6},{8,7},{9,8},{10,9... | collective-permute-start | bytes 811016 | tf_op jit(solution)/shard_map/ppermute | solution.py:22
  68.5 12.4 %collective-permute-start.9 = (f32[528,128]{1,0:T(8,128)S(1)}, f32[528,128]{1,0:T(8,128)S(1)}, u32[]{:S(2)}, u32[]{:S(2)}) collective-permute-start(f32[528,128]{1,0:T(8,128)S(1)} %get-tuple-element.36), channel_id=1, source_target_pairs={{0,1},{1,2},{2,3},{3,4},{4,5},{5,6},{6,7},{7,8},{8,9},{9,10},{10,1... | collective-permute-start | bytes 811016 | tf_op jit(solution)/shard_map/ppermute | solution.py:22
  69.0 6.8 %collective-permute-start.10 = (f32[8,128]{1,0:T(8,128)S(1)}, f32[8,128]{1,0:T(8,128)S(1)}, u32[]{:S(2)}, u32[]{:S(2)}) collective-permute-start(f32[8,128]{1,0:T(8,128)S(1)} %get-tuple-element.37), channel_id=1, source_target_pairs={{0,29},{1,30},{2,31},{3,0},{4,1},{5,2},{6,3},{7,4},{8,5},{9,6},{10... | collective-permute-start | bytes 12296 | tf_op jit(solution)/shard_map/ppermute | solution.py:22
  75.8 5.1 %collective-permute-start.11 = (f32[8,128]{1,0:T(8,128)S(1)}, f32[8,128]{1,0:T(8,128)S(1)}, u32[]{:S(2)}, u32[]{:S(2)}) collective-permute-start(f32[8,128]{1,0:T(8,128)S(1)} %get-tuple-element.38), channel_id=1, source_target_pairs={{0,3},{1,4},{2,5},{3,6},{4,7},{5,8},{6,9},{7,10},{8,11},{9,12},{10... | collective-permute-start | bytes 12296 | tf_op jit(solution)/shard_map/ppermute | solution.py:22
where the time goes:
time: 88.7 us; the launch traced here: 87.8 us
  starting transfers between devices  28.2 us (32%)
  Pallas kernels  25.3 us (29%)
  waiting for transfers between devices  16.7 us (19%)
  blocking collectives  15 us (17%)
  local copies, waits for them, and re-layouts  2.45 us (3%)
    ppermute x12, starting transfers between devices, shifted(): lax.ppermute(x, axis, [(i, (i + by) % length) for i in range(length)])  24.6 us
    all_to_all x1, blocking collectives, body(): lax.all_to_all(second.reshape(groups, COLS // groups, LEV), 'grp', 0, 0)  15 us
    pallas_call x2, Pallas kernels, deposited(): call(functools.partial(deposit_kernel, step), jax.ShapeDtypeStruct((COLS,...  12.9 us
    ppermute x12, waiting for transfers between devices, shifted(): lax.ppermute(x, axis, [(i, (i + by) % length) for i in range(length)])  9.72 us
    all_to_all x1, waiting for transfers between devices, body(): coupled = lax.all_to_all(mixed, 'grp', 0, 0).reshape(COLS, LEV)  7.03 us
    pallas_call x2, Pallas kernels, own_part(): call(functools.partial(own_kernel, step, tile_count), jax.ShapeDtypeStruc...  5.99 us
    all_to_all x1, starting transfers between devices, body(): coupled = lax.all_to_all(mixed, 'grp', 0, 0).reshape(COLS, LEV)  3.63 us
    pallas_call x1, Pallas kernels, body(): call(functools.partial(first_pack_kernel, tile_count), PACKED, [SM, VM, V...  2.48 us
  transfers between devices with their start and end apart: 13, of which 5 were waited for; matrix products, arithmetic and copies ran while one was open for 0% of the time, Pallas kernels for 8%

commit v1 on v0

--- a/solution.py
+++ b/solution.py
@@ -107,8 +107,10 @@
 
 
 def choose(keys, which):
-    slot = lax.broadcasted_iota(jnp.int32, (CAP, COLS), 0) + which * CAP
-    return jnp.where(slot == keys, 1.0, 0.0).astype(BF)
+    slot = lax.broadcasted_iota(jnp.int32, (CAP, COLS), 0).astype(jnp.int16)
+    wanted = jnp.broadcast_to(keys - which * CAP, (16, COLS)).astype(jnp.int16)
+    wanted = jnp.concatenate([wanted] * (CAP // 16), axis=0)
+    return jnp.where(slot == wanted, BF(1.0), BF(0.0))
 
 
 def spill_block(spilled, target):
@@ -150,12 +152,24 @@
     out[CAP : CAP + 8, :] = spill_block(spilled, shift)
 
 
-def first_pack_kernel(tile_count, self_ref, field, departure, fraction, *outs):
+def first_pack_kernel(tile_count, self_ref, field_hbm, departure_hbm, fraction_hbm, *refs):
+    outs, (field, departure, fraction, sems) = refs[:-4], refs[-4:]
+    copies = [
+        pltpu.make_async_copy(departure_hbm, departure, sems.at[0]),
+        pltpu.make_async_copy(fraction_hbm, fraction, sems.at[1]),
+        pltpu.make_async_copy(field_hbm, field, sems.at[2]),
+    ]
+    for copy in copies:
+        copy.start()
+    copies[0].wait()
+    copies[1].wait()
     place, offset, keys, weights = index_values(self_ref, departure[1:2, :], fraction[1:2, :], tile_count)
     meta = meta_rows(place, fraction[1:2, :])
+    spills = spill_rows(place, offset, weights)
+    copies[2].wait()
     high, low = halves(field[...])
     both = jnp.concatenate([high, low], axis=1)
-    spilled = spill_sums(spill_rows(place, offset, weights), both)
+    spilled = spill_sums(spills, both)
     outs[4][...] = spill_block(spilled, -3)
     outs[5][...] = spill_block(spilled, 3)
     outs[6][...] = spill_block(spilled, 0)
@@ -186,30 +200,47 @@
         outs[which][CAP + 8 : CAP + 16, :] = meta[8 * which : 8 * which + 8, :]
 
 
-BLOCK = 128
-
-
-def spread_block(first_cell, places, weights):
-    cells = lax.broadcasted_iota(jnp.int32, (BLOCK, places.shape[1]), 0)
-    distance = cells - (places - 1 - first_cell)
-    spread = jnp.where(distance == 0, weights[0], 0.0)
-    for k in (1, 2, 3):
-        spread = jnp.where(distance == k, weights[k], spread)
-    return halves(spread)
+BLOCK = 512
+I16 = jnp.int16
+
+
+def tiled(x, rows):
+    return jnp.concatenate([x] * (rows // 16), axis=0)
+
+
+def spread_table(place, weights):
+    shape = (16, place.shape[1])
+    start = jnp.broadcast_to(place - 1, shape).astype(I16)
+    return start, [halves(jnp.broadcast_to(w, shape)) for w in weights]
+
+
+def spread_block(first_cell, table):
+    start, weights = table
+    columns = start.shape[1]
+    cells = lax.broadcasted_iota(jnp.int32, (BLOCK, columns), 0).astype(I16)
+    first = jnp.full((16, columns), first_cell, jnp.int32).astype(I16)
+    distance = cells - tiled(start - first, BLOCK)
+    high = jnp.zeros((BLOCK, columns), BF)
+    low = high
+    for k in range(4):
+        here = distance == I16(k)
+        high = jnp.where(here, tiled(weights[k][0], BLOCK), high)
+        low = jnp.where(here, tiled(weights[k][1], BLOCK), low)
+    return high, low
 
 
 def own_kernel(step, tile_count, self_ref, field, departure, fraction, spilled, out, both_ref):
     departure = departure[step : step + 1, :]
     fraction = fraction[step : step + 1, :]
     place, offset = locate(departure, self_ref[0], tile_count)
-    weights = [jnp.where(offset == 0, w, 0.0) for w in cubic_weights(fraction)]
+    table = spread_table(place, [jnp.where(offset == 0, w, 0.0) for w in cubic_weights(fraction)])
     high, low = halves(field[...])
     both_ref[:, :LEV] = high
     both_ref[:, LEV:] = low
 
     @pl.loop(0, COLS // BLOCK)
     def _(b):
-        high, low = spread_block(b * BLOCK, place, weights)
+        high, low = spread_block(b * BLOCK, table)
         wide = dot(high, both_ref[...]) + dot(low, both_ref[...])
         out[pl.ds(b * BLOCK, BLOCK), :] = wide[:, :LEV] + wide[:, LEV:]
 
@@ -222,31 +253,39 @@
     out[COLS - 8 : COLS, :] = out[COLS - 8 : COLS, :] + jnp.where(row == 7, block, 0.0)
 
 
-def deposit_kernel(step, own, p0, p1, p2, p3, tiny_a, tiny_b, level_map, out, both_ref, sum_ref):
-    payloads = (p0, p1, p2, p3)
-    spill = tiny_a[...] + tiny_b[...]
+def deposit_sums(start, payloads, out, both_ref):
+    tables = []
     for which, payload in enumerate(payloads):
         high, low = halves(payload[0:CAP, :])
         both_ref[which, :, :LEV] = high
         both_ref[which, :, LEV:] = low
-        spill = spill + payload[CAP : CAP + 8, :]
-    tables = []
-    for payload in payloads:
         rows = [payload[CAP + 8 + c : CAP + 9 + c, :] for c in range(8)]
         fraction = jnp.concatenate(rows[:4], axis=1)
         place = jnp.concatenate(rows[4:], axis=1).astype(jnp.int32)
-        tables.append((place, cubic_weights(fraction)))
+        tables.append(spread_table(place, cubic_weights(fraction)))
 
     @pl.loop(0, COLS // BLOCK)
     def _(b):
         wide = jnp.zeros((BLOCK, 2 * LEV), F32)
-        for which in range(4):
-            place, weights = tables[which]
-            high, low = spread_block(b * BLOCK, place, weights)
+        for which, table in enumerate(tables):
+            high, low = spread_block(b * BLOCK, table)
             wide = wide + dot(high, both_ref[which]) + dot(low, both_ref[which])
-        sum_ref[pl.ds(b * BLOCK, BLOCK), :] = own[pl.ds(b * BLOCK, BLOCK), :] + wide[:, :LEV] + wide[:, LEV:]
-
-    add_spill(sum_ref, spill)
+        out[pl.ds(b * BLOCK, BLOCK), :] = start[pl.ds(b * BLOCK, BLOCK), :] + wide[:, :LEV] + wide[:, LEV:]
+
+    spill = payloads[0][CAP : CAP + 8, :]
+    for payload in payloads[1:]:
+        spill = spill + payload[CAP : CAP + 8, :]
+    return spill
+
+
+def near_kernel(start, p0, p1, out, both_ref):
+    spill = deposit_sums(start, (p0, p1), out, both_ref)
+    add_spill(out, spill)
+
+
+def far_kernel(step, start, p0, p1, tiny_a, tiny_b, level_map, out, both_ref, sum_ref):
+    spill = deposit_sums(start, (p0, p1), sum_ref, both_ref)
+    add_spill(sum_ref, spill + tiny_a[...] + tiny_b[...])
     map_high, map_low = halves(level_map[step])
     high, low = halves(sum_ref[...])
     out[...] = dot_nt(high, map_high) + (dot_nt(high, map_low) + dot_nt(low, map_high))
@@ -266,12 +305,13 @@
 
 
 VM = pl.BlockSpec(memory_space=pltpu.MemorySpace.VMEM)
+HBM = pl.BlockSpec(memory_space=pltpu.MemorySpace.HBM)
 SM = pl.BlockSpec(memory_space=pltpu.MemorySpace.SMEM)
 PARAMS = pltpu.CompilerParams(vmem_limit_bytes=40 * 1024 * 1024)
 PACKED = [jax.ShapeDtypeStruct((ROWS, LEV), F32)] * 4 + [jax.ShapeDtypeStruct((8, LEV), F32)] * 3
 
 
-def call(kernel, out_shape, in_specs, scratch=()):
+def call(kernel, out_shape, in_specs, scratch=(), flops=0):
     multiple = isinstance(out_shape, (list, tuple))
     return pl.pallas_call(
         kernel,
@@ -280,41 +320,47 @@
         out_specs=[VM] * len(out_shape) if multiple else VM,
         scratch_shapes=list(scratch),
         compiler_params=PARAMS,
+        cost_estimate=pl.CostEstimate(flops=flops, transcendentals=0, bytes_accessed=flops // 256),
     )
 
 
-def send(packed):
+def transported(step, packed, tile_count, tile_self, field, departure, fraction, level_map):
+    near = [shifted(packed[2], "tile", SHIFTS[2]), shifted(packed[3], "tile", SHIFTS[3])]
+    far = [shifted(packed[0], "tile", SHIFTS[0]), shifted(packed[1], "tile", SHIFTS[1])]
     tiny = [shifted(packed[4], "tile", -3), shifted(packed[5], "tile", 3)]
-    return [shifted(packed[w], "tile", s) for w, s in enumerate(SHIFTS)] + tiny
-
-
-def own_part(step, tile_count, tile_self, field, departure, fraction, spilled):
-    return call(
+    total = jax.ShapeDtypeStruct((COLS, LEV), F32)
+    work = 3 * 10**9
+    own = call(
         functools.partial(own_kernel, step, tile_count),
-        jax.ShapeDtypeStruct((COLS, LEV), F32),
+        total,
         [SM, VM, VM, VM, VM],
         [pltpu.VMEM((COLS, 2 * LEV), BF)],
-    )(tile_self, field, departure, fraction, spilled)
-
-
-def deposited(step, own, arrived, level_map):
+        work,
+    )(tile_self, field, departure, fraction, packed[6])
+    both = pltpu.VMEM((2, CAP, 2 * LEV), BF)
+    summed = call(near_kernel, total, [VM] * 3, [both], work)(own, *near)
     return call(
-        functools.partial(deposit_kernel, step),
-        jax.ShapeDtypeStruct((COLS, LEV), F32),
-        [VM] * 8,
-        [pltpu.VMEM((4, CAP, 2 * LEV), BF), pltpu.VMEM((COLS, LEV), F32)],
-    )(own, *arrived, level_map)
+        functools.partial(far_kernel, step),
+        total,
+        [VM] * 6,
+        [both, pltpu.VMEM((COLS, LEV), F32)],
+        work,
+    )(summed, *far, *tiny, level_map)
 
 
 def body(adjoint_in, departure, fraction, level_map, coarse_map):
     tile_count = lax.axis_size("tile")
     groups = lax.axis_size("grp")
     tile_self = lax.axis_index("tile").astype(jnp.int32).reshape(1)
-    packed = call(functools.partial(first_pack_kernel, tile_count), PACKED, [SM, VM, VM, VM])(
-        tile_self, adjoint_in, departure, fraction
+    first_scratch = [
+        pltpu.VMEM((COLS, LEV), F32),
+        pltpu.VMEM((2, COLS), jnp.int32),
+        pltpu.VMEM((2, COLS), F32),
+        pltpu.SemaphoreType.DMA((3,)),
+    ]
+    packed = call(functools.partial(first_pack_kernel, tile_count), PACKED, [SM, HBM, HBM, HBM], first_scratch)(
+        tile_self, *[pltpu.with_memory_space_constraint(x, pltpu.MemorySpace.HBM) for x in (adjoint_in, departure, fraction)]
     )
-    arrived = send(packed)
-    own = own_part(1, tile_count, tile_self, adjoint_in, departure, fraction, packed[6])
     keys, spills, meta = call(
         functools.partial(index_kernel, tile_count),
         [
@@ -323,18 +369,18 @@
             jax.ShapeDtypeStruct((32, LEV), F32),
         ],
         [SM, VM, VM],
+        (),
+        2 * 10**9,
     )(tile_self, departure, fraction)
     table = coarse_map.transpose(1, 2, 0).reshape(groups * groups, LEV)
-    second = deposited(1, own, arrived, level_map)
+    second = transported(1, packed, tile_count, tile_self, adjoint_in, departure, fraction, level_map)
 
     parts = lax.all_to_all(second.reshape(groups, COLS // groups, LEV), "grp", 0, 0)
     mixed = call(couple_kernel, jax.ShapeDtypeStruct(parts.shape, F32), [VM, VM])(table, parts)
     coupled = lax.all_to_all(mixed, "grp", 0, 0).reshape(COLS, LEV)
 
     packed = call(second_pack_kernel, PACKED, [VM] * 4)(coupled, keys, spills, meta)
-    arrived = send(packed)
-    own = own_part(0, tile_count, tile_self, coupled, departure, fraction, packed[6])
-    return deposited(0, own, arrived, level_map)
+    return transported(0, packed, tile_count, tile_self, coupled, departure, fraction, level_map)
 
 
 def solution(mesh):

time: 88.7 us -> 78.8 us (0.89)
  Pallas kernels: 25.3 us -> 18.9 us
  starting transfers between devices: 28.2 us -> 25.6 us
  local copies, waits for them, and re-layouts: 2.45 us -> 0.03 us
  blocking collectives: 15 us -> 17.3 us
    pallas_call x5 -> x7, Pallas kernels: 21.3 us -> 15 us  [the longest x2 4.9 us: transported(): call(functools.partial(far_kernel, step), total, [VM] * 6, [both, pltpu.V...]
    ppermute x12, starting transfers between devices: 24.6 us -> 22.2 us  [shifted(): lax.ppermute(x, axis, [(i, (i + by) % length) for i in range(length)])]
    unnamed x14 -> x10, local copies, waits for them, and re-layouts: 2.45 us -> 0.03 us
    all_to_all x1, blocking collectives: 15 us -> 17.3 us  [body(): lax.all_to_all(second.reshape(groups, COLS // groups, LEV), 'grp', 0, 0)]
    ppermute x12, waiting for transfers between devices: 9.72 us -> 7.43 us  [shifted(): lax.ppermute(x, axis, [(i, (i + by) % length) for i in range(length)])]
    all_to_all x1, waiting for transfers between devices: 7.03 us -> 9.15 us  [body(): coupled = lax.all_to_all(mixed, 'grp', 0, 0).reshape(COLS, LEV)]
  transfers between devices with their start and end apart: 13 -> 13, of which waited for: 5 -> 7; matrix products, arithmetic and copies ran while one was open for 0% -> 0% of each run, Pallas kernels for 8% -> 10%
where the time goes in v1:
time: 78.8 us; the launch traced here: 78.5 us
  starting transfers between devices  25.6 us (32%)
  Pallas kernels  18.9 us (24%)
  blocking collectives  17.3 us (22%)
  waiting for transfers between devices  16.6 us (21%)
    ppermute x12, starting transfers between devices, shifted(): lax.ppermute(x, axis, [(i, (i + by) % length) for i in range(length)])  22.2 us
    all_to_all x1, blocking collectives, body(): lax.all_to_all(second.reshape(groups, COLS // groups, LEV), 'grp', 0, 0)  17.3 us
    all_to_all x1, waiting for transfers between devices, body(): coupled = lax.all_to_all(mixed, 'grp', 0, 0).reshape(COLS, LEV)  9.15 us
    ppermute x12, waiting for transfers between devices, shifted(): lax.ppermute(x, axis, [(i, (i + by) % length) for i in range(length)])  7.43 us
    pallas_call x2, Pallas kernels, transported(): call(functools.partial(far_kernel, step), total, [VM] * 6, [both, pltpu.V...  4.9 us
    pallas_call x1, Pallas kernels, body(): call(functools.partial(first_pack_kernel, tile_count), PACKED, [SM, HBM,...  3.55 us
    all_to_all x1, starting transfers between devices, body(): coupled = lax.all_to_all(mixed, 'grp', 0, 0).reshape(COLS, LEV)  3.49 us
    pallas_call x2, Pallas kernels, transported(): summed = call(near_kernel, total, [VM] * 3, [both], work)(own, *near)  3.37 us
  transfers between devices with their start and end apart: 13, of which 7 were waited for; matrix products, arithmetic and copies ran while one was open for 0% of the time, Pallas kernels for 10%

profile of v1, /device:TPU:1, one launch (start us, length us, event | category | flops | bytes accessed | tf_op | source)
XLA Modules:
  0.0 78.5 jit_solution(13748309197116266983)
XLA Ops:
  0.0 0.0 copy-start
  0.0 0.0 copy-start.3
  0.0 3.6 %shard_map.55 = (f32[528,128]{1,0:T(8,128)S(1)}, f32[528,128]{1,0:T(8,128)S(1)}, f32[528,128]{1,0:T(8,128)S(1)}, f32[528,128]{1,0:T(8,128)S(1)}, f32[8,128]{1,0:...) custom-call(s32[1]{0:T(128)} %bitcast.self_ref, f32[1024,128]{1,0:T(8,128)} %field.1, s32[2,1024]{1,0:T(2,128)} %departure.5, ...), custom_call_target="tpu_custom_call" | custom-call | tf_op jit(solution)/shard_map/pallas_call | solution.py:361
  3.6 0.0 copy-start.2
  3.6 3.3 %collective-permute-start = (f32[528,128]{1,0:T(8,128)S(1)}, f32[528,128]{1,0:T(8,128)S(1)}, u32[]{:S(2)}, u32[]{:S(2)}) collective-permute-start(f32[528,128]{1,0:T(8,128)S(1)} %get-tuple-element.23), channel_id=1, source_target_pairs={{0,31},{1,0},{2,1},{3,2},{4,3},{5,4},{6,5},{7,6},{8,7},{9,8},{10,9... | collective-permute-start | bytes 811016 | tf_op jit(solution)/shard_map/ppermute | solution.py:22
  6.9 0.0 collective-permute-start.1
  6.9 8.0 %collective-permute-start.2 = (f32[528,128]{1,0:T(8,128)S(1)}, f32[528,128]{1,0:T(8,128)S(1)}, u32[]{:S(2)}, u32[]{:S(2)}) collective-permute-start(f32[528,128]{1,0:T(8,128)S(1)} %get-tuple-element.25), channel_id=1, source_target_pairs={{0,30},{1,31},{2,0},{3,1},{4,2},{5,3},{6,4},{7,5},{8,6},{9,7},{10,... | collective-permute-start | bytes 811016 | tf_op jit(solution)/shard_map/ppermute | solution.py:22
  14.9 0.0 collective-permute-start.3
  14.9 1.4 %collective-permute-start.4 = (f32[8,128]{1,0:T(8,128)S(1)}, f32[8,128]{1,0:T(8,128)S(1)}, u32[]{:S(2)}, u32[]{:S(2)}) collective-permute-start(f32[8,128]{1,0:T(8,128)S(1)} %get-tuple-element.27), channel_id=1, source_target_pairs={{0,29},{1,30},{2,31},{3,0},{4,1},{5,2},{6,3},{7,4},{8,5},{9,6},{10... | collective-permute-start | bytes 12296 | tf_op jit(solution)/shard_map/ppermute | solution.py:22
  16.3 0.0 copy-done
  16.3 0.0 copy-done.3
  16.3 0.0 copy-done.2
  16.3 1.6 %shard_map.56.start = f32[1024,128]{1,0:T(8,128)S(1)} custom-call(s32[1]{0:T(128)} %bitcast.self_ref, f32[1024,128]{1,0:T(8,128)S(1)} %copy-done, s32[2,1024]{1,0:T(2,128)S(1)} %copy-done.2, f32[2,1024]{1,0:T(2,128)S(1)} %copy-done.3, f32[8,128]{1,0:T(8,128)S(1)} %get-tuple-element.22.spilled), custom_call_target="tpu_custom_call" | custom-call | flops 3000000000 | bytes 11718750 | tf_op jit(solution)/shard_map/pallas_call | solution.py:333
  17.9 0.0 collective-permute-done.p0
  17.9 0.0 copy-start.4
  17.9 1.4 %collective-permute-start.5 = (f32[8,128]{1,0:T(8,128)S(1)}, f32[8,128]{1,0:T(8,128)S(1)}, u32[]{:S(2)}, u32[]{:S(2)}) collective-permute-start(f32[8,128]{1,0:T(8,128)S(1)} %get-tuple-element.28), channel_id=1, source_target_pairs={{0,3},{1,4},{2,5},{3,6},{4,7},{5,8},{6,9},{7,10},{8,11},{9,12},{10... | collective-permute-start | bytes 12296 | tf_op jit(solution)/shard_map/ppermute | solution.py:22
  19.3 0.0 collective-permute-done.1.p1
  19.3 1.7 %shard_map.57.start = f32[1024,128]{1,0:T(8,128)S(1)} custom-call(f32[1024,128]{1,0:T(8,128)S(1)} %shard_map.56.start, f32[528,128]{1,0:T(8,128)S(1)} %collective-permute-done.p0, f32[528,128]{1,0:T(8,128)S(1)} %collective-permute-done.1.p1), custom_call_target="tpu_custom_call" | custom-call | flops 3000000000 | bytes 11718750 | tf_op jit(solution)/shard_map/pallas_call | solution.py:341
  21.0 0.1 collective-permute-done.4.tiny_a
  21.0 2.8 %collective-permute-done.5.tiny_b = f32[8,128]{1,0:T(8,128)S(1)} collective-permute-done((f32[8,128]{1,0:T(8,128)S(1)}, f32[8,128]{1,0:T(8,128)S(1)}, u32[]{:S(2)}, u32[]{:S(2)}) %collective-permute-start.5) | collective-permute-done | bytes 4128 | tf_op jit(solution)/shard_map/ppermute | solution.py:22
  23.8 0.0 collective-permute-done.2.p0
  23.8 0.9 %collective-permute-done.3.p1 = f32[528,128]{1,0:T(8,128)S(1)} collective-permute-done((f32[528,128]{1,0:T(8,128)S(1)}, f32[528,128]{1,0:T(8,128)S(1)}, u32[]{:S(2)}, u32[]{:S(2)}) %collective-permute-start.3) | collective-permute-done | bytes 270368 | tf_op jit(solution)/shard_map/ppermute | solution.py:22
  24.7 0.0 copy-done.4
  24.7 2.1 %shard_map.58 = f32[1024,128]{1,0:T(8,128)S(1)} custom-call(f32[1024,128]{1,0:T(8,128)S(1)} %shard_map.57.start, f32[528,128]{1,0:T(8,128)S(1)} %collective-permute-done.2.p0, f32[528,128]{1,0:T(8,128)S(1)} %collective-permute-done.3.p1, f32[8,128]{1,0:T(8,128)S(1)} %collective-permute-done.4.tiny_a, f32[8,128]{1,0:T(8,128)S(1)} %collective-permute-done.5.tiny_b, ...), custom_call_target="tpu_custom_call" | custom-call | flops 3000000000 | bytes 11718750 | tf_op jit(solution)/shard_map/pallas_call | solution.py:342
  26.7 0.0 copy-start.1
  26.7 17.3 %all_to_all.10.x = f32[8,128,128]{2,1,0:T(8,128)S(1)} all-to-all(f32[8,128,128]{2,1,0:T(8,128)S(1)} %bitcast.8), channel_id=1, replica_groups=mesh['grp'=8,'tile'=32] {'grp'}, dimensions={0} | all-to-all | bytes 1048576 | tf_op jit(solution)/shard_map/all_to_all | solution.py:378
  44.0 0.0 copy-done.1
  44.0 1.2 %shard_map.59 = f32[8,128,128]{2,1,0:T(8,128)} custom-call(f32[64,128]{1,0:T(8,128)S(1)} %bitcast.9, f32[8,128,128]{2,1,0:T(8,128)S(1)} %all_to_all.10.x), custom_call_target="tpu_custom_call" | custom-call | tf_op jit(solution)/shard_map/pallas_call | solution.py:379
  45.2 3.5 %all-to-all-start.1 = ((f32[8,128,128]{2,1,0:T(8,128)}), f32[8,128,128]{2,1,0:T(8,128)S(1)}, u32[]{:S(2)}, u32[]{:S(2)}) async-start(f32[8,128,128]{2,1,0:T(8,128)} %shard_map.59), calls=%async_computation.1 | async-start | bytes 1048576 | tf_op jit(solution)/shard_map/all_to_all | solution.py:380
  48.7 1.4 %shard_map.60 = (s32[1,1024]{1,0:T(1,128)S(1)}, bf16[80,1024]{1,0:T(8,128)(2,1)S(1)}, f32[32,128]{1,0:T(8,128)S(1)}) custom-call(s32[1]{0:T(128)} %bitcast.self_ref, s32[2,1024]{1,0:T(2,128)S(1)} %copy-done.2, f32[2,1024]{1,0:T(2,128)S(1)} %copy-done.3), custom_call_target="tpu_custom_call" | custom-call | flops 2000000000 | bytes 7812500 | tf_op jit(solution)/shard_map/pallas_call | solution.py:364
  50.1 9.2 %all-to-all-done.1 = f32[8,128,128]{2,1,0:T(8,128)S(1)} async-done(((f32[8,128,128]{2,1,0:T(8,128)}), f32[8,128,128]{2,1,0:T(8,128)S(1)}, u32[]{:S(2)}, u32[]{:S(2)}) %all-to-all-start.1) | async-done | bytes 524320 | tf_op jit(solution)/shard_map/all_to_all | solution.py:380
  59.3 1.3 %shard_map.61 = (f32[528,128]{1,0:T(8,128)S(1)}, f32[528,128]{1,0:T(8,128)S(1)}, f32[528,128]{1,0:T(8,128)S(1)}, f32[528,128]{1,0:T(8,128)S(1)}, f32[8,128]{1,0:...) custom-call(f32[1024,128]{1,0:T(8,128)S(1)} %bitcast.6, s32[1,1024]{1,0:T(1,128)S(1)} %get-tuple-element.29.keys, ...), custom_call_target="tpu_custom_call" | custom-call | tf_op jit(solution)/shard_map/pallas_call | solution.py:382
  60.6 1.5 %collective-permute-start.6 = (f32[528,128]{1,0:T(8,128)S(1)}, f32[528,128]{1,0:T(8,128)S(1)}, u32[]{:S(2)}, u32[]{:S(2)}) collective-permute-start(f32[528,128]{1,0:T(8,128)S(1)} %get-tuple-element.33), channel_id=1, source_target_pairs={{0,31},{1,0},{2,1},{3,2},{4,3},{5,4},{6,5},{7,6},{8,7},{9,8},{10,9... | collective-permute-start | bytes 811016 | tf_op jit(solution)/shard_map/ppermute | solution.py:22
  62.1 0.5 collective-permute-start.7
  62.6 3.3 %collective-permute-start.8 = (f32[528,128]{1,0:T(8,128)S(1)}, f32[528,128]{1,0:T(8,128)S(1)}, u32[]{:S(2)}, u32[]{:S(2)}) collective-permute-start(f32[528,128]{1,0:T(8,128)S(1)} %get-tuple-element.35), channel_id=1, source_target_pairs={{0,30},{1,31},{2,0},{3,1},{4,2},{5,3},{6,4},{7,5},{8,6},{9,7},{10,... | collective-permute-start | bytes 811016 | tf_op jit(solution)/shard_map/ppermute | solution.py:22
  65.9 0.0 collective-permute-start.9
  65.9 1.8 %collective-permute-start.10 = (f32[8,128]{1,0:T(8,128)S(1)}, f32[8,128]{1,0:T(8,128)S(1)}, u32[]{:S(2)}, u32[]{:S(2)}) collective-permute-start(f32[8,128]{1,0:T(8,128)S(1)} %get-tuple-element.37), channel_id=1, source_target_pairs={{0,29},{1,30},{2,31},{3,0},{4,1},{5,2},{6,3},{7,4},{8,5},{9,6},{10... | collective-permute-start | bytes 12296 | tf_op jit(solution)/shard_map/ppermute | solution.py:22
  67.7 1.6 %shard_map.62.start = f32[1024,128]{1,0:T(8,128)S(1)} custom-call(s32[1]{0:T(128)} %bitcast.self_ref, f32[1024,128]{1,0:T(8,128)S(1)} %bitcast.7, s32[2,1024]{1,0:T(2,128)S(1)} %copy-done.2, f32[2,1024]{1,0:T(2,128)S(1)} %copy-done.3, f32[8,128]{1,0:T(8,128)S(1)} %get-tuple-element.32.spilled), custom_call_target="tpu_custom_call" | custom-call | flops 3000000000 | bytes 11718750 | tf_op jit(solution)/shard_map/pallas_call | solution.py:333
  69.3 0.0 collective-permute-done.6.p0
  69.3 0.9 %collective-permute-start.11 = (f32[8,128]{1,0:T(8,128)S(1)}, f32[8,128]{1,0:T(8,128)S(1)}, u32[]{:S(2)}, u32[]{:S(2)}) collective-permute-start(f32[8,128]{1,0:T(8,128)S(1)} %get-tuple-element.38), channel_id=1, source_target_pairs={{0,3},{1,4},{2,5},{3,6},{4,7},{5,8},{6,9},{7,10},{8,11},{9,12},{10... | collective-permute-start | bytes 12296 | tf_op jit(solution)/shard_map/ppermute | solution.py:22
  70.3 0.0 collective-permute-done.7.p1
  70.3 1.7 %shard_map.63.start = f32[1024,128]{1,0:T(8,128)S(1)} custom-call(f32[1024,128]{1,0:T(8,128)S(1)} %shard_map.62.start, f32[528,128]{1,0:T(8,128)S(1)} %collective-permute-done.6.p0, f32[528,128]{1,0:T(8,128)S(1)} %collective-permute-done.7.p1), custom_call_target="tpu_custom_call" | custom-call | flops 3000000000 | bytes 11718750 | tf_op jit(solution)/shard_map/pallas_call | solution.py:341
  71.9 0.2 collective-permute-done.10.tiny_a
  72.1 3.1 %collective-permute-done.11.tiny_b = f32[8,128]{1,0:T(8,128)S(1)} collective-permute-done((f32[8,128]{1,0:T(8,128)S(1)}, f32[8,128]{1,0:T(8,128)S(1)}, u32[]{:S(2)}, u32[]{:S(2)}) %collective-permute-start.11) | collective-permute-done | bytes 4128 | tf_op jit(solution)/shard_map/ppermute | solution.py:22
  75.2 0.0 collective-permute-done.8.p0
  75.2 0.5 collective-permute-done.9.p1
  75.7 2.8 %shard_map.64 = f32[1024,128]{1,0:T(8,128)} custom-call(f32[1024,128]{1,0:T(8,128)S(1)} %shard_map.63.start, f32[528,128]{1,0:T(8,128)S(1)} %collective-permute-done.8.p0, f32[528,128]{1,0:T(8,128)S(1)} %collective-permute-done.9.p1, f32[8,128]{1,0:T(8,128)S(1)} %collective-permute-done.10.tiny_a, f32[8,128]{1,0:T(8,128)S(1)} %collective-permute-done.11.tiny_b, ...), custom_call_target="tpu_custom_call" | custom-call | flops 3000000000 | bytes 11718750 | tf_op jit(solution)/shard_map/pallas_call | solution.py:342
Async XLA Ops:
  0.0 16.3 %copy-start = (f32[1024,128]{1,0:T(8,128)S(1)}, f32[1024,128]{1,0:T(8,128)}, u32[]{:S(2)}) copy-start(f32[1024,128]{1,0:T(8,128)} %field.1) | copy-start | bytes 1572868
  0.0 16.3 %copy-start.3 = (f32[2,1024]{1,0:T(2,128)S(1)}, f32[2,1024]{1,0:T(2,128)}, u32[]{:S(2)}) copy-start(f32[2,1024]{1,0:T(2,128)} %fraction.5) | copy-start | bytes 24580
  3.6 12.7 %copy-start.2 = (s32[2,1024]{1,0:T(2,128)S(1)}, s32[2,1024]{1,0:T(2,128)}, u32[]{:S(2)}) copy-start(s32[2,1024]{1,0:T(2,128)} %departure.5) | copy-start | bytes 24580
  3.6 14.3 %collective-permute-start = (f32[528,128]{1,0:T(8,128)S(1)}, f32[528,128]{1,0:T(8,128)S(1)}, u32[]{:S(2)}, u32[]{:S(2)}) collective-permute-start(f32[528,128]{1,0:T(8,128)S(1)} %get-tuple-element.23), channel_id=1, source_target_pairs={{0,31},{1,0},{2,1},{3,2},{4,3},{5,4},{6,5},{7,6},{8,7},{9,8},{10,9... | collective-permute-start | bytes 811016 | tf_op jit(solution)/shard_map/ppermute | solution.py:22
  6.9 12.4 %collective-permute-start.1 = (f32[528,128]{1,0:T(8,128)S(1)}, f32[528,128]{1,0:T(8,128)S(1)}, u32[]{:S(2)}, u32[]{:S(2)}) collective-permute-start(f32[528,128]{1,0:T(8,128)S(1)} %get-tuple-element.24), channel_id=1, source_target_pairs={{0,1},{1,2},{2,3},{3,4},{4,5},{5,6},{6,7},{7,8},{8,9},{9,10},{10,1... | collective-permute-start | bytes 811016 | tf_op jit(solution)/shard_map/ppermute | solution.py:22
  6.9 16.9 %collective-permute-start.2 = (f32[528,128]{1,0:T(8,128)S(1)}, f32[528,128]{1,0:T(8,128)S(1)}, u32[]{:S(2)}, u32[]{:S(2)}) collective-permute-start(f32[528,128]{1,0:T(8,128)S(1)} %get-tuple-element.25), channel_id=1, source_target_pairs={{0,30},{1,31},{2,0},{3,1},{4,2},{5,3},{6,4},{7,5},{8,6},{9,7},{10,... | collective-permute-start | bytes 811016 | tf_op jit(solution)/shard_map/ppermute | solution.py:22
  14.9 9.7 %collective-permute-start.3 = (f32[528,128]{1,0:T(8,128)S(1)}, f32[528,128]{1,0:T(8,128)S(1)}, u32[]{:S(2)}, u32[]{:S(2)}) collective-permute-start(f32[528,128]{1,0:T(8,128)S(1)} %get-tuple-element.26), channel_id=1, source_target_pairs={{0,2},{1,3},{2,4},{3,5},{4,6},{5,7},{6,8},{7,9},{8,10},{9,11},{10,... | collective-permute-start | bytes 811016 | tf_op jit(solution)/shard_map/ppermute | solution.py:22
  14.9 6.1 %collective-permute-start.4 = (f32[8,128]{1,0:T(8,128)S(1)}, f32[8,128]{1,0:T(8,128)S(1)}, u32[]{:S(2)}, u32[]{:S(2)}) collective-permute-start(f32[8,128]{1,0:T(8,128)S(1)} %get-tuple-element.27), channel_id=1, source_target_pairs={{0,29},{1,30},{2,31},{3,0},{4,1},{5,2},{6,3},{7,4},{8,5},{9,6},{10... | collective-permute-start | bytes 12296 | tf_op jit(solution)/shard_map/ppermute | solution.py:22
  17.9 6.8 %copy-start.4 = (f32[2,128,128]{2,1,0:T(8,128)S(1)}, f32[2,128,128]{2,1,0:T(8,128)}, u32[]{:S(2)}) copy-start(f32[2,128,128]{2,1,0:T(8,128)} %level_map.3) | copy-start | bytes 393220
  17.9 5.9 %collective-permute-start.5 = (f32[8,128]{1,0:T(8,128)S(1)}, f32[8,128]{1,0:T(8,128)S(1)}, u32[]{:S(2)}, u32[]{:S(2)}) collective-permute-start(f32[8,128]{1,0:T(8,128)S(1)} %get-tuple-element.28), channel_id=1, source_target_pairs={{0,3},{1,4},{2,5},{3,6},{4,7},{5,8},{6,9},{7,10},{8,11},{9,12},{10... | collective-permute-start | bytes 12296 | tf_op jit(solution)/shard_map/ppermute | solution.py:22
  26.7 17.3 %copy-start.1 = (f32[128,8,8]{0,2,1:T(8,128)S(1)}, f32[128,8,8]{0,2,1:T(8,128)}, u32[]{:S(2)}) copy-start(f32[128,8,8]{0,2,1:T(8,128)} %param.9) | copy-start | bytes 98308
  45.2 14.1 %all-to-all-start.1 = ((f32[8,128,128]{2,1,0:T(8,128)}), f32[8,128,128]{2,1,0:T(8,128)S(1)}, u32[]{:S(2)}, u32[]{:S(2)}) async-start(f32[8,128,128]{2,1,0:T(8,128)} %shard_map.59), calls=%async_computation.1 | async-start | bytes 1048576 | tf_op jit(solution)/shard_map/all_to_all | solution.py:380
  60.6 8.7 %collective-permute-start.6 = (f32[528,128]{1,0:T(8,128)S(1)}, f32[528,128]{1,0:T(8,128)S(1)}, u32[]{:S(2)}, u32[]{:S(2)}) collective-permute-start(f32[528,128]{1,0:T(8,128)S(1)} %get-tuple-element.33), channel_id=1, source_target_pairs={{0,31},{1,0},{2,1},{3,2},{4,3},{5,4},{6,5},{7,6},{8,7},{9,8},{10,9... | collective-permute-start | bytes 811016 | tf_op jit(solution)/shard_map/ppermute | solution.py:22
  62.1 8.2 %collective-permute-start.7 = (f32[528,128]{1,0:T(8,128)S(1)}, f32[528,128]{1,0:T(8,128)S(1)}, u32[]{:S(2)}, u32[]{:S(2)}) collective-permute-start(f32[528,128]{1,0:T(8,128)S(1)} %get-tuple-element.34), channel_id=1, source_target_pairs={{0,1},{1,2},{2,3},{3,4},{4,5},{5,6},{6,7},{7,8},{8,9},{9,10},{10,1... | collective-permute-start | bytes 811016 | tf_op jit(solution)/shard_map/ppermute | solution.py:22
  62.6 12.6 %collective-permute-start.8 = (f32[528,128]{1,0:T(8,128)S(1)}, f32[528,128]{1,0:T(8,128)S(1)}, u32[]{:S(2)}, u32[]{:S(2)}) collective-permute-start(f32[528,128]{1,0:T(8,128)S(1)} %get-tuple-element.35), channel_id=1, source_target_pairs={{0,30},{1,31},{2,0},{3,1},{4,2},{5,3},{6,4},{7,5},{8,6},{9,7},{10,... | collective-permute-start | bytes 811016 | tf_op jit(solution)/shard_map/ppermute | solution.py:22
  65.9 9.7 %collective-permute-start.9 = (f32[528,128]{1,0:T(8,128)S(1)}, f32[528,128]{1,0:T(8,128)S(1)}, u32[]{:S(2)}, u32[]{:S(2)}) collective-permute-start(f32[528,128]{1,0:T(8,128)S(1)} %get-tuple-element.36), channel_id=1, source_target_pairs={{0,2},{1,3},{2,4},{3,5},{4,6},{5,7},{6,8},{7,9},{8,10},{9,11},{10,... | collective-permute-start | bytes 811016 | tf_op jit(solution)/shard_map/ppermute | solution.py:22
  65.9 6.2 %collective-permute-start.10 = (f32[8,128]{1,0:T(8,128)S(1)}, f32[8,128]{1,0:T(8,128)S(1)}, u32[]{:S(2)}, u32[]{:S(2)}) collective-permute-start(f32[8,128]{1,0:T(8,128)S(1)} %get-tuple-element.37), channel_id=1, source_target_pairs={{0,29},{1,30},{2,31},{3,0},{4,1},{5,2},{6,3},{7,4},{8,5},{9,6},{10... | collective-permute-start | bytes 12296 | tf_op jit(solution)/shard_map/ppermute | solution.py:22
  69.3 5.8 %collective-permute-start.11 = (f32[8,128]{1,0:T(8,128)S(1)}, f32[8,128]{1,0:T(8,128)S(1)}, u32[]{:S(2)}, u32[]{:S(2)}) collective-permute-start(f32[8,128]{1,0:T(8,128)S(1)} %get-tuple-element.38), channel_id=1, source_target_pairs={{0,3},{1,4},{2,5},{3,6},{4,7},{5,8},{6,9},{7,10},{8,11},{9,12},{10... | collective-permute-start | bytes 12296 | tf_op jit(solution)/shard_map/ppermute | solution.py:22

commit v2 on v1

--- a/solution.py
+++ b/solution.py
@@ -8,7 +8,7 @@
 from jax.sharding import PartitionSpec as P
 
 REACH = 2
-SHIFTS = (-2, 2, -1, 1)
+SWAPS = 4
 COLS = 1024
 LEV = 128
 CAP = 512
@@ -17,9 +17,15 @@
 F32 = jnp.float32
 
 
-def shifted(x, axis, by):
-    length = lax.axis_size(axis)
-    return lax.ppermute(x, axis, [(i, (i + by) % length) for i in range(length)])
+def signs(tile):
+    core = 1 - 2 * (tile % 2)
+    chip = 1 - 2 * ((tile // 2) % 2)
+    return (2 * chip, -2 * chip, -core, core, 3 * core, -3 * core)
+
+
+def swapped(x, which):
+    length = lax.axis_size("tile")
+    return lax.ppermute(x, "tile", [(i, (i + signs(i)[which]) % length) for i in range(length)])
 
 
 def halves(x):
@@ -52,13 +58,13 @@
     return place, offset
 
 
-def slots_of(offset):
+def slots_of(offset, shifts):
     row = lax.broadcasted_iota(jnp.int32, (8, LEV), 0)
     lane_a = lax.broadcasted_iota(jnp.int32, (LEV, LEV), 0)
     lane_b = lax.broadcasted_iota(jnp.int32, (LEV, LEV), 1)
     before = jnp.where(lane_a < lane_b, 1.0, 0.0).astype(BF)
     number = jnp.full((1, COLS), 4, jnp.int32)
-    for which, shift in enumerate(SHIFTS):
+    for which, shift in enumerate(shifts[:SWAPS]):
         number = jnp.where(offset == shift, which, number)
     members = []
     for c in range(COLS // LEV):
@@ -115,12 +121,11 @@
 
 def spill_block(spilled, target):
     row = lax.broadcasted_iota(jnp.int32, (8, LEV), 0)
+    from_cell = jnp.where(row < 2, target - 1, jnp.where(row == 7, target + 1, -9))
     out = jnp.zeros((8, LEV), F32)
-    for o in (target - 1, target + 1):
-        if -REACH <= o <= REACH:
-            block = spilled[8 * (o + REACH) : 8 * (o + REACH) + 8]
-            keep = row < 2 if o == target - 1 else row == 7
-            out = out + jnp.where(keep, block, 0.0)
+    for o in range(-REACH, REACH + 1):
+        block = spilled[8 * (o + REACH) : 8 * (o + REACH) + 8]
+        out = out + jnp.where(from_cell == o, block, 0.0)
     return out
 
 
@@ -132,7 +137,7 @@
 
 def index_values(self_ref, departure, fraction, tile_count):
     place, offset = locate(departure, self_ref[0], tile_count)
-    keys = slots_of(offset)
+    keys = slots_of(offset, signs(self_ref[0]))
     weights = cubic_weights(fraction)
     return place, offset, keys, weights
 
@@ -170,10 +175,11 @@
     high, low = halves(field[...])
     both = jnp.concatenate([high, low], axis=1)
     spilled = spill_sums(spills, both)
-    outs[4][...] = spill_block(spilled, -3)
-    outs[5][...] = spill_block(spilled, 3)
+    shifts = signs(self_ref[0])
+    outs[4][...] = spill_block(spilled, shifts[4])
+    outs[5][...] = spill_block(spilled, shifts[5])
     outs[6][...] = spill_block(spilled, 0)
-    for which, shift in enumerate(SHIFTS):
+    for which, shift in enumerate(shifts[:SWAPS]):
         one_hot = choose(keys, which)
         pack_payload(outs[which], one_hot, both, spilled, shift)
         write_meta(outs[which], CAP + 8, meta, one_hot)
@@ -184,18 +190,19 @@
     meta = meta_rows(place, fraction[0:1, :])
     keys_out[...] = keys
     spill_out[...] = spill_rows(place, offset, weights)
-    for which in range(len(SHIFTS)):
+    for which in range(SWAPS):
         write_meta(meta_out, 8 * which, meta, choose(keys, which))
 
 
-def second_pack_kernel(field, keys, spills, meta, *outs):
+def second_pack_kernel(self_ref, field, keys, spills, meta, *outs):
     high, low = halves(field[...])
     both = jnp.concatenate([high, low], axis=1)
     spilled = spill_sums(spills[...], both)
-    outs[4][...] = spill_block(spilled, -3)
-    outs[5][...] = spill_block(spilled, 3)
+    shifts = signs(self_ref[0])
+    outs[4][...] = spill_block(spilled, shifts[4])
+    outs[5][...] = spill_block(spilled, shifts[5])
     outs[6][...] = spill_block(spilled, 0)
-    for which, shift in enumerate(SHIFTS):
+    for which, shift in enumerate(shifts[:SWAPS]):
         pack_payload(outs[which], choose(keys[...], which), both, spilled, shift)
         outs[which][CAP + 8 : CAP + 16, :] = meta[8 * which : 8 * which + 8, :]
 
@@ -229,7 +236,7 @@
     return high, low
 
 
-def own_kernel(step, tile_count, self_ref, field, departure, fraction, spilled, out, both_ref):
+def own_kernel(step, tile_count, self_ref, field, departure, fraction, spilled, tiny_a, tiny_b, out, both_ref):
     departure = departure[step : step + 1, :]
     fraction = fraction[step : step + 1, :]
     place, offset = locate(departure, self_ref[0], tile_count)
@@ -244,7 +251,7 @@
         wide = dot(high, both_ref[...]) + dot(low, both_ref[...])
         out[pl.ds(b * BLOCK, BLOCK), :] = wide[:, :LEV] + wide[:, LEV:]
 
-    add_spill(out, spilled[...])
+    add_spill(out, spilled[...] + tiny_a[...] + tiny_b[...])
 
 
 def add_spill(out, block):
@@ -283,9 +290,9 @@
     add_spill(out, spill)
 
 
-def far_kernel(step, start, p0, p1, tiny_a, tiny_b, level_map, out, both_ref, sum_ref):
+def far_kernel(step, start, p0, p1, level_map, out, both_ref, sum_ref):
     spill = deposit_sums(start, (p0, p1), sum_ref, both_ref)
-    add_spill(sum_ref, spill + tiny_a[...] + tiny_b[...])
+    add_spill(sum_ref, spill)
     map_high, map_low = halves(level_map[step])
     high, low = halves(sum_ref[...])
     out[...] = dot_nt(high, map_high) + (dot_nt(high, map_low) + dot_nt(low, map_high))
@@ -325,27 +332,27 @@
 
 
 def transported(step, packed, tile_count, tile_self, field, departure, fraction, level_map):
-    near = [shifted(packed[2], "tile", SHIFTS[2]), shifted(packed[3], "tile", SHIFTS[3])]
-    far = [shifted(packed[0], "tile", SHIFTS[0]), shifted(packed[1], "tile", SHIFTS[1])]
-    tiny = [shifted(packed[4], "tile", -3), shifted(packed[5], "tile", 3)]
+    tiny = [swapped(packed[w], w) for w in (4, 5)]
+    far = [swapped(packed[w], w) for w in (0, 1)]
+    near = [swapped(packed[w], w) for w in (2, 3)]
     total = jax.ShapeDtypeStruct((COLS, LEV), F32)
     work = 3 * 10**9
     own = call(
         functools.partial(own_kernel, step, tile_count),
         total,
-        [SM, VM, VM, VM, VM],
+        [SM] + [VM] * 6,
         [pltpu.VMEM((COLS, 2 * LEV), BF)],
         work,
-    )(tile_self, field, departure, fraction, packed[6])
+    )(tile_self, field, departure, fraction, packed[6], *tiny)
     both = pltpu.VMEM((2, CAP, 2 * LEV), BF)
     summed = call(near_kernel, total, [VM] * 3, [both], work)(own, *near)
     return call(
         functools.partial(far_kernel, step),
         total,
-        [VM] * 6,
+        [VM] * 4,
         [both, pltpu.VMEM((COLS, LEV), F32)],
         work,
-    )(summed, *far, *tiny, level_map)
+    )(summed, *far, level_map)
 
 
 def body(adjoint_in, departure, fraction, level_map, coarse_map):
@@ -379,7 +386,7 @@
     mixed = call(couple_kernel, jax.ShapeDtypeStruct(parts.shape, F32), [VM, VM])(table, parts)
     coupled = lax.all_to_all(mixed, "grp", 0, 0).reshape(COLS, LEV)
 
-    packed = call(second_pack_kernel, PACKED, [VM] * 4)(coupled, keys, spills, meta)
+    packed = call(second_pack_kernel, PACKED, [SM] + [VM] * 4)(tile_self, coupled, keys, spills, meta)
     return transported(0, packed, tile_count, tile_self, coupled, departure, fraction, level_map)
 
 

time: 78.8 us -> 79.4 us (level)
  waiting for transfers between devices: 16.6 us -> 18.4 us
  blocking collectives: 17.3 us -> 16.1 us
    ppermute x12, waiting for transfers between devices: 7.43 us -> 11.1 us  [swapped(): lax.ppermute(x, 'tile', [(i, (i + signs(i)[which]) % length) for i in ran...]
    all_to_all x1, waiting for transfers between devices: 9.15 us -> 7.27 us  [body(): coupled = lax.all_to_all(mixed, 'grp', 0, 0).reshape(COLS, LEV)]
    all_to_all x1, blocking collectives: 17.3 us -> 16.1 us  [body(): lax.all_to_all(second.reshape(groups, COLS // groups, LEV), 'grp', 0, 0)]
  transfers between devices with their start and end apart: 13 -> 13, of which waited for: 7 -> 6; matrix products, arithmetic and copies ran while one was open for 0% -> 0% of each run, Pallas kernels for 10% -> 10%
where the time goes in v2:
time: 79.4 us; the launch traced here: 79.1 us
  starting transfers between devices  25.7 us (32%)
  Pallas kernels  18.9 us (24%)
  waiting for transfers between devices  18.4 us (23%)
  blocking collectives  16.1 us (20%)
    ppermute x12, starting transfers between devices, swapped(): lax.ppermute(x, 'tile', [(i, (i + signs(i)[which]) % length) for i in ran...  21.8 us
    all_to_all x1, blocking collectives, body(): lax.all_to_all(second.reshape(groups, COLS // groups, LEV), 'grp', 0, 0)  16.1 us
    ppermute x12, waiting for transfers between devices, swapped(): lax.ppermute(x, 'tile', [(i, (i + signs(i)[which]) % length) for i in ran...  11.1 us
    all_to_all x1, waiting for transfers between devices, body(): coupled = lax.all_to_all(mixed, 'grp', 0, 0).reshape(COLS, LEV)  7.27 us
    pallas_call x2, Pallas kernels, transported(): call(functools.partial(far_kernel, step), total, [VM] * 4, [both, pltpu.V...  4.89 us
    all_to_all x1, starting transfers between devices, body(): coupled = lax.all_to_all(mixed, 'grp', 0, 0).reshape(COLS, LEV)  3.88 us
    pallas_call x1, Pallas kernels, body(): call(functools.partial(first_pack_kernel, tile_count), PACKED, [SM, HBM,...  3.55 us
    pallas_call x2, Pallas kernels, transported(): summed = call(near_kernel, total, [VM] * 3, [both], work)(own, *near)  3.37 us
  transfers between devices with their start and end apart: 13, of which 6 were waited for; matrix products, arithmetic and copies ran while one was open for 0% of the time, Pallas kernels for 10%

profile of v2, /device:TPU:1, one launch (start us, length us, event | category | flops | bytes accessed | tf_op | source)
XLA Modules:
  0.0 79.1 jit_solution(331916395907236309)
XLA Ops:
  0.0 0.0 copy-start
  0.0 0.0 copy-start.3
  0.0 3.6 %shard_map.55 = (f32[528,128]{1,0:T(8,128)S(1)}, f32[528,128]{1,0:T(8,128)S(1)}, f32[528,128]{1,0:T(8,128)S(1)}, f32[528,128]{1,0:T(8,128)S(1)}, f32[8,128]{1,0:...) custom-call(s32[1]{0:T(128)} %bitcast.self_ref, f32[1024,128]{1,0:T(8,128)} %field.1, s32[2,1024]{1,0:T(2,128)} %departure.5, ...), custom_call_target="tpu_custom_call" | custom-call | tf_op jit(solution)/shard_map/pallas_call | solution.py:368
  3.6 0.0 copy-start.2
  3.6 8.1 %collective-permute-start = (f32[8,128]{1,0:T(8,128)S(1)}, f32[8,128]{1,0:T(8,128)S(1)}, u32[]{:S(2)}, u32[]{:S(2)}) collective-permute-start(f32[8,128]{1,0:T(8,128)S(1)} %get-tuple-element.23), channel_id=1, source_target_pairs={{0,3},{1,30},{2,5},{3,0},{4,7},{5,2},{6,9},{7,4},{8,11},{9,6},{10,... | collective-permute-start | bytes 12296 | tf_op jit(solution)/shard_map/ppermute | solution.py:28
  11.6 0.0 collective-permute-start.1
  11.7 2.2 %collective-permute-start.2 = (f32[528,128]{1,0:T(8,128)S(1)}, f32[528,128]{1,0:T(8,128)S(1)}, u32[]{:S(2)}, u32[]{:S(2)}) collective-permute-start(f32[528,128]{1,0:T(8,128)S(1)} %get-tuple-element.25), channel_id=1, source_target_pairs={{0,31},{1,2},{2,1},{3,4},{4,3},{5,6},{6,5},{7,8},{8,7},{9,10},{10,... | collective-permute-start | bytes 811016 | tf_op jit(solution)/shard_map/ppermute | solution.py:28
  13.8 0.0 collective-permute-start.3
  13.8 0.7 collective-permute-start.4
  14.6 0.0 collective-permute-done.tiny_a
  14.6 2.2 %collective-permute-start.5 = (f32[528,128]{1,0:T(8,128)S(1)}, f32[528,128]{1,0:T(8,128)S(1)}, u32[]{:S(2)}, u32[]{:S(2)}) collective-permute-start(f32[528,128]{1,0:T(8,128)S(1)} %get-tuple-element.28), channel_id=1, source_target_pairs={{0,30},{1,31},{2,4},{3,5},{4,2},{5,3},{6,8},{7,9},{8,6},{9,7},{10,... | collective-permute-start | bytes 811016 | tf_op jit(solution)/shard_map/ppermute | solution.py:28
  16.8 0.0 collective-permute-done.1.tiny_b
  16.8 0.0 copy-done
  16.8 0.0 copy-done.3
  16.8 0.0 copy-done.2
  16.8 1.6 %shard_map.56.start = f32[1024,128]{1,0:T(8,128)S(1)} custom-call(s32[1]{0:T(128)} %bitcast.self_ref, f32[1024,128]{1,0:T(8,128)S(1)} %copy-done, s32[2,1024]{1,0:T(2,128)S(1)} %copy-done.2, f32[2,1024]{1,0:T(2,128)S(1)} %copy-done.3, f32[8,128]{1,0:T(8,128)S(1)} %get-tuple-element.22.spilled, f32[8,128]{1,0:T(8,128)S(1)} %collective-permute-done.tiny_a, ...), custom_call_target="tpu_custom_call" | custom-call | flops 3000000000 | bytes 11718750 | tf_op jit(solution)/shard_map/pallas_call | solution.py:340
  18.4 0.0 copy-start.4
  18.4 1.8 %collective-permute-done.2.p0 = f32[528,128]{1,0:T(8,128)S(1)} collective-permute-done((f32[528,128]{1,0:T(8,128)S(1)}, f32[528,128]{1,0:T(8,128)S(1)}, u32[]{:S(2)}, u32[]{:S(2)}) %collective-permute-start.2) | collective-permute-done | bytes 270368 | tf_op jit(solution)/shard_map/ppermute | solution.py:28
  20.1 0.0 collective-permute-done.3.p1
  20.1 1.7 %shard_map.57.start = f32[1024,128]{1,0:T(8,128)S(1)} custom-call(f32[1024,128]{1,0:T(8,128)S(1)} %shard_map.56.start, f32[528,128]{1,0:T(8,128)S(1)} %collective-permute-done.2.p0, f32[528,128]{1,0:T(8,128)S(1)} %collective-permute-done.3.p1), custom_call_target="tpu_custom_call" | custom-call | flops 3000000000 | bytes 11718750 | tf_op jit(solution)/shard_map/pallas_call | solution.py:348
  21.8 1.2 %collective-permute-done.4.p0 = f32[528,128]{1,0:T(8,128)S(1)} collective-permute-done((f32[528,128]{1,0:T(8,128)S(1)}, f32[528,128]{1,0:T(8,128)S(1)}, u32[]{:S(2)}, u32[]{:S(2)}) %collective-permute-start.4) | collective-permute-done | bytes 270368 | tf_op jit(solution)/shard_map/ppermute | solution.py:28
  23.0 3.5 %collective-permute-done.5.p1 = f32[528,128]{1,0:T(8,128)S(1)} collective-permute-done((f32[528,128]{1,0:T(8,128)S(1)}, f32[528,128]{1,0:T(8,128)S(1)}, u32[]{:S(2)}, u32[]{:S(2)}) %collective-permute-start.5) | collective-permute-done | bytes 270368 | tf_op jit(solution)/shard_map/ppermute | solution.py:28
  26.5 0.0 copy-done.4
  26.5 2.0 %shard_map.58 = f32[1024,128]{1,0:T(8,128)S(1)} custom-call(f32[1024,128]{1,0:T(8,128)S(1)} %shard_map.57.start, f32[528,128]{1,0:T(8,128)S(1)} %collective-permute-done.4.p0, f32[528,128]{1,0:T(8,128)S(1)} %collective-permute-done.5.p1, f32[2,128,128]{2,1,0:T(8,128)S(1)} %copy-done.4), custom_call_target="tpu_custom_call" | custom-call | flops 3000000000 | bytes 11718750 | tf_op jit(solution)/shard_map/pallas_call | solution.py:349
  28.6 0.0 copy-start.1
  28.6 16.1 %all_to_all.10.x = f32[8,128,128]{2,1,0:T(8,128)S(1)} all-to-all(f32[8,128,128]{2,1,0:T(8,128)S(1)} %bitcast.8), channel_id=1, replica_groups=mesh['grp'=8,'tile'=32] {'grp'}, dimensions={0} | all-to-all | bytes 1048576 | tf_op jit(solution)/shard_map/all_to_all | solution.py:385
  44.7 0.0 copy-done.1
  44.7 1.2 %shard_map.59 = f32[8,128,128]{2,1,0:T(8,128)} custom-call(f32[64,128]{1,0:T(8,128)S(1)} %bitcast.9, f32[8,128,128]{2,1,0:T(8,128)S(1)} %all_to_all.10.x), custom_call_target="tpu_custom_call" | custom-call | tf_op jit(solution)/shard_map/pallas_call | solution.py:386
  45.9 3.9 %all-to-all-start.1 = ((f32[8,128,128]{2,1,0:T(8,128)}), f32[8,128,128]{2,1,0:T(8,128)S(1)}, u32[]{:S(2)}, u32[]{:S(2)}) async-start(f32[8,128,128]{2,1,0:T(8,128)} %shard_map.59), calls=%async_computation.1 | async-start | bytes 1048576 | tf_op jit(solution)/shard_map/all_to_all | solution.py:387
  49.7 1.4 %shard_map.60 = (s32[1,1024]{1,0:T(1,128)S(1)}, bf16[80,1024]{1,0:T(8,128)(2,1)S(1)}, f32[32,128]{1,0:T(8,128)S(1)}) custom-call(s32[1]{0:T(128)} %bitcast.self_ref, s32[2,1024]{1,0:T(2,128)S(1)} %copy-done.2, f32[2,1024]{1,0:T(2,128)S(1)} %copy-done.3), custom_call_target="tpu_custom_call" | custom-call | flops 2000000000 | bytes 7812500 | tf_op jit(solution)/shard_map/pallas_call | solution.py:371
  51.1 7.3 %all-to-all-done.1 = f32[8,128,128]{2,1,0:T(8,128)S(1)} async-done(((f32[8,128,128]{2,1,0:T(8,128)}), f32[8,128,128]{2,1,0:T(8,128)S(1)}, u32[]{:S(2)}, u32[]{:S(2)}) %all-to-all-start.1) | async-done | bytes 524320 | tf_op jit(solution)/shard_map/all_to_all | solution.py:387
  58.4 1.3 %shard_map.61 = (f32[528,128]{1,0:T(8,128)S(1)}, f32[528,128]{1,0:T(8,128)S(1)}, f32[528,128]{1,0:T(8,128)S(1)}, f32[528,128]{1,0:T(8,128)S(1)}, f32[8,128]{1,0:...) custom-call(s32[1]{0:T(128)} %bitcast.self_ref, f32[1024,128]{1,0:T(8,128)S(1)} %bitcast.6, ...), custom_call_target="tpu_custom_call" | custom-call | tf_op jit(solution)/shard_map/pallas_call | solution.py:389
  59.7 2.2 %collective-permute-start.6 = (f32[8,128]{1,0:T(8,128)S(1)}, f32[8,128]{1,0:T(8,128)S(1)}, u32[]{:S(2)}, u32[]{:S(2)}) collective-permute-start(f32[8,128]{1,0:T(8,128)S(1)} %get-tuple-element.33), channel_id=1, source_target_pairs={{0,3},{1,30},{2,5},{3,0},{4,7},{5,2},{6,9},{7,4},{8,11},{9,6},{10,... | collective-permute-start | bytes 12296 | tf_op jit(solution)/shard_map/ppermute | solution.py:28
  61.9 0.6 collective-permute-start.7
  62.5 0.0 collective-permute-start.8
  62.5 2.8 %collective-permute-start.9 = (f32[528,128]{1,0:T(8,128)S(1)}, f32[528,128]{1,0:T(8,128)S(1)}, u32[]{:S(2)}, u32[]{:S(2)}) collective-permute-start(f32[528,128]{1,0:T(8,128)S(1)} %get-tuple-element.36), channel_id=1, source_target_pairs={{0,1},{1,0},{2,3},{3,2},{4,5},{5,4},{6,7},{7,6},{8,9},{9,8},{10,11... | collective-permute-start | bytes 811016 | tf_op jit(solution)/shard_map/ppermute | solution.py:28
  65.3 0.0 collective-permute-start.10
  65.3 0.0 collective-permute-done.6.tiny_a
  65.3 3.0 %collective-permute-start.11 = (f32[528,128]{1,0:T(8,128)S(1)}, f32[528,128]{1,0:T(8,128)S(1)}, u32[]{:S(2)}, u32[]{:S(2)}) collective-permute-start(f32[528,128]{1,0:T(8,128)S(1)} %get-tuple-element.38), channel_id=1, source_target_pairs={{0,30},{1,31},{2,4},{3,5},{4,2},{5,3},{6,8},{7,9},{8,6},{9,7},{10,... | collective-permute-start | bytes 811016 | tf_op jit(solution)/shard_map/ppermute | solution.py:28
  68.3 0.0 collective-permute-done.7.tiny_b
  68.3 1.6 %shard_map.62.start = f32[1024,128]{1,0:T(8,128)S(1)} custom-call(s32[1]{0:T(128)} %bitcast.self_ref, f32[1024,128]{1,0:T(8,128)S(1)} %bitcast.7, s32[2,1024]{1,0:T(2,128)S(1)} %copy-done.2, f32[2,1024]{1,0:T(2,128)S(1)} %copy-done.3, f32[8,128]{1,0:T(8,128)S(1)} %get-tuple-element.32.spilled, f32[8,128]{1,0:T(8,128)S(1)} %collective-permute-done.6.tiny_a, ...), custom_call_target="tpu_custom_call" | custom-call | flops 3000000000 | bytes 11718750 | tf_op jit(solution)/shard_map/pallas_call | solution.py:340
  69.9 0.0 collective-permute-done.8.p0
  69.9 0.0 collective-permute-done.9.p1
  69.9 1.7 %shard_map.63.start = f32[1024,128]{1,0:T(8,128)S(1)} custom-call(f32[1024,128]{1,0:T(8,128)S(1)} %shard_map.62.start, f32[528,128]{1,0:T(8,128)S(1)} %collective-permute-done.8.p0, f32[528,128]{1,0:T(8,128)S(1)} %collective-permute-done.9.p1), custom_call_target="tpu_custom_call" | custom-call | flops 3000000000 | bytes 11718750 | tf_op jit(solution)/shard_map/pallas_call | solution.py:348
  71.6 2.2 %collective-permute-done.10.p0 = f32[528,128]{1,0:T(8,128)S(1)} collective-permute-done((f32[528,128]{1,0:T(8,128)S(1)}, f32[528,128]{1,0:T(8,128)S(1)}, u32[]{:S(2)}, u32[]{:S(2)}) %collective-permute-start.10) | collective-permute-done | bytes 270368 | tf_op jit(solution)/shard_map/ppermute | solution.py:28
  73.8 2.4 %collective-permute-done.11.p1 = f32[528,128]{1,0:T(8,128)S(1)} collective-permute-done((f32[528,128]{1,0:T(8,128)S(1)}, f32[528,128]{1,0:T(8,128)S(1)}, u32[]{:S(2)}, u32[]{:S(2)}) %collective-permute-start.11) | collective-permute-done | bytes 270368 | tf_op jit(solution)/shard_map/ppermute | solution.py:28
  76.3 2.8 %shard_map.64 = f32[1024,128]{1,0:T(8,128)} custom-call(f32[1024,128]{1,0:T(8,128)S(1)} %shard_map.63.start, f32[528,128]{1,0:T(8,128)S(1)} %collective-permute-done.10.p0, f32[528,128]{1,0:T(8,128)S(1)} %collective-permute-done.11.p1, f32[2,128,128]{2,1,0:T(8,128)S(1)} %copy-done.4), custom_call_target="tpu_custom_call" | custom-call | flops 3000000000 | bytes 11718750 | tf_op jit(solution)/shard_map/pallas_call | solution.py:349
Async XLA Ops:
  0.0 16.8 %copy-start = (f32[1024,128]{1,0:T(8,128)S(1)}, f32[1024,128]{1,0:T(8,128)}, u32[]{:S(2)}) copy-start(f32[1024,128]{1,0:T(8,128)} %field.1) | copy-start | bytes 1572868
  0.0 16.8 %copy-start.3 = (f32[2,1024]{1,0:T(2,128)S(1)}, f32[2,1024]{1,0:T(2,128)}, u32[]{:S(2)}) copy-start(f32[2,1024]{1,0:T(2,128)} %fraction.5) | copy-start | bytes 24580
  3.6 13.2 %copy-start.2 = (s32[2,1024]{1,0:T(2,128)S(1)}, s32[2,1024]{1,0:T(2,128)}, u32[]{:S(2)}) copy-start(s32[2,1024]{1,0:T(2,128)} %departure.5) | copy-start | bytes 24580
  3.6 11.0 %collective-permute-start = (f32[8,128]{1,0:T(8,128)S(1)}, f32[8,128]{1,0:T(8,128)S(1)}, u32[]{:S(2)}, u32[]{:S(2)}) collective-permute-start(f32[8,128]{1,0:T(8,128)S(1)} %get-tuple-element.23), channel_id=1, source_target_pairs={{0,3},{1,30},{2,5},{3,0},{4,7},{5,2},{6,9},{7,4},{8,11},{9,6},{10,... | collective-permute-start | bytes 12296 | tf_op jit(solution)/shard_map/ppermute | solution.py:28
  11.6 5.1 %collective-permute-start.1 = (f32[8,128]{1,0:T(8,128)S(1)}, f32[8,128]{1,0:T(8,128)S(1)}, u32[]{:S(2)}, u32[]{:S(2)}) collective-permute-start(f32[8,128]{1,0:T(8,128)S(1)} %get-tuple-element.24), channel_id=1, source_target_pairs={{0,29},{1,4},{2,31},{3,6},{4,1},{5,8},{6,3},{7,10},{8,5},{9,12},{1... | collective-permute-start | bytes 12296 | tf_op jit(solution)/shard_map/ppermute | solution.py:28
  11.7 8.5 %collective-permute-start.2 = (f32[528,128]{1,0:T(8,128)S(1)}, f32[528,128]{1,0:T(8,128)S(1)}, u32[]{:S(2)}, u32[]{:S(2)}) collective-permute-start(f32[528,128]{1,0:T(8,128)S(1)} %get-tuple-element.25), channel_id=1, source_target_pairs={{0,31},{1,2},{2,1},{3,4},{4,3},{5,6},{6,5},{7,8},{8,7},{9,10},{10,... | collective-permute-start | bytes 811016 | tf_op jit(solution)/shard_map/ppermute | solution.py:28
  13.8 6.3 %collective-permute-start.3 = (f32[528,128]{1,0:T(8,128)S(1)}, f32[528,128]{1,0:T(8,128)S(1)}, u32[]{:S(2)}, u32[]{:S(2)}) collective-permute-start(f32[528,128]{1,0:T(8,128)S(1)} %get-tuple-element.26), channel_id=1, source_target_pairs={{0,1},{1,0},{2,3},{3,2},{4,5},{5,4},{6,7},{7,6},{8,9},{9,8},{10,11... | collective-permute-start | bytes 811016 | tf_op jit(solution)/shard_map/ppermute | solution.py:28
  13.8 9.2 %collective-permute-start.4 = (f32[528,128]{1,0:T(8,128)S(1)}, f32[528,128]{1,0:T(8,128)S(1)}, u32[]{:S(2)}, u32[]{:S(2)}) collective-permute-start(f32[528,128]{1,0:T(8,128)S(1)} %get-tuple-element.27), channel_id=1, source_target_pairs={{0,2},{1,3},{2,0},{3,1},{4,6},{5,7},{6,4},{7,5},{8,10},{9,11},{10,... | collective-permute-start | bytes 811016 | tf_op jit(solution)/shard_map/ppermute | solution.py:28
  14.6 11.9 %collective-permute-start.5 = (f32[528,128]{1,0:T(8,128)S(1)}, f32[528,128]{1,0:T(8,128)S(1)}, u32[]{:S(2)}, u32[]{:S(2)}) collective-permute-start(f32[528,128]{1,0:T(8,128)S(1)} %get-tuple-element.28), channel_id=1, source_target_pairs={{0,30},{1,31},{2,4},{3,5},{4,2},{5,3},{6,8},{7,9},{8,6},{9,7},{10,... | collective-permute-start | bytes 811016 | tf_op jit(solution)/shard_map/ppermute | solution.py:28
  18.4 8.1 %copy-start.4 = (f32[2,128,128]{2,1,0:T(8,128)S(1)}, f32[2,128,128]{2,1,0:T(8,128)}, u32[]{:S(2)}) copy-start(f32[2,128,128]{2,1,0:T(8,128)} %level_map.3) | copy-start | bytes 393220
  28.6 16.1 %copy-start.1 = (f32[128,8,8]{0,2,1:T(8,128)S(1)}, f32[128,8,8]{0,2,1:T(8,128)}, u32[]{:S(2)}) copy-start(f32[128,8,8]{0,2,1:T(8,128)} %param.9) | copy-start | bytes 98308
  45.9 12.5 %all-to-all-start.1 = ((f32[8,128,128]{2,1,0:T(8,128)}), f32[8,128,128]{2,1,0:T(8,128)S(1)}, u32[]{:S(2)}, u32[]{:S(2)}) async-start(f32[8,128,128]{2,1,0:T(8,128)} %shard_map.59), calls=%async_computation.1 | async-start | bytes 1048576 | tf_op jit(solution)/shard_map/all_to_all | solution.py:387
  59.7 5.6 %collective-permute-start.6 = (f32[8,128]{1,0:T(8,128)S(1)}, f32[8,128]{1,0:T(8,128)S(1)}, u32[]{:S(2)}, u32[]{:S(2)}) collective-permute-start(f32[8,128]{1,0:T(8,128)S(1)} %get-tuple-element.33), channel_id=1, source_target_pairs={{0,3},{1,30},{2,5},{3,0},{4,7},{5,2},{6,9},{7,4},{8,11},{9,6},{10,... | collective-permute-start | bytes 12296 | tf_op jit(solution)/shard_map/ppermute | solution.py:28
  61.9 6.4 %collective-permute-start.7 = (f32[8,128]{1,0:T(8,128)S(1)}, f32[8,128]{1,0:T(8,128)S(1)}, u32[]{:S(2)}, u32[]{:S(2)}) collective-permute-start(f32[8,128]{1,0:T(8,128)S(1)} %get-tuple-element.34), channel_id=1, source_target_pairs={{0,29},{1,4},{2,31},{3,6},{4,1},{5,8},{6,3},{7,10},{8,5},{9,12},{1... | collective-permute-start | bytes 12296 | tf_op jit(solution)/shard_map/ppermute | solution.py:28
  62.5 7.4 %collective-permute-start.8 = (f32[528,128]{1,0:T(8,128)S(1)}, f32[528,128]{1,0:T(8,128)S(1)}, u32[]{:S(2)}, u32[]{:S(2)}) collective-permute-start(f32[528,128]{1,0:T(8,128)S(1)} %get-tuple-element.35), channel_id=1, source_target_pairs={{0,31},{1,2},{2,1},{3,4},{4,3},{5,6},{6,5},{7,8},{8,7},{9,10},{10,... | collective-permute-start | bytes 811016 | tf_op jit(solution)/shard_map/ppermute | solution.py:28
  62.5 7.4 %collective-permute-start.9 = (f32[528,128]{1,0:T(8,128)S(1)}, f32[528,128]{1,0:T(8,128)S(1)}, u32[]{:S(2)}, u32[]{:S(2)}) collective-permute-start(f32[528,128]{1,0:T(8,128)S(1)} %get-tuple-element.36), channel_id=1, source_target_pairs={{0,1},{1,0},{2,3},{3,2},{4,5},{5,4},{6,7},{7,6},{8,9},{9,8},{10,11... | collective-permute-start | bytes 811016 | tf_op jit(solution)/shard_map/ppermute | solution.py:28
  65.3 8.6 %collective-permute-start.10 = (f32[528,128]{1,0:T(8,128)S(1)}, f32[528,128]{1,0:T(8,128)S(1)}, u32[]{:S(2)}, u32[]{:S(2)}) collective-permute-start(f32[528,128]{1,0:T(8,128)S(1)} %get-tuple-element.37), channel_id=1, source_target_pairs={{0,2},{1,3},{2,0},{3,1},{4,6},{5,7},{6,4},{7,5},{8,10},{9,11},{10,... | collective-permute-start | bytes 811016 | tf_op jit(solution)/shard_map/ppermute | solution.py:28
  65.3 11.0 %collective-permute-start.11 = (f32[528,128]{1,0:T(8,128)S(1)}, f32[528,128]{1,0:T(8,128)S(1)}, u32[]{:S(2)}, u32[]{:S(2)}) collective-permute-start(f32[528,128]{1,0:T(8,128)S(1)} %get-tuple-element.38), channel_id=1, source_target_pairs={{0,30},{1,31},{2,4},{3,5},{4,2},{5,3},{6,8},{7,9},{8,6},{9,7},{10,... | collective-permute-start | bytes 811016 | tf_op jit(solution)/shard_map/ppermute | solution.py:28

commit v3 on v2

--- a/solution.py
+++ b/solution.py
@@ -285,14 +285,12 @@
     return spill
 
 
-def near_kernel(start, p0, p1, out, both_ref):
-    spill = deposit_sums(start, (p0, p1), out, both_ref)
-    add_spill(out, spill)
-
-
-def far_kernel(step, start, p0, p1, level_map, out, both_ref, sum_ref):
-    spill = deposit_sums(start, (p0, p1), sum_ref, both_ref)
-    add_spill(sum_ref, spill)
+def middle_kernel(start, p0, p1, p2, out, both_ref):
+    add_spill(out, deposit_sums(start, (p0, p1, p2), out, both_ref))
+
+
+def last_kernel(step, start, payload, level_map, out, both_ref, sum_ref):
+    add_spill(sum_ref, deposit_sums(start, (payload,), sum_ref, both_ref))
     map_high, map_low = halves(level_map[step])
     high, low = halves(sum_ref[...])
     out[...] = dot_nt(high, map_high) + (dot_nt(high, map_low) + dot_nt(low, map_high))
@@ -334,7 +332,8 @@
 def transported(step, packed, tile_count, tile_self, field, departure, fraction, level_map):
     tiny = [swapped(packed[w], w) for w in (4, 5)]
     far = [swapped(packed[w], w) for w in (0, 1)]
-    near = [swapped(packed[w], w) for w in (2, 3)]
+    cross = swapped(packed[2], 2)
+    partner = swapped(packed[3], 3)
     total = jax.ShapeDtypeStruct((COLS, LEV), F32)
     work = 3 * 10**9
     own = call(
@@ -344,15 +343,14 @@
         [pltpu.VMEM((COLS, 2 * LEV), BF)],
         work,
     )(tile_self, field, departure, fraction, packed[6], *tiny)
-    both = pltpu.VMEM((2, CAP, 2 * LEV), BF)
-    summed = call(near_kernel, total, [VM] * 3, [both], work)(own, *near)
+    summed = call(middle_kernel, total, [VM] * 4, [pltpu.VMEM((3, CAP, 2 * LEV), BF)], work)(own, *far, partner)
     return call(
-        functools.partial(far_kernel, step),
+        functools.partial(last_kernel, step),
         total,
-        [VM] * 4,
-        [both, pltpu.VMEM((COLS, LEV), F32)],
+        [VM] * 3,
+        [pltpu.VMEM((1, CAP, 2 * LEV), BF), pltpu.VMEM((COLS, LEV), F32)],
         work,
-    )(summed, *far, level_map)
+    )(summed, cross, level_map)
 
 
 def body(adjoint_in, departure, fraction, level_map, coarse_map):

time: 79.4 us -> 77.5 us (0.976)
  waiting for transfers between devices: 18.4 us -> 15.6 us
  starting transfers between devices: 25.7 us -> 27.2 us
  blocking collectives: 16.1 us -> 15 us
    ppermute x12, waiting for transfers between devices: 11.1 us -> 8.52 us  [swapped(): lax.ppermute(x, 'tile', [(i, (i + signs(i)[which]) % length) for i in ran...]
    ppermute x12, starting transfers between devices: 21.8 us -> 23.7 us  [swapped(): lax.ppermute(x, 'tile', [(i, (i + signs(i)[which]) % length) for i in ran...]
    all_to_all x1, blocking collectives: 16.1 us -> 15 us  [body(): lax.all_to_all(second.reshape(groups, COLS // groups, LEV), 'grp', 0, 0)]
  transfers between devices with their start and end apart: 13 -> 13, of which waited for: 6 -> 7; matrix products, arithmetic and copies ran while one was open for 0% -> 0% of each run, Pallas kernels for 10% -> 12%
where the time goes in v3:
time: 77.5 us; the launch traced here: 76.7 us
  starting transfers between devices  27.2 us (35%)
  Pallas kernels  18.7 us (24%)
  waiting for transfers between devices  15.6 us (20%)
  blocking collectives  15 us (19%)
    ppermute x12, starting transfers between devices, swapped(): lax.ppermute(x, 'tile', [(i, (i + signs(i)[which]) % length) for i in ran...  23.7 us
    all_to_all x1, blocking collectives, body(): lax.all_to_all(second.reshape(groups, COLS // groups, LEV), 'grp', 0, 0)  15 us
    ppermute x12, waiting for transfers between devices, swapped(): lax.ppermute(x, 'tile', [(i, (i + signs(i)[which]) % length) for i in ran...  8.52 us
    all_to_all x1, waiting for transfers between devices, body(): coupled = lax.all_to_all(mixed, 'grp', 0, 0).reshape(COLS, LEV)  7.07 us
    pallas_call x2, Pallas kernels, transported(): call(middle_kernel, total, [VM] * 4, [pltpu.VMEM((3, CAP, 2 * LEV), BF)],...  4.64 us
    pallas_call x1, Pallas kernels, body(): call(functools.partial(first_pack_kernel, tile_count), PACKED, [SM, HBM,...  3.55 us
    pallas_call x2, Pallas kernels, transported(): call(functools.partial(last_kernel, step), total, [VM] * 3, [pltpu.VMEM((...  3.5 us
    all_to_all x1, starting transfers between devices, body(): coupled = lax.all_to_all(mixed, 'grp', 0, 0).reshape(COLS, LEV)  3.49 us
  transfers between devices with their start and end apart: 13, of which 7 were waited for; matrix products, arithmetic and copies ran while one was open for 0% of the time, Pallas kernels for 12%

profile of v3, /device:TPU:1, one launch (start us, length us, event | category | flops | bytes accessed | tf_op | source)
XLA Modules:
  0.0 76.7 jit_solution(3658117983364389540)
XLA Ops:
  0.0 0.0 copy-start
  0.0 0.0 copy-start.3
  0.0 3.6 %shard_map.55 = (f32[528,128]{1,0:T(8,128)S(1)}, f32[528,128]{1,0:T(8,128)S(1)}, f32[528,128]{1,0:T(8,128)S(1)}, f32[528,128]{1,0:T(8,128)S(1)}, f32[8,128]{1,0:...) custom-call(s32[1]{0:T(128)} %bitcast.self_ref, f32[1024,128]{1,0:T(8,128)} %field.1, s32[2,1024]{1,0:T(2,128)} %departure.5, ...), custom_call_target="tpu_custom_call" | custom-call | tf_op jit(solution)/shard_map/pallas_call | solution.py:366
  3.6 0.0 copy-start.2
  3.6 8.1 %collective-permute-start = (f32[8,128]{1,0:T(8,128)S(1)}, f32[8,128]{1,0:T(8,128)S(1)}, u32[]{:S(2)}, u32[]{:S(2)}) collective-permute-start(f32[8,128]{1,0:T(8,128)S(1)} %get-tuple-element.23), channel_id=1, source_target_pairs={{0,3},{1,30},{2,5},{3,0},{4,7},{5,2},{6,9},{7,4},{8,11},{9,6},{10,... | collective-permute-start | bytes 12296 | tf_op jit(solution)/shard_map/ppermute | solution.py:28
  11.6 0.0 collective-permute-start.1
  11.7 0.6 collective-permute-start.2
  12.3 0.9 %collective-permute-start.3 = (f32[528,128]{1,0:T(8,128)S(1)}, f32[528,128]{1,0:T(8,128)S(1)}, u32[]{:S(2)}, u32[]{:S(2)}) collective-permute-start(f32[528,128]{1,0:T(8,128)S(1)} %get-tuple-element.26), channel_id=1, source_target_pairs={{0,30},{1,31},{2,4},{3,5},{4,2},{5,3},{6,8},{7,9},{8,6},{9,7},{10,... | collective-permute-start | bytes 811016 | tf_op jit(solution)/shard_map/ppermute | solution.py:28
  13.1 1.2 %collective-permute-start.4 = (f32[528,128]{1,0:T(8,128)S(1)}, f32[528,128]{1,0:T(8,128)S(1)}, u32[]{:S(2)}, u32[]{:S(2)}) collective-permute-start(f32[528,128]{1,0:T(8,128)S(1)} %get-tuple-element.27), channel_id=1, source_target_pairs={{0,1},{1,0},{2,3},{3,2},{4,5},{5,4},{6,7},{7,6},{8,9},{9,8},{10,11... | collective-permute-start | bytes 811016 | tf_op jit(solution)/shard_map/ppermute | solution.py:28
  14.3 0.0 collective-permute-done.tiny_a
  14.3 0.6 collective-permute-start.5
  14.9 0.7 collective-permute-done.1.tiny_b
  15.6 0.0 copy-done
  15.6 0.0 copy-done.3
  15.6 0.0 copy-done.2
  15.6 1.6 %shard_map.56.start = f32[1024,128]{1,0:T(8,128)S(1)} custom-call(s32[1]{0:T(128)} %bitcast.self_ref, f32[1024,128]{1,0:T(8,128)S(1)} %copy-done, s32[2,1024]{1,0:T(2,128)S(1)} %copy-done.2, f32[2,1024]{1,0:T(2,128)S(1)} %copy-done.3, f32[8,128]{1,0:T(8,128)S(1)} %get-tuple-element.22.spilled, f32[8,128]{1,0:T(8,128)S(1)} %collective-permute-done.tiny_a, ...), custom_call_target="tpu_custom_call" | custom-call | flops 3000000000 | bytes 11718750 | tf_op jit(solution)/shard_map/pallas_call | solution.py:339
  17.2 0.0 copy-start.4
  17.2 1.0 %collective-permute-done.2.p0 = f32[528,128]{1,0:T(8,128)S(1)} collective-permute-done((f32[528,128]{1,0:T(8,128)S(1)}, f32[528,128]{1,0:T(8,128)S(1)}, u32[]{:S(2)}, u32[]{:S(2)}) %collective-permute-start.2) | collective-permute-done | bytes 270368 | tf_op jit(solution)/shard_map/ppermute | solution.py:28
  18.2 2.1 %collective-permute-done.3.p1 = f32[528,128]{1,0:T(8,128)S(1)} collective-permute-done((f32[528,128]{1,0:T(8,128)S(1)}, f32[528,128]{1,0:T(8,128)S(1)}, u32[]{:S(2)}, u32[]{:S(2)}) %collective-permute-start.3) | collective-permute-done | bytes 270368 | tf_op jit(solution)/shard_map/ppermute | solution.py:28
  20.4 0.0 collective-permute-done.4.p2
  20.4 2.3 %shard_map.57.start = f32[1024,128]{1,0:T(8,128)S(1)} custom-call(f32[1024,128]{1,0:T(8,128)S(1)} %shard_map.56.start, f32[528,128]{1,0:T(8,128)S(1)} %collective-permute-done.2.p0, f32[528,128]{1,0:T(8,128)S(1)} %collective-permute-done.3.p1, f32[528,128]{1,0:T(8,128)S(1)} %collective-permute-done.4.p2), custom_call_target="tpu_custom_call" | custom-call | flops 3000000000 | bytes 11718750 | tf_op jit(solution)/shard_map/pallas_call | solution.py:346
  22.7 0.5 collective-permute-done.5.payload
  23.1 0.0 copy-done.4
  23.1 1.4 %shard_map.58 = f32[1024,128]{1,0:T(8,128)S(1)} custom-call(f32[1024,128]{1,0:T(8,128)S(1)} %shard_map.57.start, f32[528,128]{1,0:T(8,128)S(1)} %collective-permute-done.5.payload, f32[2,128,128]{2,1,0:T(8,128)S(1)} %copy-done.4), custom_call_target="tpu_custom_call" | custom-call | flops 3000000000 | bytes 11718750 | tf_op jit(solution)/shard_map/pallas_call | solution.py:347
  24.5 0.0 copy-start.1
  24.5 15.0 %all_to_all.10.x = f32[8,128,128]{2,1,0:T(8,128)S(1)} all-to-all(f32[8,128,128]{2,1,0:T(8,128)S(1)} %bitcast.8), channel_id=1, replica_groups=mesh['grp'=8,'tile'=32] {'grp'}, dimensions={0} | all-to-all | bytes 1048576 | tf_op jit(solution)/shard_map/all_to_all | solution.py:383
  39.5 0.0 copy-done.1
  39.5 1.2 %shard_map.59 = f32[8,128,128]{2,1,0:T(8,128)} custom-call(f32[64,128]{1,0:T(8,128)S(1)} %bitcast.9, f32[8,128,128]{2,1,0:T(8,128)S(1)} %all_to_all.10.x), custom_call_target="tpu_custom_call" | custom-call | tf_op jit(solution)/shard_map/pallas_call | solution.py:384
  40.7 3.5 %all-to-all-start.1 = ((f32[8,128,128]{2,1,0:T(8,128)}), f32[8,128,128]{2,1,0:T(8,128)S(1)}, u32[]{:S(2)}, u32[]{:S(2)}) async-start(f32[8,128,128]{2,1,0:T(8,128)} %shard_map.59), calls=%async_computation.1 | async-start | bytes 1048576 | tf_op jit(solution)/shard_map/all_to_all | solution.py:385
  44.2 1.4 %shard_map.60 = (s32[1,1024]{1,0:T(1,128)S(1)}, bf16[80,1024]{1,0:T(8,128)(2,1)S(1)}, f32[32,128]{1,0:T(8,128)S(1)}) custom-call(s32[1]{0:T(128)} %bitcast.self_ref, s32[2,1024]{1,0:T(2,128)S(1)} %copy-done.2, f32[2,1024]{1,0:T(2,128)S(1)} %copy-done.3), custom_call_target="tpu_custom_call" | custom-call | flops 2000000000 | bytes 7812500 | tf_op jit(solution)/shard_map/pallas_call | solution.py:369
  45.6 7.1 %all-to-all-done.1 = f32[8,128,128]{2,1,0:T(8,128)S(1)} async-done(((f32[8,128,128]{2,1,0:T(8,128)}), f32[8,128,128]{2,1,0:T(8,128)S(1)}, u32[]{:S(2)}, u32[]{:S(2)}) %all-to-all-start.1) | async-done | bytes 524320 | tf_op jit(solution)/shard_map/all_to_all | solution.py:385
  52.6 1.3 %shard_map.61 = (f32[528,128]{1,0:T(8,128)S(1)}, f32[528,128]{1,0:T(8,128)S(1)}, f32[528,128]{1,0:T(8,128)S(1)}, f32[528,128]{1,0:T(8,128)S(1)}, f32[8,128]{1,0:...) custom-call(s32[1]{0:T(128)} %bitcast.self_ref, f32[1024,128]{1,0:T(8,128)S(1)} %bitcast.6, ...), custom_call_target="tpu_custom_call" | custom-call | tf_op jit(solution)/shard_map/pallas_call | solution.py:387
  54.0 7.1 %collective-permute-start.6 = (f32[8,128]{1,0:T(8,128)S(1)}, f32[8,128]{1,0:T(8,128)S(1)}, u32[]{:S(2)}, u32[]{:S(2)}) collective-permute-start(f32[8,128]{1,0:T(8,128)S(1)} %get-tuple-element.33), channel_id=1, source_target_pairs={{0,3},{1,30},{2,5},{3,0},{4,7},{5,2},{6,9},{7,4},{8,11},{9,6},{10,... | collective-permute-start | bytes 12296 | tf_op jit(solution)/shard_map/ppermute | solution.py:28
  61.1 0.0 collective-permute-start.7
  61.1 0.9 %collective-permute-start.10 = (f32[528,128]{1,0:T(8,128)S(1)}, f32[528,128]{1,0:T(8,128)S(1)}, u32[]{:S(2)}, u32[]{:S(2)}) collective-permute-start(f32[528,128]{1,0:T(8,128)S(1)} %get-tuple-element.37), channel_id=1, source_target_pairs={{0,1},{1,0},{2,3},{3,2},{4,5},{5,4},{6,7},{7,6},{8,9},{9,8},{10,11... | collective-permute-start | bytes 811016 | tf_op jit(solution)/shard_map/ppermute | solution.py:28
  62.0 0.8 %collective-permute-start.8 = (f32[528,128]{1,0:T(8,128)S(1)}, f32[528,128]{1,0:T(8,128)S(1)}, u32[]{:S(2)}, u32[]{:S(2)}) collective-permute-start(f32[528,128]{1,0:T(8,128)S(1)} %get-tuple-element.35), channel_id=1, source_target_pairs={{0,2},{1,3},{2,0},{3,1},{4,6},{5,7},{6,4},{7,5},{8,10},{9,11},{10,... | collective-permute-start | bytes 811016 | tf_op jit(solution)/shard_map/ppermute | solution.py:28
  62.8 3.4 %collective-permute-start.9 = (f32[528,128]{1,0:T(8,128)S(1)}, f32[528,128]{1,0:T(8,128)S(1)}, u32[]{:S(2)}, u32[]{:S(2)}) collective-permute-start(f32[528,128]{1,0:T(8,128)S(1)} %get-tuple-element.36), channel_id=1, source_target_pairs={{0,30},{1,31},{2,4},{3,5},{4,2},{5,3},{6,8},{7,9},{8,6},{9,7},{10,... | collective-permute-start | bytes 811016 | tf_op jit(solution)/shard_map/ppermute | solution.py:28
  66.2 0.0 collective-permute-done.6.tiny_a
  66.2 0.1 collective-permute-start.11
  66.3 0.0 collective-permute-done.7.tiny_b
  66.3 1.6 %shard_map.62.start = f32[1024,128]{1,0:T(8,128)S(1)} custom-call(s32[1]{0:T(128)} %bitcast.self_ref, f32[1024,128]{1,0:T(8,128)S(1)} %bitcast.7, s32[2,1024]{1,0:T(2,128)S(1)} %copy-done.2, f32[2,1024]{1,0:T(2,128)S(1)} %copy-done.3, f32[8,128]{1,0:T(8,128)S(1)} %get-tuple-element.32.spilled, f32[8,128]{1,0:T(8,128)S(1)} %collective-permute-done.6.tiny_a, ...), custom_call_target="tpu_custom_call" | custom-call | flops 3000000000 | bytes 11718750 | tf_op jit(solution)/shard_map/pallas_call | solution.py:339
  67.9 0.0 collective-permute-done.10.p2
  67.9 2.2 %collective-permute-done.8.p0 = f32[528,128]{1,0:T(8,128)S(1)} collective-permute-done((f32[528,128]{1,0:T(8,128)S(1)}, f32[528,128]{1,0:T(8,128)S(1)}, u32[]{:S(2)}, u32[]{:S(2)}) %collective-permute-start.8) | collective-permute-done | bytes 270368 | tf_op jit(solution)/shard_map/ppermute | solution.py:28
  70.2 2.0 %collective-permute-done.9.p1 = f32[528,128]{1,0:T(8,128)S(1)} collective-permute-done((f32[528,128]{1,0:T(8,128)S(1)}, f32[528,128]{1,0:T(8,128)S(1)}, u32[]{:S(2)}, u32[]{:S(2)}) %collective-permute-start.9) | collective-permute-done | bytes 270368 | tf_op jit(solution)/shard_map/ppermute | solution.py:28
  72.2 2.3 %shard_map.63.start = f32[1024,128]{1,0:T(8,128)S(1)} custom-call(f32[1024,128]{1,0:T(8,128)S(1)} %shard_map.62.start, f32[528,128]{1,0:T(8,128)S(1)} %collective-permute-done.8.p0, f32[528,128]{1,0:T(8,128)S(1)} %collective-permute-done.9.p1, f32[528,128]{1,0:T(8,128)S(1)} %collective-permute-done.10.p2), custom_call_target="tpu_custom_call" | custom-call | flops 3000000000 | bytes 11718750 | tf_op jit(solution)/shard_map/pallas_call | solution.py:346
  74.5 0.0 collective-permute-done.11.payload
  74.5 2.2 %shard_map.64 = f32[1024,128]{1,0:T(8,128)} custom-call(f32[1024,128]{1,0:T(8,128)S(1)} %shard_map.63.start, f32[528,128]{1,0:T(8,128)S(1)} %collective-permute-done.11.payload, f32[2,128,128]{2,1,0:T(8,128)S(1)} %copy-done.4), custom_call_target="tpu_custom_call" | custom-call | flops 3000000000 | bytes 11718750 | tf_op jit(solution)/shard_map/pallas_call | solution.py:347
Async XLA Ops:
  0.0 15.6 %copy-start = (f32[1024,128]{1,0:T(8,128)S(1)}, f32[1024,128]{1,0:T(8,128)}, u32[]{:S(2)}) copy-start(f32[1024,128]{1,0:T(8,128)} %field.1) | copy-start | bytes 1572868
  0.0 15.6 %copy-start.3 = (f32[2,1024]{1,0:T(2,128)S(1)}, f32[2,1024]{1,0:T(2,128)}, u32[]{:S(2)}) copy-start(f32[2,1024]{1,0:T(2,128)} %fraction.5) | copy-start | bytes 24580
  3.6 12.1 %copy-start.2 = (s32[2,1024]{1,0:T(2,128)S(1)}, s32[2,1024]{1,0:T(2,128)}, u32[]{:S(2)}) copy-start(s32[2,1024]{1,0:T(2,128)} %departure.5) | copy-start | bytes 24580
  3.6 10.8 %collective-permute-start = (f32[8,128]{1,0:T(8,128)S(1)}, f32[8,128]{1,0:T(8,128)S(1)}, u32[]{:S(2)}, u32[]{:S(2)}) collective-permute-start(f32[8,128]{1,0:T(8,128)S(1)} %get-tuple-element.23), channel_id=1, source_target_pairs={{0,3},{1,30},{2,5},{3,0},{4,7},{5,2},{6,9},{7,4},{8,11},{9,6},{10,... | collective-permute-start | bytes 12296 | tf_op jit(solution)/shard_map/ppermute | solution.py:28
  11.6 4.0 %collective-permute-start.1 = (f32[8,128]{1,0:T(8,128)S(1)}, f32[8,128]{1,0:T(8,128)S(1)}, u32[]{:S(2)}, u32[]{:S(2)}) collective-permute-start(f32[8,128]{1,0:T(8,128)S(1)} %get-tuple-element.24), channel_id=1, source_target_pairs={{0,29},{1,4},{2,31},{3,6},{4,1},{5,8},{6,3},{7,10},{8,5},{9,12},{1... | collective-permute-start | bytes 12296 | tf_op jit(solution)/shard_map/ppermute | solution.py:28
  11.7 6.6 %collective-permute-start.2 = (f32[528,128]{1,0:T(8,128)S(1)}, f32[528,128]{1,0:T(8,128)S(1)}, u32[]{:S(2)}, u32[]{:S(2)}) collective-permute-start(f32[528,128]{1,0:T(8,128)S(1)} %get-tuple-element.25), channel_id=1, source_target_pairs={{0,2},{1,3},{2,0},{3,1},{4,6},{5,7},{6,4},{7,5},{8,10},{9,11},{10,... | collective-permute-start | bytes 811016 | tf_op jit(solution)/shard_map/ppermute | solution.py:28
  12.3 8.1 %collective-permute-start.3 = (f32[528,128]{1,0:T(8,128)S(1)}, f32[528,128]{1,0:T(8,128)S(1)}, u32[]{:S(2)}, u32[]{:S(2)}) collective-permute-start(f32[528,128]{1,0:T(8,128)S(1)} %get-tuple-element.26), channel_id=1, source_target_pairs={{0,30},{1,31},{2,4},{3,5},{4,2},{5,3},{6,8},{7,9},{8,6},{9,7},{10,... | collective-permute-start | bytes 811016 | tf_op jit(solution)/shard_map/ppermute | solution.py:28
  13.1 7.3 %collective-permute-start.4 = (f32[528,128]{1,0:T(8,128)S(1)}, f32[528,128]{1,0:T(8,128)S(1)}, u32[]{:S(2)}, u32[]{:S(2)}) collective-permute-start(f32[528,128]{1,0:T(8,128)S(1)} %get-tuple-element.27), channel_id=1, source_target_pairs={{0,1},{1,0},{2,3},{3,2},{4,5},{5,4},{6,7},{7,6},{8,9},{9,8},{10,11... | collective-permute-start | bytes 811016 | tf_op jit(solution)/shard_map/ppermute | solution.py:28
  14.3 8.8 %collective-permute-start.5 = (f32[528,128]{1,0:T(8,128)S(1)}, f32[528,128]{1,0:T(8,128)S(1)}, u32[]{:S(2)}, u32[]{:S(2)}) collective-permute-start(f32[528,128]{1,0:T(8,128)S(1)} %get-tuple-element.28), channel_id=1, source_target_pairs={{0,31},{1,2},{2,1},{3,4},{4,3},{5,6},{6,5},{7,8},{8,7},{9,10},{10,... | collective-permute-start | bytes 811016 | tf_op jit(solution)/shard_map/ppermute | solution.py:28
  17.2 5.9 %copy-start.4 = (f32[2,128,128]{2,1,0:T(8,128)S(1)}, f32[2,128,128]{2,1,0:T(8,128)}, u32[]{:S(2)}) copy-start(f32[2,128,128]{2,1,0:T(8,128)} %level_map.3) | copy-start | bytes 393220
  24.5 15.0 %copy-start.1 = (f32[128,8,8]{0,2,1:T(8,128)S(1)}, f32[128,8,8]{0,2,1:T(8,128)}, u32[]{:S(2)}) copy-start(f32[128,8,8]{0,2,1:T(8,128)} %param.9) | copy-start | bytes 98308
  40.7 11.9 %all-to-all-start.1 = ((f32[8,128,128]{2,1,0:T(8,128)}), f32[8,128,128]{2,1,0:T(8,128)S(1)}, u32[]{:S(2)}, u32[]{:S(2)}) async-start(f32[8,128,128]{2,1,0:T(8,128)} %shard_map.59), calls=%async_computation.1 | async-start | bytes 1048576 | tf_op jit(solution)/shard_map/all_to_all | solution.py:385
  54.0 12.2 %collective-permute-start.6 = (f32[8,128]{1,0:T(8,128)S(1)}, f32[8,128]{1,0:T(8,128)S(1)}, u32[]{:S(2)}, u32[]{:S(2)}) collective-permute-start(f32[8,128]{1,0:T(8,128)S(1)} %get-tuple-element.33), channel_id=1, source_target_pairs={{0,3},{1,30},{2,5},{3,0},{4,7},{5,2},{6,9},{7,4},{8,11},{9,6},{10,... | collective-permute-start | bytes 12296 | tf_op jit(solution)/shard_map/ppermute | solution.py:28
  61.1 5.2 %collective-permute-start.7 = (f32[8,128]{1,0:T(8,128)S(1)}, f32[8,128]{1,0:T(8,128)S(1)}, u32[]{:S(2)}, u32[]{:S(2)}) collective-permute-start(f32[8,128]{1,0:T(8,128)S(1)} %get-tuple-element.34), channel_id=1, source_target_pairs={{0,29},{1,4},{2,31},{3,6},{4,1},{5,8},{6,3},{7,10},{8,5},{9,12},{1... | collective-permute-start | bytes 12296 | tf_op jit(solution)/shard_map/ppermute | solution.py:28
  61.1 6.8 %collective-permute-start.10 = (f32[528,128]{1,0:T(8,128)S(1)}, f32[528,128]{1,0:T(8,128)S(1)}, u32[]{:S(2)}, u32[]{:S(2)}) collective-permute-start(f32[528,128]{1,0:T(8,128)S(1)} %get-tuple-element.37), channel_id=1, source_target_pairs={{0,1},{1,0},{2,3},{3,2},{4,5},{5,4},{6,7},{7,6},{8,9},{9,8},{10,11... | collective-permute-start | bytes 811016 | tf_op jit(solution)/shard_map/ppermute | solution.py:28
  62.0 8.2 %collective-permute-start.8 = (f32[528,128]{1,0:T(8,128)S(1)}, f32[528,128]{1,0:T(8,128)S(1)}, u32[]{:S(2)}, u32[]{:S(2)}) collective-permute-start(f32[528,128]{1,0:T(8,128)S(1)} %get-tuple-element.35), channel_id=1, source_target_pairs={{0,2},{1,3},{2,0},{3,1},{4,6},{5,7},{6,4},{7,5},{8,10},{9,11},{10,... | collective-permute-start | bytes 811016 | tf_op jit(solution)/shard_map/ppermute | solution.py:28
  62.8 9.3 %collective-permute-start.9 = (f32[528,128]{1,0:T(8,128)S(1)}, f32[528,128]{1,0:T(8,128)S(1)}, u32[]{:S(2)}, u32[]{:S(2)}) collective-permute-start(f32[528,128]{1,0:T(8,128)S(1)} %get-tuple-element.36), channel_id=1, source_target_pairs={{0,30},{1,31},{2,4},{3,5},{4,2},{5,3},{6,8},{7,9},{8,6},{9,7},{10,... | collective-permute-start | bytes 811016 | tf_op jit(solution)/shard_map/ppermute | solution.py:28
  66.2 8.3 %collective-permute-start.11 = (f32[528,128]{1,0:T(8,128)S(1)}, f32[528,128]{1,0:T(8,128)S(1)}, u32[]{:S(2)}, u32[]{:S(2)}) collective-permute-start(f32[528,128]{1,0:T(8,128)S(1)} %get-tuple-element.38), channel_id=1, source_target_pairs={{0,31},{1,2},{2,1},{3,4},{4,3},{5,6},{6,5},{7,8},{8,7},{9,10},{10,... | collective-permute-start | bytes 811016 | tf_op jit(solution)/shard_map/ppermute | solution.py:28

commit v4 on v3

--- a/solution.py
+++ b/solution.py
@@ -236,22 +236,35 @@
     return high, low
 
 
-def own_kernel(step, tile_count, self_ref, field, departure, fraction, spilled, tiny_a, tiny_b, out, both_ref):
+def own_kernel(step, tile_count, self_ref, field, departure, fraction, spilled, payload, out, own_ref, both_ref):
     departure = departure[step : step + 1, :]
     fraction = fraction[step : step + 1, :]
     place, offset = locate(departure, self_ref[0], tile_count)
-    table = spread_table(place, [jnp.where(offset == 0, w, 0.0) for w in cubic_weights(fraction)])
+    own_table = spread_table(place, [jnp.where(offset == 0, w, 0.0) for w in cubic_weights(fraction)])
     high, low = halves(field[...])
-    both_ref[:, :LEV] = high
-    both_ref[:, LEV:] = low
+    own_ref[:, :LEV] = high
+    own_ref[:, LEV:] = low
+    table = payload_table(payload, both_ref, 0)
 
     @pl.loop(0, COLS // BLOCK)
     def _(b):
+        high, low = spread_block(b * BLOCK, own_table)
+        wide = dot(high, own_ref[...]) + dot(low, own_ref[...])
         high, low = spread_block(b * BLOCK, table)
-        wide = dot(high, both_ref[...]) + dot(low, both_ref[...])
+        wide = wide + dot(high, both_ref[0]) + dot(low, both_ref[0])
         out[pl.ds(b * BLOCK, BLOCK), :] = wide[:, :LEV] + wide[:, LEV:]
 
-    add_spill(out, spilled[...] + tiny_a[...] + tiny_b[...])
+    add_spill(out, spilled[...] + payload[CAP : CAP + 8, :])
+
+
+def payload_table(payload, both_ref, which):
+    high, low = halves(payload[0:CAP, :])
+    both_ref[which, :, :LEV] = high
+    both_ref[which, :, LEV:] = low
+    rows = [payload[CAP + 8 + c : CAP + 9 + c, :] for c in range(8)]
+    fraction = jnp.concatenate(rows[:4], axis=1)
+    place = jnp.concatenate(rows[4:], axis=1).astype(jnp.int32)
+    return spread_table(place, cubic_weights(fraction))
 
 
 def add_spill(out, block):
@@ -260,40 +273,50 @@
     out[COLS - 8 : COLS, :] = out[COLS - 8 : COLS, :] + jnp.where(row == 7, block, 0.0)
 
 
-def deposit_sums(start, payloads, out, both_ref):
-    tables = []
-    for which, payload in enumerate(payloads):
-        high, low = halves(payload[0:CAP, :])
-        both_ref[which, :, :LEV] = high
-        both_ref[which, :, LEV:] = low
-        rows = [payload[CAP + 8 + c : CAP + 9 + c, :] for c in range(8)]
-        fraction = jnp.concatenate(rows[:4], axis=1)
-        place = jnp.concatenate(rows[4:], axis=1).astype(jnp.int32)
-        tables.append(spread_table(place, cubic_weights(fraction)))
+def deposit_block(b, start, tables, both_ref):
+    wide = jnp.zeros((BLOCK, 2 * LEV), F32)
+    for which, table in enumerate(tables):
+        high, low = spread_block(b * BLOCK, table)
+        wide = wide + dot(high, both_ref[which]) + dot(low, both_ref[which])
+    return start[pl.ds(b * BLOCK, BLOCK), :] + wide[:, :LEV] + wide[:, LEV:]
+
+
+def middle_kernel(start, p0, p1, out, both_ref):
+    tables = [payload_table(p, both_ref, which) for which, p in enumerate((p0, p1))]
 
     @pl.loop(0, COLS // BLOCK)
     def _(b):
-        wide = jnp.zeros((BLOCK, 2 * LEV), F32)
-        for which, table in enumerate(tables):
-            high, low = spread_block(b * BLOCK, table)
-            wide = wide + dot(high, both_ref[which]) + dot(low, both_ref[which])
-        out[pl.ds(b * BLOCK, BLOCK), :] = start[pl.ds(b * BLOCK, BLOCK), :] + wide[:, :LEV] + wide[:, LEV:]
-
-    spill = payloads[0][CAP : CAP + 8, :]
-    for payload in payloads[1:]:
-        spill = spill + payload[CAP : CAP + 8, :]
-    return spill
-
-
-def middle_kernel(start, p0, p1, p2, out, both_ref):
-    add_spill(out, deposit_sums(start, (p0, p1, p2), out, both_ref))
-
-
-def last_kernel(step, start, payload, level_map, out, both_ref, sum_ref):
-    add_spill(sum_ref, deposit_sums(start, (payload,), sum_ref, both_ref))
+        out[pl.ds(b * BLOCK, BLOCK), :] = deposit_block(b, start, tables, both_ref)
+
+    add_spill(out, p0[CAP : CAP + 8, :] + p1[CAP : CAP + 8, :])
+
+
+def last_kernel(step, start, payload, tiny_a, tiny_b, level_map, out, both_ref, sum_ref, lifted_ref, sems):
+    table = payload_table(payload, both_ref, 0)
+    spill = payload[CAP : CAP + 8, :] + tiny_a[...] + tiny_b[...]
+    row = lax.broadcasted_iota(jnp.int32, (8, LEV), 0)
     map_high, map_low = halves(level_map[step])
-    high, low = halves(sum_ref[...])
-    out[...] = dot_nt(high, map_high) + (dot_nt(high, map_low) + dot_nt(low, map_high))
+
+    def copy(b):
+        rows = pl.ds(b * BLOCK, BLOCK)
+        return pltpu.make_async_copy(lifted_ref.at[rows, :], out.at[rows, :], sems.at[b])
+
+    for b in range(COLS // BLOCK):
+        sum_ref[...] = deposit_block(b, start, (table,), both_ref)
+        if b == 0:
+            sum_ref[0:8, :] = sum_ref[0:8, :] + jnp.where(row < 2, spill, 0.0)
+        if b == COLS // BLOCK - 1:
+            sum_ref[BLOCK - 8 : BLOCK, :] = sum_ref[BLOCK - 8 : BLOCK, :] + jnp.where(row == 7, spill, 0.0)
+        high, low = halves(sum_ref[...])
+        lifted = dot_nt(high, map_high) + (dot_nt(high, map_low) + dot_nt(low, map_high))
+        if step == 0:
+            lifted_ref[b * BLOCK : (b + 1) * BLOCK, :] = lifted
+            copy(b).start()
+        else:
+            out[b * BLOCK : (b + 1) * BLOCK, :] = lifted
+    if step == 0:
+        for b in range(COLS // BLOCK):
+            copy(b).wait()
 
 
 def couple_kernel(table, x, out):
@@ -316,13 +339,13 @@
 PACKED = [jax.ShapeDtypeStruct((ROWS, LEV), F32)] * 4 + [jax.ShapeDtypeStruct((8, LEV), F32)] * 3
 
 
-def call(kernel, out_shape, in_specs, scratch=(), flops=0):
+def call(kernel, out_shape, in_specs, scratch=(), flops=0, out_spec=None):
     multiple = isinstance(out_shape, (list, tuple))
     return pl.pallas_call(
         kernel,
         out_shape=out_shape,
         in_specs=in_specs,
-        out_specs=[VM] * len(out_shape) if multiple else VM,
+        out_specs=[VM] * len(out_shape) if multiple else out_spec or VM,
         scratch_shapes=list(scratch),
         compiler_params=PARAMS,
         cost_estimate=pl.CostEstimate(flops=flops, transcendentals=0, bytes_accessed=flops // 256),
@@ -330,27 +353,35 @@
 
 
 def transported(step, packed, tile_count, tile_self, field, departure, fraction, level_map):
-    tiny = [swapped(packed[w], w) for w in (4, 5)]
     far = [swapped(packed[w], w) for w in (0, 1)]
+    partner = swapped(packed[3], 3)
     cross = swapped(packed[2], 2)
-    partner = swapped(packed[3], 3)
+    late = lax.optimization_barrier((packed[4], packed[5], partner))
+    tiny = [swapped(late[w - 4], w) for w in (4, 5)]
     total = jax.ShapeDtypeStruct((COLS, LEV), F32)
+    one = pltpu.VMEM((1, CAP, 2 * LEV), BF)
     work = 3 * 10**9
     own = call(
         functools.partial(own_kernel, step, tile_count),
         total,
-        [SM] + [VM] * 6,
-        [pltpu.VMEM((COLS, 2 * LEV), BF)],
+        [SM] + [VM] * 5,
+        [pltpu.VMEM((COLS, 2 * LEV), BF), one],
         work,
-    )(tile_self, field, departure, fraction, packed[6], *tiny)
-    summed = call(middle_kernel, total, [VM] * 4, [pltpu.VMEM((3, CAP, 2 * LEV), BF)], work)(own, *far, partner)
+    )(tile_self, field, departure, fraction, packed[6], partner)
+    summed = call(middle_kernel, total, [VM] * 3, [pltpu.VMEM((2, CAP, 2 * LEV), BF)], work)(own, *far)
     return call(
         functools.partial(last_kernel, step),
         total,
-        [VM] * 3,
-        [pltpu.VMEM((1, CAP, 2 * LEV), BF), pltpu.VMEM((COLS, LEV), F32)],
+        [VM] * 5,
+        [
+            one,
+            pltpu.VMEM((BLOCK, LEV), F32),
+            pltpu.VMEM((COLS, LEV), F32),
+            pltpu.SemaphoreType.DMA((COLS // BLOCK,)),
+        ],
         work,
-    )(summed, cross, level_map)
+        HBM if step == 0 else VM,
+    )(summed, cross, *tiny, level_map)
 
 
 def body(adjoint_in, departure, fraction, level_map, coarse_map):

time: 77.5 us -> 75.1 us (0.969)
  waiting for transfers between devices: 15.6 us -> 12.1 us
  Pallas kernels: 18.7 us -> 19.7 us
    ppermute x12, waiting for transfers between devices: 8.52 us -> 5.07 us  [swapped(): lax.ppermute(x, 'tile', [(i, (i + signs(i)[which]) % length) for i in ran...]
    pallas_call x2, Pallas kernels: 3.16 us -> 4.58 us  [transported(): call(functools.partial(own_kernel, step, tile_count), total, [SM] + [VM]...]
  transfers between devices with their start and end apart: 13 -> 13, of which waited for: 7 -> 4; matrix products, arithmetic and copies ran while one was open for 0% -> 0% of each run, Pallas kernels for 12% -> 13%
where the time goes in v4:
time: 75.1 us; the launch traced here: 73.8 us
  starting transfers between devices  26.8 us (36%)
  Pallas kernels  19.7 us (26%)
  blocking collectives  14.8 us (20%)
  waiting for transfers between devices  12.1 us (16%)
    ppermute x12, starting transfers between devices, swapped(): lax.ppermute(x, 'tile', [(i, (i + signs(i)[which]) % length) for i in ran...  23.3 us
    all_to_all x1, blocking collectives, body(): lax.all_to_all(second.reshape(groups, COLS // groups, LEV), 'grp', 0, 0)  14.8 us
    all_to_all x1, waiting for transfers between devices, body(): coupled = lax.all_to_all(mixed, 'grp', 0, 0).reshape(COLS, LEV)  7.07 us
    ppermute x12, waiting for transfers between devices, swapped(): lax.ppermute(x, 'tile', [(i, (i + signs(i)[which]) % length) for i in ran...  5.07 us
    pallas_call x2, Pallas kernels, transported(): call(functools.partial(own_kernel, step, tile_count), total, [SM] + [VM]...  4.58 us
    pallas_call x2, Pallas kernels, transported(): call(functools.partial(last_kernel, step), total, [VM] * 5, [one, pltpu.V...  4.3 us
    pallas_call x1, Pallas kernels, body(): call(functools.partial(first_pack_kernel, tile_count), PACKED, [SM, HBM,...  3.55 us
    all_to_all x1, starting transfers between devices, body(): coupled = lax.all_to_all(mixed, 'grp', 0, 0).reshape(COLS, LEV)  3.49 us
  transfers between devices with their start and end apart: 13, of which 4 were waited for; matrix products, arithmetic and copies ran while one was open for 0% of the time, Pallas kernels for 13%

profile of v4, /device:TPU:1, one launch (start us, length us, event | category | flops | bytes accessed | tf_op | source)
XLA Modules:
  0.0 73.8 jit_solution(4513454673439504229)
XLA Ops:
  0.0 0.0 copy-start
  0.0 0.0 copy-start.3
  0.0 3.6 %shard_map.55 = (f32[528,128]{1,0:T(8,128)S(1)}, f32[528,128]{1,0:T(8,128)S(1)}, f32[528,128]{1,0:T(8,128)S(1)}, f32[528,128]{1,0:T(8,128)S(1)}, f32[8,128]{1,0:...) custom-call(s32[1]{0:T(128)} %bitcast.self_ref, f32[1024,128]{1,0:T(8,128)} %field.1, s32[2,1024]{1,0:T(2,128)} %departure.5, ...), custom_call_target="tpu_custom_call" | custom-call | tf_op jit(solution)/shard_map/pallas_call | solution.py:397
  3.6 0.0 copy-start.2
  3.6 3.3 %collective-permute-start = (f32[528,128]{1,0:T(8,128)S(1)}, f32[528,128]{1,0:T(8,128)S(1)}, u32[]{:S(2)}, u32[]{:S(2)}) collective-permute-start(f32[528,128]{1,0:T(8,128)S(1)} %get-tuple-element.27), channel_id=1, source_target_pairs={{0,1},{1,0},{2,3},{3,2},{4,5},{5,4},{6,7},{7,6},{8,9},{9,8},{10,11... | collective-permute-start | bytes 811016 | tf_op jit(solution)/shard_map/ppermute | solution.py:28
  6.9 0.0 collective-permute-start.1
  6.9 5.6 %collective-permute-start.2 = (f32[528,128]{1,0:T(8,128)S(1)}, f32[528,128]{1,0:T(8,128)S(1)}, u32[]{:S(2)}, u32[]{:S(2)}) collective-permute-start(f32[528,128]{1,0:T(8,128)S(1)} %get-tuple-element.29), channel_id=1, source_target_pairs={{0,30},{1,31},{2,4},{3,5},{4,2},{5,3},{6,8},{7,9},{8,6},{9,7},{10,... | collective-permute-start | bytes 811016 | tf_op jit(solution)/shard_map/ppermute | solution.py:28
  12.5 0.0 collective-permute-start.3
  12.5 0.0 collective-permute-done.payload
  12.5 1.7 %collective-permute-start.4 = (f32[8,128]{1,0:T(8,128)S(1)}, f32[8,128]{1,0:T(8,128)S(1)}, u32[]{:S(2)}, u32[]{:S(2)}) collective-permute-start(f32[8,128]{1,0:T(8,128)S(1)} %get-tuple-element.33), channel_id=1, source_target_pairs={{0,3},{1,30},{2,5},{3,0},{4,7},{5,2},{6,9},{7,4},{8,11},{9,6},{10,... | collective-permute-start | bytes 12296 | tf_op jit(solution)/shard_map/ppermute | solution.py:28
  14.2 0.0 collective-permute-start.5
  14.3 0.0 copy-done
  14.3 0.0 copy-done.3
  14.3 0.0 copy-done.2
  14.3 2.3 %shard_map.56.start = f32[1024,128]{1,0:T(8,128)S(1)} custom-call(s32[1]{0:T(128)} %bitcast.self_ref, f32[1024,128]{1,0:T(8,128)S(1)} %copy-done, s32[2,1024]{1,0:T(2,128)S(1)} %copy-done.2, f32[2,1024]{1,0:T(2,128)S(1)} %copy-done.3, f32[8,128]{1,0:T(8,128)S(1)} %get-tuple-element.26.spilled, f32[528,128]{1,0:T(8,128)S(1)} %collective-permute-done.payload), custom_call_target="tpu_custom_call" | custom-call | flops 3000000000 | bytes 11718750 | tf_op jit(solution)/shard_map/pallas_call | solution.py:364
  16.6 0.0 copy-start.4
  16.6 0.0 collective-permute-done.1.p0
  16.6 2.5 %collective-permute-done.2.p1 = f32[528,128]{1,0:T(8,128)S(1)} collective-permute-done((f32[528,128]{1,0:T(8,128)S(1)}, f32[528,128]{1,0:T(8,128)S(1)}, u32[]{:S(2)}, u32[]{:S(2)}) %collective-permute-start.2) | collective-permute-done | bytes 270368 | tf_op jit(solution)/shard_map/ppermute | solution.py:28
  19.1 1.7 %shard_map.57.start = f32[1024,128]{1,0:T(8,128)S(1)} custom-call(f32[1024,128]{1,0:T(8,128)S(1)} %shard_map.56.start, f32[528,128]{1,0:T(8,128)S(1)} %collective-permute-done.1.p0, f32[528,128]{1,0:T(8,128)S(1)} %collective-permute-done.2.p1), custom_call_target="tpu_custom_call" | custom-call | flops 3000000000 | bytes 11718750 | tf_op jit(solution)/shard_map/pallas_call | solution.py:371
  20.8 0.0 collective-permute-done.3.payload
  20.8 0.0 collective-permute-done.4.tiny_a
  20.8 0.0 collective-permute-done.5.tiny_b
  20.8 0.0 copy-done.4
  20.8 1.8 %shard_map.58 = f32[1024,128]{1,0:T(8,128)S(1)} custom-call(f32[1024,128]{1,0:T(8,128)S(1)} %shard_map.57.start, f32[528,128]{1,0:T(8,128)S(1)} %collective-permute-done.3.payload, f32[8,128]{1,0:T(8,128)S(1)} %collective-permute-done.4.tiny_a, f32[8,128]{1,0:T(8,128)S(1)} %collective-permute-done.5.tiny_b, f32[2,128,128]{2,1,0:T(8,128)S(1)} %copy-done.4), custom_call_target="tpu_custom_call" | custom-call | flops 3000000000 | bytes 11718750 | tf_op jit(solution)/shard_map/pallas_call | solution.py:372
  22.6 0.0 copy-start.1
  22.6 14.8 %all_to_all.10.x = f32[8,128,128]{2,1,0:T(8,128)S(1)} all-to-all(f32[8,128,128]{2,1,0:T(8,128)S(1)} %bitcast.8), channel_id=1, replica_groups=mesh['grp'=8,'tile'=32] {'grp'}, dimensions={0} | all-to-all | bytes 1048576 | tf_op jit(solution)/shard_map/all_to_all | solution.py:414
  37.5 0.0 copy-done.1
  37.5 1.2 %shard_map.59 = f32[8,128,128]{2,1,0:T(8,128)} custom-call(f32[64,128]{1,0:T(8,128)S(1)} %bitcast.9, f32[8,128,128]{2,1,0:T(8,128)S(1)} %all_to_all.10.x), custom_call_target="tpu_custom_call" | custom-call | tf_op jit(solution)/shard_map/pallas_call | solution.py:415
  38.7 3.5 %all-to-all-start.1 = ((f32[8,128,128]{2,1,0:T(8,128)}), f32[8,128,128]{2,1,0:T(8,128)S(1)}, u32[]{:S(2)}, u32[]{:S(2)}) async-start(f32[8,128,128]{2,1,0:T(8,128)} %shard_map.59), calls=%async_computation.1 | async-start | bytes 1048576 | tf_op jit(solution)/shard_map/all_to_all | solution.py:416
  42.2 1.4 %shard_map.60 = (s32[1,1024]{1,0:T(1,128)S(1)}, bf16[80,1024]{1,0:T(8,128)(2,1)S(1)}, f32[32,128]{1,0:T(8,128)S(1)}) custom-call(s32[1]{0:T(128)} %bitcast.self_ref, s32[2,1024]{1,0:T(2,128)S(1)} %copy-done.2, f32[2,1024]{1,0:T(2,128)S(1)} %copy-done.3), custom_call_target="tpu_custom_call" | custom-call | flops 2000000000 | bytes 7812500 | tf_op jit(solution)/shard_map/pallas_call | solution.py:400
  43.5 7.1 %all-to-all-done.1 = f32[8,128,128]{2,1,0:T(8,128)S(1)} async-done(((f32[8,128,128]{2,1,0:T(8,128)}), f32[8,128,128]{2,1,0:T(8,128)S(1)}, u32[]{:S(2)}, u32[]{:S(2)}) %all-to-all-start.1) | async-done | bytes 524320 | tf_op jit(solution)/shard_map/all_to_all | solution.py:416
  50.6 1.3 %shard_map.61 = (f32[528,128]{1,0:T(8,128)S(1)}, f32[528,128]{1,0:T(8,128)S(1)}, f32[528,128]{1,0:T(8,128)S(1)}, f32[528,128]{1,0:T(8,128)S(1)}, f32[8,128]{1,0:...) custom-call(s32[1]{0:T(128)} %bitcast.self_ref, f32[1024,128]{1,0:T(8,128)S(1)} %bitcast.6, ...), custom_call_target="tpu_custom_call" | custom-call | tf_op jit(solution)/shard_map/pallas_call | solution.py:418
  51.9 5.3 %collective-permute-start.6 = (f32[528,128]{1,0:T(8,128)S(1)}, f32[528,128]{1,0:T(8,128)S(1)}, u32[]{:S(2)}, u32[]{:S(2)}) collective-permute-start(f32[528,128]{1,0:T(8,128)S(1)} %get-tuple-element.39), channel_id=1, source_target_pairs={{0,1},{1,0},{2,3},{3,2},{4,5},{5,4},{6,7},{7,6},{8,9},{9,8},{10,11... | collective-permute-start | bytes 811016 | tf_op jit(solution)/shard_map/ppermute | solution.py:28
  57.2 0.7 %collective-permute-start.7 = (f32[528,128]{1,0:T(8,128)S(1)}, f32[528,128]{1,0:T(8,128)S(1)}, u32[]{:S(2)}, u32[]{:S(2)}) collective-permute-start(f32[528,128]{1,0:T(8,128)S(1)} %get-tuple-element.40), channel_id=1, source_target_pairs={{0,2},{1,3},{2,0},{3,1},{4,6},{5,7},{6,4},{7,5},{8,10},{9,11},{10,... | collective-permute-start | bytes 811016 | tf_op jit(solution)/shard_map/ppermute | solution.py:28
  57.9 4.4 %collective-permute-start.8 = (f32[528,128]{1,0:T(8,128)S(1)}, f32[528,128]{1,0:T(8,128)S(1)}, u32[]{:S(2)}, u32[]{:S(2)}) collective-permute-start(f32[528,128]{1,0:T(8,128)S(1)} %get-tuple-element.41), channel_id=1, source_target_pairs={{0,30},{1,31},{2,4},{3,5},{4,2},{5,3},{6,8},{7,9},{8,6},{9,7},{10,... | collective-permute-start | bytes 811016 | tf_op jit(solution)/shard_map/ppermute | solution.py:28
  62.3 0.0 collective-permute-start.9
  62.3 0.0 collective-permute-done.6.payload
  62.3 1.7 %collective-permute-start.10 = (f32[8,128]{1,0:T(8,128)S(1)}, f32[8,128]{1,0:T(8,128)S(1)}, u32[]{:S(2)}, u32[]{:S(2)}) collective-permute-start(f32[8,128]{1,0:T(8,128)S(1)} %get-tuple-element.45), channel_id=1, source_target_pairs={{0,3},{1,30},{2,5},{3,0},{4,7},{5,2},{6,9},{7,4},{8,11},{9,6},{10,... | collective-permute-start | bytes 12296 | tf_op jit(solution)/shard_map/ppermute | solution.py:28
  64.0 0.5 collective-permute-start.11
  64.6 2.3 %shard_map.62.start = f32[1024,128]{1,0:T(8,128)S(1)} custom-call(s32[1]{0:T(128)} %bitcast.self_ref, f32[1024,128]{1,0:T(8,128)S(1)} %bitcast.7, s32[2,1024]{1,0:T(2,128)S(1)} %copy-done.2, f32[2,1024]{1,0:T(2,128)S(1)} %copy-done.3, f32[8,128]{1,0:T(8,128)S(1)} %get-tuple-element.38.spilled, f32[528,128]{1,0:T(8,128)S(1)} %collective-permute-done.6.payload), custom_call_target="tpu_custom_call" | custom-call | flops 3000000000 | bytes 11718750 | tf_op jit(solution)/shard_map/pallas_call | solution.py:364
  66.9 0.0 collective-permute-done.7.p0
  66.9 2.0 %collective-permute-done.8.p1 = f32[528,128]{1,0:T(8,128)S(1)} collective-permute-done((f32[528,128]{1,0:T(8,128)S(1)}, f32[528,128]{1,0:T(8,128)S(1)}, u32[]{:S(2)}, u32[]{:S(2)}) %collective-permute-start.8) | collective-permute-done | bytes 270368 | tf_op jit(solution)/shard_map/ppermute | solution.py:28
  68.9 1.7 %shard_map.63.start = f32[1024,128]{1,0:T(8,128)S(1)} custom-call(f32[1024,128]{1,0:T(8,128)S(1)} %shard_map.62.start, f32[528,128]{1,0:T(8,128)S(1)} %collective-permute-done.7.p0, f32[528,128]{1,0:T(8,128)S(1)} %collective-permute-done.8.p1), custom_call_target="tpu_custom_call" | custom-call | flops 3000000000 | bytes 11718750 | tf_op jit(solution)/shard_map/pallas_call | solution.py:371
  70.6 0.0 collective-permute-done.9.payload
  70.6 0.0 collective-permute-done.10.tiny_a
  70.6 0.6 collective-permute-done.11.tiny_b
  71.2 2.5 %shard_map.64 = f32[1024,128]{1,0:T(8,128)} custom-call(f32[1024,128]{1,0:T(8,128)S(1)} %shard_map.63.start, f32[528,128]{1,0:T(8,128)S(1)} %collective-permute-done.9.payload, f32[8,128]{1,0:T(8,128)S(1)} %collective-permute-done.10.tiny_a, f32[8,128]{1,0:T(8,128)S(1)} %collective-permute-done.11.tiny_b, f32[2,128,128]{2,1,0:T(8,128)S(1)} %copy-done.4), custom_call_target="tpu_custom_call" | custom-call | flops 3000000000 | bytes 11718750 | tf_op jit(solution)/shard_map/pallas_call | solution.py:372
Async XLA Ops:
  0.0 14.3 %copy-start = (f32[1024,128]{1,0:T(8,128)S(1)}, f32[1024,128]{1,0:T(8,128)}, u32[]{:S(2)}) copy-start(f32[1024,128]{1,0:T(8,128)} %field.1) | copy-start | bytes 1572868
  0.0 14.3 %copy-start.3 = (f32[2,1024]{1,0:T(2,128)S(1)}, f32[2,1024]{1,0:T(2,128)}, u32[]{:S(2)}) copy-start(f32[2,1024]{1,0:T(2,128)} %fraction.5) | copy-start | bytes 24580
  3.6 10.7 %copy-start.2 = (s32[2,1024]{1,0:T(2,128)S(1)}, s32[2,1024]{1,0:T(2,128)}, u32[]{:S(2)}) copy-start(s32[2,1024]{1,0:T(2,128)} %departure.5) | copy-start | bytes 24580
  3.6 8.9 %collective-permute-start = (f32[528,128]{1,0:T(8,128)S(1)}, f32[528,128]{1,0:T(8,128)S(1)}, u32[]{:S(2)}, u32[]{:S(2)}) collective-permute-start(f32[528,128]{1,0:T(8,128)S(1)} %get-tuple-element.27), channel_id=1, source_target_pairs={{0,1},{1,0},{2,3},{3,2},{4,5},{5,4},{6,7},{7,6},{8,9},{9,8},{10,11... | collective-permute-start | bytes 811016 | tf_op jit(solution)/shard_map/ppermute | solution.py:28
  6.9 9.7 %collective-permute-start.1 = (f32[528,128]{1,0:T(8,128)S(1)}, f32[528,128]{1,0:T(8,128)S(1)}, u32[]{:S(2)}, u32[]{:S(2)}) collective-permute-start(f32[528,128]{1,0:T(8,128)S(1)} %get-tuple-element.28), channel_id=1, source_target_pairs={{0,2},{1,3},{2,0},{3,1},{4,6},{5,7},{6,4},{7,5},{8,10},{9,11},{10,... | collective-permute-start | bytes 811016 | tf_op jit(solution)/shard_map/ppermute | solution.py:28
  6.9 12.2 %collective-permute-start.2 = (f32[528,128]{1,0:T(8,128)S(1)}, f32[528,128]{1,0:T(8,128)S(1)}, u32[]{:S(2)}, u32[]{:S(2)}) collective-permute-start(f32[528,128]{1,0:T(8,128)S(1)} %get-tuple-element.29), channel_id=1, source_target_pairs={{0,30},{1,31},{2,4},{3,5},{4,2},{5,3},{6,8},{7,9},{8,6},{9,7},{10,... | collective-permute-start | bytes 811016 | tf_op jit(solution)/shard_map/ppermute | solution.py:28
  12.5 8.3 %collective-permute-start.3 = (f32[528,128]{1,0:T(8,128)S(1)}, f32[528,128]{1,0:T(8,128)S(1)}, u32[]{:S(2)}, u32[]{:S(2)}) collective-permute-start(f32[528,128]{1,0:T(8,128)S(1)} %get-tuple-element.30), channel_id=1, source_target_pairs={{0,31},{1,2},{2,1},{3,4},{4,3},{5,6},{6,5},{7,8},{8,7},{9,10},{10,... | collective-permute-start | bytes 811016 | tf_op jit(solution)/shard_map/ppermute | solution.py:28
  12.5 8.3 %collective-permute-start.4 = (f32[8,128]{1,0:T(8,128)S(1)}, f32[8,128]{1,0:T(8,128)S(1)}, u32[]{:S(2)}, u32[]{:S(2)}) collective-permute-start(f32[8,128]{1,0:T(8,128)S(1)} %get-tuple-element.33), channel_id=1, source_target_pairs={{0,3},{1,30},{2,5},{3,0},{4,7},{5,2},{6,9},{7,4},{8,11},{9,6},{10,... | collective-permute-start | bytes 12296 | tf_op jit(solution)/shard_map/ppermute | solution.py:28
  14.2 6.5 %collective-permute-start.5 = (f32[8,128]{1,0:T(8,128)S(1)}, f32[8,128]{1,0:T(8,128)S(1)}, u32[]{:S(2)}, u32[]{:S(2)}) collective-permute-start(f32[8,128]{1,0:T(8,128)S(1)} %get-tuple-element.34), channel_id=1, source_target_pairs={{0,29},{1,4},{2,31},{3,6},{4,1},{5,8},{6,3},{7,10},{8,5},{9,12},{1... | collective-permute-start | bytes 12296 | tf_op jit(solution)/shard_map/ppermute | solution.py:28
  16.6 4.2 %copy-start.4 = (f32[2,128,128]{2,1,0:T(8,128)S(1)}, f32[2,128,128]{2,1,0:T(8,128)}, u32[]{:S(2)}) copy-start(f32[2,128,128]{2,1,0:T(8,128)} %level_map.3) | copy-start | bytes 393220
  22.6 14.9 %copy-start.1 = (f32[128,8,8]{0,2,1:T(8,128)S(1)}, f32[128,8,8]{0,2,1:T(8,128)}, u32[]{:S(2)}) copy-start(f32[128,8,8]{0,2,1:T(8,128)} %param.9) | copy-start | bytes 98308
  38.7 11.9 %all-to-all-start.1 = ((f32[8,128,128]{2,1,0:T(8,128)}), f32[8,128,128]{2,1,0:T(8,128)S(1)}, u32[]{:S(2)}, u32[]{:S(2)}) async-start(f32[8,128,128]{2,1,0:T(8,128)} %shard_map.59), calls=%async_computation.1 | async-start | bytes 1048576 | tf_op jit(solution)/shard_map/all_to_all | solution.py:416
  51.9 10.4 %collective-permute-start.6 = (f32[528,128]{1,0:T(8,128)S(1)}, f32[528,128]{1,0:T(8,128)S(1)}, u32[]{:S(2)}, u32[]{:S(2)}) collective-permute-start(f32[528,128]{1,0:T(8,128)S(1)} %get-tuple-element.39), channel_id=1, source_target_pairs={{0,1},{1,0},{2,3},{3,2},{4,5},{5,4},{6,7},{7,6},{8,9},{9,8},{10,11... | collective-permute-start | bytes 811016 | tf_op jit(solution)/shard_map/ppermute | solution.py:28
  57.2 9.7 %collective-permute-start.7 = (f32[528,128]{1,0:T(8,128)S(1)}, f32[528,128]{1,0:T(8,128)S(1)}, u32[]{:S(2)}, u32[]{:S(2)}) collective-permute-start(f32[528,128]{1,0:T(8,128)S(1)} %get-tuple-element.40), channel_id=1, source_target_pairs={{0,2},{1,3},{2,0},{3,1},{4,6},{5,7},{6,4},{7,5},{8,10},{9,11},{10,... | collective-permute-start | bytes 811016 | tf_op jit(solution)/shard_map/ppermute | solution.py:28
  57.9 11.0 %collective-permute-start.8 = (f32[528,128]{1,0:T(8,128)S(1)}, f32[528,128]{1,0:T(8,128)S(1)}, u32[]{:S(2)}, u32[]{:S(2)}) collective-permute-start(f32[528,128]{1,0:T(8,128)S(1)} %get-tuple-element.41), channel_id=1, source_target_pairs={{0,30},{1,31},{2,4},{3,5},{4,2},{5,3},{6,8},{7,9},{8,6},{9,7},{10,... | collective-permute-start | bytes 811016 | tf_op jit(solution)/shard_map/ppermute | solution.py:28
  62.3 8.3 %collective-permute-start.9 = (f32[528,128]{1,0:T(8,128)S(1)}, f32[528,128]{1,0:T(8,128)S(1)}, u32[]{:S(2)}, u32[]{:S(2)}) collective-permute-start(f32[528,128]{1,0:T(8,128)S(1)} %get-tuple-element.42), channel_id=1, source_target_pairs={{0,31},{1,2},{2,1},{3,4},{4,3},{5,6},{6,5},{7,8},{8,7},{9,10},{10,... | collective-permute-start | bytes 811016 | tf_op jit(solution)/shard_map/ppermute | solution.py:28
  62.3 8.3 %collective-permute-start.10 = (f32[8,128]{1,0:T(8,128)S(1)}, f32[8,128]{1,0:T(8,128)S(1)}, u32[]{:S(2)}, u32[]{:S(2)}) collective-permute-start(f32[8,128]{1,0:T(8,128)S(1)} %get-tuple-element.45), channel_id=1, source_target_pairs={{0,3},{1,30},{2,5},{3,0},{4,7},{5,2},{6,9},{7,4},{8,11},{9,6},{10,... | collective-permute-start | bytes 12296 | tf_op jit(solution)/shard_map/ppermute | solution.py:28
  64.0 7.1 %collective-permute-start.11 = (f32[8,128]{1,0:T(8,128)S(1)}, f32[8,128]{1,0:T(8,128)S(1)}, u32[]{:S(2)}, u32[]{:S(2)}) collective-permute-start(f32[8,128]{1,0:T(8,128)S(1)} %get-tuple-element.46), channel_id=1, source_target_pairs={{0,29},{1,4},{2,31},{3,6},{4,1},{5,8},{6,3},{7,10},{8,5},{9,12},{1... | collective-permute-start | bytes 12296 | tf_op jit(solution)/shard_map/ppermute | solution.py:28

commit v5 on v4

--- a/solution.py
+++ b/solution.py
@@ -13,6 +13,7 @@
 LEV = 128
 CAP = 512
 ROWS = CAP + 16
+WIDE_ROWS = CAP + 24
 BF = jnp.bfloat16
 F32 = jnp.float32
 
@@ -157,6 +158,12 @@
     out[CAP : CAP + 8, :] = spill_block(spilled, shift)
 
 
+def beyond(outs, spilled, shifts):
+    block = spill_block(spilled, shifts[4])
+    for which in range(2):
+        outs[which][CAP + 16 : CAP + 24, :] = jnp.where(shifts[which] * shifts[4] > 0, block, 0.0)
+
+
 def first_pack_kernel(tile_count, self_ref, field_hbm, departure_hbm, fraction_hbm, *refs):
     outs, (field, departure, fraction, sems) = refs[:-4], refs[-4:]
     copies = [
@@ -176,9 +183,9 @@
     both = jnp.concatenate([high, low], axis=1)
     spilled = spill_sums(spills, both)
     shifts = signs(self_ref[0])
-    outs[4][...] = spill_block(spilled, shifts[4])
-    outs[5][...] = spill_block(spilled, shifts[5])
-    outs[6][...] = spill_block(spilled, 0)
+    beyond(outs, spilled, shifts)
+    outs[4][...] = spill_block(spilled, shifts[5])
+    outs[5][...] = spill_block(spilled, 0)
     for which, shift in enumerate(shifts[:SWAPS]):
         one_hot = choose(keys, which)
         pack_payload(outs[which], one_hot, both, spilled, shift)
@@ -199,9 +206,9 @@
     both = jnp.concatenate([high, low], axis=1)
     spilled = spill_sums(spills[...], both)
     shifts = signs(self_ref[0])
-    outs[4][...] = spill_block(spilled, shifts[4])
-    outs[5][...] = spill_block(spilled, shifts[5])
-    outs[6][...] = spill_block(spilled, 0)
+    beyond(outs, spilled, shifts)
+    outs[4][...] = spill_block(spilled, shifts[5])
+    outs[5][...] = spill_block(spilled, 0)
     for which, shift in enumerate(shifts[:SWAPS]):
         pack_payload(outs[which], choose(keys[...], which), both, spilled, shift)
         outs[which][CAP + 8 : CAP + 16, :] = meta[8 * which : 8 * which + 8, :]
@@ -292,31 +299,30 @@
 
 
 def last_kernel(step, start, payload, tiny_a, tiny_b, level_map, out, both_ref, sum_ref, lifted_ref, sems):
-    table = payload_table(payload, both_ref, 0)
-    spill = payload[CAP : CAP + 8, :] + tiny_a[...] + tiny_b[...]
-    row = lax.broadcasted_iota(jnp.int32, (8, LEV), 0)
+    tables = [payload_table(payload, both_ref, 0)]
+
+    @pl.loop(0, COLS // BLOCK)
+    def _(b):
+        sum_ref[pl.ds(b * BLOCK, BLOCK), :] = deposit_block(b, start, tables, both_ref)
+
+    add_spill(sum_ref, payload[CAP : CAP + 8, :] + tiny_a[...] + tiny_b[...])
     map_high, map_low = halves(level_map[step])
 
-    def copy(b):
-        rows = pl.ds(b * BLOCK, BLOCK)
-        return pltpu.make_async_copy(lifted_ref.at[rows, :], out.at[rows, :], sems.at[b])
-
+    def lift(rows):
+        high, low = halves(sum_ref[rows, :])
+        return dot_nt(high, map_high) + (dot_nt(high, map_low) + dot_nt(low, map_high))
+
+    if step == 1:
+        out[...] = lift(slice(0, COLS))
+        return
+    copies = []
     for b in range(COLS // BLOCK):
-        sum_ref[...] = deposit_block(b, start, (table,), both_ref)
-        if b == 0:
-            sum_ref[0:8, :] = sum_ref[0:8, :] + jnp.where(row < 2, spill, 0.0)
-        if b == COLS // BLOCK - 1:
-            sum_ref[BLOCK - 8 : BLOCK, :] = sum_ref[BLOCK - 8 : BLOCK, :] + jnp.where(row == 7, spill, 0.0)
-        high, low = halves(sum_ref[...])
-        lifted = dot_nt(high, map_high) + (dot_nt(high, map_low) + dot_nt(low, map_high))
-        if step == 0:
-            lifted_ref[b * BLOCK : (b + 1) * BLOCK, :] = lifted
-            copy(b).start()
-        else:
-            out[b * BLOCK : (b + 1) * BLOCK, :] = lifted
-    if step == 0:
-        for b in range(COLS // BLOCK):
-            copy(b).wait()
+        rows = slice(b * BLOCK, (b + 1) * BLOCK)
+        lifted_ref[rows, :] = lift(rows)
+        copies.append(pltpu.make_async_copy(lifted_ref.at[rows, :], out.at[rows, :], sems.at[b]))
+        copies[-1].start()
+    for copy in copies:
+        copy.wait()
 
 
 def couple_kernel(table, x, out):
@@ -336,7 +342,7 @@
 HBM = pl.BlockSpec(memory_space=pltpu.MemorySpace.HBM)
 SM = pl.BlockSpec(memory_space=pltpu.MemorySpace.SMEM)
 PARAMS = pltpu.CompilerParams(vmem_limit_bytes=40 * 1024 * 1024)
-PACKED = [jax.ShapeDtypeStruct((ROWS, LEV), F32)] * 4 + [jax.ShapeDtypeStruct((8, LEV), F32)] * 3
+PACKED = [jax.ShapeDtypeStruct((rows, LEV), F32) for rows in (WIDE_ROWS, WIDE_ROWS, ROWS, ROWS, 8, 8)]
 
 
 def call(kernel, out_shape, in_specs, scratch=(), flops=0, out_spec=None):
@@ -355,9 +361,10 @@
 def transported(step, packed, tile_count, tile_self, field, departure, fraction, level_map):
     far = [swapped(packed[w], w) for w in (0, 1)]
     partner = swapped(packed[3], 3)
-    cross = swapped(packed[2], 2)
-    late = lax.optimization_barrier((packed[4], packed[5], partner))
-    tiny = [swapped(late[w - 4], w) for w in (4, 5)]
+    late = lax.optimization_barrier((packed[2], packed[4], partner))
+    cross = swapped(late[0], 2)
+    tiny = swapped(late[1], 5)
+    handed = swapped(far[0][CAP + 16 :] + far[1][CAP + 16 :], 3)
     total = jax.ShapeDtypeStruct((COLS, LEV), F32)
     one = pltpu.VMEM((1, CAP, 2 * LEV), BF)
     work = 3 * 10**9
@@ -367,7 +374,7 @@
         [SM] + [VM] * 5,
         [pltpu.VMEM((COLS, 2 * LEV), BF), one],
         work,
-    )(tile_self, field, departure, fraction, packed[6], partner)
+    )(tile_self, field, departure, fraction, packed[5], partner)
     summed = call(middle_kernel, total, [VM] * 3, [pltpu.VMEM((2, CAP, 2 * LEV), BF)], work)(own, *far)
     return call(
         functools.partial(last_kernel, step),
@@ -375,13 +382,13 @@
         [VM] * 5,
         [
             one,
-            pltpu.VMEM((BLOCK, LEV), F32),
+            pltpu.VMEM((COLS, LEV), F32),
             pltpu.VMEM((COLS, LEV), F32),
             pltpu.SemaphoreType.DMA((COLS // BLOCK,)),
         ],
         work,
         HBM if step == 0 else VM,
-    )(summed, cross, *tiny, level_map)
+    )(summed, cross, tiny, handed, level_map)
 
 
 def body(adjoint_in, departure, fraction, level_map, coarse_map):

time: 75.1 us -> 74.1 us (0.987); the launches traced: 73.8 us -> 73.8 us
  blocking collectives: 14.8 us -> 15.7 us
  Pallas kernels: 19.7 us -> 18.9 us
    all_to_all x1, blocking collectives: 14.8 us -> 15.7 us  [body(): lax.all_to_all(second.reshape(groups, COLS // groups, LEV), 'grp', 0, 0)]
    pallas_call x2, Pallas kernels: 4.3 us -> 3.53 us  [transported(): call(functools.partial(last_kernel, step), total, [VM] * 5, [one, pltpu.V...]
  transfers between devices with their start and end apart: 13 -> 13, of which waited for: 4 -> 3; matrix products, arithmetic and copies ran while one was open for 0% -> 0% of each run, Pallas kernels for 13% -> 13%
where the time goes in v5:
time: 74.1 us; the launch traced here: 73.8 us
  starting transfers between devices  27.2 us (37%)
  Pallas kernels  18.9 us (26%)
  blocking collectives  15.7 us (21%)
  waiting for transfers between devices  11.6 us (16%)
    ppermute x12, starting transfers between devices, swapped(): lax.ppermute(x, 'tile', [(i, (i + signs(i)[which]) % length) for i in ran...  23.7 us
    all_to_all x1, blocking collectives, body(): lax.all_to_all(second.reshape(groups, COLS // groups, LEV), 'grp', 0, 0)  15.7 us
    all_to_all x1, waiting for transfers between devices, body(): coupled = lax.all_to_all(mixed, 'grp', 0, 0).reshape(COLS, LEV)  7.22 us
    pallas_call x2, Pallas kernels, transported(): call(functools.partial(own_kernel, step, tile_count), total, [SM] + [VM]...  4.58 us
    ppermute x12, waiting for transfers between devices, swapped(): lax.ppermute(x, 'tile', [(i, (i + signs(i)[which]) % length) for i in ran...  4.36 us
    pallas_call x1, Pallas kernels, body(): call(functools.partial(first_pack_kernel, tile_count), PACKED, [SM, HBM,...  3.55 us
    pallas_call x2, Pallas kernels, transported(): call(functools.partial(last_kernel, step), total, [VM] * 5, [one, pltpu.V...  3.53 us
    all_to_all x1, starting transfers between devices, body(): coupled = lax.all_to_all(mixed, 'grp', 0, 0).reshape(COLS, LEV)  3.49 us
  transfers between devices with their start and end apart: 13, of which 3 were waited for; matrix products, arithmetic and copies ran while one was open for 0% of the time, Pallas kernels for 13%

profile of v5, /device:TPU:1, one launch (start us, length us, event | category | flops | bytes accessed | tf_op | source)
XLA Modules:
  0.0 73.8 jit_solution(18124506972851251153)
XLA Ops:
  0.0 0.0 copy-start
  0.0 0.0 copy-start.3
  0.0 3.6 %shard_map.55 = (f32[536,128]{1,0:T(8,128)S(1)}, f32[536,128]{1,0:T(8,128)S(1)}, f32[528,128]{1,0:T(8,128)S(1)}, f32[528,128]{1,0:T(8,128)S(1)}, f32[8,128]{1,0:T(8,128)S(1)}, /*index=5*/f32[8,128]{1,0:T(8,128)S(1)}) custom-call(s32[1]{0:T(128)} %bitcast.self_ref, f32[1024,128]{1,0:T(8,128)} %field.1, s32[2,1024]{1,0:T(2,128)} %departure.5, f32[2,1024]{1,0:T(2,128)} %fraction.5), custom_call_target="tpu_custom_call" | custom-call | tf_op jit(solution)/shard_map/pallas_call | solution.py:404
  3.6 0.0 copy-start.2
  3.6 3.3 %collective-permute-start = (f32[528,128]{1,0:T(8,128)S(1)}, f32[528,128]{1,0:T(8,128)S(1)}, u32[]{:S(2)}, u32[]{:S(2)}) collective-permute-start(f32[528,128]{1,0:T(8,128)S(1)} %get-tuple-element.25), channel_id=1, source_target_pairs={{0,1},{1,0},{2,3},{3,2},{4,5},{5,4},{6,7},{7,6},{8,9},{9,8},{10,11... | collective-permute-start | bytes 811016 | tf_op jit(solution)/shard_map/ppermute | solution.py:29
  6.9 0.0 collective-permute-start.1
  6.9 5.6 %collective-permute-start.2 = (f32[536,128]{1,0:T(8,128)S(1)}, f32[536,128]{1,0:T(8,128)S(1)}, u32[]{:S(2)}, u32[]{:S(2)}) collective-permute-start(f32[536,128]{1,0:T(8,128)S(1)} %get-tuple-element.27), channel_id=1, source_target_pairs={{0,30},{1,31},{2,4},{3,5},{4,2},{5,3},{6,8},{7,9},{8,6},{9,7},{10,... | collective-permute-start | bytes 823304 | tf_op jit(solution)/shard_map/ppermute | solution.py:29
  12.5 0.0 collective-permute-done.payload
  12.5 0.0 collective-permute-start.4
  12.5 1.9 %collective-permute-start.3 = (f32[528,128]{1,0:T(8,128)S(1)}, f32[528,128]{1,0:T(8,128)S(1)}, u32[]{:S(2)}, u32[]{:S(2)}) collective-permute-start(f32[528,128]{1,0:T(8,128)S(1)} %get-tuple-element.30), channel_id=1, source_target_pairs={{0,31},{1,2},{2,1},{3,4},{4,3},{5,6},{6,5},{7,8},{8,7},{9,10},{10,... | collective-permute-start | bytes 811016 | tf_op jit(solution)/shard_map/ppermute | solution.py:29
  14.4 0.0 copy-done
  14.4 0.0 copy-done.3
  14.4 0.0 copy-done.2
  14.4 2.3 %shard_map.56.start = f32[1024,128]{1,0:T(8,128)S(1)} custom-call(s32[1]{0:T(128)} %bitcast.self_ref, f32[1024,128]{1,0:T(8,128)S(1)} %copy-done, s32[2,1024]{1,0:T(2,128)S(1)} %copy-done.2, f32[2,1024]{1,0:T(2,128)S(1)} %copy-done.3, f32[8,128]{1,0:T(8,128)S(1)} %get-tuple-element.24.spilled, f32[528,128]{1,0:T(8,128)S(1)} %collective-permute-done.payload), custom_call_target="tpu_custom_call" | custom-call | flops 3000000000 | bytes 11718750 | tf_op jit(solution)/shard_map/pallas_call | solution.py:371
  16.7 0.0 collective-permute-done.1.p0
  16.7 2.4 %collective-permute-done.2.p1 = f32[536,128]{1,0:T(8,128)S(1)} collective-permute-done((f32[536,128]{1,0:T(8,128)S(1)}, f32[536,128]{1,0:T(8,128)S(1)}, u32[]{:S(2)}, u32[]{:S(2)}) %collective-permute-start.2) | collective-permute-done | bytes 274464 | tf_op jit(solution)/shard_map/ppermute | solution.py:29
  19.2 0.0 copy-start.4
  19.2 1.4 %collective-permute-start.5 = (f32[8,128]{1,0:T(8,128)S(1)}, f32[8,128]{1,0:T(8,128)S(1)}, u32[]{:S(2)}, u32[]{:S(2)}) collective-permute-start(f32[8,128]{1,0:T(8,128)S(1)} %slice_add_fusion.1), channel_id=1, source_target_pairs={{0,1},{1,0},{2,3},{3,2},{4,5},{5,4},{6,7},{7,6},{8,9},{9,8},{10,11... | collective-permute-start | bytes 12296 | tf_op jit(solution)/shard_map/ppermute | solution.py:29
  20.6 1.7 %shard_map.57.start = f32[1024,128]{1,0:T(8,128)S(1)} custom-call(f32[1024,128]{1,0:T(8,128)S(1)} %shard_map.56.start, f32[536,128]{1,0:T(8,128)S(1)} %collective-permute-done.1.p0, f32[536,128]{1,0:T(8,128)S(1)} %collective-permute-done.2.p1), custom_call_target="tpu_custom_call" | custom-call | flops 3000000000 | bytes 11718750 | tf_op jit(solution)/shard_map/pallas_call | solution.py:378
  22.2 0.0 collective-permute-done.4.tiny_a
  22.2 0.0 collective-permute-done.5.tiny_b
  22.3 0.0 collective-permute-done.3.payload
  22.3 0.0 copy-done.4
  22.3 1.4 %shard_map.58 = f32[1024,128]{1,0:T(8,128)S(1)} custom-call(f32[1024,128]{1,0:T(8,128)S(1)} %shard_map.57.start, f32[528,128]{1,0:T(8,128)S(1)} %collective-permute-done.3.payload, f32[8,128]{1,0:T(8,128)S(1)} %collective-permute-done.4.tiny_a, f32[8,128]{1,0:T(8,128)S(1)} %collective-permute-done.5.tiny_b, f32[2,128,128]{2,1,0:T(8,128)S(1)} %copy-done.4), custom_call_target="tpu_custom_call" | custom-call | flops 3000000000 | bytes 11718750 | tf_op jit(solution)/shard_map/pallas_call | solution.py:379
  23.7 0.0 copy-start.1
  23.7 15.7 %all_to_all.10.x = f32[8,128,128]{2,1,0:T(8,128)S(1)} all-to-all(f32[8,128,128]{2,1,0:T(8,128)S(1)} %bitcast.8), channel_id=1, replica_groups=mesh['grp'=8,'tile'=32] {'grp'}, dimensions={0} | all-to-all | bytes 1048576 | tf_op jit(solution)/shard_map/all_to_all | solution.py:421
  39.4 0.0 copy-done.1
  39.4 1.2 %shard_map.59 = f32[8,128,128]{2,1,0:T(8,128)} custom-call(f32[64,128]{1,0:T(8,128)S(1)} %bitcast.9, f32[8,128,128]{2,1,0:T(8,128)S(1)} %all_to_all.10.x), custom_call_target="tpu_custom_call" | custom-call | tf_op jit(solution)/shard_map/pallas_call | solution.py:422
  40.6 3.5 %all-to-all-start.1 = ((f32[8,128,128]{2,1,0:T(8,128)}), f32[8,128,128]{2,1,0:T(8,128)S(1)}, u32[]{:S(2)}, u32[]{:S(2)}) async-start(f32[8,128,128]{2,1,0:T(8,128)} %shard_map.59), calls=%async_computation.1 | async-start | bytes 1048576 | tf_op jit(solution)/shard_map/all_to_all | solution.py:423
  44.1 1.4 %shard_map.60 = (s32[1,1024]{1,0:T(1,128)S(1)}, bf16[80,1024]{1,0:T(8,128)(2,1)S(1)}, f32[32,128]{1,0:T(8,128)S(1)}) custom-call(s32[1]{0:T(128)} %bitcast.self_ref, s32[2,1024]{1,0:T(2,128)S(1)} %copy-done.2, f32[2,1024]{1,0:T(2,128)S(1)} %copy-done.3), custom_call_target="tpu_custom_call" | custom-call | flops 2000000000 | bytes 7812500 | tf_op jit(solution)/shard_map/pallas_call | solution.py:407
  45.5 7.2 %all-to-all-done.1 = f32[8,128,128]{2,1,0:T(8,128)S(1)} async-done(((f32[8,128,128]{2,1,0:T(8,128)}), f32[8,128,128]{2,1,0:T(8,128)S(1)}, u32[]{:S(2)}, u32[]{:S(2)}) %all-to-all-start.1) | async-done | bytes 524320 | tf_op jit(solution)/shard_map/all_to_all | solution.py:423
  52.7 1.3 %shard_map.61 = (f32[536,128]{1,0:T(8,128)S(1)}, f32[536,128]{1,0:T(8,128)S(1)}, f32[528,128]{1,0:T(8,128)S(1)}, f32[528,128]{1,0:T(8,128)S(1)}, f32[8,128]{1,0:T(8,128)S(1)}, /*index=5*/f32[8,128]{1,0:T(8,128)S(1)}) custom-call(s32[1]{0:T(128)} %bitcast.self_ref, f32[1024,128]{1,0:T(8,128)S(1)} %bitcast.6, s32[1,1024]{1,0:T(1,128)S(1)} %get-tuple-element.32.keys, ...), custom_call_target="tpu_custom_call" | custom-call | tf_op jit(solution)/shard_map/pallas_call | solution.py:425
  54.0 3.7 %collective-permute-start.6 = (f32[528,128]{1,0:T(8,128)S(1)}, f32[528,128]{1,0:T(8,128)S(1)}, u32[]{:S(2)}, u32[]{:S(2)}) collective-permute-start(f32[528,128]{1,0:T(8,128)S(1)} %get-tuple-element.36), channel_id=1, source_target_pairs={{0,1},{1,0},{2,3},{3,2},{4,5},{5,4},{6,7},{7,6},{8,9},{9,8},{10,11... | collective-permute-start | bytes 811016 | tf_op jit(solution)/shard_map/ppermute | solution.py:29
  57.7 0.0 collective-permute-start.7
  57.7 4.2 %collective-permute-start.8 = (f32[536,128]{1,0:T(8,128)S(1)}, f32[536,128]{1,0:T(8,128)S(1)}, u32[]{:S(2)}, u32[]{:S(2)}) collective-permute-start(f32[536,128]{1,0:T(8,128)S(1)} %get-tuple-element.38), channel_id=1, source_target_pairs={{0,30},{1,31},{2,4},{3,5},{4,2},{5,3},{6,8},{7,9},{8,6},{9,7},{10,... | collective-permute-start | bytes 823304 | tf_op jit(solution)/shard_map/ppermute | solution.py:29
  62.0 0.0 collective-permute-done.6.payload
  62.0 0.0 collective-permute-start.10
  62.0 2.6 %collective-permute-start.9 = (f32[528,128]{1,0:T(8,128)S(1)}, f32[528,128]{1,0:T(8,128)S(1)}, u32[]{:S(2)}, u32[]{:S(2)}) collective-permute-start(f32[528,128]{1,0:T(8,128)S(1)} %get-tuple-element.41), channel_id=1, source_target_pairs={{0,31},{1,2},{2,1},{3,4},{4,3},{5,6},{6,5},{7,8},{8,7},{9,10},{10,... | collective-permute-start | bytes 811016 | tf_op jit(solution)/shard_map/ppermute | solution.py:29
  64.6 2.3 %shard_map.62.start = f32[1024,128]{1,0:T(8,128)S(1)} custom-call(s32[1]{0:T(128)} %bitcast.self_ref, f32[1024,128]{1,0:T(8,128)S(1)} %bitcast.7, s32[2,1024]{1,0:T(2,128)S(1)} %copy-done.2, f32[2,1024]{1,0:T(2,128)S(1)} %copy-done.3, f32[8,128]{1,0:T(8,128)S(1)} %get-tuple-element.35.spilled, f32[528,128]{1,0:T(8,128)S(1)} %collective-permute-done.6.payload), custom_call_target="tpu_custom_call" | custom-call | flops 3000000000 | bytes 11718750 | tf_op jit(solution)/shard_map/pallas_call | solution.py:371
  66.9 0.0 collective-permute-done.7.p0
  66.9 1.9 %collective-permute-done.8.p1 = f32[536,128]{1,0:T(8,128)S(1)} collective-permute-done((f32[536,128]{1,0:T(8,128)S(1)}, f32[536,128]{1,0:T(8,128)S(1)}, u32[]{:S(2)}, u32[]{:S(2)}) %collective-permute-start.8) | collective-permute-done | bytes 274464 | tf_op jit(solution)/shard_map/ppermute | solution.py:29
  68.8 1.0 %collective-permute-start.11 = (f32[8,128]{1,0:T(8,128)S(1)}, f32[8,128]{1,0:T(8,128)S(1)}, u32[]{:S(2)}, u32[]{:S(2)}) collective-permute-start(f32[8,128]{1,0:T(8,128)S(1)} %slice_add_fusion), channel_id=1, source_target_pairs={{0,1},{1,0},{2,3},{3,2},{4,5},{5,4},{6,7},{7,6},{8,9},{9,8},{10,11... | collective-permute-start | bytes 12296 | tf_op jit(solution)/shard_map/ppermute | solution.py:29
  69.8 1.7 %shard_map.63.start = f32[1024,128]{1,0:T(8,128)S(1)} custom-call(f32[1024,128]{1,0:T(8,128)S(1)} %shard_map.62.start, f32[536,128]{1,0:T(8,128)S(1)} %collective-permute-done.7.p0, f32[536,128]{1,0:T(8,128)S(1)} %collective-permute-done.8.p1), custom_call_target="tpu_custom_call" | custom-call | flops 3000000000 | bytes 11718750 | tf_op jit(solution)/shard_map/pallas_call | solution.py:378
  71.5 0.0 collective-permute-done.10.tiny_a
  71.5 0.0 collective-permute-done.11.tiny_b
  71.5 0.0 collective-permute-done.9.payload
  71.5 2.2 %shard_map.64 = f32[1024,128]{1,0:T(8,128)} custom-call(f32[1024,128]{1,0:T(8,128)S(1)} %shard_map.63.start, f32[528,128]{1,0:T(8,128)S(1)} %collective-permute-done.9.payload, f32[8,128]{1,0:T(8,128)S(1)} %collective-permute-done.10.tiny_a, f32[8,128]{1,0:T(8,128)S(1)} %collective-permute-done.11.tiny_b, f32[2,128,128]{2,1,0:T(8,128)S(1)} %copy-done.4), custom_call_target="tpu_custom_call" | custom-call | flops 3000000000 | bytes 11718750 | tf_op jit(solution)/shard_map/pallas_call | solution.py:379
  (2 shorter events, 0.0 us)
Async XLA Ops:
  0.0 14.4 %copy-start = (f32[1024,128]{1,0:T(8,128)S(1)}, f32[1024,128]{1,0:T(8,128)}, u32[]{:S(2)}) copy-start(f32[1024,128]{1,0:T(8,128)} %field.1) | copy-start | bytes 1572868
  0.0 14.4 %copy-start.3 = (f32[2,1024]{1,0:T(2,128)S(1)}, f32[2,1024]{1,0:T(2,128)}, u32[]{:S(2)}) copy-start(f32[2,1024]{1,0:T(2,128)} %fraction.5) | copy-start | bytes 24580
  3.6 10.8 %copy-start.2 = (s32[2,1024]{1,0:T(2,128)S(1)}, s32[2,1024]{1,0:T(2,128)}, u32[]{:S(2)}) copy-start(s32[2,1024]{1,0:T(2,128)} %departure.5) | copy-start | bytes 24580
  3.6 8.9 %collective-permute-start = (f32[528,128]{1,0:T(8,128)S(1)}, f32[528,128]{1,0:T(8,128)S(1)}, u32[]{:S(2)}, u32[]{:S(2)}) collective-permute-start(f32[528,128]{1,0:T(8,128)S(1)} %get-tuple-element.25), channel_id=1, source_target_pairs={{0,1},{1,0},{2,3},{3,2},{4,5},{5,4},{6,7},{7,6},{8,9},{9,8},{10,11... | collective-permute-start | bytes 811016 | tf_op jit(solution)/shard_map/ppermute | solution.py:29
  6.9 9.8 %collective-permute-start.1 = (f32[536,128]{1,0:T(8,128)S(1)}, f32[536,128]{1,0:T(8,128)S(1)}, u32[]{:S(2)}, u32[]{:S(2)}) collective-permute-start(f32[536,128]{1,0:T(8,128)S(1)} %get-tuple-element.26), channel_id=1, source_target_pairs={{0,2},{1,3},{2,0},{3,1},{4,6},{5,7},{6,4},{7,5},{8,10},{9,11},{10,... | collective-permute-start | bytes 823304 | tf_op jit(solution)/shard_map/ppermute | solution.py:29
  6.9 12.2 %collective-permute-start.2 = (f32[536,128]{1,0:T(8,128)S(1)}, f32[536,128]{1,0:T(8,128)S(1)}, u32[]{:S(2)}, u32[]{:S(2)}) collective-permute-start(f32[536,128]{1,0:T(8,128)S(1)} %get-tuple-element.27), channel_id=1, source_target_pairs={{0,30},{1,31},{2,4},{3,5},{4,2},{5,3},{6,8},{7,9},{8,6},{9,7},{10,... | collective-permute-start | bytes 823304 | tf_op jit(solution)/shard_map/ppermute | solution.py:29
  12.5 9.7 %collective-permute-start.4 = (f32[8,128]{1,0:T(8,128)S(1)}, f32[8,128]{1,0:T(8,128)S(1)}, u32[]{:S(2)}, u32[]{:S(2)}) collective-permute-start(f32[8,128]{1,0:T(8,128)S(1)} %get-tuple-element.31), channel_id=1, source_target_pairs={{0,29},{1,4},{2,31},{3,6},{4,1},{5,8},{6,3},{7,10},{8,5},{9,12},{1... | collective-permute-start | bytes 12296 | tf_op jit(solution)/shard_map/ppermute | solution.py:29
  12.5 9.7 %collective-permute-start.3 = (f32[528,128]{1,0:T(8,128)S(1)}, f32[528,128]{1,0:T(8,128)S(1)}, u32[]{:S(2)}, u32[]{:S(2)}) collective-permute-start(f32[528,128]{1,0:T(8,128)S(1)} %get-tuple-element.30), channel_id=1, source_target_pairs={{0,31},{1,2},{2,1},{3,4},{4,3},{5,6},{6,5},{7,8},{8,7},{9,10},{10,... | collective-permute-start | bytes 811016 | tf_op jit(solution)/shard_map/ppermute | solution.py:29
  19.2 3.1 %copy-start.4 = (f32[2,128,128]{2,1,0:T(8,128)S(1)}, f32[2,128,128]{2,1,0:T(8,128)}, u32[]{:S(2)}) copy-start(f32[2,128,128]{2,1,0:T(8,128)} %level_map.3) | copy-start | bytes 393220
  19.2 3.1 %collective-permute-start.5 = (f32[8,128]{1,0:T(8,128)S(1)}, f32[8,128]{1,0:T(8,128)S(1)}, u32[]{:S(2)}, u32[]{:S(2)}) collective-permute-start(f32[8,128]{1,0:T(8,128)S(1)} %slice_add_fusion.1), channel_id=1, source_target_pairs={{0,1},{1,0},{2,3},{3,2},{4,5},{5,4},{6,7},{7,6},{8,9},{9,8},{10,11... | collective-permute-start | bytes 12296 | tf_op jit(solution)/shard_map/ppermute | solution.py:29
  23.7 15.8 %copy-start.1 = (f32[128,8,8]{0,2,1:T(8,128)S(1)}, f32[128,8,8]{0,2,1:T(8,128)}, u32[]{:S(2)}) copy-start(f32[128,8,8]{0,2,1:T(8,128)} %param.9) | copy-start | bytes 98308
  40.6 12.1 %all-to-all-start.1 = ((f32[8,128,128]{2,1,0:T(8,128)}), f32[8,128,128]{2,1,0:T(8,128)S(1)}, u32[]{:S(2)}, u32[]{:S(2)}) async-start(f32[8,128,128]{2,1,0:T(8,128)} %shard_map.59), calls=%async_computation.1 | async-start | bytes 1048576 | tf_op jit(solution)/shard_map/all_to_all | solution.py:423
  54.0 7.9 %collective-permute-start.6 = (f32[528,128]{1,0:T(8,128)S(1)}, f32[528,128]{1,0:T(8,128)S(1)}, u32[]{:S(2)}, u32[]{:S(2)}) collective-permute-start(f32[528,128]{1,0:T(8,128)S(1)} %get-tuple-element.36), channel_id=1, source_target_pairs={{0,1},{1,0},{2,3},{3,2},{4,5},{5,4},{6,7},{7,6},{8,9},{9,8},{10,11... | collective-permute-start | bytes 811016 | tf_op jit(solution)/shard_map/ppermute | solution.py:29
  57.7 9.2 %collective-permute-start.7 = (f32[536,128]{1,0:T(8,128)S(1)}, f32[536,128]{1,0:T(8,128)S(1)}, u32[]{:S(2)}, u32[]{:S(2)}) collective-permute-start(f32[536,128]{1,0:T(8,128)S(1)} %get-tuple-element.37), channel_id=1, source_target_pairs={{0,2},{1,3},{2,0},{3,1},{4,6},{5,7},{6,4},{7,5},{8,10},{9,11},{10,... | collective-permute-start | bytes 823304 | tf_op jit(solution)/shard_map/ppermute | solution.py:29
  57.7 11.1 %collective-permute-start.8 = (f32[536,128]{1,0:T(8,128)S(1)}, f32[536,128]{1,0:T(8,128)S(1)}, u32[]{:S(2)}, u32[]{:S(2)}) collective-permute-start(f32[536,128]{1,0:T(8,128)S(1)} %get-tuple-element.38), channel_id=1, source_target_pairs={{0,30},{1,31},{2,4},{3,5},{4,2},{5,3},{6,8},{7,9},{8,6},{9,7},{10,... | collective-permute-start | bytes 823304 | tf_op jit(solution)/shard_map/ppermute | solution.py:29
  62.0 9.5 %collective-permute-start.10 = (f32[8,128]{1,0:T(8,128)S(1)}, f32[8,128]{1,0:T(8,128)S(1)}, u32[]{:S(2)}, u32[]{:S(2)}) collective-permute-start(f32[8,128]{1,0:T(8,128)S(1)} %get-tuple-element.42), channel_id=1, source_target_pairs={{0,29},{1,4},{2,31},{3,6},{4,1},{5,8},{6,3},{7,10},{8,5},{9,12},{1... | collective-permute-start | bytes 12296 | tf_op jit(solution)/shard_map/ppermute | solution.py:29
  62.0 9.5 %collective-permute-start.9 = (f32[528,128]{1,0:T(8,128)S(1)}, f32[528,128]{1,0:T(8,128)S(1)}, u32[]{:S(2)}, u32[]{:S(2)}) collective-permute-start(f32[528,128]{1,0:T(8,128)S(1)} %get-tuple-element.41), channel_id=1, source_target_pairs={{0,31},{1,2},{2,1},{3,4},{4,3},{5,6},{6,5},{7,8},{8,7},{9,10},{10,... | collective-permute-start | bytes 811016 | tf_op jit(solution)/shard_map/ppermute | solution.py:29
  68.8 2.7 %collective-permute-start.11 = (f32[8,128]{1,0:T(8,128)S(1)}, f32[8,128]{1,0:T(8,128)S(1)}, u32[]{:S(2)}, u32[]{:S(2)}) collective-permute-start(f32[8,128]{1,0:T(8,128)S(1)} %slice_add_fusion), channel_id=1, source_target_pairs={{0,1},{1,0},{2,3},{3,2},{4,5},{5,4},{6,7},{7,6},{8,9},{9,8},{10,11... | collective-permute-start | bytes 12296 | tf_op jit(solution)/shard_map/ppermute | solution.py:29

commit v6 on v5

--- a/solution.py
+++ b/solution.py
@@ -375,8 +375,23 @@
         [pltpu.VMEM((COLS, 2 * LEV), BF), one],
         work,
     )(tile_self, field, departure, fraction, packed[5], partner)
+    index = None
+    if step == 1:
+        after = lax.optimization_barrier((tile_self, own))
+        index = call(
+            functools.partial(index_kernel, tile_count),
+            [
+                jax.ShapeDtypeStruct((1, COLS), jnp.int32),
+                jax.ShapeDtypeStruct((16 * (2 * REACH + 1), COLS), BF),
+                jax.ShapeDtypeStruct((32, LEV), F32),
+            ],
+            [SM, VM, VM],
+            (),
+            2 * 10**9,
+        )(after[0], departure, fraction)
+        own, index = lax.optimization_barrier((after[1], index))
     summed = call(middle_kernel, total, [VM] * 3, [pltpu.VMEM((2, CAP, 2 * LEV), BF)], work)(own, *far)
-    return call(
+    result = call(
         functools.partial(last_kernel, step),
         total,
         [VM] * 5,
@@ -389,6 +404,7 @@
         work,
         HBM if step == 0 else VM,
     )(summed, cross, tiny, handed, level_map)
+    return result, index
 
 
 def body(adjoint_in, departure, fraction, level_map, coarse_map):
@@ -404,26 +420,15 @@
     packed = call(functools.partial(first_pack_kernel, tile_count), PACKED, [SM, HBM, HBM, HBM], first_scratch)(
         tile_self, *[pltpu.with_memory_space_constraint(x, pltpu.MemorySpace.HBM) for x in (adjoint_in, departure, fraction)]
     )
-    keys, spills, meta = call(
-        functools.partial(index_kernel, tile_count),
-        [
-            jax.ShapeDtypeStruct((1, COLS), jnp.int32),
-            jax.ShapeDtypeStruct((16 * (2 * REACH + 1), COLS), BF),
-            jax.ShapeDtypeStruct((32, LEV), F32),
-        ],
-        [SM, VM, VM],
-        (),
-        2 * 10**9,
-    )(tile_self, departure, fraction)
     table = coarse_map.transpose(1, 2, 0).reshape(groups * groups, LEV)
-    second = transported(1, packed, tile_count, tile_self, adjoint_in, departure, fraction, level_map)
+    second, index = transported(1, packed, tile_count, tile_self, adjoint_in, departure, fraction, level_map)
 
     parts = lax.all_to_all(second.reshape(groups, COLS // groups, LEV), "grp", 0, 0)
     mixed = call(couple_kernel, jax.ShapeDtypeStruct(parts.shape, F32), [VM, VM])(table, parts)
     coupled = lax.all_to_all(mixed, "grp", 0, 0).reshape(COLS, LEV)
 
-    packed = call(second_pack_kernel, PACKED, [SM] + [VM] * 4)(tile_self, coupled, keys, spills, meta)
-    return transported(0, packed, tile_count, tile_self, coupled, departure, fraction, level_map)
+    packed = call(second_pack_kernel, PACKED, [SM] + [VM] * 4)(tile_self, coupled, *index)
+    return transported(0, packed, tile_count, tile_self, coupled, departure, fraction, level_map)[0]
 
 
 def solution(mesh):

time: 74.1 us -> 73.1 us (0.987)
  blocking collectives: 15.7 us -> 27.9 us
  waiting for transfers between devices: 11.6 us -> 3 us
  starting transfers between devices: 27.2 us -> 23.6 us
  Pallas kernels: 18.9 us -> 18.1 us
    all_to_all x0 -> x1, blocking collectives: none -> 12.1 us  [body(): coupled = lax.all_to_all(mixed, 'grp', 0, 0).reshape(COLS, LEV)]
    all_to_all x1 -> x0, waiting for transfers between devices: 7.22 us -> none  [body(): coupled = lax.all_to_all(mixed, 'grp', 0, 0).reshape(COLS, LEV)]
    all_to_all x1 -> x0, starting transfers between devices: 3.49 us -> none  [body(): coupled = lax.all_to_all(mixed, 'grp', 0, 0).reshape(COLS, LEV)]
    ppermute x12, waiting for transfers between devices: 4.36 us -> 3 us  [swapped(): lax.ppermute(x, 'tile', [(i, (i + signs(i)[which]) % length) for i in ran...]
    pallas_call x1, Pallas kernels: 1.19 us -> 0.39 us  [body(): call(couple_kernel, jax.ShapeDtypeStruct(parts.shape, F32), [VM, VM])]
  transfers between devices with their start and end apart: 13 -> 12, of which waited for: 3 -> 2; matrix products, arithmetic and copies ran while one was open for 0% -> 0% of each run, Pallas kernels for 13% -> 13%
where the time goes in v6:
time: 73.1 us; the launch traced here: 72.9 us
  blocking collectives  27.9 us (38%)
  starting transfers between devices  23.6 us (32%)
  Pallas kernels  18.1 us (25%)
  waiting for transfers between devices  3 us (4%)
    ppermute x12, starting transfers between devices, swapped(): lax.ppermute(x, 'tile', [(i, (i + signs(i)[which]) % length) for i in ran...  23.6 us
    all_to_all x1, blocking collectives, body(): lax.all_to_all(second.reshape(groups, COLS // groups, LEV), 'grp', 0, 0)  15.7 us
    all_to_all x1, blocking collectives, body(): coupled = lax.all_to_all(mixed, 'grp', 0, 0).reshape(COLS, LEV)  12.1 us
    pallas_call x2, Pallas kernels, transported(): call(functools.partial(own_kernel, step, tile_count), total, [SM] + [VM]...  4.58 us
    pallas_call x1, Pallas kernels, body(): call(functools.partial(first_pack_kernel, tile_count), PACKED, [SM, HBM,...  3.55 us
    pallas_call x2, Pallas kernels, transported(): call(functools.partial(last_kernel, step), total, [VM] * 5, [one, pltpu.V...  3.54 us
    pallas_call x2, Pallas kernels, transported(): call(middle_kernel, total, [VM] * 3, [pltpu.VMEM((2, CAP, 2 * LEV), BF)],...  3.37 us
    ppermute x12, waiting for transfers between devices, swapped(): lax.ppermute(x, 'tile', [(i, (i + signs(i)[which]) % length) for i in ran...  3 us
  transfers between devices with their start and end apart: 12, of which 2 were waited for; matrix products, arithmetic and copies ran while one was open for 0% of the time, Pallas kernels for 13%

profile of v6, /device:TPU:1, one launch (start us, length us, event | category | flops | bytes accessed | tf_op | source)
XLA Modules:
  0.0 72.9 jit_solution(6798376743652619480)
XLA Ops:
  0.0 0.0 copy-start
  0.0 0.0 copy-start.3
  0.0 3.6 %shard_map.55 = (f32[536,128]{1,0:T(8,128)S(1)}, f32[536,128]{1,0:T(8,128)S(1)}, f32[528,128]{1,0:T(8,128)S(1)}, f32[528,128]{1,0:T(8,128)S(1)}, f32[8,128]{1,0:T(8,128)S(1)}, /*index=5*/f32[8,128]{1,0:T(8,128)S(1)}) custom-call(s32[1]{0:T(128)} %bitcast.self_ref, f32[1024,128]{1,0:T(8,128)} %field.1, s32[2,1024]{1,0:T(2,128)} %departure.5, f32[2,1024]{1,0:T(2,128)} %fraction.5), custom_call_target="tpu_custom_call" | custom-call | tf_op jit(solution)/shard_map/pallas_call | solution.py:420
  3.6 0.0 copy-start.2
  3.6 3.3 %collective-permute-start = (f32[528,128]{1,0:T(8,128)S(1)}, f32[528,128]{1,0:T(8,128)S(1)}, u32[]{:S(2)}, u32[]{:S(2)}) collective-permute-start(f32[528,128]{1,0:T(8,128)S(1)} %get-tuple-element.31), channel_id=1, source_target_pairs={{0,1},{1,0},{2,3},{3,2},{4,5},{5,4},{6,7},{7,6},{8,9},{9,8},{10,11... | collective-permute-start | bytes 811016 | tf_op jit(solution)/shard_map/ppermute | solution.py:29
  6.9 0.0 collective-permute-start.1
  6.9 5.6 %collective-permute-start.2 = (f32[536,128]{1,0:T(8,128)S(1)}, f32[536,128]{1,0:T(8,128)S(1)}, u32[]{:S(2)}, u32[]{:S(2)}) collective-permute-start(f32[536,128]{1,0:T(8,128)S(1)} %get-tuple-element.39), channel_id=1, source_target_pairs={{0,30},{1,31},{2,4},{3,5},{4,2},{5,3},{6,8},{7,9},{8,6},{9,7},{10,... | collective-permute-start | bytes 823304 | tf_op jit(solution)/shard_map/ppermute | solution.py:29
  12.5 0.0 collective-permute-done.payload
  12.5 0.0 collective-permute-start.4
  12.5 1.9 %collective-permute-start.3 = (f32[528,128]{1,0:T(8,128)S(1)}, f32[528,128]{1,0:T(8,128)S(1)}, u32[]{:S(2)}, u32[]{:S(2)}) collective-permute-start(f32[528,128]{1,0:T(8,128)S(1)} %get-tuple-element.42), channel_id=1, source_target_pairs={{0,31},{1,2},{2,1},{3,4},{4,3},{5,6},{6,5},{7,8},{8,7},{9,10},{10,... | collective-permute-start | bytes 811016 | tf_op jit(solution)/shard_map/ppermute | solution.py:29
  14.4 0.0 copy-done
  14.4 0.0 copy-done.3
  14.4 0.0 copy-done.2
  14.4 2.3 %shard_map.56.start = f32[1024,128]{1,0:T(8,128)S(1)} custom-call(s32[1]{0:T(128)} %bitcast.self_ref, f32[1024,128]{1,0:T(8,128)S(1)} %copy-done, s32[2,1024]{1,0:T(2,128)S(1)} %copy-done.2, f32[2,1024]{1,0:T(2,128)S(1)} %copy-done.3, f32[8,128]{1,0:T(8,128)S(1)} %get-tuple-element.30.spilled, f32[528,128]{1,0:T(8,128)S(1)} %collective-permute-done.payload), custom_call_target="tpu_custom_call" | custom-call | flops 3000000000 | bytes 11718750 | tf_op jit(solution)/shard_map/pallas_call | solution.py:371
  16.7 1.4 %shard_map.57 = (s32[1,1024]{1,0:T(1,128)S(1)}, bf16[80,1024]{1,0:T(8,128)(2,1)S(1)}, f32[32,128]{1,0:T(8,128)S(1)}) custom-call(s32[1]{0:T(128)} %bitcast.self_ref, s32[2,1024]{1,0:T(2,128)S(1)} %copy-done.2, f32[2,1024]{1,0:T(2,128)S(1)} %copy-done.3), custom_call_target="tpu_custom_call" | custom-call | flops 2000000000 | bytes 7812500 | tf_op jit(solution)/shard_map/pallas_call | solution.py:381
  18.1 0.0 collective-permute-done.1.p0
  18.1 1.1 %collective-permute-done.2.p1 = f32[536,128]{1,0:T(8,128)S(1)} collective-permute-done((f32[536,128]{1,0:T(8,128)S(1)}, f32[536,128]{1,0:T(8,128)S(1)}, u32[]{:S(2)}, u32[]{:S(2)}) %collective-permute-start.2) | collective-permute-done | bytes 274464 | tf_op jit(solution)/shard_map/ppermute | solution.py:29
  19.2 0.0 copy-start.4
  19.2 1.4 %collective-permute-start.5 = (f32[8,128]{1,0:T(8,128)S(1)}, f32[8,128]{1,0:T(8,128)S(1)}, u32[]{:S(2)}, u32[]{:S(2)}) collective-permute-start(f32[8,128]{1,0:T(8,128)S(1)} %slice_add_fusion.1), channel_id=1, source_target_pairs={{0,1},{1,0},{2,3},{3,2},{4,5},{5,4},{6,7},{7,6},{8,9},{9,8},{10,11... | collective-permute-start | bytes 12296 | tf_op jit(solution)/shard_map/ppermute | solution.py:29
  20.6 1.7 %shard_map.58.start = f32[1024,128]{1,0:T(8,128)S(1)} custom-call(f32[1024,128]{1,0:T(8,128)S(1)} %shard_map.56.start, f32[536,128]{1,0:T(8,128)S(1)} %collective-permute-done.1.p0, f32[536,128]{1,0:T(8,128)S(1)} %collective-permute-done.2.p1), custom_call_target="tpu_custom_call" | custom-call | flops 3000000000 | bytes 11718750 | tf_op jit(solution)/shard_map/pallas_call | solution.py:393
  22.2 0.0 collective-permute-done.4.tiny_a
  22.2 0.0 collective-permute-done.5.tiny_b
  22.3 0.0 collective-permute-done.3.payload
  22.3 0.0 copy-done.4
  22.3 1.4 %shard_map.59 = f32[1024,128]{1,0:T(8,128)S(1)} custom-call(f32[1024,128]{1,0:T(8,128)S(1)} %shard_map.58.start, f32[528,128]{1,0:T(8,128)S(1)} %collective-permute-done.3.payload, f32[8,128]{1,0:T(8,128)S(1)} %collective-permute-done.4.tiny_a, f32[8,128]{1,0:T(8,128)S(1)} %collective-permute-done.5.tiny_b, f32[2,128,128]{2,1,0:T(8,128)S(1)} %copy-done.4), custom_call_target="tpu_custom_call" | custom-call | flops 3000000000 | bytes 11718750 | tf_op jit(solution)/shard_map/pallas_call | solution.py:394
  23.7 0.0 copy-start.1
  23.7 15.7 %all_to_all.10.x = f32[8,128,128]{2,1,0:T(8,128)S(1)} all-to-all(f32[8,128,128]{2,1,0:T(8,128)S(1)} %bitcast.8), channel_id=1, replica_groups=mesh['grp'=8,'tile'=32] {'grp'}, dimensions={0} | all-to-all | bytes 1048576 | tf_op jit(solution)/shard_map/all_to_all | solution.py:426
  39.4 0.0 copy-done.1
  39.4 0.4 shard_map.60
  39.8 12.1 %all_to_all.11 = f32[8,128,128]{2,1,0:T(8,128)S(1)} all-to-all(f32[8,128,128]{2,1,0:T(8,128)S(1)} %shard_map.60), channel_id=1, replica_groups=mesh['grp'=8,'tile'=32] {'grp'}, dimensions={0} | all-to-all | bytes 1048576 | tf_op jit(solution)/shard_map/all_to_all | solution.py:428
  51.9 1.3 %shard_map.61 = (f32[536,128]{1,0:T(8,128)S(1)}, f32[536,128]{1,0:T(8,128)S(1)}, f32[528,128]{1,0:T(8,128)S(1)}, f32[528,128]{1,0:T(8,128)S(1)}, f32[8,128]{1,0:T(8,128)S(1)}, /*index=5*/f32[8,128]{1,0:T(8,128)S(1)}) custom-call(s32[1]{0:T(128)} %bitcast.self_ref, f32[1024,128]{1,0:T(8,128)S(1)} %bitcast.6, s32[1,1024]{1,0:T(1,128)S(1)} %get-tuple-element.44.keys, ...), custom_call_target="tpu_custom_call" | custom-call | tf_op jit(solution)/shard_map/pallas_call | solution.py:430
  53.3 3.7 %collective-permute-start.6 = (f32[528,128]{1,0:T(8,128)S(1)}, f32[528,128]{1,0:T(8,128)S(1)}, u32[]{:S(2)}, u32[]{:S(2)}) collective-permute-start(f32[528,128]{1,0:T(8,128)S(1)} %get-tuple-element.48), channel_id=1, source_target_pairs={{0,1},{1,0},{2,3},{3,2},{4,5},{5,4},{6,7},{7,6},{8,9},{9,8},{10,11... | collective-permute-start | bytes 811016 | tf_op jit(solution)/shard_map/ppermute | solution.py:29
  56.9 0.0 collective-permute-start.7
  56.9 4.1 %collective-permute-start.8 = (f32[536,128]{1,0:T(8,128)S(1)}, f32[536,128]{1,0:T(8,128)S(1)}, u32[]{:S(2)}, u32[]{:S(2)}) collective-permute-start(f32[536,128]{1,0:T(8,128)S(1)} %get-tuple-element.50), channel_id=1, source_target_pairs={{0,30},{1,31},{2,4},{3,5},{4,2},{5,3},{6,8},{7,9},{8,6},{9,7},{10,... | collective-permute-start | bytes 823304 | tf_op jit(solution)/shard_map/ppermute | solution.py:29
  61.0 0.0 collective-permute-done.6.payload
  61.0 0.0 collective-permute-start.10
  61.0 2.6 %collective-permute-start.9 = (f32[528,128]{1,0:T(8,128)S(1)}, f32[528,128]{1,0:T(8,128)S(1)}, u32[]{:S(2)}, u32[]{:S(2)}) collective-permute-start(f32[528,128]{1,0:T(8,128)S(1)} %get-tuple-element.53), channel_id=1, source_target_pairs={{0,31},{1,2},{2,1},{3,4},{4,3},{5,6},{6,5},{7,8},{8,7},{9,10},{10,... | collective-permute-start | bytes 811016 | tf_op jit(solution)/shard_map/ppermute | solution.py:29
  63.7 2.3 %shard_map.62.start = f32[1024,128]{1,0:T(8,128)S(1)} custom-call(s32[1]{0:T(128)} %bitcast.self_ref, f32[1024,128]{1,0:T(8,128)S(1)} %bitcast.7, s32[2,1024]{1,0:T(2,128)S(1)} %copy-done.2, f32[2,1024]{1,0:T(2,128)S(1)} %copy-done.3, f32[8,128]{1,0:T(8,128)S(1)} %get-tuple-element.47.spilled, f32[528,128]{1,0:T(8,128)S(1)} %collective-permute-done.6.payload), custom_call_target="tpu_custom_call" | custom-call | flops 3000000000 | bytes 11718750 | tf_op jit(solution)/shard_map/pallas_call | solution.py:371
  66.0 0.0 collective-permute-done.7.p0
  66.0 1.9 %collective-permute-done.8.p1 = f32[536,128]{1,0:T(8,128)S(1)} collective-permute-done((f32[536,128]{1,0:T(8,128)S(1)}, f32[536,128]{1,0:T(8,128)S(1)}, u32[]{:S(2)}, u32[]{:S(2)}) %collective-permute-start.8) | collective-permute-done | bytes 274464 | tf_op jit(solution)/shard_map/ppermute | solution.py:29
  67.9 1.0 %collective-permute-start.11 = (f32[8,128]{1,0:T(8,128)S(1)}, f32[8,128]{1,0:T(8,128)S(1)}, u32[]{:S(2)}, u32[]{:S(2)}) collective-permute-start(f32[8,128]{1,0:T(8,128)S(1)} %slice_add_fusion), channel_id=1, source_target_pairs={{0,1},{1,0},{2,3},{3,2},{4,5},{5,4},{6,7},{7,6},{8,9},{9,8},{10,11... | collective-permute-start | bytes 12296 | tf_op jit(solution)/shard_map/ppermute | solution.py:29
  68.9 1.7 %shard_map.63.start = f32[1024,128]{1,0:T(8,128)S(1)} custom-call(f32[1024,128]{1,0:T(8,128)S(1)} %shard_map.62.start, f32[536,128]{1,0:T(8,128)S(1)} %collective-permute-done.7.p0, f32[536,128]{1,0:T(8,128)S(1)} %collective-permute-done.8.p1), custom_call_target="tpu_custom_call" | custom-call | flops 3000000000 | bytes 11718750 | tf_op jit(solution)/shard_map/pallas_call | solution.py:393
  70.5 0.0 collective-permute-done.10.tiny_a
  70.5 0.0 collective-permute-done.11.tiny_b
  70.6 0.0 collective-permute-done.9.payload
  70.6 2.2 %shard_map.64 = f32[1024,128]{1,0:T(8,128)} custom-call(f32[1024,128]{1,0:T(8,128)S(1)} %shard_map.63.start, f32[528,128]{1,0:T(8,128)S(1)} %collective-permute-done.9.payload, f32[8,128]{1,0:T(8,128)S(1)} %collective-permute-done.10.tiny_a, f32[8,128]{1,0:T(8,128)S(1)} %collective-permute-done.11.tiny_b, f32[2,128,128]{2,1,0:T(8,128)S(1)} %copy-done.4), custom_call_target="tpu_custom_call" | custom-call | flops 3000000000 | bytes 11718750 | tf_op jit(solution)/shard_map/pallas_call | solution.py:394
  (2 shorter events, 0.0 us)
Async XLA Ops:
  0.0 14.4 %copy-start = (f32[1024,128]{1,0:T(8,128)S(1)}, f32[1024,128]{1,0:T(8,128)}, u32[]{:S(2)}) copy-start(f32[1024,128]{1,0:T(8,128)} %field.1) | copy-start | bytes 1572868
  0.0 14.4 %copy-start.3 = (f32[2,1024]{1,0:T(2,128)S(1)}, f32[2,1024]{1,0:T(2,128)}, u32[]{:S(2)}) copy-start(f32[2,1024]{1,0:T(2,128)} %fraction.5) | copy-start | bytes 24580
  3.6 10.8 %copy-start.2 = (s32[2,1024]{1,0:T(2,128)S(1)}, s32[2,1024]{1,0:T(2,128)}, u32[]{:S(2)}) copy-start(s32[2,1024]{1,0:T(2,128)} %departure.5) | copy-start | bytes 24580
  3.6 8.9 %collective-permute-start = (f32[528,128]{1,0:T(8,128)S(1)}, f32[528,128]{1,0:T(8,128)S(1)}, u32[]{:S(2)}, u32[]{:S(2)}) collective-permute-start(f32[528,128]{1,0:T(8,128)S(1)} %get-tuple-element.31), channel_id=1, source_target_pairs={{0,1},{1,0},{2,3},{3,2},{4,5},{5,4},{6,7},{7,6},{8,9},{9,8},{10,11... | collective-permute-start | bytes 811016 | tf_op jit(solution)/shard_map/ppermute | solution.py:29
  6.9 11.2 %collective-permute-start.1 = (f32[536,128]{1,0:T(8,128)S(1)}, f32[536,128]{1,0:T(8,128)S(1)}, u32[]{:S(2)}, u32[]{:S(2)}) collective-permute-start(f32[536,128]{1,0:T(8,128)S(1)} %get-tuple-element.38), channel_id=1, source_target_pairs={{0,2},{1,3},{2,0},{3,1},{4,6},{5,7},{6,4},{7,5},{8,10},{9,11},{10,... | collective-permute-start | bytes 823304 | tf_op jit(solution)/shard_map/ppermute | solution.py:29
  6.9 12.2 %collective-permute-start.2 = (f32[536,128]{1,0:T(8,128)S(1)}, f32[536,128]{1,0:T(8,128)S(1)}, u32[]{:S(2)}, u32[]{:S(2)}) collective-permute-start(f32[536,128]{1,0:T(8,128)S(1)} %get-tuple-element.39), channel_id=1, source_target_pairs={{0,30},{1,31},{2,4},{3,5},{4,2},{5,3},{6,8},{7,9},{8,6},{9,7},{10,... | collective-permute-start | bytes 823304 | tf_op jit(solution)/shard_map/ppermute | solution.py:29
  12.5 9.7 %collective-permute-start.4 = (f32[8,128]{1,0:T(8,128)S(1)}, f32[8,128]{1,0:T(8,128)S(1)}, u32[]{:S(2)}, u32[]{:S(2)}) collective-permute-start(f32[8,128]{1,0:T(8,128)S(1)} %get-tuple-element.43), channel_id=1, source_target_pairs={{0,29},{1,4},{2,31},{3,6},{4,1},{5,8},{6,3},{7,10},{8,5},{9,12},{1... | collective-permute-start | bytes 12296 | tf_op jit(solution)/shard_map/ppermute | solution.py:29
  12.5 9.7 %collective-permute-start.3 = (f32[528,128]{1,0:T(8,128)S(1)}, f32[528,128]{1,0:T(8,128)S(1)}, u32[]{:S(2)}, u32[]{:S(2)}) collective-permute-start(f32[528,128]{1,0:T(8,128)S(1)} %get-tuple-element.42), channel_id=1, source_target_pairs={{0,31},{1,2},{2,1},{3,4},{4,3},{5,6},{6,5},{7,8},{8,7},{9,10},{10,... | collective-permute-start | bytes 811016 | tf_op jit(solution)/shard_map/ppermute | solution.py:29
  19.2 3.1 %copy-start.4 = (f32[2,128,128]{2,1,0:T(8,128)S(1)}, f32[2,128,128]{2,1,0:T(8,128)}, u32[]{:S(2)}) copy-start(f32[2,128,128]{2,1,0:T(8,128)} %level_map.3) | copy-start | bytes 393220
  19.2 3.1 %collective-permute-start.5 = (f32[8,128]{1,0:T(8,128)S(1)}, f32[8,128]{1,0:T(8,128)S(1)}, u32[]{:S(2)}, u32[]{:S(2)}) collective-permute-start(f32[8,128]{1,0:T(8,128)S(1)} %slice_add_fusion.1), channel_id=1, source_target_pairs={{0,1},{1,0},{2,3},{3,2},{4,5},{5,4},{6,7},{7,6},{8,9},{9,8},{10,11... | collective-permute-start | bytes 12296 | tf_op jit(solution)/shard_map/ppermute | solution.py:29
  23.7 15.8 %copy-start.1 = (f32[128,8,8]{0,2,1:T(8,128)S(1)}, f32[128,8,8]{0,2,1:T(8,128)}, u32[]{:S(2)}) copy-start(f32[128,8,8]{0,2,1:T(8,128)} %param.9) | copy-start | bytes 98308
  53.3 7.8 %collective-permute-start.6 = (f32[528,128]{1,0:T(8,128)S(1)}, f32[528,128]{1,0:T(8,128)S(1)}, u32[]{:S(2)}, u32[]{:S(2)}) collective-permute-start(f32[528,128]{1,0:T(8,128)S(1)} %get-tuple-element.48), channel_id=1, source_target_pairs={{0,1},{1,0},{2,3},{3,2},{4,5},{5,4},{6,7},{7,6},{8,9},{9,8},{10,11... | collective-permute-start | bytes 811016 | tf_op jit(solution)/shard_map/ppermute | solution.py:29
  56.9 9.0 %collective-permute-start.7 = (f32[536,128]{1,0:T(8,128)S(1)}, f32[536,128]{1,0:T(8,128)S(1)}, u32[]{:S(2)}, u32[]{:S(2)}) collective-permute-start(f32[536,128]{1,0:T(8,128)S(1)} %get-tuple-element.49), channel_id=1, source_target_pairs={{0,2},{1,3},{2,0},{3,1},{4,6},{5,7},{6,4},{7,5},{8,10},{9,11},{10,... | collective-permute-start | bytes 823304 | tf_op jit(solution)/shard_map/ppermute | solution.py:29
  56.9 10.9 %collective-permute-start.8 = (f32[536,128]{1,0:T(8,128)S(1)}, f32[536,128]{1,0:T(8,128)S(1)}, u32[]{:S(2)}, u32[]{:S(2)}) collective-permute-start(f32[536,128]{1,0:T(8,128)S(1)} %get-tuple-element.50), channel_id=1, source_target_pairs={{0,30},{1,31},{2,4},{3,5},{4,2},{5,3},{6,8},{7,9},{8,6},{9,7},{10,... | collective-permute-start | bytes 823304 | tf_op jit(solution)/shard_map/ppermute | solution.py:29
  61.0 9.5 %collective-permute-start.10 = (f32[8,128]{1,0:T(8,128)S(1)}, f32[8,128]{1,0:T(8,128)S(1)}, u32[]{:S(2)}, u32[]{:S(2)}) collective-permute-start(f32[8,128]{1,0:T(8,128)S(1)} %get-tuple-element.54), channel_id=1, source_target_pairs={{0,29},{1,4},{2,31},{3,6},{4,1},{5,8},{6,3},{7,10},{8,5},{9,12},{1... | collective-permute-start | bytes 12296 | tf_op jit(solution)/shard_map/ppermute | solution.py:29
  61.0 9.5 %collective-permute-start.9 = (f32[528,128]{1,0:T(8,128)S(1)}, f32[528,128]{1,0:T(8,128)S(1)}, u32[]{:S(2)}, u32[]{:S(2)}) collective-permute-start(f32[528,128]{1,0:T(8,128)S(1)} %get-tuple-element.53), channel_id=1, source_target_pairs={{0,31},{1,2},{2,1},{3,4},{4,3},{5,6},{6,5},{7,8},{8,7},{9,10},{10,... | collective-permute-start | bytes 811016 | tf_op jit(solution)/shard_map/ppermute | solution.py:29
  67.9 2.7 %collective-permute-start.11 = (f32[8,128]{1,0:T(8,128)S(1)}, f32[8,128]{1,0:T(8,128)S(1)}, u32[]{:S(2)}, u32[]{:S(2)}) collective-permute-start(f32[8,128]{1,0:T(8,128)S(1)} %slice_add_fusion), channel_id=1, source_target_pairs={{0,1},{1,0},{2,3},{3,2},{4,5},{5,4},{6,7},{7,6},{8,9},{9,8},{10,11... | collective-permute-start | bytes 12296 | tf_op jit(solution)/shard_map/ppermute | solution.py:29

commit v7 on v6

--- a/solution.py
+++ b/solution.py
@@ -158,13 +158,16 @@
     out[CAP : CAP + 8, :] = spill_block(spilled, shift)
 
 
-def beyond(outs, spilled, shifts):
+def pack_far(outs, keys, both, spilled, shifts):
     block = spill_block(spilled, shifts[4])
     for which in range(2):
+        one_hot = choose(keys, which)
+        pack_payload(outs[which], one_hot, both, spilled, shifts[which])
         outs[which][CAP + 16 : CAP + 24, :] = jnp.where(shifts[which] * shifts[4] > 0, block, 0.0)
-
-
-def first_pack_kernel(tile_count, self_ref, field_hbm, departure_hbm, fraction_hbm, *refs):
+        yield one_hot
+
+
+def first_far_kernel(tile_count, self_ref, field_hbm, departure_hbm, fraction_hbm, *refs):
     outs, (field, departure, fraction, sems) = refs[:-4], refs[-4:]
     copies = [
         pltpu.make_async_copy(departure_hbm, departure, sems.at[0]),
@@ -182,14 +185,36 @@
     high, low = halves(field[...])
     both = jnp.concatenate([high, low], axis=1)
     spilled = spill_sums(spills, both)
+    outs[2][...] = both
+    outs[3][...] = spilled
+    outs[4][...] = keys
+    outs[5][...] = meta
+    for which, one_hot in enumerate(pack_far(outs, keys, both, spilled, signs(self_ref[0]))):
+        write_meta(outs[which], CAP + 8, meta, one_hot)
+
+
+def second_far_kernel(self_ref, field, keys, spills, meta, *outs):
+    high, low = halves(field[...])
+    both = jnp.concatenate([high, low], axis=1)
+    spilled = spill_sums(spills[...], both)
+    outs[2][...] = both
+    outs[3][...] = spilled
+    for which, _ in enumerate(pack_far(outs, keys[...], both, spilled, signs(self_ref[0]))):
+        outs[which][CAP + 8 : CAP + 16, :] = meta[8 * which : 8 * which + 8, :]
+
+
+def near_pack_kernel(step, self_ref, both, spilled, keys, meta, *outs):
     shifts = signs(self_ref[0])
-    beyond(outs, spilled, shifts)
-    outs[4][...] = spill_block(spilled, shifts[5])
-    outs[5][...] = spill_block(spilled, 0)
-    for which, shift in enumerate(shifts[:SWAPS]):
-        one_hot = choose(keys, which)
-        pack_payload(outs[which], one_hot, both, spilled, shift)
-        write_meta(outs[which], CAP + 8, meta, one_hot)
+    sums = spilled[...]
+    outs[2][...] = spill_block(sums, shifts[5])
+    outs[3][...] = spill_block(sums, 0)
+    for out, which in zip(outs, (2, 3)):
+        one_hot = choose(keys[...], which)
+        pack_payload(out, one_hot, both[...], sums, shifts[which])
+        if step == 1:
+            write_meta(out, CAP + 8, meta[...], one_hot)
+        else:
+            out[CAP + 8 : CAP + 16, :] = meta[8 * which : 8 * which + 8, :]
 
 
 def index_kernel(tile_count, self_ref, departure, fraction, keys_out, spill_out, meta_out):
@@ -342,7 +367,15 @@
 HBM = pl.BlockSpec(memory_space=pltpu.MemorySpace.HBM)
 SM = pl.BlockSpec(memory_space=pltpu.MemorySpace.SMEM)
 PARAMS = pltpu.CompilerParams(vmem_limit_bytes=40 * 1024 * 1024)
-PACKED = [jax.ShapeDtypeStruct((rows, LEV), F32) for rows in (WIDE_ROWS, WIDE_ROWS, ROWS, ROWS, 8, 8)]
+SPREAD_ROWS = 8 * (2 * REACH + 1)
+FAR = [
+    jax.ShapeDtypeStruct((WIDE_ROWS, LEV), F32),
+    jax.ShapeDtypeStruct((WIDE_ROWS, LEV), F32),
+    jax.ShapeDtypeStruct((COLS, 2 * LEV), BF),
+    jax.ShapeDtypeStruct((SPREAD_ROWS, LEV), F32),
+]
+NEAR = [jax.ShapeDtypeStruct((rows, LEV), F32) for rows in (ROWS, ROWS, 8, 8)]
+KEYS = jax.ShapeDtypeStruct((1, COLS), jnp.int32)
 
 
 def call(kernel, out_shape, in_specs, scratch=(), flops=0, out_spec=None):
@@ -358,31 +391,34 @@
     )
 
 
-def transported(step, packed, tile_count, tile_self, field, departure, fraction, level_map):
+def transported(step, packed, keys, meta, tile_count, tile_self, field, departure, fraction, level_map):
     far = [swapped(packed[w], w) for w in (0, 1)]
-    partner = swapped(packed[3], 3)
-    late = lax.optimization_barrier((packed[2], packed[4], partner))
-    cross = swapped(late[0], 2)
-    tiny = swapped(late[1], 5)
+    near = call(functools.partial(near_pack_kernel, step), NEAR, [SM] + [VM] * 4, (), 10**9)(
+        tile_self, packed[2], packed[3], keys, meta
+    )
+    cross = swapped(near[0], 2)
+    partner = swapped(near[1], 3)
+    late = lax.optimization_barrier((near[2], partner))
+    tiny = swapped(late[0], 5)
     handed = swapped(far[0][CAP + 16 :] + far[1][CAP + 16 :], 3)
     total = jax.ShapeDtypeStruct((COLS, LEV), F32)
     one = pltpu.VMEM((1, CAP, 2 * LEV), BF)
-    work = 3 * 10**9
+    work = 10**7
     own = call(
         functools.partial(own_kernel, step, tile_count),
         total,
         [SM] + [VM] * 5,
         [pltpu.VMEM((COLS, 2 * LEV), BF), one],
         work,
-    )(tile_self, field, departure, fraction, packed[5], partner)
+    )(tile_self, field, departure, fraction, near[3], partner)
     index = None
     if step == 1:
         after = lax.optimization_barrier((tile_self, own))
         index = call(
             functools.partial(index_kernel, tile_count),
             [
-                jax.ShapeDtypeStruct((1, COLS), jnp.int32),
-                jax.ShapeDtypeStruct((16 * (2 * REACH + 1), COLS), BF),
+                KEYS,
+                jax.ShapeDtypeStruct((2 * SPREAD_ROWS, COLS), BF),
                 jax.ShapeDtypeStruct((32, LEV), F32),
             ],
             [SM, VM, VM],
@@ -417,18 +453,24 @@
         pltpu.VMEM((2, COLS), F32),
         pltpu.SemaphoreType.DMA((3,)),
     ]
-    packed = call(functools.partial(first_pack_kernel, tile_count), PACKED, [SM, HBM, HBM, HBM], first_scratch)(
+    outputs = FAR + [KEYS, jax.ShapeDtypeStruct((8, COLS), BF)]
+    packed = call(functools.partial(first_far_kernel, tile_count), outputs, [SM, HBM, HBM, HBM], first_scratch)(
         tile_self, *[pltpu.with_memory_space_constraint(x, pltpu.MemorySpace.HBM) for x in (adjoint_in, departure, fraction)]
     )
     table = coarse_map.transpose(1, 2, 0).reshape(groups * groups, LEV)
-    second, index = transported(1, packed, tile_count, tile_self, adjoint_in, departure, fraction, level_map)
+    second, index = transported(
+        1, packed, packed[4], packed[5], tile_count, tile_self, adjoint_in, departure, fraction, level_map
+    )
 
     parts = lax.all_to_all(second.reshape(groups, COLS // groups, LEV), "grp", 0, 0)
     mixed = call(couple_kernel, jax.ShapeDtypeStruct(parts.shape, F32), [VM, VM])(table, parts)
     coupled = lax.all_to_all(mixed, "grp", 0, 0).reshape(COLS, LEV)
 
-    packed = call(second_pack_kernel, PACKED, [SM] + [VM] * 4)(tile_self, coupled, *index)
-    return transported(0, packed, tile_count, tile_self, coupled, departure, fraction, level_map)[0]
+    keys, spills, meta = index
+    packed = call(second_far_kernel, FAR, [SM] + [VM] * 4)(tile_self, coupled, keys, spills, meta)
+    return transported(
+        0, packed, keys, meta, tile_count, tile_self, coupled, departure, fraction, level_map
+    )[0]
 
 
 def solution(mesh):

time: 73.1 us -> 75.6 us (1.034)
  blocking collectives: 27.9 us -> 29.3 us
    all_to_all x1, blocking collectives: 15.7 us -> 17.1 us  [body(): lax.all_to_all(second.reshape(groups, COLS // groups, LEV), 'grp', 0, 0)]
    pallas_call x3 -> x5, Pallas kernels: 6.26 us -> 6.52 us  [the longest x1 2.42 us: body(): call(functools.partial(first_far_kernel, tile_count), outputs, [SM, HBM,...]
  transfers between devices with their start and end apart: 12 -> 12, of which waited for: 2 -> 3; matrix products, arithmetic and copies ran while one was open for 0% -> 0% of each run, Pallas kernels for 13% -> 15%
where the time goes in v7:
time: 75.6 us; the launch traced here: 75.3 us
  blocking collectives  29.3 us (39%)
  starting transfers between devices  24 us (32%)
  Pallas kernels  18.4 us (24%)
  waiting for transfers between devices  3.28 us (4%)
    ppermute x12, starting transfers between devices, swapped(): lax.ppermute(x, 'tile', [(i, (i + signs(i)[which]) % length) for i in ran...  24 us
    all_to_all x1, blocking collectives, body(): lax.all_to_all(second.reshape(groups, COLS // groups, LEV), 'grp', 0, 0)  17.1 us
    all_to_all x1, blocking collectives, body(): coupled = lax.all_to_all(mixed, 'grp', 0, 0).reshape(COLS, LEV)  12.2 us
    pallas_call x2, Pallas kernels, transported(): call(functools.partial(own_kernel, step, tile_count), total, [SM] + [VM]...  4.59 us
    pallas_call x2, Pallas kernels, transported(): call(functools.partial(last_kernel, step), total, [VM] * 5, [one, pltpu.V...  3.53 us
    pallas_call x2, Pallas kernels, transported(): call(middle_kernel, total, [VM] * 3, [pltpu.VMEM((2, CAP, 2 * LEV), BF)],...  3.4 us
    ppermute x12, waiting for transfers between devices, swapped(): lax.ppermute(x, 'tile', [(i, (i + signs(i)[which]) % length) for i in ran...  3.28 us
    pallas_call x1, Pallas kernels, body(): call(functools.partial(first_far_kernel, tile_count), outputs, [SM, HBM,...  2.42 us
  transfers between devices with their start and end apart: 12, of which 3 were waited for; matrix products, arithmetic and copies ran while one was open for 0% of the time, Pallas kernels for 15%

profile of v7, /device:TPU:1, one launch (start us, length us, event | category | flops | bytes accessed | tf_op | source)
XLA Modules:
  0.0 75.3 jit_solution(6659632504229121768)
XLA Ops:
  0.0 2.4 %shard_map.55 = (f32[536,128]{1,0:T(8,128)S(1)}, f32[536,128]{1,0:T(8,128)S(1)}, bf16[1024,256]{1,0:T(8,128)(2,1)S(1)}, f32[40,128]{1,0:T(8,128)S(1)}, s32[1,102...) custom-call(s32[1]{0:T(128)} %bitcast.self_ref, f32[1024,128]{1,0:T(8,128)} %field.1, s32[2,1024]{1,0:T(2,128)} %departure.5, ...), custom_call_target="tpu_custom_call" | custom-call | tf_op jit(solution)/shard_map/pallas_call | solution.py:457
  2.4 2.6 %collective-permute-start.1 = (f32[536,128]{1,0:T(8,128)S(1)}, f32[536,128]{1,0:T(8,128)S(1)}, u32[]{:S(2)}, u32[]{:S(2)}) collective-permute-start(f32[536,128]{1,0:T(8,128)S(1)} %get-tuple-element.46), channel_id=1, source_target_pairs={{0,2},{1,3},{2,0},{3,1},{4,6},{5,7},{6,4},{7,5},{8,10},{9,11},{10,... | collective-permute-start | bytes 823304 | tf_op jit(solution)/shard_map/ppermute | solution.py:29
  5.0 5.7 %collective-permute-start.2 = (f32[536,128]{1,0:T(8,128)S(1)}, f32[536,128]{1,0:T(8,128)S(1)}, u32[]{:S(2)}, u32[]{:S(2)}) collective-permute-start(f32[536,128]{1,0:T(8,128)S(1)} %get-tuple-element.47), channel_id=1, source_target_pairs={{0,30},{1,31},{2,4},{3,5},{4,2},{5,3},{6,8},{7,9},{8,6},{9,7},{10,... | collective-permute-start | bytes 823304 | tf_op jit(solution)/shard_map/ppermute | solution.py:29
  10.7 0.0 copy-start
  10.7 0.0 copy-start.2
  10.7 0.0 copy-start.3
  10.7 1.2 %shard_map.56 = (f32[528,128]{1,0:T(8,128)S(1)}, f32[528,128]{1,0:T(8,128)S(1)}, f32[8,128]{1,0:T(8,128)S(1)}, f32[8,128]{1,0:T(8,128)S(1)}) custom-call(s32[1]{0:T(128)} %bitcast.self_ref, bf16[1024,256]{1,0:T(8,128)(2,1)S(1)} %get-tuple-element.34.both, f32[40,128]{1,0:T(8,128)S(1)} %get-tuple-element.35.spilled, s32[1,1024]{1,0:T(1,128)S(1)} %get-tuple-element.36.keys, ...), custom_call_target="tpu_custom_call" | custom-call | flops 1000000000 | bytes 3906250 | tf_op jit(solution)/shard_map/pallas_call | solution.py:396
  11.9 1.3 %collective-permute-start = (f32[528,128]{1,0:T(8,128)S(1)}, f32[528,128]{1,0:T(8,128)S(1)}, u32[]{:S(2)}, u32[]{:S(2)}) collective-permute-start(f32[528,128]{1,0:T(8,128)S(1)} %get-tuple-element.39), channel_id=1, source_target_pairs={{0,1},{1,0},{2,3},{3,2},{4,5},{5,4},{6,7},{7,6},{8,9},{9,8},{10,11... | collective-permute-start | bytes 811016 | tf_op jit(solution)/shard_map/ppermute | solution.py:29
  13.2 0.0 collective-permute-start.3
  13.2 1.2 %collective-permute-done.payload = f32[528,128]{1,0:T(8,128)S(1)} collective-permute-done((f32[528,128]{1,0:T(8,128)S(1)}, f32[528,128]{1,0:T(8,128)S(1)}, u32[]{:S(2)}, u32[]{:S(2)}) %collective-permute-start) | collective-permute-done | bytes 270368 | tf_op jit(solution)/shard_map/ppermute | solution.py:29
  14.4 0.0 collective-permute-start.4
  14.4 0.0 copy-done
  14.4 0.0 copy-done.2
  14.4 0.0 copy-done.3
  14.4 2.3 %shard_map.57.start = f32[1024,128]{1,0:T(8,128)S(1)} custom-call(s32[1]{0:T(128)} %bitcast.self_ref, f32[1024,128]{1,0:T(8,128)S(1)} %copy-done, s32[2,1024]{1,0:T(2,128)S(1)} %copy-done.2, f32[2,1024]{1,0:T(2,128)S(1)} %copy-done.3, f32[8,128]{1,0:T(8,128)S(1)} %get-tuple-element.38.spilled, f32[528,128]{1,0:T(8,128)S(1)} %collective-permute-done.payload), custom_call_target="tpu_custom_call" | custom-call | flops 10000000 | bytes 39062 | tf_op jit(solution)/shard_map/pallas_call | solution.py:407
  16.7 0.0 collective-permute-done.1.p0
  16.7 0.0 collective-permute-done.2.p1
  16.7 1.6 %collective-permute-start.5 = (f32[8,128]{1,0:T(8,128)S(1)}, f32[8,128]{1,0:T(8,128)S(1)}, u32[]{:S(2)}, u32[]{:S(2)}) collective-permute-start(f32[8,128]{1,0:T(8,128)S(1)} %slice_add_fusion.1), channel_id=1, source_target_pairs={{0,1},{1,0},{2,3},{3,2},{4,5},{5,4},{6,7},{7,6},{8,9},{9,8},{10,11... | collective-permute-start | bytes 12296 | tf_op jit(solution)/shard_map/ppermute | solution.py:29
  18.4 1.4 %shard_map.58 = (s32[1,1024]{1,0:T(1,128)S(1)}, bf16[80,1024]{1,0:T(8,128)(2,1)S(1)}, f32[32,128]{1,0:T(8,128)S(1)}) custom-call(s32[1]{0:T(128)} %bitcast.self_ref, s32[2,1024]{1,0:T(2,128)S(1)} %copy-done.2, f32[2,1024]{1,0:T(2,128)S(1)} %copy-done.3), custom_call_target="tpu_custom_call" | custom-call | flops 2000000000 | bytes 7812500 | tf_op jit(solution)/shard_map/pallas_call | solution.py:417
  19.8 0.0 copy-start.1
  19.8 1.7 %shard_map.59.start = f32[1024,128]{1,0:T(8,128)S(1)} custom-call(f32[1024,128]{1,0:T(8,128)S(1)} %shard_map.57.start, f32[536,128]{1,0:T(8,128)S(1)} %collective-permute-done.1.p0, f32[536,128]{1,0:T(8,128)S(1)} %collective-permute-done.2.p1), custom_call_target="tpu_custom_call" | custom-call | flops 10000000 | bytes 39062 | tf_op jit(solution)/shard_map/pallas_call | solution.py:429
  21.5 0.0 collective-permute-done.3.payload
  21.5 0.0 collective-permute-done.4.tiny_a
  21.5 0.0 collective-permute-done.5.tiny_b
  21.5 0.0 copy-done.1
  21.5 1.4 %shard_map.60 = f32[1024,128]{1,0:T(8,128)S(1)} custom-call(f32[1024,128]{1,0:T(8,128)S(1)} %shard_map.59.start, f32[528,128]{1,0:T(8,128)S(1)} %collective-permute-done.3.payload, f32[8,128]{1,0:T(8,128)S(1)} %collective-permute-done.4.tiny_a, f32[8,128]{1,0:T(8,128)S(1)} %collective-permute-done.5.tiny_b, f32[2,128,128]{2,1,0:T(8,128)S(1)} %copy-done.1), custom_call_target="tpu_custom_call" | custom-call | flops 10000000 | bytes 39062 | tf_op jit(solution)/shard_map/pallas_call | solution.py:430
  22.9 0.0 copy-start.4
  22.9 17.1 %all_to_all.10.x = f32[8,128,128]{2,1,0:T(8,128)S(1)} all-to-all(f32[8,128,128]{2,1,0:T(8,128)S(1)} %bitcast.8), channel_id=1, replica_groups=mesh['grp'=8,'tile'=32] {'grp'}, dimensions={0} | all-to-all | bytes 1048576 | tf_op jit(solution)/shard_map/all_to_all | solution.py:465
  40.0 0.0 copy-done.4
  40.0 0.4 shard_map.61
  40.4 12.2 %all_to_all.11 = f32[8,128,128]{2,1,0:T(8,128)S(1)} all-to-all(f32[8,128,128]{2,1,0:T(8,128)S(1)} %shard_map.61), channel_id=1, replica_groups=mesh['grp'=8,'tile'=32] {'grp'}, dimensions={0} | all-to-all | bytes 1048576 | tf_op jit(solution)/shard_map/all_to_all | solution.py:467
  52.6 0.8 %shard_map.62 = (f32[536,128]{1,0:T(8,128)S(1)}, f32[536,128]{1,0:T(8,128)S(1)}, bf16[1024,256]{1,0:T(8,128)(2,1)S(1)}, f32[40,128]{1,0:T(8,128)S(1)}) custom-call(s32[1]{0:T(128)} %bitcast.self_ref, f32[1024,128]{1,0:T(8,128)S(1)} %bitcast.6, s32[1,1024]{1,0:T(1,128)S(1)} %get-tuple-element.51.keys, bf16[80,1024]{1,0:T(8,128)(2,1)S(1)} %get-tuple-element.52.spills, ...), custom_call_target="tpu_custom_call" | custom-call | tf_op jit(solution)/shard_map/pallas_call | solution.py:470
  53.4 2.5 %collective-permute-start.7 = (f32[536,128]{1,0:T(8,128)S(1)}, f32[536,128]{1,0:T(8,128)S(1)}, u32[]{:S(2)}, u32[]{:S(2)}) collective-permute-start(f32[536,128]{1,0:T(8,128)S(1)} %get-tuple-element.58), channel_id=1, source_target_pairs={{0,2},{1,3},{2,0},{3,1},{4,6},{5,7},{6,4},{7,5},{8,10},{9,11},{10,... | collective-permute-start | bytes 823304 | tf_op jit(solution)/shard_map/ppermute | solution.py:29
  55.9 0.7 collective-permute-start.8
  56.6 0.7 shard_map.63
  57.3 3.3 %collective-permute-start.6 = (f32[528,128]{1,0:T(8,128)S(1)}, f32[528,128]{1,0:T(8,128)S(1)}, u32[]{:S(2)}, u32[]{:S(2)}) collective-permute-start(f32[528,128]{1,0:T(8,128)S(1)} %get-tuple-element.57), channel_id=1, source_target_pairs={{0,1},{1,0},{2,3},{3,2},{4,5},{5,4},{6,7},{7,6},{8,9},{9,8},{10,11... | collective-permute-start | bytes 811016 | tf_op jit(solution)/shard_map/ppermute | solution.py:29
  60.6 0.0 collective-permute-start.9
  60.6 1.2 %collective-permute-done.6.payload = f32[528,128]{1,0:T(8,128)S(1)} collective-permute-done((f32[528,128]{1,0:T(8,128)S(1)}, f32[528,128]{1,0:T(8,128)S(1)}, u32[]{:S(2)}, u32[]{:S(2)}) %collective-permute-start.6) | collective-permute-done | bytes 270368 | tf_op jit(solution)/shard_map/ppermute | solution.py:29
  61.8 0.6 collective-permute-start.10
  62.4 0.0 collective-permute-done.7.p0
  62.4 0.9 %collective-permute-done.8.p1 = f32[536,128]{1,0:T(8,128)S(1)} collective-permute-done((f32[536,128]{1,0:T(8,128)S(1)}, f32[536,128]{1,0:T(8,128)S(1)}, u32[]{:S(2)}, u32[]{:S(2)}) %collective-permute-start.8) | collective-permute-done | bytes 274464 | tf_op jit(solution)/shard_map/ppermute | solution.py:29
  63.4 5.6 %collective-permute-start.11 = (f32[8,128]{1,0:T(8,128)S(1)}, f32[8,128]{1,0:T(8,128)S(1)}, u32[]{:S(2)}, u32[]{:S(2)}) collective-permute-start(f32[8,128]{1,0:T(8,128)S(1)} %slice_add_fusion), channel_id=1, source_target_pairs={{0,1},{1,0},{2,3},{3,2},{4,5},{5,4},{6,7},{7,6},{8,9},{9,8},{10,11... | collective-permute-start | bytes 12296 | tf_op jit(solution)/shard_map/ppermute | solution.py:29
  69.0 2.3 %shard_map.64.start = f32[1024,128]{1,0:T(8,128)S(1)} custom-call(s32[1]{0:T(128)} %bitcast.self_ref, f32[1024,128]{1,0:T(8,128)S(1)} %bitcast.7, s32[2,1024]{1,0:T(2,128)S(1)} %copy-done.2, f32[2,1024]{1,0:T(2,128)S(1)} %copy-done.3, f32[8,128]{1,0:T(8,128)S(1)} %get-tuple-element.56.spilled, f32[528,128]{1,0:T(8,128)S(1)} %collective-permute-done.6.payload), custom_call_target="tpu_custom_call" | custom-call | flops 10000000 | bytes 39062 | tf_op jit(solution)/shard_map/pallas_call | solution.py:407
  71.3 1.7 %shard_map.65.start = f32[1024,128]{1,0:T(8,128)S(1)} custom-call(f32[1024,128]{1,0:T(8,128)S(1)} %shard_map.64.start, f32[536,128]{1,0:T(8,128)S(1)} %collective-permute-done.7.p0, f32[536,128]{1,0:T(8,128)S(1)} %collective-permute-done.8.p1), custom_call_target="tpu_custom_call" | custom-call | flops 10000000 | bytes 39062 | tf_op jit(solution)/shard_map/pallas_call | solution.py:429
  73.0 0.0 collective-permute-done.9.payload
  73.0 0.0 collective-permute-done.10.tiny_a
  73.0 0.0 collective-permute-done.11.tiny_b
  73.0 2.2 %shard_map.66 = f32[1024,128]{1,0:T(8,128)} custom-call(f32[1024,128]{1,0:T(8,128)S(1)} %shard_map.65.start, f32[528,128]{1,0:T(8,128)S(1)} %collective-permute-done.9.payload, f32[8,128]{1,0:T(8,128)S(1)} %collective-permute-done.10.tiny_a, f32[8,128]{1,0:T(8,128)S(1)} %collective-permute-done.11.tiny_b, f32[2,128,128]{2,1,0:T(8,128)S(1)} %copy-done.1), custom_call_target="tpu_custom_call" | custom-call | flops 10000000 | bytes 39062 | tf_op jit(solution)/shard_map/pallas_call | solution.py:430
  (2 shorter events, 0.0 us)
Async XLA Ops:
  2.4 14.3 %collective-permute-start.1 = (f32[536,128]{1,0:T(8,128)S(1)}, f32[536,128]{1,0:T(8,128)S(1)}, u32[]{:S(2)}, u32[]{:S(2)}) collective-permute-start(f32[536,128]{1,0:T(8,128)S(1)} %get-tuple-element.46), channel_id=1, source_target_pairs={{0,2},{1,3},{2,0},{3,1},{4,6},{5,7},{6,4},{7,5},{8,10},{9,11},{10,... | collective-permute-start | bytes 823304 | tf_op jit(solution)/shard_map/ppermute | solution.py:29
  5.0 11.7 %collective-permute-start.2 = (f32[536,128]{1,0:T(8,128)S(1)}, f32[536,128]{1,0:T(8,128)S(1)}, u32[]{:S(2)}, u32[]{:S(2)}) collective-permute-start(f32[536,128]{1,0:T(8,128)S(1)} %get-tuple-element.47), channel_id=1, source_target_pairs={{0,30},{1,31},{2,4},{3,5},{4,2},{5,3},{6,8},{7,9},{8,6},{9,7},{10,... | collective-permute-start | bytes 823304 | tf_op jit(solution)/shard_map/ppermute | solution.py:29
  10.7 3.7 %copy-start = (f32[1024,128]{1,0:T(8,128)S(1)}, f32[1024,128]{1,0:T(8,128)}, u32[]{:S(2)}) copy-start(f32[1024,128]{1,0:T(8,128)} %field.1) | copy-start | bytes 1572868
  10.7 3.7 %copy-start.2 = (s32[2,1024]{1,0:T(2,128)S(1)}, s32[2,1024]{1,0:T(2,128)}, u32[]{:S(2)}) copy-start(s32[2,1024]{1,0:T(2,128)} %departure.5) | copy-start | bytes 24580
  10.7 3.7 %copy-start.3 = (f32[2,1024]{1,0:T(2,128)S(1)}, f32[2,1024]{1,0:T(2,128)}, u32[]{:S(2)}) copy-start(f32[2,1024]{1,0:T(2,128)} %fraction.5) | copy-start | bytes 24580
  11.9 2.5 %collective-permute-start = (f32[528,128]{1,0:T(8,128)S(1)}, f32[528,128]{1,0:T(8,128)S(1)}, u32[]{:S(2)}, u32[]{:S(2)}) collective-permute-start(f32[528,128]{1,0:T(8,128)S(1)} %get-tuple-element.39), channel_id=1, source_target_pairs={{0,1},{1,0},{2,3},{3,2},{4,5},{5,4},{6,7},{7,6},{8,9},{9,8},{10,11... | collective-permute-start | bytes 811016 | tf_op jit(solution)/shard_map/ppermute | solution.py:29
  13.2 8.3 %collective-permute-start.3 = (f32[528,128]{1,0:T(8,128)S(1)}, f32[528,128]{1,0:T(8,128)S(1)}, u32[]{:S(2)}, u32[]{:S(2)}) collective-permute-start(f32[528,128]{1,0:T(8,128)S(1)} %get-tuple-element.48), channel_id=1, source_target_pairs={{0,31},{1,2},{2,1},{3,4},{4,3},{5,6},{6,5},{7,8},{8,7},{9,10},{10,... | collective-permute-start | bytes 811016 | tf_op jit(solution)/shard_map/ppermute | solution.py:29
  14.4 7.1 %collective-permute-start.4 = (f32[8,128]{1,0:T(8,128)S(1)}, f32[8,128]{1,0:T(8,128)S(1)}, u32[]{:S(2)}, u32[]{:S(2)}) collective-permute-start(f32[8,128]{1,0:T(8,128)S(1)} %get-tuple-element.50), channel_id=1, source_target_pairs={{0,29},{1,4},{2,31},{3,6},{4,1},{5,8},{6,3},{7,10},{8,5},{9,12},{1... | collective-permute-start | bytes 12296 | tf_op jit(solution)/shard_map/ppermute | solution.py:29
  16.7 4.8 %collective-permute-start.5 = (f32[8,128]{1,0:T(8,128)S(1)}, f32[8,128]{1,0:T(8,128)S(1)}, u32[]{:S(2)}, u32[]{:S(2)}) collective-permute-start(f32[8,128]{1,0:T(8,128)S(1)} %slice_add_fusion.1), channel_id=1, source_target_pairs={{0,1},{1,0},{2,3},{3,2},{4,5},{5,4},{6,7},{7,6},{8,9},{9,8},{10,11... | collective-permute-start | bytes 12296 | tf_op jit(solution)/shard_map/ppermute | solution.py:29
  19.8 1.8 %copy-start.1 = (f32[2,128,128]{2,1,0:T(8,128)S(1)}, f32[2,128,128]{2,1,0:T(8,128)}, u32[]{:S(2)}) copy-start(f32[2,128,128]{2,1,0:T(8,128)} %level_map.3) | copy-start | bytes 393220
  22.9 17.1 %copy-start.4 = (f32[128,8,8]{0,2,1:T(8,128)S(1)}, f32[128,8,8]{0,2,1:T(8,128)}, u32[]{:S(2)}) copy-start(f32[128,8,8]{0,2,1:T(8,128)} %param.9) | copy-start | bytes 98308
  53.4 9.0 %collective-permute-start.7 = (f32[536,128]{1,0:T(8,128)S(1)}, f32[536,128]{1,0:T(8,128)S(1)}, u32[]{:S(2)}, u32[]{:S(2)}) collective-permute-start(f32[536,128]{1,0:T(8,128)S(1)} %get-tuple-element.58), channel_id=1, source_target_pairs={{0,2},{1,3},{2,0},{3,1},{4,6},{5,7},{6,4},{7,5},{8,10},{9,11},{10,... | collective-permute-start | bytes 823304 | tf_op jit(solution)/shard_map/ppermute | solution.py:29
  55.9 7.5 %collective-permute-start.8 = (f32[536,128]{1,0:T(8,128)S(1)}, f32[536,128]{1,0:T(8,128)S(1)}, u32[]{:S(2)}, u32[]{:S(2)}) collective-permute-start(f32[536,128]{1,0:T(8,128)S(1)} %get-tuple-element.59), channel_id=1, source_target_pairs={{0,30},{1,31},{2,4},{3,5},{4,2},{5,3},{6,8},{7,9},{8,6},{9,7},{10,... | collective-permute-start | bytes 823304 | tf_op jit(solution)/shard_map/ppermute | solution.py:29
  57.3 4.5 %collective-permute-start.6 = (f32[528,128]{1,0:T(8,128)S(1)}, f32[528,128]{1,0:T(8,128)S(1)}, u32[]{:S(2)}, u32[]{:S(2)}) collective-permute-start(f32[528,128]{1,0:T(8,128)S(1)} %get-tuple-element.57), channel_id=1, source_target_pairs={{0,1},{1,0},{2,3},{3,2},{4,5},{5,4},{6,7},{7,6},{8,9},{9,8},{10,11... | collective-permute-start | bytes 811016 | tf_op jit(solution)/shard_map/ppermute | solution.py:29
  60.6 12.3 %collective-permute-start.9 = (f32[528,128]{1,0:T(8,128)S(1)}, f32[528,128]{1,0:T(8,128)S(1)}, u32[]{:S(2)}, u32[]{:S(2)}) collective-permute-start(f32[528,128]{1,0:T(8,128)S(1)} %get-tuple-element.60), channel_id=1, source_target_pairs={{0,31},{1,2},{2,1},{3,4},{4,3},{5,6},{6,5},{7,8},{8,7},{9,10},{10,... | collective-permute-start | bytes 811016 | tf_op jit(solution)/shard_map/ppermute | solution.py:29
  61.8 11.2 %collective-permute-start.10 = (f32[8,128]{1,0:T(8,128)S(1)}, f32[8,128]{1,0:T(8,128)S(1)}, u32[]{:S(2)}, u32[]{:S(2)}) collective-permute-start(f32[8,128]{1,0:T(8,128)S(1)} %get-tuple-element.62), channel_id=1, source_target_pairs={{0,29},{1,4},{2,31},{3,6},{4,1},{5,8},{6,3},{7,10},{8,5},{9,12},{1... | collective-permute-start | bytes 12296 | tf_op jit(solution)/shard_map/ppermute | solution.py:29
  63.4 9.6 %collective-permute-start.11 = (f32[8,128]{1,0:T(8,128)S(1)}, f32[8,128]{1,0:T(8,128)S(1)}, u32[]{:S(2)}, u32[]{:S(2)}) collective-permute-start(f32[8,128]{1,0:T(8,128)S(1)} %slice_add_fusion), channel_id=1, source_target_pairs={{0,1},{1,0},{2,3},{3,2},{4,5},{5,4},{6,7},{7,6},{8,9},{9,8},{10,11... | collective-permute-start | bytes 12296 | tf_op jit(solution)/shard_map/ppermute | solution.py:29

commit v8 on v7

--- a/solution.py
+++ b/solution.py
@@ -393,23 +393,22 @@
 
 def transported(step, packed, keys, meta, tile_count, tile_self, field, departure, fraction, level_map):
     far = [swapped(packed[w], w) for w in (0, 1)]
-    near = call(functools.partial(near_pack_kernel, step), NEAR, [SM] + [VM] * 4, (), 10**9)(
+    near = call(functools.partial(near_pack_kernel, step), NEAR, [SM] + [VM] * 4, (), 1000000000)(
         tile_self, packed[2], packed[3], keys, meta
     )
     cross = swapped(near[0], 2)
     partner = swapped(near[1], 3)
     late = lax.optimization_barrier((near[2], partner))
     tiny = swapped(late[0], 5)
-    handed = swapped(far[0][CAP + 16 :] + far[1][CAP + 16 :], 3)
     total = jax.ShapeDtypeStruct((COLS, LEV), F32)
     one = pltpu.VMEM((1, CAP, 2 * LEV), BF)
-    work = 10**7
+    work = 10000000
     own = call(
         functools.partial(own_kernel, step, tile_count),
         total,
         [SM] + [VM] * 5,
         [pltpu.VMEM((COLS, 2 * LEV), BF), one],
-        work,
+        10000000,
     )(tile_self, field, departure, fraction, near[3], partner)
     index = None
     if step == 1:
@@ -423,9 +422,11 @@
             ],
             [SM, VM, VM],
             (),
-            2 * 10**9,
+            10000000,
         )(after[0], departure, fraction)
         own, index = lax.optimization_barrier((after[1], index))
+    own, *far = lax.optimization_barrier((own, *far))
+    handed = swapped(far[0][CAP + 16 :] + far[1][CAP + 16 :], 3)
     summed = call(middle_kernel, total, [VM] * 3, [pltpu.VMEM((2, CAP, 2 * LEV), BF)], work)(own, *far)
     result = call(
         functools.partial(last_kernel, step),

time: 75.6 us -> 73.3 us (0.970)
  starting transfers between devices: 24 us -> 22.6 us
  waiting for transfers between devices: 3.28 us -> 2.4 us
    ppermute x12, starting transfers between devices: 24 us -> 22.6 us  [swapped(): lax.ppermute(x, 'tile', [(i, (i + signs(i)[which]) % length) for i in ran...]
    ppermute x12, waiting for transfers between devices: 3.28 us -> 2.4 us  [swapped(): lax.ppermute(x, 'tile', [(i, (i + signs(i)[which]) % length) for i in ran...]
  transfers between devices with their start and end apart: 12 -> 12, of which waited for: 3 -> 2; matrix products, arithmetic and copies ran while one was open for 0% -> 0% of each run, Pallas kernels for 15% -> 15%
where the time goes in v8:
time: 73.3 us; the launch traced here: 73 us
  blocking collectives  29.3 us (40%)
  starting transfers between devices  22.6 us (31%)
  Pallas kernels  18.4 us (25%)
  waiting for transfers between devices  2.4 us (3%)
    ppermute x12, starting transfers between devices, swapped(): lax.ppermute(x, 'tile', [(i, (i + signs(i)[which]) % length) for i in ran...  22.6 us
    all_to_all x1, blocking collectives, body(): lax.all_to_all(second.reshape(groups, COLS // groups, LEV), 'grp', 0, 0)  17.1 us
    all_to_all x1, blocking collectives, body(): coupled = lax.all_to_all(mixed, 'grp', 0, 0).reshape(COLS, LEV)  12.1 us
    pallas_call x2, Pallas kernels, transported(): call(functools.partial(own_kernel, step, tile_count), total, [SM] + [VM]...  4.59 us
    pallas_call x2, Pallas kernels, transported(): call(functools.partial(last_kernel, step), total, [VM] * 5, [one, pltpu.V...  3.54 us
    pallas_call x2, Pallas kernels, transported(): call(middle_kernel, total, [VM] * 3, [pltpu.VMEM((2, CAP, 2 * LEV), BF)],...  3.37 us
    pallas_call x1, Pallas kernels, body(): call(functools.partial(first_far_kernel, tile_count), outputs, [SM, HBM,...  2.42 us
    ppermute x12, waiting for transfers between devices, swapped(): lax.ppermute(x, 'tile', [(i, (i + signs(i)[which]) % length) for i in ran...  2.4 us
  transfers between devices with their start and end apart: 12, of which 2 were waited for; matrix products, arithmetic and copies ran while one was open for 0% of the time, Pallas kernels for 15%

profile of v8, /device:TPU:1, one launch (start us, length us, event | category | flops | bytes accessed | tf_op | source)
XLA Modules:
  0.0 73.0 jit_solution(2536369653143153824)
XLA Ops:
  0.0 2.4 %shard_map.55 = (f32[536,128]{1,0:T(8,128)S(1)}, f32[536,128]{1,0:T(8,128)S(1)}, bf16[1024,256]{1,0:T(8,128)(2,1)S(1)}, f32[40,128]{1,0:T(8,128)S(1)}, s32[1,102...) custom-call(s32[1]{0:T(128)} %bitcast.self_ref, f32[1024,128]{1,0:T(8,128)} %field.1, s32[2,1024]{1,0:T(2,128)} %departure.5, ...), custom_call_target="tpu_custom_call" | custom-call | tf_op jit(solution)/shard_map/pallas_call | solution.py:458
  2.4 2.6 %collective-permute-start.1 = (f32[536,128]{1,0:T(8,128)S(1)}, f32[536,128]{1,0:T(8,128)S(1)}, u32[]{:S(2)}, u32[]{:S(2)}) collective-permute-start(f32[536,128]{1,0:T(8,128)S(1)} %get-tuple-element.52), channel_id=1, source_target_pairs={{0,2},{1,3},{2,0},{3,1},{4,6},{5,7},{6,4},{7,5},{8,10},{9,11},{10,... | collective-permute-start | bytes 823304 | tf_op jit(solution)/shard_map/ppermute | solution.py:29
  5.0 5.7 %collective-permute-start.2 = (f32[536,128]{1,0:T(8,128)S(1)}, f32[536,128]{1,0:T(8,128)S(1)}, u32[]{:S(2)}, u32[]{:S(2)}) collective-permute-start(f32[536,128]{1,0:T(8,128)S(1)} %get-tuple-element.53), channel_id=1, source_target_pairs={{0,30},{1,31},{2,4},{3,5},{4,2},{5,3},{6,8},{7,9},{8,6},{9,7},{10,... | collective-permute-start | bytes 823304 | tf_op jit(solution)/shard_map/ppermute | solution.py:29
  10.7 0.0 copy-start
  10.7 0.0 copy-start.2
  10.7 0.0 copy-start.3
  10.7 1.2 %shard_map.56 = (f32[528,128]{1,0:T(8,128)S(1)}, f32[528,128]{1,0:T(8,128)S(1)}, f32[8,128]{1,0:T(8,128)S(1)}, f32[8,128]{1,0:T(8,128)S(1)}) custom-call(s32[1]{0:T(128)} %bitcast.self_ref, bf16[1024,256]{1,0:T(8,128)(2,1)S(1)} %get-tuple-element.40.both, f32[40,128]{1,0:T(8,128)S(1)} %get-tuple-element.41.spilled, s32[1,1024]{1,0:T(1,128)S(1)} %get-tuple-element.42.keys, ...), custom_call_target="tpu_custom_call" | custom-call | flops 1000000000 | bytes 3906250 | tf_op jit(solution)/shard_map/pallas_call | solution.py:396
  11.9 1.3 %collective-permute-start = (f32[528,128]{1,0:T(8,128)S(1)}, f32[528,128]{1,0:T(8,128)S(1)}, u32[]{:S(2)}, u32[]{:S(2)}) collective-permute-start(f32[528,128]{1,0:T(8,128)S(1)} %get-tuple-element.45), channel_id=1, source_target_pairs={{0,1},{1,0},{2,3},{3,2},{4,5},{5,4},{6,7},{7,6},{8,9},{9,8},{10,11... | collective-permute-start | bytes 811016 | tf_op jit(solution)/shard_map/ppermute | solution.py:29
  13.2 0.0 collective-permute-start.3
  13.2 1.2 %collective-permute-done.payload = f32[528,128]{1,0:T(8,128)S(1)} collective-permute-done((f32[528,128]{1,0:T(8,128)S(1)}, f32[528,128]{1,0:T(8,128)S(1)}, u32[]{:S(2)}, u32[]{:S(2)}) %collective-permute-start) | collective-permute-done | bytes 270368 | tf_op jit(solution)/shard_map/ppermute | solution.py:29
  14.4 0.0 collective-permute-start.4
  14.4 0.0 copy-done
  14.4 0.0 copy-done.2
  14.4 0.0 copy-done.3
  14.4 2.3 %shard_map.57.start = f32[1024,128]{1,0:T(8,128)S(1)} custom-call(s32[1]{0:T(128)} %bitcast.self_ref, f32[1024,128]{1,0:T(8,128)S(1)} %copy-done, s32[2,1024]{1,0:T(2,128)S(1)} %copy-done.2, f32[2,1024]{1,0:T(2,128)S(1)} %copy-done.3, f32[8,128]{1,0:T(8,128)S(1)} %get-tuple-element.44.spilled, f32[528,128]{1,0:T(8,128)S(1)} %collective-permute-done.payload), custom_call_target="tpu_custom_call" | custom-call | flops 10000000 | bytes 39062 | tf_op jit(solution)/shard_map/pallas_call | solution.py:406
  16.7 1.4 %shard_map.58 = (s32[1,1024]{1,0:T(1,128)S(1)}, bf16[80,1024]{1,0:T(8,128)(2,1)S(1)}, f32[32,128]{1,0:T(8,128)S(1)}) custom-call(s32[1]{0:T(128)} %bitcast.self_ref, s32[2,1024]{1,0:T(2,128)S(1)} %copy-done.2, f32[2,1024]{1,0:T(2,128)S(1)} %copy-done.3), custom_call_target="tpu_custom_call" | custom-call | flops 10000000 | bytes 39062 | tf_op jit(solution)/shard_map/pallas_call | solution.py:416
  18.1 0.0 collective-permute-done.1.p0
  18.1 0.0 collective-permute-done.2.p1
  18.1 0.0 copy-start.1
  18.2 1.6 %collective-permute-start.5 = (f32[8,128]{1,0:T(8,128)S(1)}, f32[8,128]{1,0:T(8,128)S(1)}, u32[]{:S(2)}, u32[]{:S(2)}) collective-permute-start(f32[8,128]{1,0:T(8,128)S(1)} %slice_add_fusion.1), channel_id=1, source_target_pairs={{0,1},{1,0},{2,3},{3,2},{4,5},{5,4},{6,7},{7,6},{8,9},{9,8},{10,11... | collective-permute-start | bytes 12296 | tf_op jit(solution)/shard_map/ppermute | solution.py:29
  19.8 1.7 %shard_map.59.start = f32[1024,128]{1,0:T(8,128)S(1)} custom-call(f32[1024,128]{1,0:T(8,128)S(1)} %shard_map.57.start, f32[536,128]{1,0:T(8,128)S(1)} %collective-permute-done.1.p0, f32[536,128]{1,0:T(8,128)S(1)} %collective-permute-done.2.p1), custom_call_target="tpu_custom_call" | custom-call | flops 10000000 | bytes 39062 | tf_op jit(solution)/shard_map/pallas_call | solution.py:430
  21.5 0.0 collective-permute-done.3.payload
  21.5 0.0 collective-permute-done.4.tiny_a
  21.5 0.0 collective-permute-done.5.tiny_b
  21.5 0.0 copy-done.1
  21.5 1.4 %shard_map.60 = f32[1024,128]{1,0:T(8,128)S(1)} custom-call(f32[1024,128]{1,0:T(8,128)S(1)} %shard_map.59.start, f32[528,128]{1,0:T(8,128)S(1)} %collective-permute-done.3.payload, f32[8,128]{1,0:T(8,128)S(1)} %collective-permute-done.4.tiny_a, f32[8,128]{1,0:T(8,128)S(1)} %collective-permute-done.5.tiny_b, f32[2,128,128]{2,1,0:T(8,128)S(1)} %copy-done.1), custom_call_target="tpu_custom_call" | custom-call | flops 10000000 | bytes 39062 | tf_op jit(solution)/shard_map/pallas_call | solution.py:431
  22.9 0.0 copy-start.4
  22.9 17.1 %all_to_all.10.x = f32[8,128,128]{2,1,0:T(8,128)S(1)} all-to-all(f32[8,128,128]{2,1,0:T(8,128)S(1)} %bitcast.8), channel_id=1, replica_groups=mesh['grp'=8,'tile'=32] {'grp'}, dimensions={0} | all-to-all | bytes 1048576 | tf_op jit(solution)/shard_map/all_to_all | solution.py:466
  40.1 0.0 copy-done.4
  40.1 0.4 shard_map.61
  40.5 12.1 %all_to_all.11 = f32[8,128,128]{2,1,0:T(8,128)S(1)} all-to-all(f32[8,128,128]{2,1,0:T(8,128)S(1)} %shard_map.61), channel_id=1, replica_groups=mesh['grp'=8,'tile'=32] {'grp'}, dimensions={0} | all-to-all | bytes 1048576 | tf_op jit(solution)/shard_map/all_to_all | solution.py:468
  52.6 0.8 %shard_map.62 = (f32[536,128]{1,0:T(8,128)S(1)}, f32[536,128]{1,0:T(8,128)S(1)}, bf16[1024,256]{1,0:T(8,128)(2,1)S(1)}, f32[40,128]{1,0:T(8,128)S(1)}) custom-call(s32[1]{0:T(128)} %bitcast.self_ref, f32[1024,128]{1,0:T(8,128)S(1)} %bitcast.6, s32[1,1024]{1,0:T(1,128)S(1)} %get-tuple-element.60.keys, bf16[80,1024]{1,0:T(8,128)(2,1)S(1)} %get-tuple-element.61.spills, ...), custom_call_target="tpu_custom_call" | custom-call | tf_op jit(solution)/shard_map/pallas_call | solution.py:471
  53.4 2.5 %collective-permute-start.7 = (f32[536,128]{1,0:T(8,128)S(1)}, f32[536,128]{1,0:T(8,128)S(1)}, u32[]{:S(2)}, u32[]{:S(2)}) collective-permute-start(f32[536,128]{1,0:T(8,128)S(1)} %get-tuple-element.67), channel_id=1, source_target_pairs={{0,2},{1,3},{2,0},{3,1},{4,6},{5,7},{6,4},{7,5},{8,10},{9,11},{10,... | collective-permute-start | bytes 823304 | tf_op jit(solution)/shard_map/ppermute | solution.py:29
  55.9 0.7 collective-permute-start.8
  56.6 0.7 shard_map.63
  57.3 3.3 %collective-permute-start.6 = (f32[528,128]{1,0:T(8,128)S(1)}, f32[528,128]{1,0:T(8,128)S(1)}, u32[]{:S(2)}, u32[]{:S(2)}) collective-permute-start(f32[528,128]{1,0:T(8,128)S(1)} %get-tuple-element.66), channel_id=1, source_target_pairs={{0,1},{1,0},{2,3},{3,2},{4,5},{5,4},{6,7},{7,6},{8,9},{9,8},{10,11... | collective-permute-start | bytes 811016 | tf_op jit(solution)/shard_map/ppermute | solution.py:29
  60.6 0.0 collective-permute-start.9
  60.6 1.2 %collective-permute-done.6.payload = f32[528,128]{1,0:T(8,128)S(1)} collective-permute-done((f32[528,128]{1,0:T(8,128)S(1)}, f32[528,128]{1,0:T(8,128)S(1)}, u32[]{:S(2)}, u32[]{:S(2)}) %collective-permute-start.6) | collective-permute-done | bytes 270368 | tf_op jit(solution)/shard_map/ppermute | solution.py:29
  61.8 0.6 collective-permute-start.10
  62.4 2.3 %shard_map.64.start = f32[1024,128]{1,0:T(8,128)S(1)} custom-call(s32[1]{0:T(128)} %bitcast.self_ref, f32[1024,128]{1,0:T(8,128)S(1)} %bitcast.7, s32[2,1024]{1,0:T(2,128)S(1)} %copy-done.2, f32[2,1024]{1,0:T(2,128)S(1)} %copy-done.3, f32[8,128]{1,0:T(8,128)S(1)} %get-tuple-element.65.spilled, f32[528,128]{1,0:T(8,128)S(1)} %collective-permute-done.6.payload), custom_call_target="tpu_custom_call" | custom-call | flops 10000000 | bytes 39062 | tf_op jit(solution)/shard_map/pallas_call | solution.py:406
  64.7 0.0 collective-permute-done.7.p0
  64.7 0.0 collective-permute-done.8.p1
  64.8 4.2 %collective-permute-start.11 = (f32[8,128]{1,0:T(8,128)S(1)}, f32[8,128]{1,0:T(8,128)S(1)}, u32[]{:S(2)}, u32[]{:S(2)}) collective-permute-start(f32[8,128]{1,0:T(8,128)S(1)} %slice_add_fusion), channel_id=1, source_target_pairs={{0,1},{1,0},{2,3},{3,2},{4,5},{5,4},{6,7},{7,6},{8,9},{9,8},{10,11... | collective-permute-start | bytes 12296 | tf_op jit(solution)/shard_map/ppermute | solution.py:29
  69.0 1.7 %shard_map.65.start = f32[1024,128]{1,0:T(8,128)S(1)} custom-call(f32[1024,128]{1,0:T(8,128)S(1)} %shard_map.64.start, f32[536,128]{1,0:T(8,128)S(1)} %collective-permute-done.7.p0, f32[536,128]{1,0:T(8,128)S(1)} %collective-permute-done.8.p1), custom_call_target="tpu_custom_call" | custom-call | flops 10000000 | bytes 39062 | tf_op jit(solution)/shard_map/pallas_call | solution.py:430
  70.7 0.0 collective-permute-done.9.payload
  70.7 0.0 collective-permute-done.10.tiny_a
  70.7 0.0 collective-permute-done.11.tiny_b
  70.7 2.2 %shard_map.66 = f32[1024,128]{1,0:T(8,128)} custom-call(f32[1024,128]{1,0:T(8,128)S(1)} %shard_map.65.start, f32[528,128]{1,0:T(8,128)S(1)} %collective-permute-done.9.payload, f32[8,128]{1,0:T(8,128)S(1)} %collective-permute-done.10.tiny_a, f32[8,128]{1,0:T(8,128)S(1)} %collective-permute-done.11.tiny_b, f32[2,128,128]{2,1,0:T(8,128)S(1)} %copy-done.1), custom_call_target="tpu_custom_call" | custom-call | flops 10000000 | bytes 39062 | tf_op jit(solution)/shard_map/pallas_call | solution.py:431
  (2 shorter events, 0.0 us)
Async XLA Ops:
  2.4 15.7 %collective-permute-start.1 = (f32[536,128]{1,0:T(8,128)S(1)}, f32[536,128]{1,0:T(8,128)S(1)}, u32[]{:S(2)}, u32[]{:S(2)}) collective-permute-start(f32[536,128]{1,0:T(8,128)S(1)} %get-tuple-element.52), channel_id=1, source_target_pairs={{0,2},{1,3},{2,0},{3,1},{4,6},{5,7},{6,4},{7,5},{8,10},{9,11},{10,... | collective-permute-start | bytes 823304 | tf_op jit(solution)/shard_map/ppermute | solution.py:29
  5.0 13.1 %collective-permute-start.2 = (f32[536,128]{1,0:T(8,128)S(1)}, f32[536,128]{1,0:T(8,128)S(1)}, u32[]{:S(2)}, u32[]{:S(2)}) collective-permute-start(f32[536,128]{1,0:T(8,128)S(1)} %get-tuple-element.53), channel_id=1, source_target_pairs={{0,30},{1,31},{2,4},{3,5},{4,2},{5,3},{6,8},{7,9},{8,6},{9,7},{10,... | collective-permute-start | bytes 823304 | tf_op jit(solution)/shard_map/ppermute | solution.py:29
  10.7 3.7 %copy-start = (f32[1024,128]{1,0:T(8,128)S(1)}, f32[1024,128]{1,0:T(8,128)}, u32[]{:S(2)}) copy-start(f32[1024,128]{1,0:T(8,128)} %field.1) | copy-start | bytes 1572868
  10.7 3.7 %copy-start.2 = (s32[2,1024]{1,0:T(2,128)S(1)}, s32[2,1024]{1,0:T(2,128)}, u32[]{:S(2)}) copy-start(s32[2,1024]{1,0:T(2,128)} %departure.5) | copy-start | bytes 24580
  10.7 3.7 %copy-start.3 = (f32[2,1024]{1,0:T(2,128)S(1)}, f32[2,1024]{1,0:T(2,128)}, u32[]{:S(2)}) copy-start(f32[2,1024]{1,0:T(2,128)} %fraction.5) | copy-start | bytes 24580
  11.9 2.5 %collective-permute-start = (f32[528,128]{1,0:T(8,128)S(1)}, f32[528,128]{1,0:T(8,128)S(1)}, u32[]{:S(2)}, u32[]{:S(2)}) collective-permute-start(f32[528,128]{1,0:T(8,128)S(1)} %get-tuple-element.45), channel_id=1, source_target_pairs={{0,1},{1,0},{2,3},{3,2},{4,5},{5,4},{6,7},{7,6},{8,9},{9,8},{10,11... | collective-permute-start | bytes 811016 | tf_op jit(solution)/shard_map/ppermute | solution.py:29
  13.2 8.3 %collective-permute-start.3 = (f32[528,128]{1,0:T(8,128)S(1)}, f32[528,128]{1,0:T(8,128)S(1)}, u32[]{:S(2)}, u32[]{:S(2)}) collective-permute-start(f32[528,128]{1,0:T(8,128)S(1)} %get-tuple-element.57), channel_id=1, source_target_pairs={{0,31},{1,2},{2,1},{3,4},{4,3},{5,6},{6,5},{7,8},{8,7},{9,10},{10,... | collective-permute-start | bytes 811016 | tf_op jit(solution)/shard_map/ppermute | solution.py:29
  14.4 7.1 %collective-permute-start.4 = (f32[8,128]{1,0:T(8,128)S(1)}, f32[8,128]{1,0:T(8,128)S(1)}, u32[]{:S(2)}, u32[]{:S(2)}) collective-permute-start(f32[8,128]{1,0:T(8,128)S(1)} %get-tuple-element.59), channel_id=1, source_target_pairs={{0,29},{1,4},{2,31},{3,6},{4,1},{5,8},{6,3},{7,10},{8,5},{9,12},{1... | collective-permute-start | bytes 12296 | tf_op jit(solution)/shard_map/ppermute | solution.py:29
  18.1 3.4 %copy-start.1 = (f32[2,128,128]{2,1,0:T(8,128)S(1)}, f32[2,128,128]{2,1,0:T(8,128)}, u32[]{:S(2)}) copy-start(f32[2,128,128]{2,1,0:T(8,128)} %level_map.3) | copy-start | bytes 393220
  18.2 3.4 %collective-permute-start.5 = (f32[8,128]{1,0:T(8,128)S(1)}, f32[8,128]{1,0:T(8,128)S(1)}, u32[]{:S(2)}, u32[]{:S(2)}) collective-permute-start(f32[8,128]{1,0:T(8,128)S(1)} %slice_add_fusion.1), channel_id=1, source_target_pairs={{0,1},{1,0},{2,3},{3,2},{4,5},{5,4},{6,7},{7,6},{8,9},{9,8},{10,11... | collective-permute-start | bytes 12296 | tf_op jit(solution)/shard_map/ppermute | solution.py:29
  22.9 17.2 %copy-start.4 = (f32[128,8,8]{0,2,1:T(8,128)S(1)}, f32[128,8,8]{0,2,1:T(8,128)}, u32[]{:S(2)}) copy-start(f32[128,8,8]{0,2,1:T(8,128)} %param.9) | copy-start | bytes 98308
  53.4 11.3 %collective-permute-start.7 = (f32[536,128]{1,0:T(8,128)S(1)}, f32[536,128]{1,0:T(8,128)S(1)}, u32[]{:S(2)}, u32[]{:S(2)}) collective-permute-start(f32[536,128]{1,0:T(8,128)S(1)} %get-tuple-element.67), channel_id=1, source_target_pairs={{0,2},{1,3},{2,0},{3,1},{4,6},{5,7},{6,4},{7,5},{8,10},{9,11},{10,... | collective-permute-start | bytes 823304 | tf_op jit(solution)/shard_map/ppermute | solution.py:29
  55.9 8.8 %collective-permute-start.8 = (f32[536,128]{1,0:T(8,128)S(1)}, f32[536,128]{1,0:T(8,128)S(1)}, u32[]{:S(2)}, u32[]{:S(2)}) collective-permute-start(f32[536,128]{1,0:T(8,128)S(1)} %get-tuple-element.68), channel_id=1, source_target_pairs={{0,30},{1,31},{2,4},{3,5},{4,2},{5,3},{6,8},{7,9},{8,6},{9,7},{10,... | collective-permute-start | bytes 823304 | tf_op jit(solution)/shard_map/ppermute | solution.py:29
  57.3 4.5 %collective-permute-start.6 = (f32[528,128]{1,0:T(8,128)S(1)}, f32[528,128]{1,0:T(8,128)S(1)}, u32[]{:S(2)}, u32[]{:S(2)}) collective-permute-start(f32[528,128]{1,0:T(8,128)S(1)} %get-tuple-element.66), channel_id=1, source_target_pairs={{0,1},{1,0},{2,3},{3,2},{4,5},{5,4},{6,7},{7,6},{8,9},{9,8},{10,11... | collective-permute-start | bytes 811016 | tf_op jit(solution)/shard_map/ppermute | solution.py:29
  60.6 10.0 %collective-permute-start.9 = (f32[528,128]{1,0:T(8,128)S(1)}, f32[528,128]{1,0:T(8,128)S(1)}, u32[]{:S(2)}, u32[]{:S(2)}) collective-permute-start(f32[528,128]{1,0:T(8,128)S(1)} %get-tuple-element.72), channel_id=1, source_target_pairs={{0,31},{1,2},{2,1},{3,4},{4,3},{5,6},{6,5},{7,8},{8,7},{9,10},{10,... | collective-permute-start | bytes 811016 | tf_op jit(solution)/shard_map/ppermute | solution.py:29
  61.8 8.9 %collective-permute-start.10 = (f32[8,128]{1,0:T(8,128)S(1)}, f32[8,128]{1,0:T(8,128)S(1)}, u32[]{:S(2)}, u32[]{:S(2)}) collective-permute-start(f32[8,128]{1,0:T(8,128)S(1)} %get-tuple-element.74), channel_id=1, source_target_pairs={{0,29},{1,4},{2,31},{3,6},{4,1},{5,8},{6,3},{7,10},{8,5},{9,12},{1... | collective-permute-start | bytes 12296 | tf_op jit(solution)/shard_map/ppermute | solution.py:29
  64.8 5.9 %collective-permute-start.11 = (f32[8,128]{1,0:T(8,128)S(1)}, f32[8,128]{1,0:T(8,128)S(1)}, u32[]{:S(2)}, u32[]{:S(2)}) collective-permute-start(f32[8,128]{1,0:T(8,128)S(1)} %slice_add_fusion), channel_id=1, source_target_pairs={{0,1},{1,0},{2,3},{3,2},{4,5},{5,4},{6,7},{7,6},{8,9},{9,8},{10,11... | collective-permute-start | bytes 12296 | tf_op jit(solution)/shard_map/ppermute | solution.py:29

commit v9 on v8

--- a/solution.py
+++ b/solution.py
@@ -422,7 +422,7 @@
             ],
             [SM, VM, VM],
             (),
-            10000000,
+            300000000,
         )(after[0], departure, fraction)
         own, index = lax.optimization_barrier((after[1], index))
     own, *far = lax.optimization_barrier((own, *far))

time: 73.3 us -> 71.9 us (0.981)
  blocking collectives: 29.3 us -> 27.3 us
  waiting for transfers between devices: 2.4 us -> 4.13 us
  starting transfers between devices: 22.6 us -> 21.5 us
    ppermute x12, waiting for transfers between devices: 2.4 us -> 4.13 us  [swapped(): lax.ppermute(x, 'tile', [(i, (i + signs(i)[which]) % length) for i in ran...]
    all_to_all x1, blocking collectives: 17.1 us -> 15.7 us  [body(): lax.all_to_all(second.reshape(groups, COLS // groups, LEV), 'grp', 0, 0)]
    ppermute x12, starting transfers between devices: 22.6 us -> 21.5 us  [swapped(): lax.ppermute(x, 'tile', [(i, (i + signs(i)[which]) % length) for i in ran...]
  transfers between devices with their start and end apart: 12 -> 12, of which waited for: 2 -> 2; matrix products, arithmetic and copies ran while one was open for 0% -> 0% of each run, Pallas kernels for 15% -> 14%
where the time goes in v9:
time: 71.9 us; the launch traced here: 71.7 us
  blocking collectives  27.3 us (38%)
  starting transfers between devices  21.5 us (30%)
  Pallas kernels  18.4 us (26%)
  waiting for transfers between devices  4.13 us (6%)
    ppermute x12, starting transfers between devices, swapped(): lax.ppermute(x, 'tile', [(i, (i + signs(i)[which]) % length) for i in ran...  21.5 us
    all_to_all x1, blocking collectives, body(): lax.all_to_all(second.reshape(groups, COLS // groups, LEV), 'grp', 0, 0)  15.7 us
    all_to_all x1, blocking collectives, body(): coupled = lax.all_to_all(mixed, 'grp', 0, 0).reshape(COLS, LEV)  11.6 us
    pallas_call x2, Pallas kernels, transported(): call(functools.partial(own_kernel, step, tile_count), total, [SM] + [VM]...  4.58 us
    ppermute x12, waiting for transfers between devices, swapped(): lax.ppermute(x, 'tile', [(i, (i + signs(i)[which]) % length) for i in ran...  4.13 us
    pallas_call x2, Pallas kernels, transported(): call(functools.partial(last_kernel, step), total, [VM] * 5, [one, pltpu.V...  3.53 us
    pallas_call x2, Pallas kernels, transported(): call(middle_kernel, total, [VM] * 3, [pltpu.VMEM((2, CAP, 2 * LEV), BF)],...  3.36 us
    pallas_call x1, Pallas kernels, body(): call(functools.partial(first_far_kernel, tile_count), outputs, [SM, HBM,...  2.42 us
  transfers between devices with their start and end apart: 12, of which 2 were waited for; matrix products, arithmetic and copies ran while one was open for 0% of the time, Pallas kernels for 14%

profile of v9, /device:TPU:1, one launch (start us, length us, event | category | flops | bytes accessed | tf_op | source)
XLA Modules:
  0.0 71.7 jit_solution(5956254600607599610)
XLA Ops:
  0.0 2.4 %shard_map.55 = (f32[536,128]{1,0:T(8,128)S(1)}, f32[536,128]{1,0:T(8,128)S(1)}, bf16[1024,256]{1,0:T(8,128)(2,1)S(1)}, f32[40,128]{1,0:T(8,128)S(1)}, s32[1,102...) custom-call(s32[1]{0:T(128)} %bitcast.self_ref, f32[1024,128]{1,0:T(8,128)} %field.1, s32[2,1024]{1,0:T(2,128)} %departure.5, ...), custom_call_target="tpu_custom_call" | custom-call | tf_op jit(solution)/shard_map/pallas_call | solution.py:458
  2.4 0.0 copy-start
  2.4 0.0 copy-start.3
  2.5 1.2 %shard_map.56 = (f32[528,128]{1,0:T(8,128)S(1)}, f32[528,128]{1,0:T(8,128)S(1)}, f32[8,128]{1,0:T(8,128)S(1)}, f32[8,128]{1,0:T(8,128)S(1)}) custom-call(s32[1]{0:T(128)} %bitcast.self_ref, bf16[1024,256]{1,0:T(8,128)(2,1)S(1)} %get-tuple-element.40.both, f32[40,128]{1,0:T(8,128)S(1)} %get-tuple-element.41.spilled, s32[1,1024]{1,0:T(1,128)S(1)} %get-tuple-element.42.keys, ...), custom_call_target="tpu_custom_call" | custom-call | flops 1000000000 | bytes 3906250 | tf_op jit(solution)/shard_map/pallas_call | solution.py:396
  3.7 0.0 copy-start.2
  3.7 3.3 %collective-permute-start = (f32[528,128]{1,0:T(8,128)S(1)}, f32[528,128]{1,0:T(8,128)S(1)}, u32[]{:S(2)}, u32[]{:S(2)}) collective-permute-start(f32[528,128]{1,0:T(8,128)S(1)} %get-tuple-element.45), channel_id=1, source_target_pairs={{0,1},{1,0},{2,3},{3,2},{4,5},{5,4},{6,7},{7,6},{8,9},{9,8},{10,11... | collective-permute-start | bytes 811016 | tf_op jit(solution)/shard_map/ppermute | solution.py:29
  7.0 0.0 collective-permute-start.1
  7.0 5.6 %collective-permute-start.2 = (f32[536,128]{1,0:T(8,128)S(1)}, f32[536,128]{1,0:T(8,128)S(1)}, u32[]{:S(2)}, u32[]{:S(2)}) collective-permute-start(f32[536,128]{1,0:T(8,128)S(1)} %get-tuple-element.53), channel_id=1, source_target_pairs={{0,30},{1,31},{2,4},{3,5},{4,2},{5,3},{6,8},{7,9},{8,6},{9,7},{10,... | collective-permute-start | bytes 823304 | tf_op jit(solution)/shard_map/ppermute | solution.py:29
  12.6 0.0 collective-permute-start.3
  12.6 0.0 collective-permute-done.payload
  12.6 0.0 collective-permute-start.4
  12.7 0.0 copy-done
  12.7 0.0 copy-done.3
  12.7 0.0 copy-done.2
  12.7 2.3 %shard_map.57.start = f32[1024,128]{1,0:T(8,128)S(1)} custom-call(s32[1]{0:T(128)} %bitcast.self_ref, f32[1024,128]{1,0:T(8,128)S(1)} %copy-done, s32[2,1024]{1,0:T(2,128)S(1)} %copy-done.2, f32[2,1024]{1,0:T(2,128)S(1)} %copy-done.3, f32[8,128]{1,0:T(8,128)S(1)} %get-tuple-element.44.spilled, f32[528,128]{1,0:T(8,128)S(1)} %collective-permute-done.payload), custom_call_target="tpu_custom_call" | custom-call | flops 10000000 | bytes 39062 | tf_op jit(solution)/shard_map/pallas_call | solution.py:406
  15.0 1.4 %shard_map.58 = (s32[1,1024]{1,0:T(1,128)S(1)}, bf16[80,1024]{1,0:T(8,128)(2,1)S(1)}, f32[32,128]{1,0:T(8,128)S(1)}) custom-call(s32[1]{0:T(128)} %bitcast.self_ref, s32[2,1024]{1,0:T(2,128)S(1)} %copy-done.2, f32[2,1024]{1,0:T(2,128)S(1)} %copy-done.3), custom_call_target="tpu_custom_call" | custom-call | flops 300000000 | bytes 1171875 | tf_op jit(solution)/shard_map/pallas_call | solution.py:416
  16.4 0.0 collective-permute-done.1.p0
  16.4 2.9 %collective-permute-done.2.p1 = f32[536,128]{1,0:T(8,128)S(1)} collective-permute-done((f32[536,128]{1,0:T(8,128)S(1)}, f32[536,128]{1,0:T(8,128)S(1)}, u32[]{:S(2)}, u32[]{:S(2)}) %collective-permute-start.2) | collective-permute-done | bytes 274464 | tf_op jit(solution)/shard_map/ppermute | solution.py:29
  19.3 0.0 copy-start.1
  19.3 1.3 %collective-permute-start.5 = (f32[8,128]{1,0:T(8,128)S(1)}, f32[8,128]{1,0:T(8,128)S(1)}, u32[]{:S(2)}, u32[]{:S(2)}) collective-permute-start(f32[8,128]{1,0:T(8,128)S(1)} %slice_add_fusion.1), channel_id=1, source_target_pairs={{0,1},{1,0},{2,3},{3,2},{4,5},{5,4},{6,7},{7,6},{8,9},{9,8},{10,11... | collective-permute-start | bytes 12296 | tf_op jit(solution)/shard_map/ppermute | solution.py:29
  20.6 1.7 %shard_map.59.start = f32[1024,128]{1,0:T(8,128)S(1)} custom-call(f32[1024,128]{1,0:T(8,128)S(1)} %shard_map.57.start, f32[536,128]{1,0:T(8,128)S(1)} %collective-permute-done.1.p0, f32[536,128]{1,0:T(8,128)S(1)} %collective-permute-done.2.p1), custom_call_target="tpu_custom_call" | custom-call | flops 10000000 | bytes 39062 | tf_op jit(solution)/shard_map/pallas_call | solution.py:430
  22.3 0.0 collective-permute-done.3.payload
  22.3 0.0 collective-permute-done.4.tiny_a
  22.3 0.0 collective-permute-done.5.tiny_b
  22.4 0.0 copy-done.1
  22.4 1.4 %shard_map.60 = f32[1024,128]{1,0:T(8,128)S(1)} custom-call(f32[1024,128]{1,0:T(8,128)S(1)} %shard_map.59.start, f32[528,128]{1,0:T(8,128)S(1)} %collective-permute-done.3.payload, f32[8,128]{1,0:T(8,128)S(1)} %collective-permute-done.4.tiny_a, f32[8,128]{1,0:T(8,128)S(1)} %collective-permute-done.5.tiny_b, f32[2,128,128]{2,1,0:T(8,128)S(1)} %copy-done.1), custom_call_target="tpu_custom_call" | custom-call | flops 10000000 | bytes 39062 | tf_op jit(solution)/shard_map/pallas_call | solution.py:431
  23.7 0.0 copy-start.4
  23.8 15.7 %all_to_all.10.x = f32[8,128,128]{2,1,0:T(8,128)S(1)} all-to-all(f32[8,128,128]{2,1,0:T(8,128)S(1)} %bitcast.8), channel_id=1, replica_groups=mesh['grp'=8,'tile'=32] {'grp'}, dimensions={0} | all-to-all | bytes 1048576 | tf_op jit(solution)/shard_map/all_to_all | solution.py:466
  39.4 0.0 copy-done.4
  39.4 0.4 shard_map.61
  39.8 11.6 %all_to_all.11 = f32[8,128,128]{2,1,0:T(8,128)S(1)} all-to-all(f32[8,128,128]{2,1,0:T(8,128)S(1)} %shard_map.61), channel_id=1, replica_groups=mesh['grp'=8,'tile'=32] {'grp'}, dimensions={0} | all-to-all | bytes 1048576 | tf_op jit(solution)/shard_map/all_to_all | solution.py:468
  51.4 0.8 %shard_map.62 = (f32[536,128]{1,0:T(8,128)S(1)}, f32[536,128]{1,0:T(8,128)S(1)}, bf16[1024,256]{1,0:T(8,128)(2,1)S(1)}, f32[40,128]{1,0:T(8,128)S(1)}) custom-call(s32[1]{0:T(128)} %bitcast.self_ref, f32[1024,128]{1,0:T(8,128)S(1)} %bitcast.6, s32[1,1024]{1,0:T(1,128)S(1)} %get-tuple-element.60.keys, bf16[80,1024]{1,0:T(8,128)(2,1)S(1)} %get-tuple-element.61.spills, ...), custom_call_target="tpu_custom_call" | custom-call | tf_op jit(solution)/shard_map/pallas_call | solution.py:471
  52.2 3.6 %collective-permute-start.7 = (f32[536,128]{1,0:T(8,128)S(1)}, f32[536,128]{1,0:T(8,128)S(1)}, u32[]{:S(2)}, u32[]{:S(2)}) collective-permute-start(f32[536,128]{1,0:T(8,128)S(1)} %get-tuple-element.67), channel_id=1, source_target_pairs={{0,2},{1,3},{2,0},{3,1},{4,6},{5,7},{6,4},{7,5},{8,10},{9,11},{10,... | collective-permute-start | bytes 823304 | tf_op jit(solution)/shard_map/ppermute | solution.py:29
  55.9 3.5 %collective-permute-start.8 = (f32[536,128]{1,0:T(8,128)S(1)}, f32[536,128]{1,0:T(8,128)S(1)}, u32[]{:S(2)}, u32[]{:S(2)}) collective-permute-start(f32[536,128]{1,0:T(8,128)S(1)} %get-tuple-element.68), channel_id=1, source_target_pairs={{0,30},{1,31},{2,4},{3,5},{4,2},{5,3},{6,8},{7,9},{8,6},{9,7},{10,... | collective-permute-start | bytes 823304 | tf_op jit(solution)/shard_map/ppermute | solution.py:29
  59.4 0.7 shard_map.63
  60.1 1.8 %collective-permute-start.6 = (f32[528,128]{1,0:T(8,128)S(1)}, f32[528,128]{1,0:T(8,128)S(1)}, u32[]{:S(2)}, u32[]{:S(2)}) collective-permute-start(f32[528,128]{1,0:T(8,128)S(1)} %get-tuple-element.66), channel_id=1, source_target_pairs={{0,1},{1,0},{2,3},{3,2},{4,5},{5,4},{6,7},{7,6},{8,9},{9,8},{10,11... | collective-permute-start | bytes 811016 | tf_op jit(solution)/shard_map/ppermute | solution.py:29
  61.9 0.0 collective-permute-start.9
  61.9 1.2 %collective-permute-done.6.payload = f32[528,128]{1,0:T(8,128)S(1)} collective-permute-done((f32[528,128]{1,0:T(8,128)S(1)}, f32[528,128]{1,0:T(8,128)S(1)}, u32[]{:S(2)}, u32[]{:S(2)}) %collective-permute-start.6) | collective-permute-done | bytes 270368 | tf_op jit(solution)/shard_map/ppermute | solution.py:29
  63.1 0.0 collective-permute-start.10
  63.1 2.3 %shard_map.64.start = f32[1024,128]{1,0:T(8,128)S(1)} custom-call(s32[1]{0:T(128)} %bitcast.self_ref, f32[1024,128]{1,0:T(8,128)S(1)} %bitcast.7, s32[2,1024]{1,0:T(2,128)S(1)} %copy-done.2, f32[2,1024]{1,0:T(2,128)S(1)} %copy-done.3, f32[8,128]{1,0:T(8,128)S(1)} %get-tuple-element.65.spilled, f32[528,128]{1,0:T(8,128)S(1)} %collective-permute-done.6.payload), custom_call_target="tpu_custom_call" | custom-call | flops 10000000 | bytes 39062 | tf_op jit(solution)/shard_map/pallas_call | solution.py:406
  65.4 0.0 collective-permute-done.7.p0
  65.4 0.0 collective-permute-done.8.p1
  65.4 2.2 %collective-permute-start.11 = (f32[8,128]{1,0:T(8,128)S(1)}, f32[8,128]{1,0:T(8,128)S(1)}, u32[]{:S(2)}, u32[]{:S(2)}) collective-permute-start(f32[8,128]{1,0:T(8,128)S(1)} %slice_add_fusion), channel_id=1, source_target_pairs={{0,1},{1,0},{2,3},{3,2},{4,5},{5,4},{6,7},{7,6},{8,9},{9,8},{10,11... | collective-permute-start | bytes 12296 | tf_op jit(solution)/shard_map/ppermute | solution.py:29
  67.6 1.7 %shard_map.65.start = f32[1024,128]{1,0:T(8,128)S(1)} custom-call(f32[1024,128]{1,0:T(8,128)S(1)} %shard_map.64.start, f32[536,128]{1,0:T(8,128)S(1)} %collective-permute-done.7.p0, f32[536,128]{1,0:T(8,128)S(1)} %collective-permute-done.8.p1), custom_call_target="tpu_custom_call" | custom-call | flops 10000000 | bytes 39062 | tf_op jit(solution)/shard_map/pallas_call | solution.py:430
  69.3 0.0 collective-permute-done.9.payload
  69.3 0.0 collective-permute-done.10.tiny_a
  69.3 0.0 collective-permute-done.11.tiny_b
  69.3 2.2 %shard_map.66 = f32[1024,128]{1,0:T(8,128)} custom-call(f32[1024,128]{1,0:T(8,128)S(1)} %shard_map.65.start, f32[528,128]{1,0:T(8,128)S(1)} %collective-permute-done.9.payload, f32[8,128]{1,0:T(8,128)S(1)} %collective-permute-done.10.tiny_a, f32[8,128]{1,0:T(8,128)S(1)} %collective-permute-done.11.tiny_b, f32[2,128,128]{2,1,0:T(8,128)S(1)} %copy-done.1), custom_call_target="tpu_custom_call" | custom-call | flops 10000000 | bytes 39062 | tf_op jit(solution)/shard_map/pallas_call | solution.py:431
  (2 shorter events, 0.0 us)
Async XLA Ops:
  2.4 10.2 %copy-start = (f32[1024,128]{1,0:T(8,128)S(1)}, f32[1024,128]{1,0:T(8,128)}, u32[]{:S(2)}) copy-start(f32[1024,128]{1,0:T(8,128)} %field.1) | copy-start | bytes 1572868
  2.4 10.2 %copy-start.3 = (f32[2,1024]{1,0:T(2,128)S(1)}, f32[2,1024]{1,0:T(2,128)}, u32[]{:S(2)}) copy-start(f32[2,1024]{1,0:T(2,128)} %fraction.5) | copy-start | bytes 24580
  3.7 9.0 %copy-start.2 = (s32[2,1024]{1,0:T(2,128)S(1)}, s32[2,1024]{1,0:T(2,128)}, u32[]{:S(2)}) copy-start(s32[2,1024]{1,0:T(2,128)} %departure.5) | copy-start | bytes 24580
  3.7 8.9 %collective-permute-start = (f32[528,128]{1,0:T(8,128)S(1)}, f32[528,128]{1,0:T(8,128)S(1)}, u32[]{:S(2)}, u32[]{:S(2)}) collective-permute-start(f32[528,128]{1,0:T(8,128)S(1)} %get-tuple-element.45), channel_id=1, source_target_pairs={{0,1},{1,0},{2,3},{3,2},{4,5},{5,4},{6,7},{7,6},{8,9},{9,8},{10,11... | collective-permute-start | bytes 811016 | tf_op jit(solution)/shard_map/ppermute | solution.py:29
  7.0 9.3 %collective-permute-start.1 = (f32[536,128]{1,0:T(8,128)S(1)}, f32[536,128]{1,0:T(8,128)S(1)}, u32[]{:S(2)}, u32[]{:S(2)}) collective-permute-start(f32[536,128]{1,0:T(8,128)S(1)} %get-tuple-element.52), channel_id=1, source_target_pairs={{0,2},{1,3},{2,0},{3,1},{4,6},{5,7},{6,4},{7,5},{8,10},{9,11},{10,... | collective-permute-start | bytes 823304 | tf_op jit(solution)/shard_map/ppermute | solution.py:29
  7.0 12.2 %collective-permute-start.2 = (f32[536,128]{1,0:T(8,128)S(1)}, f32[536,128]{1,0:T(8,128)S(1)}, u32[]{:S(2)}, u32[]{:S(2)}) collective-permute-start(f32[536,128]{1,0:T(8,128)S(1)} %get-tuple-element.53), channel_id=1, source_target_pairs={{0,30},{1,31},{2,4},{3,5},{4,2},{5,3},{6,8},{7,9},{8,6},{9,7},{10,... | collective-permute-start | bytes 823304 | tf_op jit(solution)/shard_map/ppermute | solution.py:29
  12.6 9.7 %collective-permute-start.3 = (f32[528,128]{1,0:T(8,128)S(1)}, f32[528,128]{1,0:T(8,128)S(1)}, u32[]{:S(2)}, u32[]{:S(2)}) collective-permute-start(f32[528,128]{1,0:T(8,128)S(1)} %get-tuple-element.57), channel_id=1, source_target_pairs={{0,31},{1,2},{2,1},{3,4},{4,3},{5,6},{6,5},{7,8},{8,7},{9,10},{10,... | collective-permute-start | bytes 811016 | tf_op jit(solution)/shard_map/ppermute | solution.py:29
  12.6 9.7 %collective-permute-start.4 = (f32[8,128]{1,0:T(8,128)S(1)}, f32[8,128]{1,0:T(8,128)S(1)}, u32[]{:S(2)}, u32[]{:S(2)}) collective-permute-start(f32[8,128]{1,0:T(8,128)S(1)} %get-tuple-element.59), channel_id=1, source_target_pairs={{0,29},{1,4},{2,31},{3,6},{4,1},{5,8},{6,3},{7,10},{8,5},{9,12},{1... | collective-permute-start | bytes 12296 | tf_op jit(solution)/shard_map/ppermute | solution.py:29
  19.3 3.1 %copy-start.1 = (f32[2,128,128]{2,1,0:T(8,128)S(1)}, f32[2,128,128]{2,1,0:T(8,128)}, u32[]{:S(2)}) copy-start(f32[2,128,128]{2,1,0:T(8,128)} %level_map.3) | copy-start | bytes 393220
  19.3 3.1 %collective-permute-start.5 = (f32[8,128]{1,0:T(8,128)S(1)}, f32[8,128]{1,0:T(8,128)S(1)}, u32[]{:S(2)}, u32[]{:S(2)}) collective-permute-start(f32[8,128]{1,0:T(8,128)S(1)} %slice_add_fusion.1), channel_id=1, source_target_pairs={{0,1},{1,0},{2,3},{3,2},{4,5},{5,4},{6,7},{7,6},{8,9},{9,8},{10,11... | collective-permute-start | bytes 12296 | tf_op jit(solution)/shard_map/ppermute | solution.py:29
  23.7 15.7 %copy-start.4 = (f32[128,8,8]{0,2,1:T(8,128)S(1)}, f32[128,8,8]{0,2,1:T(8,128)}, u32[]{:S(2)}) copy-start(f32[128,8,8]{0,2,1:T(8,128)} %param.9) | copy-start | bytes 98308
  52.2 13.2 %collective-permute-start.7 = (f32[536,128]{1,0:T(8,128)S(1)}, f32[536,128]{1,0:T(8,128)S(1)}, u32[]{:S(2)}, u32[]{:S(2)}) collective-permute-start(f32[536,128]{1,0:T(8,128)S(1)} %get-tuple-element.67), channel_id=1, source_target_pairs={{0,2},{1,3},{2,0},{3,1},{4,6},{5,7},{6,4},{7,5},{8,10},{9,11},{10,... | collective-permute-start | bytes 823304 | tf_op jit(solution)/shard_map/ppermute | solution.py:29
  55.9 9.6 %collective-permute-start.8 = (f32[536,128]{1,0:T(8,128)S(1)}, f32[536,128]{1,0:T(8,128)S(1)}, u32[]{:S(2)}, u32[]{:S(2)}) collective-permute-start(f32[536,128]{1,0:T(8,128)S(1)} %get-tuple-element.68), channel_id=1, source_target_pairs={{0,30},{1,31},{2,4},{3,5},{4,2},{5,3},{6,8},{7,9},{8,6},{9,7},{10,... | collective-permute-start | bytes 823304 | tf_op jit(solution)/shard_map/ppermute | solution.py:29
  60.1 3.0 %collective-permute-start.6 = (f32[528,128]{1,0:T(8,128)S(1)}, f32[528,128]{1,0:T(8,128)S(1)}, u32[]{:S(2)}, u32[]{:S(2)}) collective-permute-start(f32[528,128]{1,0:T(8,128)S(1)} %get-tuple-element.66), channel_id=1, source_target_pairs={{0,1},{1,0},{2,3},{3,2},{4,5},{5,4},{6,7},{7,6},{8,9},{9,8},{10,11... | collective-permute-start | bytes 811016 | tf_op jit(solution)/shard_map/ppermute | solution.py:29
  61.9 7.4 %collective-permute-start.9 = (f32[528,128]{1,0:T(8,128)S(1)}, f32[528,128]{1,0:T(8,128)S(1)}, u32[]{:S(2)}, u32[]{:S(2)}) collective-permute-start(f32[528,128]{1,0:T(8,128)S(1)} %get-tuple-element.72), channel_id=1, source_target_pairs={{0,31},{1,2},{2,1},{3,4},{4,3},{5,6},{6,5},{7,8},{8,7},{9,10},{10,... | collective-permute-start | bytes 811016 | tf_op jit(solution)/shard_map/ppermute | solution.py:29
  63.1 6.2 %collective-permute-start.10 = (f32[8,128]{1,0:T(8,128)S(1)}, f32[8,128]{1,0:T(8,128)S(1)}, u32[]{:S(2)}, u32[]{:S(2)}) collective-permute-start(f32[8,128]{1,0:T(8,128)S(1)} %get-tuple-element.74), channel_id=1, source_target_pairs={{0,29},{1,4},{2,31},{3,6},{4,1},{5,8},{6,3},{7,10},{8,5},{9,12},{1... | collective-permute-start | bytes 12296 | tf_op jit(solution)/shard_map/ppermute | solution.py:29
  65.4 3.9 %collective-permute-start.11 = (f32[8,128]{1,0:T(8,128)S(1)}, f32[8,128]{1,0:T(8,128)S(1)}, u32[]{:S(2)}, u32[]{:S(2)}) collective-permute-start(f32[8,128]{1,0:T(8,128)S(1)} %slice_add_fusion), channel_id=1, source_target_pairs={{0,1},{1,0},{2,3},{3,2},{4,5},{5,4},{6,7},{7,6},{8,9},{9,8},{10,11... | collective-permute-start | bytes 12296 | tf_op jit(solution)/shard_map/ppermute | solution.py:29

commit v10 on v9

--- a/solution.py
+++ b/solution.py
@@ -392,10 +392,27 @@
 
 
 def transported(step, packed, keys, meta, tile_count, tile_self, field, departure, fraction, level_map):
-    far = [swapped(packed[w], w) for w in (0, 1)]
-    near = call(functools.partial(near_pack_kernel, step), NEAR, [SM] + [VM] * 4, (), 1000000000)(
+    near = call(functools.partial(near_pack_kernel, step), NEAR, [SM] + [VM] * 4, (), 10**9)(
         tile_self, packed[2], packed[3], keys, meta
     )
+    index = None
+    ready = packed[:2]
+    if step == 1:
+        after = lax.optimization_barrier((tile_self, near))
+        index = call(
+            functools.partial(index_kernel, tile_count),
+            [
+                KEYS,
+                jax.ShapeDtypeStruct((2 * SPREAD_ROWS, COLS), BF),
+                jax.ShapeDtypeStruct((32, LEV), F32),
+            ],
+            [SM, VM, VM],
+            (),
+            3 * 10**8,
+        )(after[0], departure, fraction)
+        near = after[1]
+        ready, near, index = lax.optimization_barrier((ready, near, index))
+    far = [swapped(x, w) for w, x in enumerate(ready)]
     cross = swapped(near[0], 2)
     partner = swapped(near[1], 3)
     late = lax.optimization_barrier((near[2], partner))
@@ -410,21 +427,6 @@
         [pltpu.VMEM((COLS, 2 * LEV), BF), one],
         10000000,
     )(tile_self, field, departure, fraction, near[3], partner)
-    index = None
-    if step == 1:
-        after = lax.optimization_barrier((tile_self, own))
-        index = call(
-            functools.partial(index_kernel, tile_count),
-            [
-                KEYS,
-                jax.ShapeDtypeStruct((2 * SPREAD_ROWS, COLS), BF),
-                jax.ShapeDtypeStruct((32, LEV), F32),
-            ],
-            [SM, VM, VM],
-            (),
-            300000000,
-        )(after[0], departure, fraction)
-        own, index = lax.optimization_barrier((after[1], index))
     own, *far = lax.optimization_barrier((own, *far))
     handed = swapped(far[0][CAP + 16 :] + far[1][CAP + 16 :], 3)
     summed = call(middle_kernel, total, [VM] * 3, [pltpu.VMEM((2, CAP, 2 * LEV), BF)], work)(own, *far)

time: 71.9 us -> 72.4 us (level)
  blocking collectives: 27.3 us -> 29.3 us
  starting transfers between devices: 21.5 us -> 20.4 us
    all_to_all x1, blocking collectives: 11.6 us -> 13.3 us  [body(): coupled = lax.all_to_all(mixed, 'grp', 0, 0).reshape(COLS, LEV)]
    ppermute x12, starting transfers between devices: 21.5 us -> 20.4 us  [swapped(): lax.ppermute(x, 'tile', [(i, (i + signs(i)[which]) % length) for i in ran...]
  transfers between devices with their start and end apart: 12 -> 12, of which waited for: 2 -> 3; matrix products, arithmetic and copies ran while one was open for 0% -> 0% of each run, Pallas kernels for 14% -> 12%
where the time goes in v10:
time: 72.4 us; the launch traced here: 72.1 us
  blocking collectives  29.3 us (40%)
  starting transfers between devices  20.4 us (28%)
  Pallas kernels  18.4 us (25%)
  waiting for transfers between devices  3.61 us (5%)
    ppermute x12, starting transfers between devices, swapped(): lax.ppermute(x, 'tile', [(i, (i + signs(i)[which]) % length) for i in ran...  20.4 us
    all_to_all x1, blocking collectives, body(): lax.all_to_all(second.reshape(groups, COLS // groups, LEV), 'grp', 0, 0)  16 us
    all_to_all x1, blocking collectives, body(): coupled = lax.all_to_all(mixed, 'grp', 0, 0).reshape(COLS, LEV)  13.3 us
    pallas_call x2, Pallas kernels, transported(): call(functools.partial(own_kernel, step, tile_count), total, [SM] + [VM]...  4.58 us
    ppermute x12, waiting for transfers between devices, swapped(): lax.ppermute(x, 'tile', [(i, (i + signs(i)[which]) % length) for i in ran...  3.61 us
    pallas_call x2, Pallas kernels, transported(): call(functools.partial(last_kernel, step), total, [VM] * 5, [one, pltpu.V...  3.53 us
    pallas_call x2, Pallas kernels, transported(): call(middle_kernel, total, [VM] * 3, [pltpu.VMEM((2, CAP, 2 * LEV), BF)],...  3.37 us
    pallas_call x1, Pallas kernels, body(): call(functools.partial(first_far_kernel, tile_count), outputs, [SM, HBM,...  2.42 us
  transfers between devices with their start and end apart: 12, of which 3 were waited for; matrix products, arithmetic and copies ran while one was open for 0% of the time, Pallas kernels for 12%

profile of v10, /device:TPU:1, one launch (start us, length us, event | category | flops | bytes accessed | tf_op | source)
XLA Modules:
  0.0 72.1 jit_solution(3709528424543874058)
XLA Ops:
  0.0 2.4 %shard_map.55 = (f32[536,128]{1,0:T(8,128)S(1)}, f32[536,128]{1,0:T(8,128)S(1)}, bf16[1024,256]{1,0:T(8,128)(2,1)S(1)}, f32[40,128]{1,0:T(8,128)S(1)}, s32[1,102...) custom-call(s32[1]{0:T(128)} %bitcast.self_ref, f32[1024,128]{1,0:T(8,128)} %field.1, s32[2,1024]{1,0:T(2,128)} %departure.5, ...), custom_call_target="tpu_custom_call" | custom-call | tf_op jit(solution)/shard_map/pallas_call | solution.py:460
  2.4 0.0 copy-start.2
  2.4 0.0 copy-start.3
  2.5 1.2 %shard_map.56 = (f32[528,128]{1,0:T(8,128)S(1)}, f32[528,128]{1,0:T(8,128)S(1)}, f32[8,128]{1,0:T(8,128)S(1)}, f32[8,128]{1,0:T(8,128)S(1)}) custom-call(s32[1]{0:T(128)} %bitcast.self_ref, bf16[1024,256]{1,0:T(8,128)(2,1)S(1)} %get-tuple-element.50.both, f32[40,128]{1,0:T(8,128)S(1)} %get-tuple-element.51.spilled, s32[1,1024]{1,0:T(1,128)S(1)} %get-tuple-element.52.keys, ...), custom_call_target="tpu_custom_call" | custom-call | flops 1000000000 | bytes 3906250 | tf_op jit(solution)/shard_map/pallas_call | solution.py:395
  3.7 0.0 copy-done.2
  3.7 0.0 copy-done.3
  3.7 0.0 copy-start
  3.7 1.4 %shard_map.57 = (s32[1,1024]{1,0:T(1,128)S(1)}, bf16[80,1024]{1,0:T(8,128)(2,1)S(1)}, f32[32,128]{1,0:T(8,128)S(1)}) custom-call(s32[1]{0:T(128)} %bitcast.self_ref, s32[2,1024]{1,0:T(2,128)S(1)} %copy-done.2, f32[2,1024]{1,0:T(2,128)S(1)} %copy-done.3), custom_call_target="tpu_custom_call" | custom-call | flops 300000000 | bytes 1171875 | tf_op jit(solution)/shard_map/pallas_call | solution.py:402
  5.1 2.5 %collective-permute-start.1 = (f32[536,128]{1,0:T(8,128)S(1)}, f32[536,128]{1,0:T(8,128)S(1)}, u32[]{:S(2)}, u32[]{:S(2)}) collective-permute-start(f32[536,128]{1,0:T(8,128)S(1)} %get-tuple-element.68), channel_id=1, source_target_pairs={{0,2},{1,3},{2,0},{3,1},{4,6},{5,7},{6,4},{7,5},{8,10},{9,11},{10,... | collective-permute-start | bytes 823304 | tf_op jit(solution)/shard_map/ppermute | solution.py:29
  7.6 5.7 %collective-permute-start.2 = (f32[536,128]{1,0:T(8,128)S(1)}, f32[536,128]{1,0:T(8,128)S(1)}, u32[]{:S(2)}, u32[]{:S(2)}) collective-permute-start(f32[536,128]{1,0:T(8,128)S(1)} %get-tuple-element.69), channel_id=1, source_target_pairs={{0,30},{1,31},{2,4},{3,5},{4,2},{5,3},{6,8},{7,9},{8,6},{9,7},{10,... | collective-permute-start | bytes 823304 | tf_op jit(solution)/shard_map/ppermute | solution.py:29
  13.3 1.2 %collective-permute-start = (f32[528,128]{1,0:T(8,128)S(1)}, f32[528,128]{1,0:T(8,128)S(1)}, u32[]{:S(2)}, u32[]{:S(2)}) collective-permute-start(f32[528,128]{1,0:T(8,128)S(1)} %get-tuple-element.67), channel_id=1, source_target_pairs={{0,1},{1,0},{2,3},{3,2},{4,5},{5,4},{6,7},{7,6},{8,9},{9,8},{10,11... | collective-permute-start | bytes 811016 | tf_op jit(solution)/shard_map/ppermute | solution.py:29
  14.5 0.0 collective-permute-start.3
  14.5 1.2 %collective-permute-done.payload = f32[528,128]{1,0:T(8,128)S(1)} collective-permute-done((f32[528,128]{1,0:T(8,128)S(1)}, f32[528,128]{1,0:T(8,128)S(1)}, u32[]{:S(2)}, u32[]{:S(2)}) %collective-permute-start) | collective-permute-done | bytes 270368 | tf_op jit(solution)/shard_map/ppermute | solution.py:29
  15.7 0.0 collective-permute-start.4
  15.7 0.0 copy-done
  15.7 2.3 %shard_map.58.start = f32[1024,128]{1,0:T(8,128)S(1)} custom-call(s32[1]{0:T(128)} %bitcast.self_ref, f32[1024,128]{1,0:T(8,128)S(1)} %copy-done, s32[2,1024]{1,0:T(2,128)S(1)} %copy-done.2, f32[2,1024]{1,0:T(2,128)S(1)} %copy-done.3, f32[8,128]{1,0:T(8,128)S(1)} %get-tuple-element.66.spilled, f32[528,128]{1,0:T(8,128)S(1)} %collective-permute-done.payload), custom_call_target="tpu_custom_call" | custom-call | flops 10000000 | bytes 39062 | tf_op jit(solution)/shard_map/pallas_call | solution.py:423
  18.0 0.0 collective-permute-done.1.p0
  18.0 1.2 %collective-permute-done.2.p1 = f32[536,128]{1,0:T(8,128)S(1)} collective-permute-done((f32[536,128]{1,0:T(8,128)S(1)}, f32[536,128]{1,0:T(8,128)S(1)}, u32[]{:S(2)}, u32[]{:S(2)}) %collective-permute-start.2) | collective-permute-done | bytes 274464 | tf_op jit(solution)/shard_map/ppermute | solution.py:29
  19.3 0.0 copy-start.1
  19.3 2.7 %collective-permute-start.5 = (f32[8,128]{1,0:T(8,128)S(1)}, f32[8,128]{1,0:T(8,128)S(1)}, u32[]{:S(2)}, u32[]{:S(2)}) collective-permute-start(f32[8,128]{1,0:T(8,128)S(1)} %slice_add_fusion.1), channel_id=1, source_target_pairs={{0,1},{1,0},{2,3},{3,2},{4,5},{5,4},{6,7},{7,6},{8,9},{9,8},{10,11... | collective-permute-start | bytes 12296 | tf_op jit(solution)/shard_map/ppermute | solution.py:29
  22.0 1.7 %shard_map.59.start = f32[1024,128]{1,0:T(8,128)S(1)} custom-call(f32[1024,128]{1,0:T(8,128)S(1)} %shard_map.58.start, f32[536,128]{1,0:T(8,128)S(1)} %collective-permute-done.1.p0, f32[536,128]{1,0:T(8,128)S(1)} %collective-permute-done.2.p1), custom_call_target="tpu_custom_call" | custom-call | flops 10000000 | bytes 39062 | tf_op jit(solution)/shard_map/pallas_call | solution.py:432
  23.7 0.0 collective-permute-done.3.payload
  23.7 0.0 collective-permute-done.4.tiny_a
  23.7 0.0 collective-permute-done.5.tiny_b
  23.7 0.0 copy-done.1
  23.7 1.4 %shard_map.60 = f32[1024,128]{1,0:T(8,128)S(1)} custom-call(f32[1024,128]{1,0:T(8,128)S(1)} %shard_map.59.start, f32[528,128]{1,0:T(8,128)S(1)} %collective-permute-done.3.payload, f32[8,128]{1,0:T(8,128)S(1)} %collective-permute-done.4.tiny_a, f32[8,128]{1,0:T(8,128)S(1)} %collective-permute-done.5.tiny_b, f32[2,128,128]{2,1,0:T(8,128)S(1)} %copy-done.1), custom_call_target="tpu_custom_call" | custom-call | flops 10000000 | bytes 39062 | tf_op jit(solution)/shard_map/pallas_call | solution.py:433
  25.1 0.0 copy-start.4
  25.1 16.0 %all_to_all.10.x = f32[8,128,128]{2,1,0:T(8,128)S(1)} all-to-all(f32[8,128,128]{2,1,0:T(8,128)S(1)} %bitcast.8), channel_id=1, replica_groups=mesh['grp'=8,'tile'=32] {'grp'}, dimensions={0} | all-to-all | bytes 1048576 | tf_op jit(solution)/shard_map/all_to_all | solution.py:468
  41.0 0.0 copy-done.4
  41.0 0.4 shard_map.61
  41.4 13.3 %all_to_all.11 = f32[8,128,128]{2,1,0:T(8,128)S(1)} all-to-all(f32[8,128,128]{2,1,0:T(8,128)S(1)} %shard_map.61), channel_id=1, replica_groups=mesh['grp'=8,'tile'=32] {'grp'}, dimensions={0} | all-to-all | bytes 1048576 | tf_op jit(solution)/shard_map/all_to_all | solution.py:470
  54.8 0.8 %shard_map.62 = (f32[536,128]{1,0:T(8,128)S(1)}, f32[536,128]{1,0:T(8,128)S(1)}, bf16[1024,256]{1,0:T(8,128)(2,1)S(1)}, f32[40,128]{1,0:T(8,128)S(1)}) custom-call(s32[1]{0:T(128)} %bitcast.self_ref, f32[1024,128]{1,0:T(8,128)S(1)} %bitcast.6, s32[1,1024]{1,0:T(1,128)S(1)} %get-tuple-element.76.keys, bf16[80,1024]{1,0:T(8,128)(2,1)S(1)} %get-tuple-element.77.spills, ...), custom_call_target="tpu_custom_call" | custom-call | tf_op jit(solution)/shard_map/pallas_call | solution.py:473
  55.6 0.1 collective-permute-start.7
  55.7 4.7 %collective-permute-start.8 = (f32[536,128]{1,0:T(8,128)S(1)}, f32[536,128]{1,0:T(8,128)S(1)}, u32[]{:S(2)}, u32[]{:S(2)}) collective-permute-start(f32[536,128]{1,0:T(8,128)S(1)} %get-tuple-element.84), channel_id=1, source_target_pairs={{0,30},{1,31},{2,4},{3,5},{4,2},{5,3},{6,8},{7,9},{8,6},{9,7},{10,... | collective-permute-start | bytes 823304 | tf_op jit(solution)/shard_map/ppermute | solution.py:29
  60.3 0.7 shard_map.63
  61.0 1.8 %collective-permute-start.6 = (f32[528,128]{1,0:T(8,128)S(1)}, f32[528,128]{1,0:T(8,128)S(1)}, u32[]{:S(2)}, u32[]{:S(2)}) collective-permute-start(f32[528,128]{1,0:T(8,128)S(1)} %get-tuple-element.82), channel_id=1, source_target_pairs={{0,1},{1,0},{2,3},{3,2},{4,5},{5,4},{6,7},{7,6},{8,9},{9,8},{10,11... | collective-permute-start | bytes 811016 | tf_op jit(solution)/shard_map/ppermute | solution.py:29
  62.9 0.0 collective-permute-start.9
  62.9 1.2 %collective-permute-done.6.payload = f32[528,128]{1,0:T(8,128)S(1)} collective-permute-done((f32[528,128]{1,0:T(8,128)S(1)}, f32[528,128]{1,0:T(8,128)S(1)}, u32[]{:S(2)}, u32[]{:S(2)}) %collective-permute-start.6) | collective-permute-done | bytes 270368 | tf_op jit(solution)/shard_map/ppermute | solution.py:29
  64.0 0.0 collective-permute-start.10
  64.0 2.3 %shard_map.64.start = f32[1024,128]{1,0:T(8,128)S(1)} custom-call(s32[1]{0:T(128)} %bitcast.self_ref, f32[1024,128]{1,0:T(8,128)S(1)} %bitcast.7, s32[2,1024]{1,0:T(2,128)S(1)} %copy-done.2, f32[2,1024]{1,0:T(2,128)S(1)} %copy-done.3, f32[8,128]{1,0:T(8,128)S(1)} %get-tuple-element.81.spilled, f32[528,128]{1,0:T(8,128)S(1)} %collective-permute-done.6.payload), custom_call_target="tpu_custom_call" | custom-call | flops 10000000 | bytes 39062 | tf_op jit(solution)/shard_map/pallas_call | solution.py:423
  66.3 0.0 collective-permute-done.7.p0
  66.3 0.0 collective-permute-done.8.p1
  66.4 1.7 %collective-permute-start.11 = (f32[8,128]{1,0:T(8,128)S(1)}, f32[8,128]{1,0:T(8,128)S(1)}, u32[]{:S(2)}, u32[]{:S(2)}) collective-permute-start(f32[8,128]{1,0:T(8,128)S(1)} %slice_add_fusion), channel_id=1, source_target_pairs={{0,1},{1,0},{2,3},{3,2},{4,5},{5,4},{6,7},{7,6},{8,9},{9,8},{10,11... | collective-permute-start | bytes 12296 | tf_op jit(solution)/shard_map/ppermute | solution.py:29
  68.1 1.7 %shard_map.65.start = f32[1024,128]{1,0:T(8,128)S(1)} custom-call(f32[1024,128]{1,0:T(8,128)S(1)} %shard_map.64.start, f32[536,128]{1,0:T(8,128)S(1)} %collective-permute-done.7.p0, f32[536,128]{1,0:T(8,128)S(1)} %collective-permute-done.8.p1), custom_call_target="tpu_custom_call" | custom-call | flops 10000000 | bytes 39062 | tf_op jit(solution)/shard_map/pallas_call | solution.py:432
  69.8 0.0 collective-permute-done.9.payload
  69.8 0.0 collective-permute-done.10.tiny_a
  69.8 0.0 collective-permute-done.11.tiny_b
  69.8 2.2 %shard_map.66 = f32[1024,128]{1,0:T(8,128)} custom-call(f32[1024,128]{1,0:T(8,128)S(1)} %shard_map.65.start, f32[528,128]{1,0:T(8,128)S(1)} %collective-permute-done.9.payload, f32[8,128]{1,0:T(8,128)S(1)} %collective-permute-done.10.tiny_a, f32[8,128]{1,0:T(8,128)S(1)} %collective-permute-done.11.tiny_b, f32[2,128,128]{2,1,0:T(8,128)S(1)} %copy-done.1), custom_call_target="tpu_custom_call" | custom-call | flops 10000000 | bytes 39062 | tf_op jit(solution)/shard_map/pallas_call | solution.py:433
  (2 shorter events, 0.0 us)
Async XLA Ops:
  2.4 1.3 %copy-start.2 = (s32[2,1024]{1,0:T(2,128)S(1)}, s32[2,1024]{1,0:T(2,128)}, u32[]{:S(2)}) copy-start(s32[2,1024]{1,0:T(2,128)} %departure.5) | copy-start | bytes 24580
  2.4 1.3 %copy-start.3 = (f32[2,1024]{1,0:T(2,128)S(1)}, f32[2,1024]{1,0:T(2,128)}, u32[]{:S(2)}) copy-start(f32[2,1024]{1,0:T(2,128)} %fraction.5) | copy-start | bytes 24580
  3.7 12.0 %copy-start = (f32[1024,128]{1,0:T(8,128)S(1)}, f32[1024,128]{1,0:T(8,128)}, u32[]{:S(2)}) copy-start(f32[1024,128]{1,0:T(8,128)} %field.1) | copy-start | bytes 1572868
  5.1 12.9 %collective-permute-start.1 = (f32[536,128]{1,0:T(8,128)S(1)}, f32[536,128]{1,0:T(8,128)S(1)}, u32[]{:S(2)}, u32[]{:S(2)}) collective-permute-start(f32[536,128]{1,0:T(8,128)S(1)} %get-tuple-element.68), channel_id=1, source_target_pairs={{0,2},{1,3},{2,0},{3,1},{4,6},{5,7},{6,4},{7,5},{8,10},{9,11},{10,... | collective-permute-start | bytes 823304 | tf_op jit(solution)/shard_map/ppermute | solution.py:29
  7.6 11.6 %collective-permute-start.2 = (f32[536,128]{1,0:T(8,128)S(1)}, f32[536,128]{1,0:T(8,128)S(1)}, u32[]{:S(2)}, u32[]{:S(2)}) collective-permute-start(f32[536,128]{1,0:T(8,128)S(1)} %get-tuple-element.69), channel_id=1, source_target_pairs={{0,30},{1,31},{2,4},{3,5},{4,2},{5,3},{6,8},{7,9},{8,6},{9,7},{10,... | collective-permute-start | bytes 823304 | tf_op jit(solution)/shard_map/ppermute | solution.py:29
  13.3 2.4 %collective-permute-start = (f32[528,128]{1,0:T(8,128)S(1)}, f32[528,128]{1,0:T(8,128)S(1)}, u32[]{:S(2)}, u32[]{:S(2)}) collective-permute-start(f32[528,128]{1,0:T(8,128)S(1)} %get-tuple-element.67), channel_id=1, source_target_pairs={{0,1},{1,0},{2,3},{3,2},{4,5},{5,4},{6,7},{7,6},{8,9},{9,8},{10,11... | collective-permute-start | bytes 811016 | tf_op jit(solution)/shard_map/ppermute | solution.py:29
  14.5 9.1 %collective-permute-start.3 = (f32[528,128]{1,0:T(8,128)S(1)}, f32[528,128]{1,0:T(8,128)S(1)}, u32[]{:S(2)}, u32[]{:S(2)}) collective-permute-start(f32[528,128]{1,0:T(8,128)S(1)} %get-tuple-element.73), channel_id=1, source_target_pairs={{0,31},{1,2},{2,1},{3,4},{4,3},{5,6},{6,5},{7,8},{8,7},{9,10},{10,... | collective-permute-start | bytes 811016 | tf_op jit(solution)/shard_map/ppermute | solution.py:29
  15.7 8.0 %collective-permute-start.4 = (f32[8,128]{1,0:T(8,128)S(1)}, f32[8,128]{1,0:T(8,128)S(1)}, u32[]{:S(2)}, u32[]{:S(2)}) collective-permute-start(f32[8,128]{1,0:T(8,128)S(1)} %get-tuple-element.75), channel_id=1, source_target_pairs={{0,29},{1,4},{2,31},{3,6},{4,1},{5,8},{6,3},{7,10},{8,5},{9,12},{1... | collective-permute-start | bytes 12296 | tf_op jit(solution)/shard_map/ppermute | solution.py:29
  19.3 4.4 %copy-start.1 = (f32[2,128,128]{2,1,0:T(8,128)S(1)}, f32[2,128,128]{2,1,0:T(8,128)}, u32[]{:S(2)}) copy-start(f32[2,128,128]{2,1,0:T(8,128)} %level_map.3) | copy-start | bytes 393220
  19.3 4.4 %collective-permute-start.5 = (f32[8,128]{1,0:T(8,128)S(1)}, f32[8,128]{1,0:T(8,128)S(1)}, u32[]{:S(2)}, u32[]{:S(2)}) collective-permute-start(f32[8,128]{1,0:T(8,128)S(1)} %slice_add_fusion.1), channel_id=1, source_target_pairs={{0,1},{1,0},{2,3},{3,2},{4,5},{5,4},{6,7},{7,6},{8,9},{9,8},{10,11... | collective-permute-start | bytes 12296 | tf_op jit(solution)/shard_map/ppermute | solution.py:29
  25.1 16.0 %copy-start.4 = (f32[128,8,8]{0,2,1:T(8,128)S(1)}, f32[128,8,8]{0,2,1:T(8,128)}, u32[]{:S(2)}) copy-start(f32[128,8,8]{0,2,1:T(8,128)} %param.9) | copy-start | bytes 98308
  55.6 10.8 %collective-permute-start.7 = (f32[536,128]{1,0:T(8,128)S(1)}, f32[536,128]{1,0:T(8,128)S(1)}, u32[]{:S(2)}, u32[]{:S(2)}) collective-permute-start(f32[536,128]{1,0:T(8,128)S(1)} %get-tuple-element.83), channel_id=1, source_target_pairs={{0,2},{1,3},{2,0},{3,1},{4,6},{5,7},{6,4},{7,5},{8,10},{9,11},{10,... | collective-permute-start | bytes 823304 | tf_op jit(solution)/shard_map/ppermute | solution.py:29
  55.7 10.7 %collective-permute-start.8 = (f32[536,128]{1,0:T(8,128)S(1)}, f32[536,128]{1,0:T(8,128)S(1)}, u32[]{:S(2)}, u32[]{:S(2)}) collective-permute-start(f32[536,128]{1,0:T(8,128)S(1)} %get-tuple-element.84), channel_id=1, source_target_pairs={{0,30},{1,31},{2,4},{3,5},{4,2},{5,3},{6,8},{7,9},{8,6},{9,7},{10,... | collective-permute-start | bytes 823304 | tf_op jit(solution)/shard_map/ppermute | solution.py:29
  61.0 3.0 %collective-permute-start.6 = (f32[528,128]{1,0:T(8,128)S(1)}, f32[528,128]{1,0:T(8,128)S(1)}, u32[]{:S(2)}, u32[]{:S(2)}) collective-permute-start(f32[528,128]{1,0:T(8,128)S(1)} %get-tuple-element.82), channel_id=1, source_target_pairs={{0,1},{1,0},{2,3},{3,2},{4,5},{5,4},{6,7},{7,6},{8,9},{9,8},{10,11... | collective-permute-start | bytes 811016 | tf_op jit(solution)/shard_map/ppermute | solution.py:29
  62.9 6.9 %collective-permute-start.9 = (f32[528,128]{1,0:T(8,128)S(1)}, f32[528,128]{1,0:T(8,128)S(1)}, u32[]{:S(2)}, u32[]{:S(2)}) collective-permute-start(f32[528,128]{1,0:T(8,128)S(1)} %get-tuple-element.88), channel_id=1, source_target_pairs={{0,31},{1,2},{2,1},{3,4},{4,3},{5,6},{6,5},{7,8},{8,7},{9,10},{10,... | collective-permute-start | bytes 811016 | tf_op jit(solution)/shard_map/ppermute | solution.py:29
  64.0 5.8 %collective-permute-start.10 = (f32[8,128]{1,0:T(8,128)S(1)}, f32[8,128]{1,0:T(8,128)S(1)}, u32[]{:S(2)}, u32[]{:S(2)}) collective-permute-start(f32[8,128]{1,0:T(8,128)S(1)} %get-tuple-element.90), channel_id=1, source_target_pairs={{0,29},{1,4},{2,31},{3,6},{4,1},{5,8},{6,3},{7,10},{8,5},{9,12},{1... | collective-permute-start | bytes 12296 | tf_op jit(solution)/shard_map/ppermute | solution.py:29
  66.4 3.5 %collective-permute-start.11 = (f32[8,128]{1,0:T(8,128)S(1)}, f32[8,128]{1,0:T(8,128)S(1)}, u32[]{:S(2)}, u32[]{:S(2)}) collective-permute-start(f32[8,128]{1,0:T(8,128)S(1)} %slice_add_fusion), channel_id=1, source_target_pairs={{0,1},{1,0},{2,3},{3,2},{4,5},{5,4},{6,7},{7,6},{8,9},{9,8},{10,11... | collective-permute-start | bytes 12296 | tf_op jit(solution)/shard_map/ppermute | solution.py:29

commit v11 on v9

--- a/solution.py
+++ b/solution.py
@@ -239,7 +239,8 @@
         outs[which][CAP + 8 : CAP + 16, :] = meta[8 * which : 8 * which + 8, :]
 
 
-BLOCK = 512
+BLOCK = 1024
+HALF = 512
 I16 = jnp.int16
 
 
@@ -341,8 +342,8 @@
         out[...] = lift(slice(0, COLS))
         return
     copies = []
-    for b in range(COLS // BLOCK):
-        rows = slice(b * BLOCK, (b + 1) * BLOCK)
+    for b in range(COLS // HALF):
+        rows = slice(b * HALF, (b + 1) * HALF)
         lifted_ref[rows, :] = lift(rows)
         copies.append(pltpu.make_async_copy(lifted_ref.at[rows, :], out.at[rows, :], sems.at[b]))
         copies[-1].start()
@@ -436,7 +437,7 @@
             one,
             pltpu.VMEM((COLS, LEV), F32),
             pltpu.VMEM((COLS, LEV), F32),
-            pltpu.SemaphoreType.DMA((COLS // BLOCK,)),
+            pltpu.SemaphoreType.DMA((COLS // HALF,)),
         ],
         work,
         HBM if step == 0 else VM,

time: 71.9 us -> 71.4 us (level)
  no operation moved by 1% of the time
where the time goes in v11:
time: 71.4 us; the launch traced here: 71.1 us
  blocking collectives  27.1 us (38%)
  starting transfers between devices  21.5 us (30%)
  Pallas kernels  17.9 us (25%)
  waiting for transfers between devices  4.17 us (6%)
    ppermute x12, starting transfers between devices, swapped(): lax.ppermute(x, 'tile', [(i, (i + signs(i)[which]) % length) for i in ran...  21.5 us
    all_to_all x1, blocking collectives, body(): lax.all_to_all(second.reshape(groups, COLS // groups, LEV), 'grp', 0, 0)  15.8 us
    all_to_all x1, blocking collectives, body(): coupled = lax.all_to_all(mixed, 'grp', 0, 0).reshape(COLS, LEV)  11.4 us
    pallas_call x2, Pallas kernels, transported(): call(functools.partial(own_kernel, step, tile_count), total, [SM] + [VM]...  4.5 us
    ppermute x12, waiting for transfers between devices, swapped(): lax.ppermute(x, 'tile', [(i, (i + signs(i)[which]) % length) for i in ran...  4.17 us
    pallas_call x2, Pallas kernels, transported(): call(functools.partial(last_kernel, step), total, [VM] * 5, [one, pltpu.V...  3.35 us
    pallas_call x2, Pallas kernels, transported(): call(middle_kernel, total, [VM] * 3, [pltpu.VMEM((2, CAP, 2 * LEV), BF)],...  3.13 us
    pallas_call x1, Pallas kernels, body(): call(functools.partial(first_far_kernel, tile_count), outputs, [SM, HBM,...  2.42 us
  transfers between devices with their start and end apart: 12, of which 2 were waited for; matrix products, arithmetic and copies ran while one was open for 0% of the time, Pallas kernels for 14%

profile of v11, /device:TPU:1, one launch (start us, length us, event | category | flops | bytes accessed | tf_op | source)
XLA Modules:
  0.0 71.1 jit_solution(4955250921496184731)
XLA Ops:
  0.0 2.4 %shard_map.55 = (f32[536,128]{1,0:T(8,128)S(1)}, f32[536,128]{1,0:T(8,128)S(1)}, bf16[1024,256]{1,0:T(8,128)(2,1)S(1)}, f32[40,128]{1,0:T(8,128)S(1)}, s32[1,102...) custom-call(s32[1]{0:T(128)} %bitcast.self_ref, f32[1024,128]{1,0:T(8,128)} %field.1, s32[2,1024]{1,0:T(2,128)} %departure.5, ...), custom_call_target="tpu_custom_call" | custom-call | tf_op jit(solution)/shard_map/pallas_call | solution.py:459
  2.4 0.0 copy-start
  2.4 0.0 copy-start.3
  2.5 1.2 %shard_map.56 = (f32[528,128]{1,0:T(8,128)S(1)}, f32[528,128]{1,0:T(8,128)S(1)}, f32[8,128]{1,0:T(8,128)S(1)}, f32[8,128]{1,0:T(8,128)S(1)}) custom-call(s32[1]{0:T(128)} %bitcast.self_ref, bf16[1024,256]{1,0:T(8,128)(2,1)S(1)} %get-tuple-element.40.both, f32[40,128]{1,0:T(8,128)S(1)} %get-tuple-element.41.spilled, s32[1,1024]{1,0:T(1,128)S(1)} %get-tuple-element.42.keys, ...), custom_call_target="tpu_custom_call" | custom-call | flops 1000000000 | bytes 3906250 | tf_op jit(solution)/shard_map/pallas_call | solution.py:397
  3.7 0.0 copy-start.2
  3.7 3.3 %collective-permute-start = (f32[528,128]{1,0:T(8,128)S(1)}, f32[528,128]{1,0:T(8,128)S(1)}, u32[]{:S(2)}, u32[]{:S(2)}) collective-permute-start(f32[528,128]{1,0:T(8,128)S(1)} %get-tuple-element.45), channel_id=1, source_target_pairs={{0,1},{1,0},{2,3},{3,2},{4,5},{5,4},{6,7},{7,6},{8,9},{9,8},{10,11... | collective-permute-start | bytes 811016 | tf_op jit(solution)/shard_map/ppermute | solution.py:29
  7.0 0.0 collective-permute-start.1
  7.0 5.6 %collective-permute-start.2 = (f32[536,128]{1,0:T(8,128)S(1)}, f32[536,128]{1,0:T(8,128)S(1)}, u32[]{:S(2)}, u32[]{:S(2)}) collective-permute-start(f32[536,128]{1,0:T(8,128)S(1)} %get-tuple-element.53), channel_id=1, source_target_pairs={{0,30},{1,31},{2,4},{3,5},{4,2},{5,3},{6,8},{7,9},{8,6},{9,7},{10,... | collective-permute-start | bytes 823304 | tf_op jit(solution)/shard_map/ppermute | solution.py:29
  12.6 0.0 collective-permute-start.3
  12.6 0.0 collective-permute-done.payload
  12.6 0.0 collective-permute-start.4
  12.7 0.0 copy-done
  12.7 0.0 copy-done.3
  12.7 0.0 copy-done.2
  12.7 2.3 %shard_map.57.start = f32[1024,128]{1,0:T(8,128)S(1)} custom-call(s32[1]{0:T(128)} %bitcast.self_ref, f32[1024,128]{1,0:T(8,128)S(1)} %copy-done, s32[2,1024]{1,0:T(2,128)S(1)} %copy-done.2, f32[2,1024]{1,0:T(2,128)S(1)} %copy-done.3, f32[8,128]{1,0:T(8,128)S(1)} %get-tuple-element.44.spilled, f32[528,128]{1,0:T(8,128)S(1)} %collective-permute-done.payload), custom_call_target="tpu_custom_call" | custom-call | flops 10000000 | bytes 39062 | tf_op jit(solution)/shard_map/pallas_call | solution.py:407
  14.9 1.4 %shard_map.58 = (s32[1,1024]{1,0:T(1,128)S(1)}, bf16[80,1024]{1,0:T(8,128)(2,1)S(1)}, f32[32,128]{1,0:T(8,128)S(1)}) custom-call(s32[1]{0:T(128)} %bitcast.self_ref, s32[2,1024]{1,0:T(2,128)S(1)} %copy-done.2, f32[2,1024]{1,0:T(2,128)S(1)} %copy-done.3), custom_call_target="tpu_custom_call" | custom-call | flops 300000000 | bytes 1171875 | tf_op jit(solution)/shard_map/pallas_call | solution.py:417
  16.3 0.0 collective-permute-done.1.p0
  16.3 3.0 %collective-permute-done.2.p1 = f32[536,128]{1,0:T(8,128)S(1)} collective-permute-done((f32[536,128]{1,0:T(8,128)S(1)}, f32[536,128]{1,0:T(8,128)S(1)}, u32[]{:S(2)}, u32[]{:S(2)}) %collective-permute-start.2) | collective-permute-done | bytes 274464 | tf_op jit(solution)/shard_map/ppermute | solution.py:29
  19.3 0.0 copy-start.1
  19.3 1.3 %collective-permute-start.5 = (f32[8,128]{1,0:T(8,128)S(1)}, f32[8,128]{1,0:T(8,128)S(1)}, u32[]{:S(2)}, u32[]{:S(2)}) collective-permute-start(f32[8,128]{1,0:T(8,128)S(1)} %slice_add_fusion.1), channel_id=1, source_target_pairs={{0,1},{1,0},{2,3},{3,2},{4,5},{5,4},{6,7},{7,6},{8,9},{9,8},{10,11... | collective-permute-start | bytes 12296 | tf_op jit(solution)/shard_map/ppermute | solution.py:29
  20.6 1.6 %shard_map.59.start = f32[1024,128]{1,0:T(8,128)S(1)} custom-call(f32[1024,128]{1,0:T(8,128)S(1)} %shard_map.57.start, f32[536,128]{1,0:T(8,128)S(1)} %collective-permute-done.1.p0, f32[536,128]{1,0:T(8,128)S(1)} %collective-permute-done.2.p1), custom_call_target="tpu_custom_call" | custom-call | flops 10000000 | bytes 39062 | tf_op jit(solution)/shard_map/pallas_call | solution.py:431
  22.2 0.0 collective-permute-done.3.payload
  22.2 0.0 collective-permute-done.4.tiny_a
  22.2 0.0 collective-permute-done.5.tiny_b
  22.2 0.0 copy-done.1
  22.3 1.4 %shard_map.60 = f32[1024,128]{1,0:T(8,128)S(1)} custom-call(f32[1024,128]{1,0:T(8,128)S(1)} %shard_map.59.start, f32[528,128]{1,0:T(8,128)S(1)} %collective-permute-done.3.payload, f32[8,128]{1,0:T(8,128)S(1)} %collective-permute-done.4.tiny_a, f32[8,128]{1,0:T(8,128)S(1)} %collective-permute-done.5.tiny_b, f32[2,128,128]{2,1,0:T(8,128)S(1)} %copy-done.1), custom_call_target="tpu_custom_call" | custom-call | flops 10000000 | bytes 39062 | tf_op jit(solution)/shard_map/pallas_call | solution.py:432
  23.6 0.0 copy-start.4
  23.6 15.8 %all_to_all.10.x = f32[8,128,128]{2,1,0:T(8,128)S(1)} all-to-all(f32[8,128,128]{2,1,0:T(8,128)S(1)} %bitcast.8), channel_id=1, replica_groups=mesh['grp'=8,'tile'=32] {'grp'}, dimensions={0} | all-to-all | bytes 1048576 | tf_op jit(solution)/shard_map/all_to_all | solution.py:467
  39.4 0.0 copy-done.4
  39.4 0.4 shard_map.61
  39.8 11.4 %all_to_all.11 = f32[8,128,128]{2,1,0:T(8,128)S(1)} all-to-all(f32[8,128,128]{2,1,0:T(8,128)S(1)} %shard_map.61), channel_id=1, replica_groups=mesh['grp'=8,'tile'=32] {'grp'}, dimensions={0} | all-to-all | bytes 1048576 | tf_op jit(solution)/shard_map/all_to_all | solution.py:469
  51.2 0.8 %shard_map.62 = (f32[536,128]{1,0:T(8,128)S(1)}, f32[536,128]{1,0:T(8,128)S(1)}, bf16[1024,256]{1,0:T(8,128)(2,1)S(1)}, f32[40,128]{1,0:T(8,128)S(1)}) custom-call(s32[1]{0:T(128)} %bitcast.self_ref, f32[1024,128]{1,0:T(8,128)S(1)} %bitcast.6, s32[1,1024]{1,0:T(1,128)S(1)} %get-tuple-element.60.keys, bf16[80,1024]{1,0:T(8,128)(2,1)S(1)} %get-tuple-element.61.spills, ...), custom_call_target="tpu_custom_call" | custom-call | tf_op jit(solution)/shard_map/pallas_call | solution.py:472
  52.0 3.9 %collective-permute-start.7 = (f32[536,128]{1,0:T(8,128)S(1)}, f32[536,128]{1,0:T(8,128)S(1)}, u32[]{:S(2)}, u32[]{:S(2)}) collective-permute-start(f32[536,128]{1,0:T(8,128)S(1)} %get-tuple-element.67), channel_id=1, source_target_pairs={{0,2},{1,3},{2,0},{3,1},{4,6},{5,7},{6,4},{7,5},{8,10},{9,11},{10,... | collective-permute-start | bytes 823304 | tf_op jit(solution)/shard_map/ppermute | solution.py:29
  55.8 3.7 %collective-permute-start.8 = (f32[536,128]{1,0:T(8,128)S(1)}, f32[536,128]{1,0:T(8,128)S(1)}, u32[]{:S(2)}, u32[]{:S(2)}) collective-permute-start(f32[536,128]{1,0:T(8,128)S(1)} %get-tuple-element.68), channel_id=1, source_target_pairs={{0,30},{1,31},{2,4},{3,5},{4,2},{5,3},{6,8},{7,9},{8,6},{9,7},{10,... | collective-permute-start | bytes 823304 | tf_op jit(solution)/shard_map/ppermute | solution.py:29
  59.5 0.7 shard_map.63
  60.3 1.8 %collective-permute-start.6 = (f32[528,128]{1,0:T(8,128)S(1)}, f32[528,128]{1,0:T(8,128)S(1)}, u32[]{:S(2)}, u32[]{:S(2)}) collective-permute-start(f32[528,128]{1,0:T(8,128)S(1)} %get-tuple-element.66), channel_id=1, source_target_pairs={{0,1},{1,0},{2,3},{3,2},{4,5},{5,4},{6,7},{7,6},{8,9},{9,8},{10,11... | collective-permute-start | bytes 811016 | tf_op jit(solution)/shard_map/ppermute | solution.py:29
  62.1 0.0 collective-permute-start.9
  62.1 1.2 %collective-permute-done.6.payload = f32[528,128]{1,0:T(8,128)S(1)} collective-permute-done((f32[528,128]{1,0:T(8,128)S(1)}, f32[528,128]{1,0:T(8,128)S(1)}, u32[]{:S(2)}, u32[]{:S(2)}) %collective-permute-start.6) | collective-permute-done | bytes 270368 | tf_op jit(solution)/shard_map/ppermute | solution.py:29
  63.3 0.0 collective-permute-start.10
  63.3 2.2 %shard_map.64.start = f32[1024,128]{1,0:T(8,128)S(1)} custom-call(s32[1]{0:T(128)} %bitcast.self_ref, f32[1024,128]{1,0:T(8,128)S(1)} %bitcast.7, s32[2,1024]{1,0:T(2,128)S(1)} %copy-done.2, f32[2,1024]{1,0:T(2,128)S(1)} %copy-done.3, f32[8,128]{1,0:T(8,128)S(1)} %get-tuple-element.65.spilled, f32[528,128]{1,0:T(8,128)S(1)} %collective-permute-done.6.payload), custom_call_target="tpu_custom_call" | custom-call | flops 10000000 | bytes 39062 | tf_op jit(solution)/shard_map/pallas_call | solution.py:407
  65.5 0.0 collective-permute-done.7.p0
  65.5 0.0 collective-permute-done.8.p1
  65.6 1.8 %collective-permute-start.11 = (f32[8,128]{1,0:T(8,128)S(1)}, f32[8,128]{1,0:T(8,128)S(1)}, u32[]{:S(2)}, u32[]{:S(2)}) collective-permute-start(f32[8,128]{1,0:T(8,128)S(1)} %slice_add_fusion), channel_id=1, source_target_pairs={{0,1},{1,0},{2,3},{3,2},{4,5},{5,4},{6,7},{7,6},{8,9},{9,8},{10,11... | collective-permute-start | bytes 12296 | tf_op jit(solution)/shard_map/ppermute | solution.py:29
  67.4 1.6 %shard_map.65.start = f32[1024,128]{1,0:T(8,128)S(1)} custom-call(f32[1024,128]{1,0:T(8,128)S(1)} %shard_map.64.start, f32[536,128]{1,0:T(8,128)S(1)} %collective-permute-done.7.p0, f32[536,128]{1,0:T(8,128)S(1)} %collective-permute-done.8.p1), custom_call_target="tpu_custom_call" | custom-call | flops 10000000 | bytes 39062 | tf_op jit(solution)/shard_map/pallas_call | solution.py:431
  68.9 0.0 collective-permute-done.9.payload
  68.9 0.0 collective-permute-done.10.tiny_a
  69.0 0.0 collective-permute-done.11.tiny_b
  69.0 2.0 %shard_map.66 = f32[1024,128]{1,0:T(8,128)} custom-call(f32[1024,128]{1,0:T(8,128)S(1)} %shard_map.65.start, f32[528,128]{1,0:T(8,128)S(1)} %collective-permute-done.9.payload, f32[8,128]{1,0:T(8,128)S(1)} %collective-permute-done.10.tiny_a, f32[8,128]{1,0:T(8,128)S(1)} %collective-permute-done.11.tiny_b, f32[2,128,128]{2,1,0:T(8,128)S(1)} %copy-done.1), custom_call_target="tpu_custom_call" | custom-call | flops 10000000 | bytes 39062 | tf_op jit(solution)/shard_map/pallas_call | solution.py:432
  (2 shorter events, 0.0 us)
Async XLA Ops:
  2.4 10.2 %copy-start = (f32[1024,128]{1,0:T(8,128)S(1)}, f32[1024,128]{1,0:T(8,128)}, u32[]{:S(2)}) copy-start(f32[1024,128]{1,0:T(8,128)} %field.1) | copy-start | bytes 1572868
  2.4 10.2 %copy-start.3 = (f32[2,1024]{1,0:T(2,128)S(1)}, f32[2,1024]{1,0:T(2,128)}, u32[]{:S(2)}) copy-start(f32[2,1024]{1,0:T(2,128)} %fraction.5) | copy-start | bytes 24580
  3.7 9.0 %copy-start.2 = (s32[2,1024]{1,0:T(2,128)S(1)}, s32[2,1024]{1,0:T(2,128)}, u32[]{:S(2)}) copy-start(s32[2,1024]{1,0:T(2,128)} %departure.5) | copy-start | bytes 24580
  3.7 8.9 %collective-permute-start = (f32[528,128]{1,0:T(8,128)S(1)}, f32[528,128]{1,0:T(8,128)S(1)}, u32[]{:S(2)}, u32[]{:S(2)}) collective-permute-start(f32[528,128]{1,0:T(8,128)S(1)} %get-tuple-element.45), channel_id=1, source_target_pairs={{0,1},{1,0},{2,3},{3,2},{4,5},{5,4},{6,7},{7,6},{8,9},{9,8},{10,11... | collective-permute-start | bytes 811016 | tf_op jit(solution)/shard_map/ppermute | solution.py:29
  7.0 9.3 %collective-permute-start.1 = (f32[536,128]{1,0:T(8,128)S(1)}, f32[536,128]{1,0:T(8,128)S(1)}, u32[]{:S(2)}, u32[]{:S(2)}) collective-permute-start(f32[536,128]{1,0:T(8,128)S(1)} %get-tuple-element.52), channel_id=1, source_target_pairs={{0,2},{1,3},{2,0},{3,1},{4,6},{5,7},{6,4},{7,5},{8,10},{9,11},{10,... | collective-permute-start | bytes 823304 | tf_op jit(solution)/shard_map/ppermute | solution.py:29
  7.0 12.2 %collective-permute-start.2 = (f32[536,128]{1,0:T(8,128)S(1)}, f32[536,128]{1,0:T(8,128)S(1)}, u32[]{:S(2)}, u32[]{:S(2)}) collective-permute-start(f32[536,128]{1,0:T(8,128)S(1)} %get-tuple-element.53), channel_id=1, source_target_pairs={{0,30},{1,31},{2,4},{3,5},{4,2},{5,3},{6,8},{7,9},{8,6},{9,7},{10,... | collective-permute-start | bytes 823304 | tf_op jit(solution)/shard_map/ppermute | solution.py:29
  12.6 9.6 %collective-permute-start.3 = (f32[528,128]{1,0:T(8,128)S(1)}, f32[528,128]{1,0:T(8,128)S(1)}, u32[]{:S(2)}, u32[]{:S(2)}) collective-permute-start(f32[528,128]{1,0:T(8,128)S(1)} %get-tuple-element.57), channel_id=1, source_target_pairs={{0,31},{1,2},{2,1},{3,4},{4,3},{5,6},{6,5},{7,8},{8,7},{9,10},{10,... | collective-permute-start | bytes 811016 | tf_op jit(solution)/shard_map/ppermute | solution.py:29
  12.6 9.6 %collective-permute-start.4 = (f32[8,128]{1,0:T(8,128)S(1)}, f32[8,128]{1,0:T(8,128)S(1)}, u32[]{:S(2)}, u32[]{:S(2)}) collective-permute-start(f32[8,128]{1,0:T(8,128)S(1)} %get-tuple-element.59), channel_id=1, source_target_pairs={{0,29},{1,4},{2,31},{3,6},{4,1},{5,8},{6,3},{7,10},{8,5},{9,12},{1... | collective-permute-start | bytes 12296 | tf_op jit(solution)/shard_map/ppermute | solution.py:29
  19.3 3.0 %copy-start.1 = (f32[2,128,128]{2,1,0:T(8,128)S(1)}, f32[2,128,128]{2,1,0:T(8,128)}, u32[]{:S(2)}) copy-start(f32[2,128,128]{2,1,0:T(8,128)} %level_map.3) | copy-start | bytes 393220
  19.3 2.9 %collective-permute-start.5 = (f32[8,128]{1,0:T(8,128)S(1)}, f32[8,128]{1,0:T(8,128)S(1)}, u32[]{:S(2)}, u32[]{:S(2)}) collective-permute-start(f32[8,128]{1,0:T(8,128)S(1)} %slice_add_fusion.1), channel_id=1, source_target_pairs={{0,1},{1,0},{2,3},{3,2},{4,5},{5,4},{6,7},{7,6},{8,9},{9,8},{10,11... | collective-permute-start | bytes 12296 | tf_op jit(solution)/shard_map/ppermute | solution.py:29
  23.6 15.8 %copy-start.4 = (f32[128,8,8]{0,2,1:T(8,128)S(1)}, f32[128,8,8]{0,2,1:T(8,128)}, u32[]{:S(2)}) copy-start(f32[128,8,8]{0,2,1:T(8,128)} %param.9) | copy-start | bytes 98308
  52.0 13.6 %collective-permute-start.7 = (f32[536,128]{1,0:T(8,128)S(1)}, f32[536,128]{1,0:T(8,128)S(1)}, u32[]{:S(2)}, u32[]{:S(2)}) collective-permute-start(f32[536,128]{1,0:T(8,128)S(1)} %get-tuple-element.67), channel_id=1, source_target_pairs={{0,2},{1,3},{2,0},{3,1},{4,6},{5,7},{6,4},{7,5},{8,10},{9,11},{10,... | collective-permute-start | bytes 823304 | tf_op jit(solution)/shard_map/ppermute | solution.py:29
  55.8 9.7 %collective-permute-start.8 = (f32[536,128]{1,0:T(8,128)S(1)}, f32[536,128]{1,0:T(8,128)S(1)}, u32[]{:S(2)}, u32[]{:S(2)}) collective-permute-start(f32[536,128]{1,0:T(8,128)S(1)} %get-tuple-element.68), channel_id=1, source_target_pairs={{0,30},{1,31},{2,4},{3,5},{4,2},{5,3},{6,8},{7,9},{8,6},{9,7},{10,... | collective-permute-start | bytes 823304 | tf_op jit(solution)/shard_map/ppermute | solution.py:29
  60.3 3.0 %collective-permute-start.6 = (f32[528,128]{1,0:T(8,128)S(1)}, f32[528,128]{1,0:T(8,128)S(1)}, u32[]{:S(2)}, u32[]{:S(2)}) collective-permute-start(f32[528,128]{1,0:T(8,128)S(1)} %get-tuple-element.66), channel_id=1, source_target_pairs={{0,1},{1,0},{2,3},{3,2},{4,5},{5,4},{6,7},{7,6},{8,9},{9,8},{10,11... | collective-permute-start | bytes 811016 | tf_op jit(solution)/shard_map/ppermute | solution.py:29
  62.1 6.8 %collective-permute-start.9 = (f32[528,128]{1,0:T(8,128)S(1)}, f32[528,128]{1,0:T(8,128)S(1)}, u32[]{:S(2)}, u32[]{:S(2)}) collective-permute-start(f32[528,128]{1,0:T(8,128)S(1)} %get-tuple-element.72), channel_id=1, source_target_pairs={{0,31},{1,2},{2,1},{3,4},{4,3},{5,6},{6,5},{7,8},{8,7},{9,10},{10,... | collective-permute-start | bytes 811016 | tf_op jit(solution)/shard_map/ppermute | solution.py:29
  63.3 5.7 %collective-permute-start.10 = (f32[8,128]{1,0:T(8,128)S(1)}, f32[8,128]{1,0:T(8,128)S(1)}, u32[]{:S(2)}, u32[]{:S(2)}) collective-permute-start(f32[8,128]{1,0:T(8,128)S(1)} %get-tuple-element.74), channel_id=1, source_target_pairs={{0,29},{1,4},{2,31},{3,6},{4,1},{5,8},{6,3},{7,10},{8,5},{9,12},{1... | collective-permute-start | bytes 12296 | tf_op jit(solution)/shard_map/ppermute | solution.py:29
  65.6 3.4 %collective-permute-start.11 = (f32[8,128]{1,0:T(8,128)S(1)}, f32[8,128]{1,0:T(8,128)S(1)}, u32[]{:S(2)}, u32[]{:S(2)}) collective-permute-start(f32[8,128]{1,0:T(8,128)S(1)} %slice_add_fusion), channel_id=1, source_target_pairs={{0,1},{1,0},{2,3},{3,2},{4,5},{5,4},{6,7},{7,6},{8,9},{9,8},{10,11... | collective-permute-start | bytes 12296 | tf_op jit(solution)/shard_map/ppermute | solution.py:29

commit v12 on v11

--- a/solution.py
+++ b/solution.py
@@ -282,10 +282,12 @@
     @pl.loop(0, COLS // BLOCK)
     def _(b):
         high, low = spread_block(b * BLOCK, own_table)
-        wide = dot(high, own_ref[...]) + dot(low, own_ref[...])
+        wide = dot(high, own_ref[...])
+        slim = dot(low, own_ref[:, :LEV])
         high, low = spread_block(b * BLOCK, table)
-        wide = wide + dot(high, both_ref[0]) + dot(low, both_ref[0])
-        out[pl.ds(b * BLOCK, BLOCK), :] = wide[:, :LEV] + wide[:, LEV:]
+        wide = wide + dot(high, both_ref[0])
+        slim = slim + dot(low, both_ref[0, :, :LEV])
+        out[pl.ds(b * BLOCK, BLOCK), :] = wide[:, :LEV] + (wide[:, LEV:] + slim)
 
     add_spill(out, spilled[...] + payload[CAP : CAP + 8, :])
 
@@ -308,10 +310,12 @@
 
 def deposit_block(b, start, tables, both_ref):
     wide = jnp.zeros((BLOCK, 2 * LEV), F32)
+    slim = jnp.zeros((BLOCK, LEV), F32)
     for which, table in enumerate(tables):
         high, low = spread_block(b * BLOCK, table)
-        wide = wide + dot(high, both_ref[which]) + dot(low, both_ref[which])
-    return start[pl.ds(b * BLOCK, BLOCK), :] + wide[:, :LEV] + wide[:, LEV:]
+        wide = wide + dot(high, both_ref[which])
+        slim = slim + dot(low, both_ref[which, :, :LEV])
+    return start[pl.ds(b * BLOCK, BLOCK), :] + wide[:, :LEV] + (wide[:, LEV:] + slim)
 
 
 def middle_kernel(start, p0, p1, out, both_ref):

time: 71.4 us -> 70.8 us (level)
  Pallas kernels: 17.9 us -> 16.8 us
  transfers between devices with their start and end apart: 12 -> 12, of which waited for: 2 -> 3; matrix products, arithmetic and copies ran while one was open for 0% -> 0% of each run, Pallas kernels for 14% -> 12%
where the time goes in v12:
time: 70.8 us; the launch traced here: 70.4 us
  blocking collectives  27 us (38%)
  starting transfers between devices  21.7 us (31%)
  Pallas kernels  16.8 us (24%)
  waiting for transfers between devices  4.51 us (6%)
    ppermute x12, starting transfers between devices, swapped(): lax.ppermute(x, 'tile', [(i, (i + signs(i)[which]) % length) for i in ran...  21.7 us
    all_to_all x1, blocking collectives, body(): lax.all_to_all(second.reshape(groups, COLS // groups, LEV), 'grp', 0, 0)  15.1 us
    all_to_all x1, blocking collectives, body(): coupled = lax.all_to_all(mixed, 'grp', 0, 0).reshape(COLS, LEV)  11.8 us
    ppermute x12, waiting for transfers between devices, swapped(): lax.ppermute(x, 'tile', [(i, (i + signs(i)[which]) % length) for i in ran...  4.51 us
    pallas_call x2, Pallas kernels, transported(): call(functools.partial(own_kernel, step, tile_count), total, [SM] + [VM]...  3.93 us
    pallas_call x2, Pallas kernels, transported(): call(functools.partial(last_kernel, step), total, [VM] * 5, [one, pltpu.V...  3.27 us
    pallas_call x2, Pallas kernels, transported(): call(middle_kernel, total, [VM] * 3, [pltpu.VMEM((2, CAP, 2 * LEV), BF)],...  2.73 us
    pallas_call x1, Pallas kernels, body(): call(functools.partial(first_far_kernel, tile_count), outputs, [SM, HBM,...  2.42 us
  transfers between devices with their start and end apart: 12, of which 3 were waited for; matrix products, arithmetic and copies ran while one was open for 0% of the time, Pallas kernels for 12%

profile of v12, /device:TPU:1, one launch (start us, length us, event | category | flops | bytes accessed | tf_op | source)
XLA Modules:
  0.0 70.4 jit_solution(17501677867050990931)
XLA Ops:
  0.0 2.4 %shard_map.55 = (f32[536,128]{1,0:T(8,128)S(1)}, f32[536,128]{1,0:T(8,128)S(1)}, bf16[1024,256]{1,0:T(8,128)(2,1)S(1)}, f32[40,128]{1,0:T(8,128)S(1)}, s32[1,102...) custom-call(s32[1]{0:T(128)} %bitcast.self_ref, f32[1024,128]{1,0:T(8,128)} %field.1, s32[2,1024]{1,0:T(2,128)} %departure.5, ...), custom_call_target="tpu_custom_call" | custom-call | tf_op jit(solution)/shard_map/pallas_call | solution.py:463
  2.4 0.0 copy-start
  2.4 0.0 copy-start.3
  2.5 1.2 %shard_map.56 = (f32[528,128]{1,0:T(8,128)S(1)}, f32[528,128]{1,0:T(8,128)S(1)}, f32[8,128]{1,0:T(8,128)S(1)}, f32[8,128]{1,0:T(8,128)S(1)}) custom-call(s32[1]{0:T(128)} %bitcast.self_ref, bf16[1024,256]{1,0:T(8,128)(2,1)S(1)} %get-tuple-element.40.both, f32[40,128]{1,0:T(8,128)S(1)} %get-tuple-element.41.spilled, s32[1,1024]{1,0:T(1,128)S(1)} %get-tuple-element.42.keys, ...), custom_call_target="tpu_custom_call" | custom-call | flops 1000000000 | bytes 3906250 | tf_op jit(solution)/shard_map/pallas_call | solution.py:401
  3.7 0.0 copy-start.2
  3.7 3.3 %collective-permute-start = (f32[528,128]{1,0:T(8,128)S(1)}, f32[528,128]{1,0:T(8,128)S(1)}, u32[]{:S(2)}, u32[]{:S(2)}) collective-permute-start(f32[528,128]{1,0:T(8,128)S(1)} %get-tuple-element.45), channel_id=1, source_target_pairs={{0,1},{1,0},{2,3},{3,2},{4,5},{5,4},{6,7},{7,6},{8,9},{9,8},{10,11... | collective-permute-start | bytes 811016 | tf_op jit(solution)/shard_map/ppermute | solution.py:29
  7.0 0.0 collective-permute-start.1
  7.0 5.6 %collective-permute-start.2 = (f32[536,128]{1,0:T(8,128)S(1)}, f32[536,128]{1,0:T(8,128)S(1)}, u32[]{:S(2)}, u32[]{:S(2)}) collective-permute-start(f32[536,128]{1,0:T(8,128)S(1)} %get-tuple-element.53), channel_id=1, source_target_pairs={{0,30},{1,31},{2,4},{3,5},{4,2},{5,3},{6,8},{7,9},{8,6},{9,7},{10,... | collective-permute-start | bytes 823304 | tf_op jit(solution)/shard_map/ppermute | solution.py:29
  12.6 0.0 collective-permute-start.3
  12.6 0.0 collective-permute-done.payload
  12.6 0.0 collective-permute-start.4
  12.7 0.0 copy-done
  12.7 0.0 copy-done.3
  12.7 0.0 copy-done.2
  12.7 2.0 %shard_map.57.start = f32[1024,128]{1,0:T(8,128)S(1)} custom-call(s32[1]{0:T(128)} %bitcast.self_ref, f32[1024,128]{1,0:T(8,128)S(1)} %copy-done, s32[2,1024]{1,0:T(2,128)S(1)} %copy-done.2, f32[2,1024]{1,0:T(2,128)S(1)} %copy-done.3, f32[8,128]{1,0:T(8,128)S(1)} %get-tuple-element.44.spilled, f32[528,128]{1,0:T(8,128)S(1)} %collective-permute-done.payload), custom_call_target="tpu_custom_call" | custom-call | flops 10000000 | bytes 39062 | tf_op jit(solution)/shard_map/pallas_call | solution.py:411
  14.7 1.4 %shard_map.58 = (s32[1,1024]{1,0:T(1,128)S(1)}, bf16[80,1024]{1,0:T(8,128)(2,1)S(1)}, f32[32,128]{1,0:T(8,128)S(1)}) custom-call(s32[1]{0:T(128)} %bitcast.self_ref, s32[2,1024]{1,0:T(2,128)S(1)} %copy-done.2, f32[2,1024]{1,0:T(2,128)S(1)} %copy-done.3), custom_call_target="tpu_custom_call" | custom-call | flops 300000000 | bytes 1171875 | tf_op jit(solution)/shard_map/pallas_call | solution.py:421
  16.0 0.0 collective-permute-done.1.p0
  16.0 3.3 %collective-permute-done.2.p1 = f32[536,128]{1,0:T(8,128)S(1)} collective-permute-done((f32[536,128]{1,0:T(8,128)S(1)}, f32[536,128]{1,0:T(8,128)S(1)}, u32[]{:S(2)}, u32[]{:S(2)}) %collective-permute-start.2) | collective-permute-done | bytes 274464 | tf_op jit(solution)/shard_map/ppermute | solution.py:29
  19.3 0.0 copy-start.1
  19.3 1.3 %collective-permute-start.5 = (f32[8,128]{1,0:T(8,128)S(1)}, f32[8,128]{1,0:T(8,128)S(1)}, u32[]{:S(2)}, u32[]{:S(2)}) collective-permute-start(f32[8,128]{1,0:T(8,128)S(1)} %slice_add_fusion.1), channel_id=1, source_target_pairs={{0,1},{1,0},{2,3},{3,2},{4,5},{5,4},{6,7},{7,6},{8,9},{9,8},{10,11... | collective-permute-start | bytes 12296 | tf_op jit(solution)/shard_map/ppermute | solution.py:29
  20.6 1.4 %shard_map.59.start = f32[1024,128]{1,0:T(8,128)S(1)} custom-call(f32[1024,128]{1,0:T(8,128)S(1)} %shard_map.57.start, f32[536,128]{1,0:T(8,128)S(1)} %collective-permute-done.1.p0, f32[536,128]{1,0:T(8,128)S(1)} %collective-permute-done.2.p1), custom_call_target="tpu_custom_call" | custom-call | flops 10000000 | bytes 39062 | tf_op jit(solution)/shard_map/pallas_call | solution.py:435
  22.0 0.0 collective-permute-done.3.payload
  22.0 0.0 collective-permute-done.4.tiny_a
  22.0 0.0 collective-permute-done.5.tiny_b
  22.0 0.0 copy-done.1
  22.1 1.5 %shard_map.60 = f32[1024,128]{1,0:T(8,128)S(1)} custom-call(f32[1024,128]{1,0:T(8,128)S(1)} %shard_map.59.start, f32[528,128]{1,0:T(8,128)S(1)} %collective-permute-done.3.payload, f32[8,128]{1,0:T(8,128)S(1)} %collective-permute-done.4.tiny_a, f32[8,128]{1,0:T(8,128)S(1)} %collective-permute-done.5.tiny_b, f32[2,128,128]{2,1,0:T(8,128)S(1)} %copy-done.1), custom_call_target="tpu_custom_call" | custom-call | flops 10000000 | bytes 39062 | tf_op jit(solution)/shard_map/pallas_call | solution.py:436
  23.6 0.0 copy-start.4
  23.6 15.1 %all_to_all.10.x = f32[8,128,128]{2,1,0:T(8,128)S(1)} all-to-all(f32[8,128,128]{2,1,0:T(8,128)S(1)} %bitcast.8), channel_id=1, replica_groups=mesh['grp'=8,'tile'=32] {'grp'}, dimensions={0} | all-to-all | bytes 1048576 | tf_op jit(solution)/shard_map/all_to_all | solution.py:471
  38.7 0.0 copy-done.4
  38.7 0.4 shard_map.61
  39.1 11.8 %all_to_all.11 = f32[8,128,128]{2,1,0:T(8,128)S(1)} all-to-all(f32[8,128,128]{2,1,0:T(8,128)S(1)} %shard_map.61), channel_id=1, replica_groups=mesh['grp'=8,'tile'=32] {'grp'}, dimensions={0} | all-to-all | bytes 1048576 | tf_op jit(solution)/shard_map/all_to_all | solution.py:473
  50.9 0.8 %shard_map.62 = (f32[536,128]{1,0:T(8,128)S(1)}, f32[536,128]{1,0:T(8,128)S(1)}, bf16[1024,256]{1,0:T(8,128)(2,1)S(1)}, f32[40,128]{1,0:T(8,128)S(1)}) custom-call(s32[1]{0:T(128)} %bitcast.self_ref, f32[1024,128]{1,0:T(8,128)S(1)} %bitcast.6, s32[1,1024]{1,0:T(1,128)S(1)} %get-tuple-element.60.keys, bf16[80,1024]{1,0:T(8,128)(2,1)S(1)} %get-tuple-element.61.spills, ...), custom_call_target="tpu_custom_call" | custom-call | tf_op jit(solution)/shard_map/pallas_call | solution.py:476
  51.7 1.7 %collective-permute-start.7 = (f32[536,128]{1,0:T(8,128)S(1)}, f32[536,128]{1,0:T(8,128)S(1)}, u32[]{:S(2)}, u32[]{:S(2)}) collective-permute-start(f32[536,128]{1,0:T(8,128)S(1)} %get-tuple-element.67), channel_id=1, source_target_pairs={{0,2},{1,3},{2,0},{3,1},{4,6},{5,7},{6,4},{7,5},{8,10},{9,11},{10,... | collective-permute-start | bytes 823304 | tf_op jit(solution)/shard_map/ppermute | solution.py:29
  53.4 6.1 %collective-permute-start.8 = (f32[536,128]{1,0:T(8,128)S(1)}, f32[536,128]{1,0:T(8,128)S(1)}, u32[]{:S(2)}, u32[]{:S(2)}) collective-permute-start(f32[536,128]{1,0:T(8,128)S(1)} %get-tuple-element.68), channel_id=1, source_target_pairs={{0,30},{1,31},{2,4},{3,5},{4,2},{5,3},{6,8},{7,9},{8,6},{9,7},{10,... | collective-permute-start | bytes 823304 | tf_op jit(solution)/shard_map/ppermute | solution.py:29
  59.5 0.7 shard_map.63
  60.2 2.0 %collective-permute-start.6 = (f32[528,128]{1,0:T(8,128)S(1)}, f32[528,128]{1,0:T(8,128)S(1)}, u32[]{:S(2)}, u32[]{:S(2)}) collective-permute-start(f32[528,128]{1,0:T(8,128)S(1)} %get-tuple-element.66), channel_id=1, source_target_pairs={{0,1},{1,0},{2,3},{3,2},{4,5},{5,4},{6,7},{7,6},{8,9},{9,8},{10,11... | collective-permute-start | bytes 811016 | tf_op jit(solution)/shard_map/ppermute | solution.py:29
  62.2 0.0 collective-permute-start.9
  62.2 1.2 %collective-permute-done.6.payload = f32[528,128]{1,0:T(8,128)S(1)} collective-permute-done((f32[528,128]{1,0:T(8,128)S(1)}, f32[528,128]{1,0:T(8,128)S(1)}, u32[]{:S(2)}, u32[]{:S(2)}) %collective-permute-start.6) | collective-permute-done | bytes 270368 | tf_op jit(solution)/shard_map/ppermute | solution.py:29
  63.4 0.0 collective-permute-start.10
  63.4 2.0 %shard_map.64.start = f32[1024,128]{1,0:T(8,128)S(1)} custom-call(s32[1]{0:T(128)} %bitcast.self_ref, f32[1024,128]{1,0:T(8,128)S(1)} %bitcast.7, s32[2,1024]{1,0:T(2,128)S(1)} %copy-done.2, f32[2,1024]{1,0:T(2,128)S(1)} %copy-done.3, f32[8,128]{1,0:T(8,128)S(1)} %get-tuple-element.65.spilled, f32[528,128]{1,0:T(8,128)S(1)} %collective-permute-done.6.payload), custom_call_target="tpu_custom_call" | custom-call | flops 10000000 | bytes 39062 | tf_op jit(solution)/shard_map/pallas_call | solution.py:411
  65.4 0.0 collective-permute-done.7.p0
  65.4 0.0 collective-permute-done.8.p1
  65.4 1.6 %collective-permute-start.11 = (f32[8,128]{1,0:T(8,128)S(1)}, f32[8,128]{1,0:T(8,128)S(1)}, u32[]{:S(2)}, u32[]{:S(2)}) collective-permute-start(f32[8,128]{1,0:T(8,128)S(1)} %slice_add_fusion), channel_id=1, source_target_pairs={{0,1},{1,0},{2,3},{3,2},{4,5},{5,4},{6,7},{7,6},{8,9},{9,8},{10,11... | collective-permute-start | bytes 12296 | tf_op jit(solution)/shard_map/ppermute | solution.py:29
  67.0 1.4 %shard_map.65.start = f32[1024,128]{1,0:T(8,128)S(1)} custom-call(f32[1024,128]{1,0:T(8,128)S(1)} %shard_map.64.start, f32[536,128]{1,0:T(8,128)S(1)} %collective-permute-done.7.p0, f32[536,128]{1,0:T(8,128)S(1)} %collective-permute-done.8.p1), custom_call_target="tpu_custom_call" | custom-call | flops 10000000 | bytes 39062 | tf_op jit(solution)/shard_map/pallas_call | solution.py:435
  68.4 0.1 collective-permute-done.9.payload
  68.5 0.0 collective-permute-done.10.tiny_a
  68.5 0.0 collective-permute-done.11.tiny_b
  68.5 1.8 %shard_map.66 = f32[1024,128]{1,0:T(8,128)} custom-call(f32[1024,128]{1,0:T(8,128)S(1)} %shard_map.65.start, f32[528,128]{1,0:T(8,128)S(1)} %collective-permute-done.9.payload, f32[8,128]{1,0:T(8,128)S(1)} %collective-permute-done.10.tiny_a, f32[8,128]{1,0:T(8,128)S(1)} %collective-permute-done.11.tiny_b, f32[2,128,128]{2,1,0:T(8,128)S(1)} %copy-done.1), custom_call_target="tpu_custom_call" | custom-call | flops 10000000 | bytes 39062 | tf_op jit(solution)/shard_map/pallas_call | solution.py:436
  (2 shorter events, 0.0 us)
Async XLA Ops:
  2.4 10.2 %copy-start = (f32[1024,128]{1,0:T(8,128)S(1)}, f32[1024,128]{1,0:T(8,128)}, u32[]{:S(2)}) copy-start(f32[1024,128]{1,0:T(8,128)} %field.1) | copy-start | bytes 1572868
  2.4 10.2 %copy-start.3 = (f32[2,1024]{1,0:T(2,128)S(1)}, f32[2,1024]{1,0:T(2,128)}, u32[]{:S(2)}) copy-start(f32[2,1024]{1,0:T(2,128)} %fraction.5) | copy-start | bytes 24580
  3.7 9.0 %copy-start.2 = (s32[2,1024]{1,0:T(2,128)S(1)}, s32[2,1024]{1,0:T(2,128)}, u32[]{:S(2)}) copy-start(s32[2,1024]{1,0:T(2,128)} %departure.5) | copy-start | bytes 24580
  3.7 8.9 %collective-permute-start = (f32[528,128]{1,0:T(8,128)S(1)}, f32[528,128]{1,0:T(8,128)S(1)}, u32[]{:S(2)}, u32[]{:S(2)}) collective-permute-start(f32[528,128]{1,0:T(8,128)S(1)} %get-tuple-element.45), channel_id=1, source_target_pairs={{0,1},{1,0},{2,3},{3,2},{4,5},{5,4},{6,7},{7,6},{8,9},{9,8},{10,11... | collective-permute-start | bytes 811016 | tf_op jit(solution)/shard_map/ppermute | solution.py:29
  7.0 9.0 %collective-permute-start.1 = (f32[536,128]{1,0:T(8,128)S(1)}, f32[536,128]{1,0:T(8,128)S(1)}, u32[]{:S(2)}, u32[]{:S(2)}) collective-permute-start(f32[536,128]{1,0:T(8,128)S(1)} %get-tuple-element.52), channel_id=1, source_target_pairs={{0,2},{1,3},{2,0},{3,1},{4,6},{5,7},{6,4},{7,5},{8,10},{9,11},{10,... | collective-permute-start | bytes 823304 | tf_op jit(solution)/shard_map/ppermute | solution.py:29
  7.0 12.2 %collective-permute-start.2 = (f32[536,128]{1,0:T(8,128)S(1)}, f32[536,128]{1,0:T(8,128)S(1)}, u32[]{:S(2)}, u32[]{:S(2)}) collective-permute-start(f32[536,128]{1,0:T(8,128)S(1)} %get-tuple-element.53), channel_id=1, source_target_pairs={{0,30},{1,31},{2,4},{3,5},{4,2},{5,3},{6,8},{7,9},{8,6},{9,7},{10,... | collective-permute-start | bytes 823304 | tf_op jit(solution)/shard_map/ppermute | solution.py:29
  12.6 9.4 %collective-permute-start.3 = (f32[528,128]{1,0:T(8,128)S(1)}, f32[528,128]{1,0:T(8,128)S(1)}, u32[]{:S(2)}, u32[]{:S(2)}) collective-permute-start(f32[528,128]{1,0:T(8,128)S(1)} %get-tuple-element.57), channel_id=1, source_target_pairs={{0,31},{1,2},{2,1},{3,4},{4,3},{5,6},{6,5},{7,8},{8,7},{9,10},{10,... | collective-permute-start | bytes 811016 | tf_op jit(solution)/shard_map/ppermute | solution.py:29
  12.6 9.4 %collective-permute-start.4 = (f32[8,128]{1,0:T(8,128)S(1)}, f32[8,128]{1,0:T(8,128)S(1)}, u32[]{:S(2)}, u32[]{:S(2)}) collective-permute-start(f32[8,128]{1,0:T(8,128)S(1)} %get-tuple-element.59), channel_id=1, source_target_pairs={{0,29},{1,4},{2,31},{3,6},{4,1},{5,8},{6,3},{7,10},{8,5},{9,12},{1... | collective-permute-start | bytes 12296 | tf_op jit(solution)/shard_map/ppermute | solution.py:29
  19.3 2.8 %copy-start.1 = (f32[2,128,128]{2,1,0:T(8,128)S(1)}, f32[2,128,128]{2,1,0:T(8,128)}, u32[]{:S(2)}) copy-start(f32[2,128,128]{2,1,0:T(8,128)} %level_map.3) | copy-start | bytes 393220
  19.3 2.7 %collective-permute-start.5 = (f32[8,128]{1,0:T(8,128)S(1)}, f32[8,128]{1,0:T(8,128)S(1)}, u32[]{:S(2)}, u32[]{:S(2)}) collective-permute-start(f32[8,128]{1,0:T(8,128)S(1)} %slice_add_fusion.1), channel_id=1, source_target_pairs={{0,1},{1,0},{2,3},{3,2},{4,5},{5,4},{6,7},{7,6},{8,9},{9,8},{10,11... | collective-permute-start | bytes 12296 | tf_op jit(solution)/shard_map/ppermute | solution.py:29
  23.6 15.2 %copy-start.4 = (f32[128,8,8]{0,2,1:T(8,128)S(1)}, f32[128,8,8]{0,2,1:T(8,128)}, u32[]{:S(2)}) copy-start(f32[128,8,8]{0,2,1:T(8,128)} %param.9) | copy-start | bytes 98308
  51.7 13.6 %collective-permute-start.7 = (f32[536,128]{1,0:T(8,128)S(1)}, f32[536,128]{1,0:T(8,128)S(1)}, u32[]{:S(2)}, u32[]{:S(2)}) collective-permute-start(f32[536,128]{1,0:T(8,128)S(1)} %get-tuple-element.67), channel_id=1, source_target_pairs={{0,2},{1,3},{2,0},{3,1},{4,6},{5,7},{6,4},{7,5},{8,10},{9,11},{10,... | collective-permute-start | bytes 823304 | tf_op jit(solution)/shard_map/ppermute | solution.py:29
  53.4 11.9 %collective-permute-start.8 = (f32[536,128]{1,0:T(8,128)S(1)}, f32[536,128]{1,0:T(8,128)S(1)}, u32[]{:S(2)}, u32[]{:S(2)}) collective-permute-start(f32[536,128]{1,0:T(8,128)S(1)} %get-tuple-element.68), channel_id=1, source_target_pairs={{0,30},{1,31},{2,4},{3,5},{4,2},{5,3},{6,8},{7,9},{8,6},{9,7},{10,... | collective-permute-start | bytes 823304 | tf_op jit(solution)/shard_map/ppermute | solution.py:29
  60.2 3.2 %collective-permute-start.6 = (f32[528,128]{1,0:T(8,128)S(1)}, f32[528,128]{1,0:T(8,128)S(1)}, u32[]{:S(2)}, u32[]{:S(2)}) collective-permute-start(f32[528,128]{1,0:T(8,128)S(1)} %get-tuple-element.66), channel_id=1, source_target_pairs={{0,1},{1,0},{2,3},{3,2},{4,5},{5,4},{6,7},{7,6},{8,9},{9,8},{10,11... | collective-permute-start | bytes 811016 | tf_op jit(solution)/shard_map/ppermute | solution.py:29
  62.2 6.2 %collective-permute-start.9 = (f32[528,128]{1,0:T(8,128)S(1)}, f32[528,128]{1,0:T(8,128)S(1)}, u32[]{:S(2)}, u32[]{:S(2)}) collective-permute-start(f32[528,128]{1,0:T(8,128)S(1)} %get-tuple-element.72), channel_id=1, source_target_pairs={{0,31},{1,2},{2,1},{3,4},{4,3},{5,6},{6,5},{7,8},{8,7},{9,10},{10,... | collective-permute-start | bytes 811016 | tf_op jit(solution)/shard_map/ppermute | solution.py:29
  63.4 5.1 %collective-permute-start.10 = (f32[8,128]{1,0:T(8,128)S(1)}, f32[8,128]{1,0:T(8,128)S(1)}, u32[]{:S(2)}, u32[]{:S(2)}) collective-permute-start(f32[8,128]{1,0:T(8,128)S(1)} %get-tuple-element.74), channel_id=1, source_target_pairs={{0,29},{1,4},{2,31},{3,6},{4,1},{5,8},{6,3},{7,10},{8,5},{9,12},{1... | collective-permute-start | bytes 12296 | tf_op jit(solution)/shard_map/ppermute | solution.py:29
  65.4 3.1 %collective-permute-start.11 = (f32[8,128]{1,0:T(8,128)S(1)}, f32[8,128]{1,0:T(8,128)S(1)}, u32[]{:S(2)}, u32[]{:S(2)}) collective-permute-start(f32[8,128]{1,0:T(8,128)S(1)} %slice_add_fusion), channel_id=1, source_target_pairs={{0,1},{1,0},{2,3},{3,2},{4,5},{5,4},{6,7},{7,6},{8,9},{9,8},{10,11... | collective-permute-start | bytes 12296 | tf_op jit(solution)/shard_map/ppermute | solution.py:29

commit v13 on v12

--- a/solution.py
+++ b/solution.py
@@ -240,7 +240,7 @@
 
 
 BLOCK = 1024
-HALF = 512
+HALF = 256
 I16 = jnp.int16
 
 

time: 70.8 us -> 70.8 us (level)
  no operation moved by 1% of the time
where the time goes in v13:
time: 70.8 us; the launch traced here: 70.3 us
  blocking collectives  27 us (38%)
  starting transfers between devices  21.7 us (31%)
  Pallas kernels  16.8 us (24%)
  waiting for transfers between devices  4.51 us (6%)
    ppermute x12, starting transfers between devices, swapped(): lax.ppermute(x, 'tile', [(i, (i + signs(i)[which]) % length) for i in ran...  21.7 us
    all_to_all x1, blocking collectives, body(): lax.all_to_all(second.reshape(groups, COLS // groups, LEV), 'grp', 0, 0)  15.1 us
    all_to_all x1, blocking collectives, body(): coupled = lax.all_to_all(mixed, 'grp', 0, 0).reshape(COLS, LEV)  11.8 us
    ppermute x12, waiting for transfers between devices, swapped(): lax.ppermute(x, 'tile', [(i, (i + signs(i)[which]) % length) for i in ran...  4.51 us
    pallas_call x2, Pallas kernels, transported(): call(functools.partial(own_kernel, step, tile_count), total, [SM] + [VM]...  3.93 us
    pallas_call x2, Pallas kernels, transported(): call(functools.partial(last_kernel, step), total, [VM] * 5, [one, pltpu.V...  3.22 us
    pallas_call x2, Pallas kernels, transported(): call(middle_kernel, total, [VM] * 3, [pltpu.VMEM((2, CAP, 2 * LEV), BF)],...  2.73 us
    pallas_call x1, Pallas kernels, body(): call(functools.partial(first_far_kernel, tile_count), outputs, [SM, HBM,...  2.42 us
  transfers between devices with their start and end apart: 12, of which 3 were waited for; matrix products, arithmetic and copies ran while one was open for 0% of the time, Pallas kernels for 12%

profile of v13, /device:TPU:1, one launch (start us, length us, event | category | flops | bytes accessed | tf_op | source)
XLA Modules:
  0.0 70.3 jit_solution(17928762817294657449)
XLA Ops:
  0.0 2.4 %shard_map.55 = (f32[536,128]{1,0:T(8,128)S(1)}, f32[536,128]{1,0:T(8,128)S(1)}, bf16[1024,256]{1,0:T(8,128)(2,1)S(1)}, f32[40,128]{1,0:T(8,128)S(1)}, s32[1,102...) custom-call(s32[1]{0:T(128)} %bitcast.self_ref, f32[1024,128]{1,0:T(8,128)} %field.1, s32[2,1024]{1,0:T(2,128)} %departure.5, ...), custom_call_target="tpu_custom_call" | custom-call | tf_op jit(solution)/shard_map/pallas_call | solution.py:463
  2.4 0.0 copy-start
  2.4 0.0 copy-start.3
  2.5 1.2 %shard_map.56 = (f32[528,128]{1,0:T(8,128)S(1)}, f32[528,128]{1,0:T(8,128)S(1)}, f32[8,128]{1,0:T(8,128)S(1)}, f32[8,128]{1,0:T(8,128)S(1)}) custom-call(s32[1]{0:T(128)} %bitcast.self_ref, bf16[1024,256]{1,0:T(8,128)(2,1)S(1)} %get-tuple-element.40.both, f32[40,128]{1,0:T(8,128)S(1)} %get-tuple-element.41.spilled, s32[1,1024]{1,0:T(1,128)S(1)} %get-tuple-element.42.keys, ...), custom_call_target="tpu_custom_call" | custom-call | flops 1000000000 | bytes 3906250 | tf_op jit(solution)/shard_map/pallas_call | solution.py:401
  3.7 0.0 copy-start.2
  3.7 3.3 %collective-permute-start = (f32[528,128]{1,0:T(8,128)S(1)}, f32[528,128]{1,0:T(8,128)S(1)}, u32[]{:S(2)}, u32[]{:S(2)}) collective-permute-start(f32[528,128]{1,0:T(8,128)S(1)} %get-tuple-element.45), channel_id=1, source_target_pairs={{0,1},{1,0},{2,3},{3,2},{4,5},{5,4},{6,7},{7,6},{8,9},{9,8},{10,11... | collective-permute-start | bytes 811016 | tf_op jit(solution)/shard_map/ppermute | solution.py:29
  7.0 0.0 collective-permute-start.1
  7.0 5.6 %collective-permute-start.2 = (f32[536,128]{1,0:T(8,128)S(1)}, f32[536,128]{1,0:T(8,128)S(1)}, u32[]{:S(2)}, u32[]{:S(2)}) collective-permute-start(f32[536,128]{1,0:T(8,128)S(1)} %get-tuple-element.53), channel_id=1, source_target_pairs={{0,30},{1,31},{2,4},{3,5},{4,2},{5,3},{6,8},{7,9},{8,6},{9,7},{10,... | collective-permute-start | bytes 823304 | tf_op jit(solution)/shard_map/ppermute | solution.py:29
  12.6 0.0 collective-permute-start.3
  12.6 0.0 collective-permute-done.payload
  12.6 0.0 collective-permute-start.4
  12.7 0.0 copy-done
  12.7 0.0 copy-done.3
  12.7 0.0 copy-done.2
  12.7 2.0 %shard_map.57.start = f32[1024,128]{1,0:T(8,128)S(1)} custom-call(s32[1]{0:T(128)} %bitcast.self_ref, f32[1024,128]{1,0:T(8,128)S(1)} %copy-done, s32[2,1024]{1,0:T(2,128)S(1)} %copy-done.2, f32[2,1024]{1,0:T(2,128)S(1)} %copy-done.3, f32[8,128]{1,0:T(8,128)S(1)} %get-tuple-element.44.spilled, f32[528,128]{1,0:T(8,128)S(1)} %collective-permute-done.payload), custom_call_target="tpu_custom_call" | custom-call | flops 10000000 | bytes 39062 | tf_op jit(solution)/shard_map/pallas_call | solution.py:411
  14.7 1.4 %shard_map.58 = (s32[1,1024]{1,0:T(1,128)S(1)}, bf16[80,1024]{1,0:T(8,128)(2,1)S(1)}, f32[32,128]{1,0:T(8,128)S(1)}) custom-call(s32[1]{0:T(128)} %bitcast.self_ref, s32[2,1024]{1,0:T(2,128)S(1)} %copy-done.2, f32[2,1024]{1,0:T(2,128)S(1)} %copy-done.3), custom_call_target="tpu_custom_call" | custom-call | flops 300000000 | bytes 1171875 | tf_op jit(solution)/shard_map/pallas_call | solution.py:421
  16.0 0.0 collective-permute-done.1.p0
  16.0 3.3 %collective-permute-done.2.p1 = f32[536,128]{1,0:T(8,128)S(1)} collective-permute-done((f32[536,128]{1,0:T(8,128)S(1)}, f32[536,128]{1,0:T(8,128)S(1)}, u32[]{:S(2)}, u32[]{:S(2)}) %collective-permute-start.2) | collective-permute-done | bytes 274464 | tf_op jit(solution)/shard_map/ppermute | solution.py:29
  19.3 0.0 copy-start.1
  19.3 1.3 %collective-permute-start.5 = (f32[8,128]{1,0:T(8,128)S(1)}, f32[8,128]{1,0:T(8,128)S(1)}, u32[]{:S(2)}, u32[]{:S(2)}) collective-permute-start(f32[8,128]{1,0:T(8,128)S(1)} %slice_add_fusion.1), channel_id=1, source_target_pairs={{0,1},{1,0},{2,3},{3,2},{4,5},{5,4},{6,7},{7,6},{8,9},{9,8},{10,11... | collective-permute-start | bytes 12296 | tf_op jit(solution)/shard_map/ppermute | solution.py:29
  20.6 1.4 %shard_map.59.start = f32[1024,128]{1,0:T(8,128)S(1)} custom-call(f32[1024,128]{1,0:T(8,128)S(1)} %shard_map.57.start, f32[536,128]{1,0:T(8,128)S(1)} %collective-permute-done.1.p0, f32[536,128]{1,0:T(8,128)S(1)} %collective-permute-done.2.p1), custom_call_target="tpu_custom_call" | custom-call | flops 10000000 | bytes 39062 | tf_op jit(solution)/shard_map/pallas_call | solution.py:435
  22.0 0.0 collective-permute-done.3.payload
  22.0 0.0 collective-permute-done.4.tiny_a
  22.0 0.0 collective-permute-done.5.tiny_b
  22.0 0.0 copy-done.1
  22.1 1.5 %shard_map.60 = f32[1024,128]{1,0:T(8,128)S(1)} custom-call(f32[1024,128]{1,0:T(8,128)S(1)} %shard_map.59.start, f32[528,128]{1,0:T(8,128)S(1)} %collective-permute-done.3.payload, f32[8,128]{1,0:T(8,128)S(1)} %collective-permute-done.4.tiny_a, f32[8,128]{1,0:T(8,128)S(1)} %collective-permute-done.5.tiny_b, f32[2,128,128]{2,1,0:T(8,128)S(1)} %copy-done.1), custom_call_target="tpu_custom_call" | custom-call | flops 10000000 | bytes 39062 | tf_op jit(solution)/shard_map/pallas_call | solution.py:436
  23.6 0.0 copy-start.4
  23.6 15.1 %all_to_all.10.x = f32[8,128,128]{2,1,0:T(8,128)S(1)} all-to-all(f32[8,128,128]{2,1,0:T(8,128)S(1)} %bitcast.8), channel_id=1, replica_groups=mesh['grp'=8,'tile'=32] {'grp'}, dimensions={0} | all-to-all | bytes 1048576 | tf_op jit(solution)/shard_map/all_to_all | solution.py:471
  38.7 0.0 copy-done.4
  38.7 0.4 shard_map.61
  39.1 11.8 %all_to_all.11 = f32[8,128,128]{2,1,0:T(8,128)S(1)} all-to-all(f32[8,128,128]{2,1,0:T(8,128)S(1)} %shard_map.61), channel_id=1, replica_groups=mesh['grp'=8,'tile'=32] {'grp'}, dimensions={0} | all-to-all | bytes 1048576 | tf_op jit(solution)/shard_map/all_to_all | solution.py:473
  51.0 0.8 %shard_map.62 = (f32[536,128]{1,0:T(8,128)S(1)}, f32[536,128]{1,0:T(8,128)S(1)}, bf16[1024,256]{1,0:T(8,128)(2,1)S(1)}, f32[40,128]{1,0:T(8,128)S(1)}) custom-call(s32[1]{0:T(128)} %bitcast.self_ref, f32[1024,128]{1,0:T(8,128)S(1)} %bitcast.6, s32[1,1024]{1,0:T(1,128)S(1)} %get-tuple-element.60.keys, bf16[80,1024]{1,0:T(8,128)(2,1)S(1)} %get-tuple-element.61.spills, ...), custom_call_target="tpu_custom_call" | custom-call | tf_op jit(solution)/shard_map/pallas_call | solution.py:476
  51.8 1.7 %collective-permute-start.7 = (f32[536,128]{1,0:T(8,128)S(1)}, f32[536,128]{1,0:T(8,128)S(1)}, u32[]{:S(2)}, u32[]{:S(2)}) collective-permute-start(f32[536,128]{1,0:T(8,128)S(1)} %get-tuple-element.67), channel_id=1, source_target_pairs={{0,2},{1,3},{2,0},{3,1},{4,6},{5,7},{6,4},{7,5},{8,10},{9,11},{10,... | collective-permute-start | bytes 823304 | tf_op jit(solution)/shard_map/ppermute | solution.py:29
  53.5 6.1 %collective-permute-start.8 = (f32[536,128]{1,0:T(8,128)S(1)}, f32[536,128]{1,0:T(8,128)S(1)}, u32[]{:S(2)}, u32[]{:S(2)}) collective-permute-start(f32[536,128]{1,0:T(8,128)S(1)} %get-tuple-element.68), channel_id=1, source_target_pairs={{0,30},{1,31},{2,4},{3,5},{4,2},{5,3},{6,8},{7,9},{8,6},{9,7},{10,... | collective-permute-start | bytes 823304 | tf_op jit(solution)/shard_map/ppermute | solution.py:29
  59.5 0.7 %shard_map.63 = (f32[528,128]{1,0:T(8,128)S(1)}, f32[528,128]{1,0:T(8,128)S(1)}, f32[8,128]{1,0:T(8,128)S(1)}, f32[8,128]{1,0:T(8,128)S(1)}) custom-call(s32[1]{0:T(128)} %bitcast.self_ref, bf16[1024,256]{1,0:T(8,128)(2,1)S(1)} %get-tuple-element.63.both, f32[40,128]{1,0:T(8,128)S(1)} %get-tuple-element.64.spilled, s32[1,1024]{1,0:T(1,128)S(1)} %get-tuple-element.60.keys, ...), custom_call_target="tpu_custom_call" | custom-call | flops 1000000000 | bytes 3906250 | tf_op jit(solution)/shard_map/pallas_call | solution.py:401
  60.2 2.0 %collective-permute-start.6 = (f32[528,128]{1,0:T(8,128)S(1)}, f32[528,128]{1,0:T(8,128)S(1)}, u32[]{:S(2)}, u32[]{:S(2)}) collective-permute-start(f32[528,128]{1,0:T(8,128)S(1)} %get-tuple-element.66), channel_id=1, source_target_pairs={{0,1},{1,0},{2,3},{3,2},{4,5},{5,4},{6,7},{7,6},{8,9},{9,8},{10,11... | collective-permute-start | bytes 811016 | tf_op jit(solution)/shard_map/ppermute | solution.py:29
  62.3 0.0 collective-permute-start.9
  62.3 1.2 %collective-permute-done.6.payload = f32[528,128]{1,0:T(8,128)S(1)} collective-permute-done((f32[528,128]{1,0:T(8,128)S(1)}, f32[528,128]{1,0:T(8,128)S(1)}, u32[]{:S(2)}, u32[]{:S(2)}) %collective-permute-start.6) | collective-permute-done | bytes 270368 | tf_op jit(solution)/shard_map/ppermute | solution.py:29
  63.4 0.0 collective-permute-start.10
  63.4 2.0 %shard_map.64.start = f32[1024,128]{1,0:T(8,128)S(1)} custom-call(s32[1]{0:T(128)} %bitcast.self_ref, f32[1024,128]{1,0:T(8,128)S(1)} %bitcast.7, s32[2,1024]{1,0:T(2,128)S(1)} %copy-done.2, f32[2,1024]{1,0:T(2,128)S(1)} %copy-done.3, f32[8,128]{1,0:T(8,128)S(1)} %get-tuple-element.65.spilled, f32[528,128]{1,0:T(8,128)S(1)} %collective-permute-done.6.payload), custom_call_target="tpu_custom_call" | custom-call | flops 10000000 | bytes 39062 | tf_op jit(solution)/shard_map/pallas_call | solution.py:411
  65.4 0.0 collective-permute-done.7.p0
  65.4 0.0 collective-permute-done.8.p1
  65.4 1.6 %collective-permute-start.11 = (f32[8,128]{1,0:T(8,128)S(1)}, f32[8,128]{1,0:T(8,128)S(1)}, u32[]{:S(2)}, u32[]{:S(2)}) collective-permute-start(f32[8,128]{1,0:T(8,128)S(1)} %slice_add_fusion), channel_id=1, source_target_pairs={{0,1},{1,0},{2,3},{3,2},{4,5},{5,4},{6,7},{7,6},{8,9},{9,8},{10,11... | collective-permute-start | bytes 12296 | tf_op jit(solution)/shard_map/ppermute | solution.py:29
  67.1 1.4 %shard_map.65.start = f32[1024,128]{1,0:T(8,128)S(1)} custom-call(f32[1024,128]{1,0:T(8,128)S(1)} %shard_map.64.start, f32[536,128]{1,0:T(8,128)S(1)} %collective-permute-done.7.p0, f32[536,128]{1,0:T(8,128)S(1)} %collective-permute-done.8.p1), custom_call_target="tpu_custom_call" | custom-call | flops 10000000 | bytes 39062 | tf_op jit(solution)/shard_map/pallas_call | solution.py:435
  68.4 0.1 collective-permute-done.9.payload
  68.5 0.0 collective-permute-done.10.tiny_a
  68.5 0.0 collective-permute-done.11.tiny_b
  68.5 1.7 %shard_map.66 = f32[1024,128]{1,0:T(8,128)} custom-call(f32[1024,128]{1,0:T(8,128)S(1)} %shard_map.65.start, f32[528,128]{1,0:T(8,128)S(1)} %collective-permute-done.9.payload, f32[8,128]{1,0:T(8,128)S(1)} %collective-permute-done.10.tiny_a, f32[8,128]{1,0:T(8,128)S(1)} %collective-permute-done.11.tiny_b, f32[2,128,128]{2,1,0:T(8,128)S(1)} %copy-done.1), custom_call_target="tpu_custom_call" | custom-call | flops 10000000 | bytes 39062 | tf_op jit(solution)/shard_map/pallas_call | solution.py:436
  (2 shorter events, 0.0 us)
Async XLA Ops:
  2.4 10.2 %copy-start = (f32[1024,128]{1,0:T(8,128)S(1)}, f32[1024,128]{1,0:T(8,128)}, u32[]{:S(2)}) copy-start(f32[1024,128]{1,0:T(8,128)} %field.1) | copy-start | bytes 1572868
  2.4 10.2 %copy-start.3 = (f32[2,1024]{1,0:T(2,128)S(1)}, f32[2,1024]{1,0:T(2,128)}, u32[]{:S(2)}) copy-start(f32[2,1024]{1,0:T(2,128)} %fraction.5) | copy-start | bytes 24580
  3.7 9.0 %copy-start.2 = (s32[2,1024]{1,0:T(2,128)S(1)}, s32[2,1024]{1,0:T(2,128)}, u32[]{:S(2)}) copy-start(s32[2,1024]{1,0:T(2,128)} %departure.5) | copy-start | bytes 24580
  3.7 8.9 %collective-permute-start = (f32[528,128]{1,0:T(8,128)S(1)}, f32[528,128]{1,0:T(8,128)S(1)}, u32[]{:S(2)}, u32[]{:S(2)}) collective-permute-start(f32[528,128]{1,0:T(8,128)S(1)} %get-tuple-element.45), channel_id=1, source_target_pairs={{0,1},{1,0},{2,3},{3,2},{4,5},{5,4},{6,7},{7,6},{8,9},{9,8},{10,11... | collective-permute-start | bytes 811016 | tf_op jit(solution)/shard_map/ppermute | solution.py:29
  7.0 9.0 %collective-permute-start.1 = (f32[536,128]{1,0:T(8,128)S(1)}, f32[536,128]{1,0:T(8,128)S(1)}, u32[]{:S(2)}, u32[]{:S(2)}) collective-permute-start(f32[536,128]{1,0:T(8,128)S(1)} %get-tuple-element.52), channel_id=1, source_target_pairs={{0,2},{1,3},{2,0},{3,1},{4,6},{5,7},{6,4},{7,5},{8,10},{9,11},{10,... | collective-permute-start | bytes 823304 | tf_op jit(solution)/shard_map/ppermute | solution.py:29
  7.0 12.2 %collective-permute-start.2 = (f32[536,128]{1,0:T(8,128)S(1)}, f32[536,128]{1,0:T(8,128)S(1)}, u32[]{:S(2)}, u32[]{:S(2)}) collective-permute-start(f32[536,128]{1,0:T(8,128)S(1)} %get-tuple-element.53), channel_id=1, source_target_pairs={{0,30},{1,31},{2,4},{3,5},{4,2},{5,3},{6,8},{7,9},{8,6},{9,7},{10,... | collective-permute-start | bytes 823304 | tf_op jit(solution)/shard_map/ppermute | solution.py:29
  12.6 9.4 %collective-permute-start.3 = (f32[528,128]{1,0:T(8,128)S(1)}, f32[528,128]{1,0:T(8,128)S(1)}, u32[]{:S(2)}, u32[]{:S(2)}) collective-permute-start(f32[528,128]{1,0:T(8,128)S(1)} %get-tuple-element.57), channel_id=1, source_target_pairs={{0,31},{1,2},{2,1},{3,4},{4,3},{5,6},{6,5},{7,8},{8,7},{9,10},{10,... | collective-permute-start | bytes 811016 | tf_op jit(solution)/shard_map/ppermute | solution.py:29
  12.6 9.4 %collective-permute-start.4 = (f32[8,128]{1,0:T(8,128)S(1)}, f32[8,128]{1,0:T(8,128)S(1)}, u32[]{:S(2)}, u32[]{:S(2)}) collective-permute-start(f32[8,128]{1,0:T(8,128)S(1)} %get-tuple-element.59), channel_id=1, source_target_pairs={{0,29},{1,4},{2,31},{3,6},{4,1},{5,8},{6,3},{7,10},{8,5},{9,12},{1... | collective-permute-start | bytes 12296 | tf_op jit(solution)/shard_map/ppermute | solution.py:29
  19.3 2.8 %copy-start.1 = (f32[2,128,128]{2,1,0:T(8,128)S(1)}, f32[2,128,128]{2,1,0:T(8,128)}, u32[]{:S(2)}) copy-start(f32[2,128,128]{2,1,0:T(8,128)} %level_map.3) | copy-start | bytes 393220
  19.3 2.7 %collective-permute-start.5 = (f32[8,128]{1,0:T(8,128)S(1)}, f32[8,128]{1,0:T(8,128)S(1)}, u32[]{:S(2)}, u32[]{:S(2)}) collective-permute-start(f32[8,128]{1,0:T(8,128)S(1)} %slice_add_fusion.1), channel_id=1, source_target_pairs={{0,1},{1,0},{2,3},{3,2},{4,5},{5,4},{6,7},{7,6},{8,9},{9,8},{10,11... | collective-permute-start | bytes 12296 | tf_op jit(solution)/shard_map/ppermute | solution.py:29
  23.6 15.2 %copy-start.4 = (f32[128,8,8]{0,2,1:T(8,128)S(1)}, f32[128,8,8]{0,2,1:T(8,128)}, u32[]{:S(2)}) copy-start(f32[128,8,8]{0,2,1:T(8,128)} %param.9) | copy-start | bytes 98308
  51.8 13.6 %collective-permute-start.7 = (f32[536,128]{1,0:T(8,128)S(1)}, f32[536,128]{1,0:T(8,128)S(1)}, u32[]{:S(2)}, u32[]{:S(2)}) collective-permute-start(f32[536,128]{1,0:T(8,128)S(1)} %get-tuple-element.67), channel_id=1, source_target_pairs={{0,2},{1,3},{2,0},{3,1},{4,6},{5,7},{6,4},{7,5},{8,10},{9,11},{10,... | collective-permute-start | bytes 823304 | tf_op jit(solution)/shard_map/ppermute | solution.py:29
  53.5 12.0 %collective-permute-start.8 = (f32[536,128]{1,0:T(8,128)S(1)}, f32[536,128]{1,0:T(8,128)S(1)}, u32[]{:S(2)}, u32[]{:S(2)}) collective-permute-start(f32[536,128]{1,0:T(8,128)S(1)} %get-tuple-element.68), channel_id=1, source_target_pairs={{0,30},{1,31},{2,4},{3,5},{4,2},{5,3},{6,8},{7,9},{8,6},{9,7},{10,... | collective-permute-start | bytes 823304 | tf_op jit(solution)/shard_map/ppermute | solution.py:29
  60.2 3.2 %collective-permute-start.6 = (f32[528,128]{1,0:T(8,128)S(1)}, f32[528,128]{1,0:T(8,128)S(1)}, u32[]{:S(2)}, u32[]{:S(2)}) collective-permute-start(f32[528,128]{1,0:T(8,128)S(1)} %get-tuple-element.66), channel_id=1, source_target_pairs={{0,1},{1,0},{2,3},{3,2},{4,5},{5,4},{6,7},{7,6},{8,9},{9,8},{10,11... | collective-permute-start | bytes 811016 | tf_op jit(solution)/shard_map/ppermute | solution.py:29
  62.3 6.2 %collective-permute-start.9 = (f32[528,128]{1,0:T(8,128)S(1)}, f32[528,128]{1,0:T(8,128)S(1)}, u32[]{:S(2)}, u32[]{:S(2)}) collective-permute-start(f32[528,128]{1,0:T(8,128)S(1)} %get-tuple-element.72), channel_id=1, source_target_pairs={{0,31},{1,2},{2,1},{3,4},{4,3},{5,6},{6,5},{7,8},{8,7},{9,10},{10,... | collective-permute-start | bytes 811016 | tf_op jit(solution)/shard_map/ppermute | solution.py:29
  63.4 5.1 %collective-permute-start.10 = (f32[8,128]{1,0:T(8,128)S(1)}, f32[8,128]{1,0:T(8,128)S(1)}, u32[]{:S(2)}, u32[]{:S(2)}) collective-permute-start(f32[8,128]{1,0:T(8,128)S(1)} %get-tuple-element.74), channel_id=1, source_target_pairs={{0,29},{1,4},{2,31},{3,6},{4,1},{5,8},{6,3},{7,10},{8,5},{9,12},{1... | collective-permute-start | bytes 12296 | tf_op jit(solution)/shard_map/ppermute | solution.py:29
  65.4 3.1 %collective-permute-start.11 = (f32[8,128]{1,0:T(8,128)S(1)}, f32[8,128]{1,0:T(8,128)S(1)}, u32[]{:S(2)}, u32[]{:S(2)}) collective-permute-start(f32[8,128]{1,0:T(8,128)S(1)} %slice_add_fusion), channel_id=1, source_target_pairs={{0,1},{1,0},{2,3},{3,2},{4,5},{5,4},{6,7},{7,6},{8,9},{9,8},{10,11... | collective-permute-start | bytes 12296 | tf_op jit(solution)/shard_map/ppermute | solution.py:29
